TPU v7x, 32 devices: a whole 2x2x4 slice. The times are simulated.
32 devices in a mesh: arc: 8 (over z, x), vec: 4 (over y, core).
Axes of the slice: x: 2, y: 2, z: 4, core: 2. Of those that a mesh axis runs over, the one named last changes fastest.
Arguments:
- right_side: float32 [640, 128, 128], P(('arc', 'vec')), may hold values from -6 to 6
- prior_diag: float32 [640, 128], P(('arc', 'vec')), may hold values from 0.5 to 4
- inv_factor: bfloat16 [512, 256, 256], P(('arc', 'vec'))
- coupling_panel: bfloat16 [512, 256, 1024], P(('arc', 'vec')), may hold values from -0.09375 to 0.09375
- coupling_owner: int32 [512, 8], replicated, may hold values from 0 to 31, all different within a row; in each aligned block of 16 rows (0 to 15, 16 to 31, ...) at most 5 rows name the same one
- coupling_block: int32 [512, 8], replicated, may hold values from 0 to 19
Outputs:
- solution_field: float32 [640, 128, 128], P(('arc', 'vec'))
- residual: float32 [640, 128, 128], P(('arc', 'vec'))
Inputs may be any that keep to these rules, and one draw needn't show every extreme that they name: `coupling_owner`: the 8 holders named for one arc are different. Among the 16 arcs of one device (aligned blocks of rows) no holder is named more than 5 times; some holder is named exactly 5 times.
All inputs are finite; a program needn't handle non-finite values.
Results may differ from a plain program's by a relative error of at most 0.006.
The roundings to bfloat16 on the way count: a program that leaves them out, or rounds other values in their place, can miss the bound.
Values may be sent and summed in bfloat16 or wider, within the bound.
No kernel may reach another device: no remote copies, remote signals or barrier semaphores. Data moves between devices by JAX's collectives and lax.ppermute only.
A program may use at most 128 MiB of HBM per device.

v0:
```python
import functools

import jax
import jax.numpy as jnp
from jax import lax
from jax.experimental import pallas as pl
from jax.experimental.pallas import tpu as pltpu
from jax.sharding import PartitionSpec as P


ITERS = 2
GROUP = 2
AXES = ("arc", "vec")
SMEM = pltpu.MemorySpace.SMEM
VMEM = pltpu.MemorySpace.VMEM


def inner_gram(left, right):
    return jnp.einsum("grc,grd->cd", left, right, precision=lax.Precision.HIGHEST)


def combine_cols(field, weights):
    return jnp.einsum("grc,cd->grd", field, weights, precision=lax.Precision.HIGHEST)


def times_high(left, right):
    return jnp.dot(left, right, precision=lax.Precision.HIGHEST)


def trade(buffer):
    return lax.all_to_all(buffer, AXES, split_axis=0, concat_axis=0, tiled=True)


def sum_all(grams):
    device_count = lax.axis_size(AXES)
    stacked = jnp.concatenate(grams, axis=0)
    rows, cols = stacked.shape
    pieces = stacked.reshape(device_count, rows // device_count, cols)
    mine = jnp.sum(trade(pieces), axis=0)
    shared = jnp.broadcast_to(mine[None], pieces.shape)
    total = trade(shared).reshape(len(grams), rows // len(grams), cols)
    return total


class Plan:
    def __init__(self, mesh, arcs_here, links, blocks_here):
        arc, vec = mesh.shape["arc"], mesh.shape["vec"]
        half = max(1, vec // 2)
        self.rings = arc // half if arc % half == 0 else arc
        self.devices = arc * vec
        self.plane = self.devices // self.rings
        self.arcs, self.links, self.blocks = arcs_here, links, blocks_here
        entries = arcs_here * links
        self.cap = (entries + self.devices - 1) // self.devices + 1
        self.slots = self.plane * self.cap
        self.pos_row = self.slots
        self.own_row = self.slots + arcs_here
        self.rows = self.slots + 2 * arcs_here
        self.order = [self.plane_at(i) for i in range(self.rings)]
        self.ring = [
            (self.order[i] * self.plane + p, self.order[(i + 1) % self.rings] * self.plane + p)
            for i in range(self.rings)
            for p in range(self.plane)
        ]
        self.paired = self.plane & (self.plane - 1) == 0
        half = self.rings // 2
        onward, reverse = list(range(half, 0, -1)), list(range(half + 1, self.rings))
        self.back = []
        while onward or reverse:
            self.back += onward[:1] + reverse[:1]
            onward, reverse = onward[1:], reverse[1:]
        self.back.append(0)

    def follows(self, step):
        half = self.rings // 2
        sources = [step + 1] if step < half else []
        if step > half + 1 or (step == 0 and self.rings > half + 1):
            sources.append((step - 1) % self.rings)
        return sources

    def shift_back(self, step):
        move = 1 if step <= self.rings // 2 else -1
        return [
            (self.order[i] * self.plane + p, self.order[(i - move) % self.rings] * self.plane + p)
            for i in range(self.rings)
            for p in range(self.plane)
        ]

    def target(self, p, offset):
        return p ^ offset if self.paired else (p + offset) % self.plane

    def target_traced(self, p, offset):
        return p ^ offset if self.paired else lax.rem(p + offset, self.plane)

    def source_traced(self, p, offset):
        return p ^ offset if self.paired else lax.rem(p - offset + self.plane, self.plane)

    def shift_plane(self, offset):
        return [
            (z * self.plane + p, z * self.plane + self.target(p, offset))
            for z in range(self.rings)
            for p in range(self.plane)
        ]

    def plane_at(self, place):
        return 2 * place if 2 * place < self.rings else 2 * self.rings - 1 - 2 * place

    def place_of(self, z):
        half = lax.div(z, 2)
        return jnp.where(lax.rem(z, 2) == 0, half, self.rings - 1 - half)

    def source_plane(self, me, step):
        place = self.place_of(lax.div(me, self.plane))
        place = lax.rem(place - step + self.rings, self.rings)
        doubled = 2 * place
        return jnp.where(doubled < self.rings, doubled, 2 * self.rings - 1 - doubled)


def tables_kernel(plan, me_ref, owner_cols, block_cols, tab_ref, owner_ref, block_ref):
    me = me_ref[0]
    arcs, links, lanes = plan.arcs, plan.links, tab_ref.shape[1]
    z = lax.div(me, plan.plane)
    span = plan.plane * arcs
    first = pl.multiple_of(z * span, span)
    owner_ref[...] = owner_cols[:, pl.ds(first, span)].T
    block_ref[...] = block_cols[:, pl.ds(first, span)].T
    owners = lax.broadcasted_iota(jnp.int32, (arcs, lanes), 1)
    low = lax.broadcasted_iota(jnp.int32, (arcs, arcs), 0)
    high = lax.broadcasted_iota(jnp.int32, (arcs, arcs), 1)
    before = (high < low).astype(jnp.float32)

    def incidence(row):
        owner = owner_ref[pl.ds(row, arcs), :]
        block = block_ref[pl.ds(row, arcs), :]
        named = jnp.zeros((arcs, lanes), jnp.float32)
        held = jnp.zeros((arcs, lanes), jnp.int32)
        for k in range(links):
            same = owner[:, k : k + 1] == owners
            named = jnp.where(same, 1.0, named)
            held = jnp.where(same, block[:, k : k + 1] + 1, held)
        rank = jnp.dot(before, named, preferred_element_type=jnp.float32).astype(jnp.int32)
        return held, rank

    for q in range(plan.plane):
        held, rank = incidence(q * arcs)
        for r in range(plan.cap):
            at_rank = jnp.where(rank == r, held, 0)
            tab_ref[r * plan.plane + q : r * plan.plane + q + 1, :] = jnp.sum(
                at_rank, axis=0, keepdims=True
            )
    row = pl.multiple_of(lax.rem(me, plan.plane) * arcs, arcs)
    held, rank = incidence(row)
    place = plan.place_of(z)
    other = plan.place_of(lax.div(owners, plan.plane))
    step = lax.rem(place - other + plan.rings, plan.rings)
    here, there = lax.rem(me, plan.plane), lax.rem(owners, plan.plane)
    offset = here ^ there if plan.paired else lax.rem(here - there + plan.plane, plan.plane)
    slot = step * plan.slots + offset * plan.cap + rank
    tab_ref[plan.pos_row : plan.pos_row + arcs, :] = slot
    mine = jnp.zeros((arcs, lanes), jnp.int32)
    owner = owner_ref[pl.ds(row, arcs), :]
    for k in range(links):
        mine = jnp.where(owners == k, owner[:, k : k + 1], mine)
    tab_ref[plan.own_row : plan.own_row + arcs, :] = mine


def make_tables(plan, me, coupling_owner, coupling_block):
    lanes = -(-plan.devices // 128) * 128
    return pl.pallas_call(
        functools.partial(tables_kernel, plan),
        out_shape=jax.ShapeDtypeStruct((plan.rows, lanes), jnp.int32),
        in_specs=[
            pl.BlockSpec(memory_space=SMEM),
            pl.BlockSpec(memory_space=VMEM),
            pl.BlockSpec(memory_space=VMEM),
        ],
        out_specs=pl.BlockSpec(memory_space=VMEM),
        scratch_shapes=[pltpu.VMEM((plan.plane * plan.arcs, plan.links), jnp.int32)] * 2,
        name="tables",
    )(me, coupling_owner.T, coupling_block.T)


def pick_kernel(plan, step, me_ref, tab_ref, chunk_ref, *out_refs):
    me = me_ref[0]
    here = lax.rem(me, plan.plane)
    column = plan.source_plane(me, step) * plan.plane + here
    for offset, out_ref in enumerate(out_refs):
        q = plan.target_traced(here, offset)
        for r in range(plan.cap):
            block = jnp.maximum(tab_ref[r * plan.plane + q, column] - 1, 0)
            out_ref[r] = chunk_ref[block]


def pick(plan, step, me, tab, chunk):
    shape = (plan.cap,) + chunk.shape[1:]
    return pl.pallas_call(
        functools.partial(pick_kernel, plan, step),
        out_shape=[jax.ShapeDtypeStruct(shape, chunk.dtype)] * plan.plane,
        in_specs=[
            pl.BlockSpec(memory_space=SMEM),
            pl.BlockSpec(memory_space=SMEM),
            pl.BlockSpec(memory_space=VMEM),
        ],
        out_specs=[pl.BlockSpec(memory_space=VMEM)] * plan.plane,
        name="pick",
    )(me, tab, chunk)


def narrow_dot(left, right, contract=1):
    product = lax.dot_general(
        left, right, (((contract,), (0,)), ((), ())), preferred_element_type=jnp.float32
    )
    return product.astype(jnp.bfloat16)


def arcs_kernel(plan, tab_ref, *refs):
    count, cap = plan.rings * plan.plane, plan.cap
    arrived_refs = refs[:count]
    panel_ref, factor_ref = refs[count], refs[count + 1]
    out_refs = refs[count + 2 : 2 * count + 2]
    arrived, leaving, fetched, sems = refs[2 * count + 2 :]
    arc = pl.program_id(0)
    rows = arrived.shape[1]

    def inward(s):
        return pltpu.make_async_copy(
            arrived_refs[s], arrived.at[pl.ds(s * cap, cap)], sems.at[s]
        )

    def outward(s):
        return pltpu.make_async_copy(
            leaving.at[pl.ds(s * cap, cap)], out_refs[s], sems.at[s]
        )

    @pl.when(arc == 0)
    def _():
        for s in range(count):
            inward(s).start()
        for s in range(count):
            inward(s).wait()

    group = range(panel_ref.shape[0])
    spots = [[] for _ in group]
    for g in group:
        row = arc * len(group) + g
        for k in range(plan.links):
            spot = tab_ref[plan.pos_row + row, tab_ref[plan.own_row + row, k]]
            spots[g].append(spot)
            fetched[g, k * rows : (k + 1) * rows, :] = arrived[spot]
    coupled = [narrow_dot(panel_ref[g], fetched[g]) for g in group]
    whitened = [narrow_dot(factor_ref[g], coupled[g]) for g in group]
    smoothed = [narrow_dot(whitened[g], factor_ref[g], 0) for g in group]
    for g in group:
        projected = narrow_dot(smoothed[g], panel_ref[g])
        for k in range(plan.links):
            leaving[spots[g][k]] = projected[:, k * rows : (k + 1) * rows]

    @pl.when(arc == pl.num_programs(0) - 1)
    def _():
        for s in range(count):
            outward(s).start()
        for s in range(count):
            outward(s).wait()


def run_arcs(plan, tab, arrived, coupling_panel, inv_factor):
    arcs, arc_rows, width = coupling_panel.shape
    block = arrived[0].shape[1:]
    total = plan.rings * plan.slots
    group = GROUP if arcs % GROUP == 0 else 1
    anywhere = pl.BlockSpec(memory_space=pl.ANY)
    return pl.pallas_call(
        functools.partial(arcs_kernel, plan),
        grid_spec=pltpu.PrefetchScalarGridSpec(
            num_scalar_prefetch=1,
            grid=(arcs // group,),
            in_specs=[anywhere] * (plan.rings * plan.plane)
            + [
                pl.BlockSpec((group, arc_rows, width), lambda i, t: (i, 0, 0)),
                pl.BlockSpec((group, arc_rows, arc_rows), lambda i, t: (i, 0, 0)),
            ],
            out_specs=[anywhere] * (plan.rings * plan.plane),
            scratch_shapes=[
                pltpu.VMEM((total,) + block, jnp.bfloat16),
                pltpu.VMEM((total,) + block, jnp.bfloat16),
                pltpu.VMEM((group, width, block[1]), jnp.bfloat16),
                pltpu.SemaphoreType.DMA((plan.rings * plan.plane,)),
            ],
        ),
        out_shape=[jax.ShapeDtypeStruct((plan.cap,) + block, jnp.bfloat16)]
        * (plan.rings * plan.plane),
        name="arcs",
    )(tab, *arrived, coupling_panel, inv_factor)


def fold_kernel(plan, step, me_ref, tab_ref, *refs):
    me = me_ref[0]
    here = lax.rem(me, plan.plane)
    got_refs, part_refs = refs[: plan.plane], refs[plan.plane : -2]
    out_ref, acc = refs[-2], refs[-1]
    column = plan.source_plane(me, step) * plan.plane + here
    start = jnp.zeros(acc.shape, jnp.float32)
    for part_ref in part_refs:
        start = start + part_ref[...].astype(jnp.float32)
    acc[...] = start
    for offset, got_ref in enumerate(got_refs):
        q = plan.source_traced(here, offset)
        for r in range(plan.cap):
            held = tab_ref[r * plan.plane + q, column]

            @pl.when(held > 0)
            def _():
                acc[held - 1] += got_ref[r].astype(jnp.float32)

    if step == 0:

        @pl.loop(0, plan.blocks)
        def _(b):
            out_ref[b] = acc[b].T
    else:
        out_ref[...] = acc[...].astype(out_ref.dtype)


def fold(plan, step, me, tab, got, parts):
    shape = (plan.blocks,) + got[0].shape[1:]
    args = (me, tab, *got, *parts)
    specs = [pl.BlockSpec(memory_space=SMEM)] * 2 + [pl.BlockSpec(memory_space=VMEM)] * (
        len(args) - 2
    )
    return pl.pallas_call(
        functools.partial(fold_kernel, plan, step),
        out_shape=jax.ShapeDtypeStruct(shape, jnp.bfloat16 if step else jnp.float32),
        in_specs=specs,
        out_specs=pl.BlockSpec(memory_space=VMEM),
        scratch_shapes=[pltpu.VMEM(shape, jnp.float32)],
        name="fold",
    )(*args)


def identity(size):
    rows = lax.broadcasted_iota(jnp.int32, (size, size), 0)
    lanes = lax.broadcasted_iota(jnp.int32, (size, size), 1)
    return jnp.where(rows == lanes, 1.0, 0.0)


def eliminate(matrix):
    size = matrix.shape[0]
    rows = lax.broadcasted_iota(jnp.int32, (size, size), 0)
    lanes = lax.broadcasted_iota(jnp.int32, (size, size), 1)

    def pivot(k, matrix):
        on_row, on_lane = rows == k, lanes == k
        column = jnp.sum(jnp.where(on_lane, matrix, 0.0), axis=1, keepdims=True)
        row = jnp.sum(jnp.where(on_row, matrix, 0.0), axis=0, keepdims=True)
        scale = 1.0 / jnp.sum(jnp.where(on_lane[:1], row, 0.0), axis=1, keepdims=True)
        row = jnp.where(on_lane[:1], 1.0, row) * scale
        rest = jnp.where(on_lane, 0.0, matrix) - column * row
        return jnp.where(on_row, row, rest)

    return lax.fori_loop(0, size, pivot, matrix)


def invert_into(out_refs, matrices):
    size = matrices[0].shape[0]
    eye = identity(size)
    scales, scaled = [], []
    for matrix in matrices:
        diagonal = eye * matrix
        down = lax.rsqrt(jnp.sum(diagonal, axis=1, keepdims=True))
        along = lax.rsqrt(jnp.sum(diagonal, axis=0, keepdims=True))
        scales.append((down, along))
        scaled.append(matrix * down * along)
    off = [matrix - eye for matrix in scaled]
    second = [times_high(e, e) for e in off]
    fourth = [times_high(e, e) for e in second]
    third = [times_high(e, f) for e, f in zip(off, second)]
    guess = [eye - e + f - g for e, f, g in zip(off, second, third)]
    guess = [x + times_high(x, e) for x, e in zip(guess, fourth)]
    left = [eye - times_high(a, x) for a, x in zip(scaled, guess)]
    guess = [x + times_high(x, r) for x, r in zip(guess, left)]
    for out_ref, x, r, a, (down, along) in zip(out_refs, guess, left, scaled, scales):
        out_ref[...] = x * down * along
        worst = jnp.max(jnp.sum(jnp.abs(r), axis=1, keepdims=True))

        @pl.when(jnp.logical_not(worst < 1e-3))
        def _():
            y = eliminate(a)
            y = y + times_high(y, eye - times_high(a, y))
            out_ref[...] = y * down * along


def step_kernel(grams_ref, step_ref, beta_ref, new_ref, first_inv, second_inv):
    res, cross, image = grams_ref[0], grams_ref[1], grams_ref[2]
    invert_into([first_inv, second_inv], [0.5 * (cross + cross.T), 0.5 * (res + res.T)])
    step = times_high(first_inv[...], res)
    step_ref[...] = step
    moved = times_high(cross, step)
    new = res - moved.T - moved + times_high(step.T, times_high(image, step))
    new_ref[...] = new
    beta_ref[...] = times_high(second_inv[...], new)


def last_kernel(grams_ref, res_ref, step_ref, first_inv):
    curv = grams_ref[0]
    invert_into([first_inv], [0.5 * (curv + curv.T)])
    step_ref[...] = times_high(first_inv[...], res_ref[...])


def small_solve(kernel, args, outputs, scratch):
    shape = args[0].shape[1:]
    return pl.pallas_call(
        kernel,
        out_shape=[jax.ShapeDtypeStruct(shape, jnp.float32)] * outputs,
        scratch_shapes=[pltpu.VMEM(shape, jnp.float32)] * scratch,
        name="solve",
    )(*args)


def trade_plane(plan, buffers):
    moved = [None] * plan.plane
    moved[0] = buffers[0]
    for offset in range(plan.plane - 1, 0, -1):
        moved[offset] = lax.ppermute(buffers[offset], AXES, plan.shift_plane(offset))
    return moved


def gate_kernel(in_ref, out_ref):
    out_ref[0] = in_ref[0]


def gate(me):
    return pl.pallas_call(
        gate_kernel,
        out_shape=jax.ShapeDtypeStruct(me.shape, me.dtype),
        in_specs=[pl.BlockSpec(memory_space=SMEM)],
        out_specs=pl.BlockSpec(memory_space=SMEM),
        name="gate",
    )(me)


def coupled_sum(plan, me, tab, rounded, coupling_panel, inv_factor):
    chunk, arrived = rounded, []
    for s in range(plan.rings):
        following = None
        if s + 1 < plan.rings:
            following = lax.ppermute(chunk, AXES, plan.ring)
        chosen = pick(plan, s, me, tab, chunk)
        arrived += trade_plane(plan, chosen)
        if s + 1 < plan.rings:
            me = gate(me)
        chunk = following
    leaving = run_arcs(plan, tab, arrived, coupling_panel, inv_factor)
    moved, folded = {}, []
    for j, s in enumerate(plan.back):
        buffers = leaving[s * plan.plane : (s + 1) * plan.plane]
        if j >= 2:
            *buffers, _ = lax.optimization_barrier((*buffers, folded[j - 2]))
        got = trade_plane(plan, buffers)
        sources = [moved[source] for source in plan.follows(s)]
        if s:
            me = gate(me)
        folded.append(fold(plan, s, me, tab, got, sources))
        if s:
            moved[s] = lax.ppermute(folded[j], AXES, plan.shift_back(s))
    return folded[-1], me


def per_device(
    mesh, right_side, prior_diag, inv_factor, coupling_panel, coupling_owner, coupling_block
):
    plan = Plan(mesh, coupling_panel.shape[0], coupling_owner.shape[1], right_side.shape[0])
    me = lax.axis_index(AXES).astype(jnp.int32).reshape(1)
    tab = make_tables(plan, me, coupling_owner, coupling_block)
    solution_field = jnp.zeros_like(right_side)
    residual = right_side
    direction = right_side
    start_gram = inner_gram(residual, residual)
    for sweep_index in range(ITERS):
        summed, me = coupled_sum(
            plan, me, tab, direction.astype(jnp.bfloat16), coupling_panel, inv_factor
        )
        image_vec = prior_diag[:, :, None] * direction + summed
        last = sweep_index + 1 == ITERS
        if last:
            grams = sum_all([inner_gram(direction, image_vec)])
            (step_mat,) = small_solve(last_kernel, (grams, res_gram), 1, 1)
        else:
            grams = sum_all(
                [start_gram, inner_gram(direction, image_vec), inner_gram(image_vec, image_vec)]
            )
            step_mat, beta_mat, res_gram = small_solve(step_kernel, (grams,), 3, 2)
        solution_field = solution_field + combine_cols(direction, step_mat)
        residual = residual - combine_cols(image_vec, step_mat)
        if not last:
            direction = residual + combine_cols(direction, beta_mat)
    return (solution_field, residual)


def solution(mesh):
    in_specs = (
        P(AXES, None, None),
        P(AXES, None),
        P(AXES, None, None),
        P(AXES, None, None),
        P(),
        P(),
    )
    out_specs = (P(AXES, None, None), P(AXES, None, None))
    return jax.shard_map(
        functools.partial(per_device, mesh),
        mesh=mesh,
        in_specs=in_specs,
        out_specs=out_specs,
        check_vma=False,
    )
```

profile of v0, /device:TPU:0, one launch (start us, length us, event | category | flops | bytes accessed | tf_op | source)
XLA Modules:
  0.0 565.1 jit_solution(9406779888832957843)
XLA Ops:
  2.1 4.1 collective-permute-start.7
  6.2 14.0 %collective-permute-done.7.chunk_ref = bf16[20,128,128]{2,1,0:T(8,128)(2,1)S(1)} collective-permute-done((bf16[20,128,128]{2,1,0:T(8,128)(2,1)S(1)}, bf16[20,128,128]{2,1,0:T(8,128)(2,1)S(1)}, u32[]{:S(2)}, u32[]{:S(2)}) %collective-permute-start.7) | collective-permute-done | bytes 655392 | tf_op jit(solution)/shard_map/ppermute | solution.py:446
  20.2 3.4 collective-permute-start.15
  28.1 8.6 %collective-permute-done.15.chunk_ref = bf16[20,128,128]{2,1,0:T(8,128)(2,1)S(1)} collective-permute-done((bf16[20,128,128]{2,1,0:T(8,128)(2,1)S(1)}, bf16[20,128,128]{2,1,0:T(8,128)(2,1)S(1)}, u32[]{:S(2)}, u32[]{:S(2)}) %collective-permute-start.15) | collective-permute-done | bytes 655392 | tf_op jit(solution)/shard_map/ppermute | solution.py:446
  36.7 3.4 collective-permute-start.23
  44.1 3.2 pick.9
  70.3 3.3 collective-permute-done.14.refs_15_
  88.3 3.6 collective-permute-done.21.refs_22_
  100.8 5.7 %collective-permute-done.29.refs_30_ = bf16[5,128,128]{2,1,0:T(8,128)(2,1)} collective-permute-done((bf16[5,128,128]{2,1,0:T(8,128)(2,1)}, bf16[5,128,128]{2,1,0:T(8,128)(2,1)}, u32[]{:S(2)}, u32[]{:S(2)}) %collective-permute-start.29) | collective-permute-done | bytes 163872 | tf_op jit(solution)/shard_map/ppermute | solution.py:423
  108.1 16.9 %arcs.2 = (bf16[5,128,128]{2,1,0:T(8,128)(2,1)}, bf16[5,128,128]{2,1,0:T(8,128)(2,1)}, bf16[5,128,128]{2,1,0:T(8,128)(2,1)}, bf16[5,128,128]{2,1,0:T(8,128)(2,1)...) custom-call(s32[72,128]{1,0:T(8,128)} %tables.1.tab_ref, ...), custom_call_target="tpu_custom_call" | custom-call | tf_op jit(solution)/shard_map/arcs/pallas_call | solution.py:272
  137.9 4.1 collective-permute-done.50.refs_6_
  145.7 3.5 fold.9
  160.4 4.1 collective-permute-done.36.refs_6_
  177.6 3.5 fold.8
  185.7 3.8 fold.10
  193.5 5.3 collective-permute-done.39.refs_2_
  208.6 3.6 collective-permute-done.44.refs_7_
  215.6 6.2 %fold.11 = f32[20,128,128]{2,1,0:T(8,128)} custom-call(s32[1]{0:T(128)} %gate.17.me_ref.in_ref, s32[72,128]{1,0:T(8,128)} %tables.1.tab_ref, bf16[5,128,128]{2,1,0:T(8,128)(2,1)} %get-tuple-element.213.refs_0_, bf16[5,128,128]{2,1,0:T(8,128)(2,1)} %copy-done.64, bf16[5,128,128]{2,1,0:T(8,128)(2,1)} %copy-done.68, bf16[5,128,128]{2,1,0:T(8,128)(2,1)} %copy-done.73, ...), custom_call_target="tpu_custom_call" | custom-call | tf_op jit(solution)/shard_map/fold/pallas_call | solution.py:330
  221.8 4.8 convolution_bitcast_fusion.2
  229.2 14.4 %all_to_all.20 = f32[32,12,128]{2,1,0:T(8,128)S(1)} all-to-all(f32[32,12,128]{2,1,0:T(8,128)S(1)} %reshape.23), channel_id=1, replica_groups=mesh['arc'=8,'vec'=4] {'arc','vec'}, dimensions={0} | all-to-all | bytes 393216 | tf_op jit(solution)/shard_map/all_to_all | solution.py:31
  243.7 12.8 %all_to_all.21 = f32[32,12,128]{2,1,0:T(8,128)S(1)} all-to-all(f32[32,12,128]{2,1,0:T(8,128)S(1)} %broadcast_in_dim.4), channel_id=1, replica_groups=mesh['arc'=8,'vec'=4] {'arc','vec'}, dimensions={0} | all-to-all | bytes 393216 | tf_op jit(solution)/shard_map/all_to_all | solution.py:31
  257.2 35.3 %solve.2 = (f32[128,128]{1,0:T(8,128)}, f32[128,128]{1,0:T(8,128)}, f32[128,128]{1,0:T(8,128)}) custom-call(f32[3,128,128]{2,1,0:T(8,128)} %reshape.24.grams_ref), custom_call_target="tpu_custom_call" | custom-call | tf_op jit(solution)/shard_map/solve/pallas_call | solution.py:411
  296.3 16.4 %collective-permute-done.69.chunk_ref = bf16[20,128,128]{2,1,0:T(8,128)(2,1)} collective-permute-done((bf16[20,128,128]{2,1,0:T(8,128)(2,1)S(1)}, bf16[20,128,128]{2,1,0:T(8,128)(2,1)}, u32[]{:S(2)}, u32[]{:S(2)}) %collective-permute-start.69) | collective-permute-done | bytes 655392 | tf_op jit(solution)/shard_map/ppermute | solution.py:446
  314.5 3.2 pick.12
  317.7 11.0 %collective-permute-done.77.chunk_ref = bf16[20,128,128]{2,1,0:T(8,128)(2,1)} collective-permute-done((bf16[20,128,128]{2,1,0:T(8,128)(2,1)}, bf16[20,128,128]{2,1,0:T(8,128)(2,1)}, u32[]{:S(2)}, u32[]{:S(2)}) %collective-permute-start.77) | collective-permute-done | bytes 655392 | tf_op jit(solution)/shard_map/ppermute | solution.py:446
  328.7 3.4 collective-permute-start.85
  332.1 3.5 collective-permute-start.66
  343.3 4.9 collective-permute-done.67.refs_6_
  362.1 3.2 collective-permute-done.75.refs_14_
  378.4 3.3 collective-permute-done.83.refs_22_
  388.8 3.3 collective-permute-done.88.refs_27_
  392.2 3.7 collective-permute-done.91.refs_30_
  398.1 16.9 %arcs.3 = (bf16[5,128,128]{2,1,0:T(8,128)(2,1)}, bf16[5,128,128]{2,1,0:T(8,128)(2,1)}, bf16[5,128,128]{2,1,0:T(8,128)(2,1)}, bf16[5,128,128]{2,1,0:T(8,128)(2,1)...) custom-call(s32[72,128]{1,0:T(8,128)} %tables.1.tab_ref, ...), custom_call_target="tpu_custom_call" | custom-call | tf_op jit(solution)/shard_map/arcs/pallas_call | solution.py:272
  428.1 3.4 collective-permute-done.112.refs_6_
  434.6 3.6 fold.13
  450.0 3.7 collective-permute-done.98.refs_6_
  467.7 3.6 fold.12
  474.3 3.7 fold.14
  483.1 4.8 collective-permute-done.101.refs_2_
  494.4 3.4 collective-permute-done.105.refs_6_
  497.7 3.8 collective-permute-done.106.refs_7_
  502.2 3.8 collective-permute-done.122.refs_8_
  506.0 6.1 %fold.15 = f32[20,128,128]{2,1,0:T(8,128)} custom-call(s32[1]{0:T(128)} %gate.23.me_ref, s32[72,128]{1,0:T(8,128)} %tables.1.tab_ref, bf16[5,128,128]{2,1,0:T(8,128)(2,1)} %get-tuple-element.295.refs_0_, bf16[5,128,128]{2,1,0:T(8,128)(2,1)} %copy-done.63, bf16[5,128,128]{2,1,0:T(8,128)(2,1)} %copy-done.67, bf16[5,128,128]{2,1,0:T(8,128)(2,1)} %copy-done.72, ...), custom_call_target="tpu_custom_call" | custom-call | tf_op jit(solution)/shard_map/fold/pallas_call | solution.py:330
  512.1 3.9 fusion.1
  516.0 9.8 %all_to_all.22 = f32[32,4,128]{2,1,0:T(4,128)S(1)} all-to-all(f32[32,4,128]{2,1,0:T(4,128)S(1)} %bitcast.44), channel_id=1, replica_groups=mesh['arc'=8,'vec'=4] {'arc','vec'}, dimensions={0} | all-to-all | bytes 131072 | tf_op jit(solution)/shard_map/all_to_all | solution.py:31
  531.4 5.0 all-to-all-done.3
  537.1 18.5 %solve.3 = f32[128,128]{1,0:T(8,128)} custom-call(f32[1,128,128]{2,1,0:T(8,128)} %bitcast.45, f32[128,128]{1,0:T(8,128)} %get-tuple-element.327.res_ref), custom_call_target="tpu_custom_call" | custom-call | tf_op jit(solution)/shard_map/solve/pallas_call | solution.py:411
  555.6 4.1 convolution_subtract_fusion
  (448 shorter events, 241.9 us)
Async XLA Ops:
  2.1 18.1 %collective-permute-start.7 = (bf16[20,128,128]{2,1,0:T(8,128)(2,1)S(1)}, bf16[20,128,128]{2,1,0:T(8,128)(2,1)S(1)}, u32[]{:S(2)}, u32[]{:S(2)}) collective-permute-start(bf16[20,128,128]{2,1,0:T(8,128)(2,1)S(1)} %convert_element_type.6.chunk_ref), channel_id=1, source_target_pairs={{0,16},{1,17},{2,18},{3,19},{4,20},{5,21},{6,22},{7,23},{16,24},{1... | collective-permute-start | bytes 1966088 | tf_op jit(solution)/shard_map/ppermute | solution.py:446
  20.2 16.5 %collective-permute-start.15 = (bf16[20,128,128]{2,1,0:T(8,128)(2,1)S(1)}, bf16[20,128,128]{2,1,0:T(8,128)(2,1)S(1)}, u32[]{:S(2)}, u32[]{:S(2)}) collective-permute-start(bf16[20,128,128]{2,1,0:T(8,128)(2,1)S(1)} %collective-permute-done.7.chunk_ref), channel_id=1, source_target_pairs={{0,16},{1,17},{2,18},{3,19},{4,20},{5,21},{6,22},{7,23},{16,24},{1... | collective-permute-start | bytes 1966088 | tf_op jit(solution)/shard_map/ppermute | solution.py:446
  28.1 15.0 %collective-permute-start = (bf16[5,128,128]{2,1,0:T(8,128)(2,1)}, bf16[5,128,128]{2,1,0:T(8,128)(2,1)S(1)}, u32[]{:S(2)}, u32[]{:S(2)}) collective-permute-start(bf16[5,128,128]{2,1,0:T(8,128)(2,1)} %get-tuple-element.166), channel_id=1, source_target_pairs={{0,1},{1,0},{2,3},{3,2},{4,5},{5,4},{6,7},{7,6},{8,9},{9,8},{10,11... | collective-permute-start | bytes 491528 | tf_op jit(solution)/shard_map/ppermute | solution.py:423
  36.7 37.9 %collective-permute-start.23 = (bf16[20,128,128]{2,1,0:T(8,128)(2,1)S(1)}, bf16[20,128,128]{2,1,0:T(8,128)(2,1)S(1)}, u32[]{:S(2)}, u32[]{:S(2)}) collective-permute-start(bf16[20,128,128]{2,1,0:T(8,128)(2,1)S(1)} %collective-permute-done.15.chunk_ref), channel_id=1, source_target_pairs={{0,16},{1,17},{2,18},{3,19},{4,20},{5,21},{6,22},{7,23},{16,24},{1... | collective-permute-start | bytes 1966088 | tf_op jit(solution)/shard_map/ppermute | solution.py:446
  51.2 11.6 %collective-permute-start.10 = (bf16[5,128,128]{2,1,0:T(8,128)(2,1)}, bf16[5,128,128]{2,1,0:T(8,128)(2,1)S(1)}, u32[]{:S(2)}, u32[]{:S(2)}) collective-permute-start(bf16[5,128,128]{2,1,0:T(8,128)(2,1)} %get-tuple-element.176), channel_id=1, source_target_pairs={{0,3},{1,2},{2,1},{3,0},{4,7},{5,6},{6,5},{7,4},{8,11},{9,10},{10,... | collective-permute-start | bytes 491528 | tf_op jit(solution)/shard_map/ppermute | solution.py:423
  51.7 13.0 %collective-permute-start.11 = (bf16[5,128,128]{2,1,0:T(8,128)(2,1)}, bf16[5,128,128]{2,1,0:T(8,128)(2,1)S(1)}, u32[]{:S(2)}, u32[]{:S(2)}) collective-permute-start(bf16[5,128,128]{2,1,0:T(8,128)(2,1)} %get-tuple-element.177), channel_id=1, source_target_pairs={{0,4},{1,5},{2,6},{3,7},{4,0},{5,1},{6,2},{7,3},{8,12},{9,13},{10,... | collective-permute-start | bytes 491528 | tf_op jit(solution)/shard_map/ppermute | solution.py:423
  55.6 13.6 %collective-permute-start.12 = (bf16[5,128,128]{2,1,0:T(8,128)(2,1)}, bf16[5,128,128]{2,1,0:T(8,128)(2,1)S(1)}, u32[]{:S(2)}, u32[]{:S(2)}) collective-permute-start(bf16[5,128,128]{2,1,0:T(8,128)(2,1)} %get-tuple-element.178), channel_id=1, source_target_pairs={{0,5},{1,4},{2,7},{3,6},{4,1},{5,0},{6,3},{7,2},{8,13},{9,12},{10,... | collective-permute-start | bytes 491528 | tf_op jit(solution)/shard_map/ppermute | solution.py:423
  83.0 11.3 %collective-permute-start.22 = (bf16[5,128,128]{2,1,0:T(8,128)(2,1)}, bf16[5,128,128]{2,1,0:T(8,128)(2,1)S(1)}, u32[]{:S(2)}, u32[]{:S(2)}) collective-permute-start(bf16[5,128,128]{2,1,0:T(8,128)(2,1)} %get-tuple-element.188), channel_id=1, source_target_pairs={{0,7},{1,6},{2,5},{3,4},{4,3},{5,2},{6,1},{7,0},{8,15},{9,14},{10,... | collective-permute-start | bytes 491528 | tf_op jit(solution)/shard_map/ppermute | solution.py:423
  83.7 11.6 %collective-permute-start.24 = (bf16[5,128,128]{2,1,0:T(8,128)(2,1)}, bf16[5,128,128]{2,1,0:T(8,128)(2,1)S(1)}, u32[]{:S(2)}, u32[]{:S(2)}) collective-permute-start(bf16[5,128,128]{2,1,0:T(8,128)(2,1)} %get-tuple-element.190), channel_id=1, source_target_pairs={{0,1},{1,0},{2,3},{3,2},{4,5},{5,4},{6,7},{7,6},{8,9},{9,8},{10,11... | collective-permute-start | bytes 491528 | tf_op jit(solution)/shard_map/ppermute | solution.py:423
  84.3 13.9 %collective-permute-start.25 = (bf16[5,128,128]{2,1,0:T(8,128)(2,1)}, bf16[5,128,128]{2,1,0:T(8,128)(2,1)S(1)}, u32[]{:S(2)}, u32[]{:S(2)}) collective-permute-start(bf16[5,128,128]{2,1,0:T(8,128)(2,1)} %get-tuple-element.191), channel_id=1, source_target_pairs={{0,2},{1,3},{2,0},{3,1},{4,6},{5,7},{6,4},{7,5},{8,10},{9,11},{10,... | collective-permute-start | bytes 491528 | tf_op jit(solution)/shard_map/ppermute | solution.py:423
  86.2 14.6 %collective-permute-start.26 = (bf16[5,128,128]{2,1,0:T(8,128)(2,1)}, bf16[5,128,128]{2,1,0:T(8,128)(2,1)S(1)}, u32[]{:S(2)}, u32[]{:S(2)}) collective-permute-start(bf16[5,128,128]{2,1,0:T(8,128)(2,1)} %get-tuple-element.192), channel_id=1, source_target_pairs={{0,3},{1,2},{2,1},{3,0},{4,7},{5,6},{6,5},{7,4},{8,11},{9,10},{10,... | collective-permute-start | bytes 491528 | tf_op jit(solution)/shard_map/ppermute | solution.py:423
  129.5 12.5 %collective-permute-start.50 = (bf16[5,128,128]{2,1,0:T(8,128)(2,1)}, bf16[5,128,128]{2,1,0:T(8,128)(2,1)S(1)}, u32[]{:S(2)}, u32[]{:S(2)}) collective-permute-start(bf16[5,128,128]{2,1,0:T(8,128)(2,1)} %get-tuple-element.235), channel_id=1, source_target_pairs={{0,6},{1,7},{2,4},{3,5},{4,2},{5,3},{6,0},{7,1},{8,14},{9,15},{10,... | collective-permute-start | bytes 491528 | tf_op jit(solution)/shard_map/ppermute | solution.py:423
  133.3 11.8 %collective-permute-start.51 = (bf16[5,128,128]{2,1,0:T(8,128)(2,1)}, bf16[5,128,128]{2,1,0:T(8,128)(2,1)S(1)}, u32[]{:S(2)}, u32[]{:S(2)}) collective-permute-start(bf16[5,128,128]{2,1,0:T(8,128)(2,1)} %get-tuple-element.236), channel_id=1, source_target_pairs={{0,7},{1,6},{2,5},{3,4},{4,3},{5,2},{6,1},{7,0},{8,15},{9,14},{10,... | collective-permute-start | bytes 491528 | tf_op jit(solution)/shard_map/ppermute | solution.py:423
  135.0 15.6 %collective-permute-start.31 = (bf16[5,128,128]{2,1,0:T(8,128)(2,1)}, bf16[5,128,128]{2,1,0:T(8,128)(2,1)S(1)}, u32[]{:S(2)}, u32[]{:S(2)}) collective-permute-start(bf16[5,128,128]{2,1,0:T(8,128)(2,1)} %get-tuple-element.206), channel_id=1, source_target_pairs={{0,1},{1,0},{2,3},{3,2},{4,5},{5,4},{6,7},{7,6},{8,9},{9,8},{10,11... | collective-permute-start | bytes 491528 | tf_op jit(solution)/shard_map/ppermute | solution.py:423
  136.0 15.9 %collective-permute-start.32 = (bf16[5,128,128]{2,1,0:T(8,128)(2,1)}, bf16[5,128,128]{2,1,0:T(8,128)(2,1)S(1)}, u32[]{:S(2)}, u32[]{:S(2)}) collective-permute-start(bf16[5,128,128]{2,1,0:T(8,128)(2,1)} %get-tuple-element.207), channel_id=1, source_target_pairs={{0,2},{1,3},{2,0},{3,1},{4,6},{5,7},{6,4},{7,5},{8,10},{9,11},{10,... | collective-permute-start | bytes 491528 | tf_op jit(solution)/shard_map/ppermute | solution.py:423
  149.2 35.2 %collective-permute-start.59 = (bf16[20,128,128]{2,1,0:T(8,128)(2,1)}, bf16[20,128,128]{2,1,0:T(8,128)(2,1)S(1)}, u32[]{:S(2)}, u32[]{:S(2)}) collective-permute-start(bf16[20,128,128]{2,1,0:T(8,128)(2,1)} %fold.9), channel_id=1, source_target_pairs={{0,8},{1,9},{2,10},{3,11},{4,12},{5,13},{6,14},{7,15},{16,0},{17,1... | collective-permute-start | bytes 1966088 | tf_op jit(solution)/shard_map/ppermute | solution.py:464
  152.0 12.5 %collective-permute-start.36 = (bf16[5,128,128]{2,1,0:T(8,128)(2,1)S(1)}, bf16[5,128,128]{2,1,0:T(8,128)(2,1)S(1)}, u32[]{:S(2)}, u32[]{:S(2)}) collective-permute-start(bf16[5,128,128]{2,1,0:T(8,128)(2,1)S(1)} %copy-done.93), channel_id=1, source_target_pairs={{0,6},{1,7},{2,4},{3,5},{4,2},{5,3},{6,0},{7,1},{8,14},{9,15},{10,... | collective-permute-start | bytes 491528 | tf_op jit(solution)/shard_map/ppermute | solution.py:423
  155.6 11.3 %collective-permute-start.37 = (bf16[5,128,128]{2,1,0:T(8,128)(2,1)S(1)}, bf16[5,128,128]{2,1,0:T(8,128)(2,1)S(1)}, u32[]{:S(2)}, u32[]{:S(2)}) collective-permute-start(bf16[5,128,128]{2,1,0:T(8,128)(2,1)S(1)} %copy-done.92), channel_id=1, source_target_pairs={{0,7},{1,6},{2,5},{3,4},{4,3},{5,2},{6,1},{7,0},{8,15},{9,14},{10,... | collective-permute-start | bytes 491528 | tf_op jit(solution)/shard_map/ppermute | solution.py:423
  159.6 11.2 %collective-permute-start.53 = (bf16[5,128,128]{2,1,0:T(8,128)(2,1)}, bf16[5,128,128]{2,1,0:T(8,128)(2,1)S(1)}, u32[]{:S(2)}, u32[]{:S(2)}) collective-permute-start(bf16[5,128,128]{2,1,0:T(8,128)(2,1)} %get-tuple-element.239), channel_id=1, source_target_pairs={{0,2},{1,3},{2,0},{3,1},{4,6},{5,7},{6,4},{7,5},{8,10},{9,11},{10,... | collective-permute-start | bytes 491528 | tf_op jit(solution)/shard_map/ppermute | solution.py:423
  166.9 14.2 %collective-permute-start.55 = (bf16[5,128,128]{2,1,0:T(8,128)(2,1)}, bf16[5,128,128]{2,1,0:T(8,128)(2,1)S(1)}, u32[]{:S(2)}, u32[]{:S(2)}) collective-permute-start(bf16[5,128,128]{2,1,0:T(8,128)(2,1)} %get-tuple-element.241), channel_id=1, source_target_pairs={{0,4},{1,5},{2,6},{3,7},{4,0},{5,1},{6,2},{7,3},{8,12},{9,13},{10,... | collective-permute-start | bytes 491528 | tf_op jit(solution)/shard_map/ppermute | solution.py:423
  167.6 16.6 %collective-permute-start.56 = (bf16[5,128,128]{2,1,0:T(8,128)(2,1)}, bf16[5,128,128]{2,1,0:T(8,128)(2,1)S(1)}, u32[]{:S(2)}, u32[]{:S(2)}) collective-permute-start(bf16[5,128,128]{2,1,0:T(8,128)(2,1)} %get-tuple-element.242), channel_id=1, source_target_pairs={{0,5},{1,4},{2,7},{3,6},{4,1},{5,0},{6,3},{7,2},{8,13},{9,12},{10,... | collective-permute-start | bytes 491528 | tf_op jit(solution)/shard_map/ppermute | solution.py:423
  170.9 13.3 %collective-permute-start.57 = (bf16[5,128,128]{2,1,0:T(8,128)(2,1)}, bf16[5,128,128]{2,1,0:T(8,128)(2,1)}, u32[]{:S(2)}, u32[]{:S(2)}) collective-permute-start(bf16[5,128,128]{2,1,0:T(8,128)(2,1)} %get-tuple-element.243), channel_id=1, source_target_pairs={{0,6},{1,7},{2,4},{3,5},{4,2},{5,3},{6,0},{7,1},{8,14},{9,15},{10,... | collective-permute-start | bytes 491528 | tf_op jit(solution)/shard_map/ppermute | solution.py:423
  181.2 31.0 %collective-permute-start.61 = (bf16[20,128,128]{2,1,0:T(8,128)(2,1)}, bf16[20,128,128]{2,1,0:T(8,128)(2,1)S(1)}, u32[]{:S(2)}, u32[]{:S(2)}) collective-permute-start(bf16[20,128,128]{2,1,0:T(8,128)(2,1)} %fold.8), channel_id=1, source_target_pairs={{0,16},{1,17},{2,18},{3,19},{4,20},{5,21},{6,22},{7,23},{16,24},{1... | collective-permute-start | bytes 1966088 | tf_op jit(solution)/shard_map/ppermute | solution.py:464
  189.5 25.2 %collective-permute-start.60 = (bf16[20,128,128]{2,1,0:T(8,128)(2,1)}, bf16[20,128,128]{2,1,0:T(8,128)(2,1)S(1)}, u32[]{:S(2)}, u32[]{:S(2)}) collective-permute-start(bf16[20,128,128]{2,1,0:T(8,128)(2,1)} %fold.10), channel_id=1, source_target_pairs={{0,8},{1,9},{2,10},{3,11},{4,12},{5,13},{6,14},{7,15},{16,0},{17,1... | collective-permute-start | bytes 1966088 | tf_op jit(solution)/shard_map/ppermute | solution.py:464
  295.9 16.7 %collective-permute-start.69 = (bf16[20,128,128]{2,1,0:T(8,128)(2,1)S(1)}, bf16[20,128,128]{2,1,0:T(8,128)(2,1)}, u32[]{:S(2)}, u32[]{:S(2)}) collective-permute-start(bf16[20,128,128]{2,1,0:T(8,128)(2,1)S(1)} %get-tuple-element.332.chunk_ref), channel_id=1, source_target_pairs={{0,16},{1,17},{2,18},{3,19},{4,20},{5,21},{6,22},{7,23},{16,24},{1... | collective-permute-start | bytes 1966088 | tf_op jit(solution)/shard_map/ppermute | solution.py:446
  312.6 16.1 %collective-permute-start.77 = (bf16[20,128,128]{2,1,0:T(8,128)(2,1)}, bf16[20,128,128]{2,1,0:T(8,128)(2,1)}, u32[]{:S(2)}, u32[]{:S(2)}) collective-permute-start(bf16[20,128,128]{2,1,0:T(8,128)(2,1)} %collective-permute-done.69.chunk_ref), channel_id=1, source_target_pairs={{0,16},{1,17},{2,18},{3,19},{4,20},{5,21},{6,22},{7,23},{16,24},{1... | collective-permute-start | bytes 1966088 | tf_op jit(solution)/shard_map/ppermute | solution.py:446
  317.6 14.4 %collective-permute-start.62 = (bf16[5,128,128]{2,1,0:T(8,128)(2,1)}, bf16[5,128,128]{2,1,0:T(8,128)(2,1)S(1)}, u32[]{:S(2)}, u32[]{:S(2)}) collective-permute-start(bf16[5,128,128]{2,1,0:T(8,128)(2,1)} %get-tuple-element.248), channel_id=1, source_target_pairs={{0,1},{1,0},{2,3},{3,2},{4,5},{5,4},{6,7},{7,6},{8,9},{9,8},{10,11... | collective-permute-start | bytes 491528 | tf_op jit(solution)/shard_map/ppermute | solution.py:423
  328.7 36.7 %collective-permute-start.85 = (bf16[20,128,128]{2,1,0:T(8,128)(2,1)}, bf16[20,128,128]{2,1,0:T(8,128)(2,1)S(1)}, u32[]{:S(2)}, u32[]{:S(2)}) collective-permute-start(bf16[20,128,128]{2,1,0:T(8,128)(2,1)} %collective-permute-done.77.chunk_ref), channel_id=1, source_target_pairs={{0,16},{1,17},{2,18},{3,19},{4,20},{5,21},{6,22},{7,23},{16,24},{1... | collective-permute-start | bytes 1966088 | tf_op jit(solution)/shard_map/ppermute | solution.py:446
  350.2 11.2 %collective-permute-start.74 = (bf16[5,128,128]{2,1,0:T(8,128)(2,1)}, bf16[5,128,128]{2,1,0:T(8,128)(2,1)}, u32[]{:S(2)}, u32[]{:S(2)}) collective-permute-start(bf16[5,128,128]{2,1,0:T(8,128)(2,1)} %get-tuple-element.260), channel_id=1, source_target_pairs={{0,5},{1,4},{2,7},{3,6},{4,1},{5,0},{6,3},{7,2},{8,13},{9,12},{10,... | collective-permute-start | bytes 491528 | tf_op jit(solution)/shard_map/ppermute | solution.py:423
  354.1 11.2 %collective-permute-start.75 = (bf16[5,128,128]{2,1,0:T(8,128)(2,1)}, bf16[5,128,128]{2,1,0:T(8,128)(2,1)}, u32[]{:S(2)}, u32[]{:S(2)}) collective-permute-start(bf16[5,128,128]{2,1,0:T(8,128)(2,1)} %get-tuple-element.261), channel_id=1, source_target_pairs={{0,6},{1,7},{2,4},{3,5},{4,2},{5,3},{6,0},{7,1},{8,14},{9,15},{10,... | collective-permute-start | bytes 491528 | tf_op jit(solution)/shard_map/ppermute | solution.py:423
  361.4 11.4 %collective-permute-start.79 = (bf16[5,128,128]{2,1,0:T(8,128)(2,1)}, bf16[5,128,128]{2,1,0:T(8,128)(2,1)}, u32[]{:S(2)}, u32[]{:S(2)}) collective-permute-start(bf16[5,128,128]{2,1,0:T(8,128)(2,1)} %get-tuple-element.265), channel_id=1, source_target_pairs={{0,2},{1,3},{2,0},{3,1},{4,6},{5,7},{6,4},{7,5},{8,10},{9,11},{10,... | collective-permute-start | bytes 491528 | tf_op jit(solution)/shard_map/ppermute | solution.py:423
  372.9 11.2 %collective-permute-start.84 = (bf16[5,128,128]{2,1,0:T(8,128)(2,1)}, bf16[5,128,128]{2,1,0:T(8,128)(2,1)S(1)}, u32[]{:S(2)}, u32[]{:S(2)}) collective-permute-start(bf16[5,128,128]{2,1,0:T(8,128)(2,1)} %get-tuple-element.270), channel_id=1, source_target_pairs={{0,7},{1,6},{2,5},{3,4},{4,3},{5,2},{6,1},{7,0},{8,15},{9,14},{10,... | collective-permute-start | bytes 491528 | tf_op jit(solution)/shard_map/ppermute | solution.py:423
  374.9 13.3 %collective-permute-start.87 = (bf16[5,128,128]{2,1,0:T(8,128)(2,1)}, bf16[5,128,128]{2,1,0:T(8,128)(2,1)}, u32[]{:S(2)}, u32[]{:S(2)}) collective-permute-start(bf16[5,128,128]{2,1,0:T(8,128)(2,1)} %get-tuple-element.273), channel_id=1, source_target_pairs={{0,2},{1,3},{2,0},{3,1},{4,6},{5,7},{6,4},{7,5},{8,10},{9,11},{10,... | collective-permute-start | bytes 491528 | tf_op jit(solution)/shard_map/ppermute | solution.py:423
  376.3 15.9 %collective-permute-start.88 = (bf16[5,128,128]{2,1,0:T(8,128)(2,1)}, bf16[5,128,128]{2,1,0:T(8,128)(2,1)}, u32[]{:S(2)}, u32[]{:S(2)}) collective-permute-start(bf16[5,128,128]{2,1,0:T(8,128)(2,1)} %get-tuple-element.274), channel_id=1, source_target_pairs={{0,3},{1,2},{2,1},{3,0},{4,7},{5,6},{6,5},{7,4},{8,11},{9,10},{10,... | collective-permute-start | bytes 491528 | tf_op jit(solution)/shard_map/ppermute | solution.py:423
  419.0 12.5 %collective-permute-start.112 = (bf16[5,128,128]{2,1,0:T(8,128)(2,1)}, bf16[5,128,128]{2,1,0:T(8,128)(2,1)}, u32[]{:S(2)}, u32[]{:S(2)}) collective-permute-start(bf16[5,128,128]{2,1,0:T(8,128)(2,1)} %get-tuple-element.317), channel_id=1, source_target_pairs={{0,6},{1,7},{2,4},{3,5},{4,2},{5,3},{6,0},{7,1},{8,14},{9,15},{10,... | collective-permute-start | bytes 491528 | tf_op jit(solution)/shard_map/ppermute | solution.py:423
  422.8 11.7 %collective-permute-start.113 = (bf16[5,128,128]{2,1,0:T(8,128)(2,1)}, bf16[5,128,128]{2,1,0:T(8,128)(2,1)}, u32[]{:S(2)}, u32[]{:S(2)}) collective-permute-start(bf16[5,128,128]{2,1,0:T(8,128)(2,1)} %get-tuple-element.318), channel_id=1, source_target_pairs={{0,7},{1,6},{2,5},{3,4},{4,3},{5,2},{6,1},{7,0},{8,15},{9,14},{10,... | collective-permute-start | bytes 491528 | tf_op jit(solution)/shard_map/ppermute | solution.py:423
  424.5 16.0 %collective-permute-start.93 = (bf16[5,128,128]{2,1,0:T(8,128)(2,1)}, bf16[5,128,128]{2,1,0:T(8,128)(2,1)S(1)}, u32[]{:S(2)}, u32[]{:S(2)}) collective-permute-start(bf16[5,128,128]{2,1,0:T(8,128)(2,1)} %get-tuple-element.288), channel_id=1, source_target_pairs={{0,1},{1,0},{2,3},{3,2},{4,5},{5,4},{6,7},{7,6},{8,9},{9,8},{10,11... | collective-permute-start | bytes 491528 | tf_op jit(solution)/shard_map/ppermute | solution.py:423
  426.4 14.6 %collective-permute-start.94 = (bf16[5,128,128]{2,1,0:T(8,128)(2,1)}, bf16[5,128,128]{2,1,0:T(8,128)(2,1)S(1)}, u32[]{:S(2)}, u32[]{:S(2)}) collective-permute-start(bf16[5,128,128]{2,1,0:T(8,128)(2,1)} %get-tuple-element.289), channel_id=1, source_target_pairs={{0,2},{1,3},{2,0},{3,1},{4,6},{5,7},{6,4},{7,5},{8,10},{9,11},{10,... | collective-permute-start | bytes 491528 | tf_op jit(solution)/shard_map/ppermute | solution.py:423
  438.1 36.2 %collective-permute-start.121 = (bf16[20,128,128]{2,1,0:T(8,128)(2,1)}, bf16[20,128,128]{2,1,0:T(8,128)(2,1)}, u32[]{:S(2)}, u32[]{:S(2)}) collective-permute-start(bf16[20,128,128]{2,1,0:T(8,128)(2,1)} %fold.13), channel_id=1, source_target_pairs={{0,8},{1,9},{2,10},{3,11},{4,12},{5,13},{6,14},{7,15},{16,0},{17,1... | collective-permute-start | bytes 1966088 | tf_op jit(solution)/shard_map/ppermute | solution.py:464
  441.0 12.7 %collective-permute-start.98 = (bf16[5,128,128]{2,1,0:T(8,128)(2,1)}, bf16[5,128,128]{2,1,0:T(8,128)(2,1)S(1)}, u32[]{:S(2)}, u32[]{:S(2)}) collective-permute-start(bf16[5,128,128]{2,1,0:T(8,128)(2,1)} %get-tuple-element.293), channel_id=1, source_target_pairs={{0,6},{1,7},{2,4},{3,5},{4,2},{5,3},{6,0},{7,1},{8,14},{9,15},{10,... | collective-permute-start | bytes 491528 | tf_op jit(solution)/shard_map/ppermute | solution.py:423
  444.7 11.5 %collective-permute-start.99 = (bf16[5,128,128]{2,1,0:T(8,128)(2,1)}, bf16[5,128,128]{2,1,0:T(8,128)(2,1)S(1)}, u32[]{:S(2)}, u32[]{:S(2)}) collective-permute-start(bf16[5,128,128]{2,1,0:T(8,128)(2,1)} %get-tuple-element.294), channel_id=1, source_target_pairs={{0,7},{1,6},{2,5},{3,4},{4,3},{5,2},{6,1},{7,0},{8,15},{9,14},{10,... | collective-permute-start | bytes 491528 | tf_op jit(solution)/shard_map/ppermute | solution.py:423
  446.6 11.2 %collective-permute-start.114 = (bf16[5,128,128]{2,1,0:T(8,128)(2,1)}, bf16[5,128,128]{2,1,0:T(8,128)(2,1)S(1)}, u32[]{:S(2)}, u32[]{:S(2)}) collective-permute-start(bf16[5,128,128]{2,1,0:T(8,128)(2,1)} %get-tuple-element.320), channel_id=1, source_target_pairs={{0,1},{1,0},{2,3},{3,2},{4,5},{5,4},{6,7},{7,6},{8,9},{9,8},{10,11... | collective-permute-start | bytes 491528 | tf_op jit(solution)/shard_map/ppermute | solution.py:423
  449.0 11.2 %collective-permute-start.115 = (bf16[5,128,128]{2,1,0:T(8,128)(2,1)}, bf16[5,128,128]{2,1,0:T(8,128)(2,1)}, u32[]{:S(2)}, u32[]{:S(2)}) collective-permute-start(bf16[5,128,128]{2,1,0:T(8,128)(2,1)} %get-tuple-element.321), channel_id=1, source_target_pairs={{0,2},{1,3},{2,0},{3,1},{4,6},{5,7},{6,4},{7,5},{8,10},{9,11},{10,... | collective-permute-start | bytes 491528 | tf_op jit(solution)/shard_map/ppermute | solution.py:423
  456.2 15.1 %collective-permute-start.117 = (bf16[5,128,128]{2,1,0:T(8,128)(2,1)}, bf16[5,128,128]{2,1,0:T(8,128)(2,1)}, u32[]{:S(2)}, u32[]{:S(2)}) collective-permute-start(bf16[5,128,128]{2,1,0:T(8,128)(2,1)} %get-tuple-element.323), channel_id=1, source_target_pairs={{0,4},{1,5},{2,6},{3,7},{4,0},{5,1},{6,2},{7,3},{8,12},{9,13},{10,... | collective-permute-start | bytes 491528 | tf_op jit(solution)/shard_map/ppermute | solution.py:423
  457.8 16.5 %collective-permute-start.118 = (bf16[5,128,128]{2,1,0:T(8,128)(2,1)}, bf16[5,128,128]{2,1,0:T(8,128)(2,1)}, u32[]{:S(2)}, u32[]{:S(2)}) collective-permute-start(bf16[5,128,128]{2,1,0:T(8,128)(2,1)} %get-tuple-element.324), channel_id=1, source_target_pairs={{0,5},{1,4},{2,7},{3,6},{4,1},{5,0},{6,3},{7,2},{8,13},{9,12},{10,... | collective-permute-start | bytes 491528 | tf_op jit(solution)/shard_map/ppermute | solution.py:423
  460.2 14.1 %collective-permute-start.119 = (bf16[5,128,128]{2,1,0:T(8,128)(2,1)}, bf16[5,128,128]{2,1,0:T(8,128)(2,1)}, u32[]{:S(2)}, u32[]{:S(2)}) collective-permute-start(bf16[5,128,128]{2,1,0:T(8,128)(2,1)} %get-tuple-element.325), channel_id=1, source_target_pairs={{0,6},{1,7},{2,4},{3,5},{4,2},{5,3},{6,0},{7,1},{8,14},{9,15},{10,... | collective-permute-start | bytes 491528 | tf_op jit(solution)/shard_map/ppermute | solution.py:423
  471.3 30.2 %collective-permute-start.123 = (bf16[20,128,128]{2,1,0:T(8,128)(2,1)}, bf16[20,128,128]{2,1,0:T(8,128)(2,1)S(1)}, u32[]{:S(2)}, u32[]{:S(2)}) collective-permute-start(bf16[20,128,128]{2,1,0:T(8,128)(2,1)} %fold.12), channel_id=1, source_target_pairs={{0,16},{1,17},{2,18},{3,19},{4,20},{5,21},{6,22},{7,23},{16,24},{1... | collective-permute-start | bytes 1966088 | tf_op jit(solution)/shard_map/ppermute | solution.py:464
  478.0 28.0 %collective-permute-start.122 = (bf16[20,128,128]{2,1,0:T(8,128)(2,1)}, bf16[20,128,128]{2,1,0:T(8,128)(2,1)}, u32[]{:S(2)}, u32[]{:S(2)}) collective-permute-start(bf16[20,128,128]{2,1,0:T(8,128)(2,1)} %fold.14), channel_id=1, source_target_pairs={{0,8},{1,9},{2,10},{3,11},{4,12},{5,13},{6,14},{7,15},{16,0},{17,1... | collective-permute-start | bytes 1966088 | tf_op jit(solution)/shard_map/ppermute | solution.py:464
  (173 other events, 2427.7 us)
where the time goes:
time: 574 us; the launch traced here: 565 us
  waiting for transfers between devices  197 us (34%)
  Pallas kernels  161 us (28%)
  starting transfers between devices  131 us (23%)
  blocking collectives  37 us (6%)
  matrix products  25.8 us (4%)
  local copies, waits for them, and re-layouts  9.84 us (2%)
    ppermute x112, waiting for transfers between devices, trade_plane(): lax.ppermute(buffers[offset], AXES, plan.shift_plane(offset))  136 us
    ppermute x112, starting transfers between devices, trade_plane(): lax.ppermute(buffers[offset], AXES, plan.shift_plane(offset))  103 us
    pallas_call x2, Pallas kernels, small_solve(): pl.pallas_call(kernel, out_shape=[jax.ShapeDtypeStruct(shape, jnp.float32...  53.7 us
    ppermute x6, waiting for transfers between devices, coupled_sum(): following = lax.ppermute(chunk, AXES, plan.ring)  50 us
    all_to_all x3, blocking collectives, trade(): return lax.all_to_all(buffer, AXES, split_axis=0, concat_axis=0, tiled=True)  37 us
    pallas_call x8, Pallas kernels, fold(): pl.pallas_call(functools.partial(fold_kernel, plan, step), out_shape=jax....  34 us
    pallas_call x2, Pallas kernels, run_arcs(): pl.pallas_call(functools.partial(arcs_kernel, plan), grid_spec=pltpu.Pref...  33.8 us
    pallas_call x8, Pallas kernels, pick(): pl.pallas_call(functools.partial(pick_kernel, plan, step), out_shape=[jax...  24.1 us
  transfers between devices with their start and end apart: 125, of which 64 were waited for; matrix products, arithmetic and copies ran while one was open for 1% of the time, Pallas kernels for 11%

commit v1 on v0

--- a/solution.py
+++ b/solution.py
@@ -9,7 +9,7 @@
 
 
 ITERS = 2
-GROUP = 2
+GROUP = 4
 AXES = ("arc", "vec")
 SMEM = pltpu.MemorySpace.SMEM
 VMEM = pltpu.MemorySpace.VMEM
@@ -33,13 +33,11 @@
 
 def sum_all(grams):
     device_count = lax.axis_size(AXES)
-    stacked = jnp.concatenate(grams, axis=0)
-    rows, cols = stacked.shape
-    pieces = stacked.reshape(device_count, rows // device_count, cols)
+    count, rows, cols = grams.shape
+    pieces = grams.reshape(device_count, count * rows // device_count, cols)
     mine = jnp.sum(trade(pieces), axis=0)
     shared = jnp.broadcast_to(mine[None], pieces.shape)
-    total = trade(shared).reshape(len(grams), rows // len(grams), cols)
-    return total
+    return trade(shared).reshape(grams.shape)
 
 
 class Plan:
@@ -293,11 +291,9 @@
     )(tab, *arrived, coupling_panel, inv_factor)
 
 
-def fold_kernel(plan, step, me_ref, tab_ref, *refs):
+def add_up(plan, step, me_ref, tab_ref, got_refs, part_refs, acc):
     me = me_ref[0]
     here = lax.rem(me, plan.plane)
-    got_refs, part_refs = refs[: plan.plane], refs[plan.plane : -2]
-    out_ref, acc = refs[-2], refs[-1]
     column = plan.source_plane(me, step) * plan.plane + here
     start = jnp.zeros(acc.shape, jnp.float32)
     for part_ref in part_refs:
@@ -312,29 +308,100 @@
             def _():
                 acc[held - 1] += got_ref[r].astype(jnp.float32)
 
-    if step == 0:
-
-        @pl.loop(0, plan.blocks)
-        def _(b):
-            out_ref[b] = acc[b].T
-    else:
-        out_ref[...] = acc[...].astype(out_ref.dtype)
+
+def fold_kernel(plan, step, me_ref, tab_ref, *refs):
+    got_refs, part_refs = refs[: plan.plane], refs[plan.plane : -2]
+    out_ref, acc = refs[-2], refs[-1]
+    add_up(plan, step, me_ref, tab_ref, got_refs, part_refs, acc)
+    out_ref[...] = acc[...].astype(out_ref.dtype)
+
+
+def image_kernel(plan, both, me_ref, tab_ref, field_ref, prior_ref, *refs):
+    got_refs, part_refs = refs[: plan.plane], refs[plan.plane : -3]
+    image_ref, gram_ref, acc = refs[-3:]
+    add_up(plan, 0, me_ref, tab_ref, got_refs, part_refs, acc)
+    rows = acc.shape[1]
+    for b in range(plan.blocks):
+        image_ref[b] = acc[b].T + prior_ref[:, b : b + 1] * field_ref[b]
+    gram_ref[...] = jnp.zeros_like(gram_ref)
+    batch = max(n for n in range(1, 6) if plan.blocks % n == 0)
+
+    @pl.loop(0, plan.blocks, step=batch)
+    def _(b):
+        field = field_ref[pl.ds(b, batch)].reshape(batch * rows, -1)
+        image = image_ref[pl.ds(b, batch)].reshape(batch * rows, -1)
+        gram_ref[0] += gram_of(field, image)
+        if both:
+            gram_ref[1] += gram_of(image, image)
+
+
+def gram_of(left, right):
+    return lax.dot_general(
+        left,
+        right,
+        (((0,), (0,)), ((), ())),
+        precision=lax.Precision.HIGHEST,
+        preferred_element_type=jnp.float32,
+    )
+
+
+def fold_specs(args):
+    return [pl.BlockSpec(memory_space=SMEM)] * 2 + [pl.BlockSpec(memory_space=VMEM)] * (
+        len(args) - 2
+    )
 
 
 def fold(plan, step, me, tab, got, parts):
     shape = (plan.blocks,) + got[0].shape[1:]
     args = (me, tab, *got, *parts)
-    specs = [pl.BlockSpec(memory_space=SMEM)] * 2 + [pl.BlockSpec(memory_space=VMEM)] * (
-        len(args) - 2
-    )
     return pl.pallas_call(
         functools.partial(fold_kernel, plan, step),
-        out_shape=jax.ShapeDtypeStruct(shape, jnp.bfloat16 if step else jnp.float32),
-        in_specs=specs,
+        out_shape=jax.ShapeDtypeStruct(shape, jnp.bfloat16),
+        in_specs=fold_specs(args),
         out_specs=pl.BlockSpec(memory_space=VMEM),
         scratch_shapes=[pltpu.VMEM(shape, jnp.float32)],
         name="fold",
     )(*args)
+
+
+def fold_image(plan, me, tab, got, parts, field, prior_cols, both):
+    shape, cols = field.shape, field.shape[2]
+    args = (me, tab, field, prior_cols, *got, *parts)
+    return pl.pallas_call(
+        functools.partial(image_kernel, plan, both),
+        out_shape=[
+            jax.ShapeDtypeStruct(shape, jnp.float32),
+            jax.ShapeDtypeStruct((2 if both else 1, cols, cols), jnp.float32),
+        ],
+        in_specs=fold_specs(args),
+        out_specs=[pl.BlockSpec(memory_space=VMEM)] * 2,
+        scratch_shapes=[pltpu.VMEM(shape, jnp.float32)],
+        name="image",
+    )(*args)
+
+
+def update_kernel(field_ref, image_ref, sol_ref, res_ref, step_ref, sol_out, res_out):
+    blocks, rows, cols = field_ref.shape
+    step = step_ref[...]
+    size = (blocks * rows, cols)
+    moved = times_high(field_ref[...].reshape(size), step).reshape(field_ref.shape)
+    sol_out[...] = sol_ref[...] + moved
+    moved = times_high(image_ref[...].reshape(size), step).reshape(field_ref.shape)
+    res_out[...] = res_ref[...] - moved
+
+
+def update(field, image, solution_field, residual, step_mat):
+    blocks, rows, cols = field.shape
+    batch = max(n for n in range(1, 5) if blocks % n == 0)
+    spec = pl.BlockSpec((batch, rows, cols), lambda i: (i, 0, 0))
+    return pl.pallas_call(
+        update_kernel,
+        grid=(blocks // batch,),
+        out_shape=[jax.ShapeDtypeStruct(field.shape, jnp.float32)] * 2,
+        in_specs=[spec] * 4 + [pl.BlockSpec((cols, cols), lambda i: (0, 0))],
+        out_specs=[spec] * 2,
+        name="update",
+    )(field, image, solution_field, residual, step_mat)
 
 
 def identity(size):
@@ -438,8 +505,8 @@
     )(me)
 
 
-def coupled_sum(plan, me, tab, rounded, coupling_panel, inv_factor):
-    chunk, arrived = rounded, []
+def apply_schur(plan, me, tab, field, prior_cols, coupling_panel, inv_factor, both):
+    chunk, arrived = field.astype(jnp.bfloat16), []
     for s in range(plan.rings):
         following = None
         if s + 1 < plan.rings:
@@ -459,10 +526,11 @@
         sources = [moved[source] for source in plan.follows(s)]
         if s:
             me = gate(me)
+        if s == 0:
+            image, grams = fold_image(plan, me, tab, got, sources, field, prior_cols, both)
+            return image, grams, me
         folded.append(fold(plan, s, me, tab, got, sources))
-        if s:
-            moved[s] = lax.ppermute(folded[j], AXES, plan.shift_back(s))
-    return folded[-1], me
+        moved[s] = lax.ppermute(folded[j], AXES, plan.shift_back(s))
 
 
 def per_device(
@@ -471,29 +539,24 @@
     plan = Plan(mesh, coupling_panel.shape[0], coupling_owner.shape[1], right_side.shape[0])
     me = lax.axis_index(AXES).astype(jnp.int32).reshape(1)
     tab = make_tables(plan, me, coupling_owner, coupling_block)
-    solution_field = jnp.zeros_like(right_side)
+    prior_cols = prior_diag.T
+    solution_field = None
     residual = right_side
     direction = right_side
     start_gram = inner_gram(residual, residual)
     for sweep_index in range(ITERS):
-        summed, me = coupled_sum(
-            plan, me, tab, direction.astype(jnp.bfloat16), coupling_panel, inv_factor
+        last = sweep_index + 1 == ITERS
+        image_vec, grams, me = apply_schur(
+            plan, me, tab, direction, prior_cols, coupling_panel, inv_factor, not last
         )
-        image_vec = prior_diag[:, :, None] * direction + summed
-        last = sweep_index + 1 == ITERS
         if last:
-            grams = sum_all([inner_gram(direction, image_vec)])
-            (step_mat,) = small_solve(last_kernel, (grams, res_gram), 1, 1)
-        else:
-            grams = sum_all(
-                [start_gram, inner_gram(direction, image_vec), inner_gram(image_vec, image_vec)]
-            )
-            step_mat, beta_mat, res_gram = small_solve(step_kernel, (grams,), 3, 2)
-        solution_field = solution_field + combine_cols(direction, step_mat)
+            (step_mat,) = small_solve(last_kernel, (sum_all(grams), res_gram), 1, 1)
+            return tuple(update(direction, image_vec, solution_field, residual, step_mat))
+        grams = jnp.concatenate([start_gram[None], grams], axis=0)
+        step_mat, beta_mat, res_gram = small_solve(step_kernel, (sum_all(grams),), 3, 2)
+        solution_field = combine_cols(direction, step_mat)
         residual = residual - combine_cols(image_vec, step_mat)
-        if not last:
-            direction = residual + combine_cols(direction, beta_mat)
-    return (solution_field, residual)
+        direction = residual + combine_cols(direction, beta_mat)
 
 
 def solution(mesh):

time: 574 us -> 552 us (0.962); the launches traced: 565 us -> 551 us
  matrix products: 25.8 us -> 8.85 us
    pallas_call x0 -> x3, Pallas kernels: none -> 21.3 us  [the longest x2 14.7 us: fold_image(): pl.pallas_call(functools.partial(image_kernel, plan, both), out_shape=[ja...]
    pallas_call x8 -> x6, Pallas kernels: 34 us -> 21.8 us  [fold(): pl.pallas_call(functools.partial(fold_kernel, plan, step), out_shape=jax....]
    dot_general x4 -> x1, matrix products: 13.5 us -> 2.23 us  [inner_gram(): jnp.einsum('grc,grd->cd', left, right, precision=lax.Precision.HIGHEST)]
    dot_general x5 -> x3, matrix products: 12.3 us -> 6.63 us  [combine_cols(): jnp.einsum('grc,cd->grd', field, weights, precision=lax.Precision.HIGHEST)]
  transfers between devices with their start and end apart: 125 -> 125, of which waited for: 64 -> 61; matrix products, arithmetic and copies ran while one was open for 1% -> 1% of each run, Pallas kernels for 11% -> 11%
where the time goes in v1:
time: 552 us; the launch traced here: 551 us
  waiting for transfers between devices  196 us (36%)
  Pallas kernels  165 us (30%)
  starting transfers between devices  131 us (24%)
  blocking collectives  37.1 us (7%)
  matrix products  8.85 us (2%)
  local copies, waits for them, and re-layouts  8.26 us (1%)
    ppermute x112, waiting for transfers between devices, trade_plane(): lax.ppermute(buffers[offset], AXES, plan.shift_plane(offset))  135 us
    ppermute x112, starting transfers between devices, trade_plane(): lax.ppermute(buffers[offset], AXES, plan.shift_plane(offset))  103 us
    pallas_call x2, Pallas kernels, small_solve(): pl.pallas_call(kernel, out_shape=[jax.ShapeDtypeStruct(shape, jnp.float32...  53.6 us
    ppermute x6, waiting for transfers between devices, apply_schur(): following = lax.ppermute(chunk, AXES, plan.ring)  49.6 us
    all_to_all x3, blocking collectives, trade(): return lax.all_to_all(buffer, AXES, split_axis=0, concat_axis=0, tiled=True)  37.1 us
    pallas_call x2, Pallas kernels, run_arcs(): pl.pallas_call(functools.partial(arcs_kernel, plan), grid_spec=pltpu.Pref...  28.5 us
    pallas_call x8, Pallas kernels, pick(): pl.pallas_call(functools.partial(pick_kernel, plan, step), out_shape=[jax...  24.3 us
    pallas_call x6, Pallas kernels, fold(): pl.pallas_call(functools.partial(fold_kernel, plan, step), out_shape=jax....  21.8 us
  transfers between devices with their start and end apart: 125, of which 61 were waited for; matrix products, arithmetic and copies ran while one was open for 1% of the time, Pallas kernels for 11%

profile of v1, /device:TPU:0, one launch (start us, length us, event | category | flops | bytes accessed | tf_op | source)
XLA Modules:
  0.0 550.8 jit_solution(7195053087283407808)
XLA Ops:
  2.1 4.1 collective-permute-start.7
  6.2 14.0 %collective-permute-done.7.chunk_ref = bf16[20,128,128]{2,1,0:T(8,128)(2,1)S(1)} collective-permute-done((bf16[20,128,128]{2,1,0:T(8,128)(2,1)S(1)}, bf16[20,128,128]{2,1,0:T(8,128)(2,1)S(1)}, u32[]{:S(2)}, u32[]{:S(2)}) %collective-permute-start.7) | collective-permute-done | bytes 655392 | tf_op jit(solution)/shard_map/ppermute | solution.py:513
  20.2 3.4 collective-permute-start.15
  28.1 8.6 %collective-permute-done.15.chunk_ref = bf16[20,128,128]{2,1,0:T(8,128)(2,1)S(1)} collective-permute-done((bf16[20,128,128]{2,1,0:T(8,128)(2,1)S(1)}, bf16[20,128,128]{2,1,0:T(8,128)(2,1)S(1)}, u32[]{:S(2)}, u32[]{:S(2)}) %collective-permute-start.15) | collective-permute-done | bytes 655392 | tf_op jit(solution)/shard_map/ppermute | solution.py:513
  36.7 3.4 collective-permute-start.23
  66.2 3.1 pick.10
  70.3 3.3 collective-permute-done.14.refs_15_
  77.2 3.1 pick.11
  88.4 3.6 collective-permute-done.21.refs_22_
  101.1 5.7 %collective-permute-done.29.refs_30_ = bf16[5,128,128]{2,1,0:T(8,128)(2,1)} collective-permute-done((bf16[5,128,128]{2,1,0:T(8,128)(2,1)}, bf16[5,128,128]{2,1,0:T(8,128)(2,1)}, u32[]{:S(2)}, u32[]{:S(2)}) %collective-permute-start.29) | collective-permute-done | bytes 163872 | tf_op jit(solution)/shard_map/ppermute | solution.py:490
  108.1 14.3 %arcs.2 = (bf16[5,128,128]{2,1,0:T(8,128)(2,1)}, bf16[5,128,128]{2,1,0:T(8,128)(2,1)}, bf16[5,128,128]{2,1,0:T(8,128)(2,1)}, bf16[5,128,128]{2,1,0:T(8,128)(2,1)...) custom-call(s32[72,128]{1,0:T(8,128)} %tables.1.tab_ref, ...), custom_call_target="tpu_custom_call" | custom-call | tf_op jit(solution)/shard_map/arcs/pallas_call | solution.py:270
  135.5 4.0 collective-permute-done.50.refs_6_
  143.1 3.6 fold.7
  158.0 4.1 collective-permute-done.36.refs_6_
  175.6 3.6 fold.6
  183.6 3.7 fold.8
  191.5 4.6 collective-permute-done.39.refs_2_
  205.8 3.6 collective-permute-done.44.refs_7_
  209.4 3.3 collective-permute-done.60.refs_8_
  213.5 7.9 %image.2 = (f32[20,128,128]{2,1,0:T(8,128)}, f32[2,128,128]{2,1,0:T(8,128)}) custom-call(s32[1]{0:T(128)} %gate.17.me_ref.in_ref, s32[72,128]{1,0:T(8,128)} %tables.1.tab_ref, f32[20,128,128]{2,1,0:T(8,128)} %field_ref.1, f32[128,20]{1,0:T(8,128)} %bitcast.31, bf16[5,128,128]{2,1,0:T(8,128)(2,1)} %get-tuple-element.217.refs_0_, ...), custom_call_target="tpu_custom_call" | custom-call | tf_op jit(solution)/shard_map/image/pallas_call | solution.py:370
  222.3 14.3 %all_to_all.20 = f32[32,12,128]{2,1,0:T(8,128)S(1)} all-to-all(f32[32,12,128]{2,1,0:T(8,128)S(1)} %reshape.22), channel_id=1, replica_groups=mesh['arc'=8,'vec'=4] {'arc','vec'}, dimensions={0} | all-to-all | bytes 393216 | tf_op jit(solution)/shard_map/all_to_all | solution.py:31
  236.7 12.8 %all_to_all.21 = f32[32,12,128]{2,1,0:T(8,128)S(1)} all-to-all(f32[32,12,128]{2,1,0:T(8,128)S(1)} %broadcast_in_dim.7), channel_id=1, replica_groups=mesh['arc'=8,'vec'=4] {'arc','vec'}, dimensions={0} | all-to-all | bytes 393216 | tf_op jit(solution)/shard_map/all_to_all | solution.py:31
  250.2 35.1 %solve.2 = (f32[128,128]{1,0:T(8,128)}, f32[128,128]{1,0:T(8,128)}, f32[128,128]{1,0:T(8,128)}) custom-call(f32[3,128,128]{2,1,0:T(8,128)} %reshape.23.grams_ref), custom_call_target="tpu_custom_call" | custom-call | tf_op jit(solution)/shard_map/solve/pallas_call | solution.py:478
  289.9 16.3 %collective-permute-done.69.chunk_ref = bf16[20,128,128]{2,1,0:T(8,128)(2,1)S(1)} collective-permute-done((bf16[20,128,128]{2,1,0:T(8,128)(2,1)S(1)}, bf16[20,128,128]{2,1,0:T(8,128)(2,1)S(1)}, u32[]{:S(2)}, u32[]{:S(2)}) %collective-permute-start.69) | collective-permute-done | bytes 655392 | tf_op jit(solution)/shard_map/ppermute | solution.py:513
  308.1 3.1 pick.12
  311.2 10.8 %collective-permute-done.77.chunk_ref = bf16[20,128,128]{2,1,0:T(8,128)(2,1)S(1)} collective-permute-done((bf16[20,128,128]{2,1,0:T(8,128)(2,1)S(1)}, bf16[20,128,128]{2,1,0:T(8,128)(2,1)S(1)}, u32[]{:S(2)}, u32[]{:S(2)}) %collective-permute-start.77) | collective-permute-done | bytes 655392 | tf_op jit(solution)/shard_map/ppermute | solution.py:513
  321.9 3.4 collective-permute-start.85
  325.4 3.5 collective-permute-start.66
  330.0 3.2 pick.13
  336.5 5.0 collective-permute-done.67.refs_6_
  348.9 3.2 pick.14
  371.1 3.6 collective-permute-done.83.refs_22_
  385.1 3.8 collective-permute-done.91.refs_30_
  391.2 14.3 %arcs.3 = (bf16[5,128,128]{2,1,0:T(8,128)(2,1)}, bf16[5,128,128]{2,1,0:T(8,128)(2,1)}, bf16[5,128,128]{2,1,0:T(8,128)(2,1)}, bf16[5,128,128]{2,1,0:T(8,128)(2,1)...) custom-call(s32[72,128]{1,0:T(8,128)} %tables.1.tab_ref, ...), custom_call_target="tpu_custom_call" | custom-call | tf_op jit(solution)/shard_map/arcs/pallas_call | solution.py:270
  417.9 4.1 collective-permute-done.112.refs_6_
  425.6 3.6 fold.10
  441.4 3.7 collective-permute-done.98.refs_6_
  459.2 3.5 fold.9
  466.1 3.7 fold.11
  474.9 4.3 collective-permute-done.101.refs_2_
  486.0 3.6 collective-permute-done.105.refs_6_
  489.6 3.7 collective-permute-done.106.refs_7_
  493.3 3.4 collective-permute-done.122.refs_8_
  497.6 6.8 %image.3 = (f32[20,128,128]{2,1,0:T(8,128)}, f32[1,128,128]{2,1,0:T(8,128)}) custom-call(s32[1]{0:T(128)} %gate.23.me_ref, s32[72,128]{1,0:T(8,128)} %tables.1.tab_ref, f32[20,128,128]{2,1,0:T(8,128)} %get-tuple-element.337.field_ref, f32[128,20]{1,0:T(8,128)} %bitcast.32, bf16[5,128,128]{2,1,0:T(8,128)(2,1)} %get-tuple-element.301.refs_0_, ...), custom_call_target="tpu_custom_call" | custom-call | tf_op jit(solution)/shard_map/image/pallas_call | solution.py:370
  504.4 10.0 %all_to_all.22 = f32[32,4,128]{2,1,0:T(4,128)S(1)} all-to-all(f32[32,4,128]{2,1,0:T(4,128)} %bitcast.34), channel_id=1, replica_groups=mesh['arc'=8,'vec'=4] {'arc','vec'}, dimensions={0} | all-to-all | bytes 131072 | tf_op jit(solution)/shard_map/all_to_all | solution.py:31
  520.2 4.8 all-to-all-done.3
  525.7 18.5 %solve.3.step_ref = f32[128,128]{1,0:T(8,128)} custom-call(f32[1,128,128]{2,1,0:T(8,128)} %bitcast.33, f32[128,128]{1,0:T(8,128)} %get-tuple-element.335.res_ref), custom_call_target="tpu_custom_call" | custom-call | tf_op jit(solution)/shard_map/solve/pallas_call | solution.py:478
  544.2 6.6 %update.1 = (f32[20,128,128]{2,1,0:T(8,128)}, f32[20,128,128]{2,1,0:T(8,128)}) custom-call(f32[20,128,128]{2,1,0:T(8,128)} %get-tuple-element.337.field_ref, f32[20,128,128]{2,1,0:T(8,128)} %get-tuple-element.333.image_ref, f32[20,128,128]{2,1,0:T(8,128)} %convolution_bitcast_fusion.sol_ref, f32[20,128,128]{2,1,0:T(8,128)} %copy-done.2, ...), custom_call_target="tpu_custom_call" | custom-call | tf_op jit(solution)/shard_map/update/pallas_call | solution.py:397
  (484 shorter events, 231.5 us)
Async XLA Ops:
  2.1 18.1 %collective-permute-start.7 = (bf16[20,128,128]{2,1,0:T(8,128)(2,1)S(1)}, bf16[20,128,128]{2,1,0:T(8,128)(2,1)S(1)}, u32[]{:S(2)}, u32[]{:S(2)}) collective-permute-start(bf16[20,128,128]{2,1,0:T(8,128)(2,1)S(1)} %convert_element_type.6.chunk_ref), channel_id=1, source_target_pairs={{0,16},{1,17},{2,18},{3,19},{4,20},{5,21},{6,22},{7,23},{16,24},{1... | collective-permute-start | bytes 1966088 | tf_op jit(solution)/shard_map/ppermute | solution.py:513
  20.2 16.5 %collective-permute-start.15 = (bf16[20,128,128]{2,1,0:T(8,128)(2,1)S(1)}, bf16[20,128,128]{2,1,0:T(8,128)(2,1)S(1)}, u32[]{:S(2)}, u32[]{:S(2)}) collective-permute-start(bf16[20,128,128]{2,1,0:T(8,128)(2,1)S(1)} %collective-permute-done.7.chunk_ref), channel_id=1, source_target_pairs={{0,16},{1,17},{2,18},{3,19},{4,20},{5,21},{6,22},{7,23},{16,24},{1... | collective-permute-start | bytes 1966088 | tf_op jit(solution)/shard_map/ppermute | solution.py:513
  28.1 15.0 %collective-permute-start = (bf16[5,128,128]{2,1,0:T(8,128)(2,1)}, bf16[5,128,128]{2,1,0:T(8,128)(2,1)S(1)}, u32[]{:S(2)}, u32[]{:S(2)}) collective-permute-start(bf16[5,128,128]{2,1,0:T(8,128)(2,1)} %get-tuple-element.170), channel_id=1, source_target_pairs={{0,1},{1,0},{2,3},{3,2},{4,5},{5,4},{6,7},{7,6},{8,9},{9,8},{10,11... | collective-permute-start | bytes 491528 | tf_op jit(solution)/shard_map/ppermute | solution.py:490
  36.7 37.8 %collective-permute-start.23 = (bf16[20,128,128]{2,1,0:T(8,128)(2,1)S(1)}, bf16[20,128,128]{2,1,0:T(8,128)(2,1)S(1)}, u32[]{:S(2)}, u32[]{:S(2)}) collective-permute-start(bf16[20,128,128]{2,1,0:T(8,128)(2,1)S(1)} %collective-permute-done.15.chunk_ref), channel_id=1, source_target_pairs={{0,16},{1,17},{2,18},{3,19},{4,20},{5,21},{6,22},{7,23},{16,24},{1... | collective-permute-start | bytes 1966088 | tf_op jit(solution)/shard_map/ppermute | solution.py:513
  51.2 11.6 %collective-permute-start.10 = (bf16[5,128,128]{2,1,0:T(8,128)(2,1)}, bf16[5,128,128]{2,1,0:T(8,128)(2,1)S(1)}, u32[]{:S(2)}, u32[]{:S(2)}) collective-permute-start(bf16[5,128,128]{2,1,0:T(8,128)(2,1)} %get-tuple-element.180), channel_id=1, source_target_pairs={{0,3},{1,2},{2,1},{3,0},{4,7},{5,6},{6,5},{7,4},{8,11},{9,10},{10,... | collective-permute-start | bytes 491528 | tf_op jit(solution)/shard_map/ppermute | solution.py:490
  51.7 13.0 %collective-permute-start.11 = (bf16[5,128,128]{2,1,0:T(8,128)(2,1)}, bf16[5,128,128]{2,1,0:T(8,128)(2,1)S(1)}, u32[]{:S(2)}, u32[]{:S(2)}) collective-permute-start(bf16[5,128,128]{2,1,0:T(8,128)(2,1)} %get-tuple-element.181), channel_id=1, source_target_pairs={{0,4},{1,5},{2,6},{3,7},{4,0},{5,1},{6,2},{7,3},{8,12},{9,13},{10,... | collective-permute-start | bytes 491528 | tf_op jit(solution)/shard_map/ppermute | solution.py:490
  55.6 13.7 %collective-permute-start.12 = (bf16[5,128,128]{2,1,0:T(8,128)(2,1)}, bf16[5,128,128]{2,1,0:T(8,128)(2,1)S(1)}, u32[]{:S(2)}, u32[]{:S(2)}) collective-permute-start(bf16[5,128,128]{2,1,0:T(8,128)(2,1)} %get-tuple-element.182), channel_id=1, source_target_pairs={{0,5},{1,4},{2,7},{3,6},{4,1},{5,0},{6,3},{7,2},{8,13},{9,12},{10,... | collective-permute-start | bytes 491528 | tf_op jit(solution)/shard_map/ppermute | solution.py:490
  83.1 11.3 %collective-permute-start.22 = (bf16[5,128,128]{2,1,0:T(8,128)(2,1)}, bf16[5,128,128]{2,1,0:T(8,128)(2,1)S(1)}, u32[]{:S(2)}, u32[]{:S(2)}) collective-permute-start(bf16[5,128,128]{2,1,0:T(8,128)(2,1)} %get-tuple-element.192), channel_id=1, source_target_pairs={{0,7},{1,6},{2,5},{3,4},{4,3},{5,2},{6,1},{7,0},{8,15},{9,14},{10,... | collective-permute-start | bytes 491528 | tf_op jit(solution)/shard_map/ppermute | solution.py:490
  83.7 11.7 %collective-permute-start.24 = (bf16[5,128,128]{2,1,0:T(8,128)(2,1)}, bf16[5,128,128]{2,1,0:T(8,128)(2,1)S(1)}, u32[]{:S(2)}, u32[]{:S(2)}) collective-permute-start(bf16[5,128,128]{2,1,0:T(8,128)(2,1)} %get-tuple-element.194), channel_id=1, source_target_pairs={{0,1},{1,0},{2,3},{3,2},{4,5},{5,4},{6,7},{7,6},{8,9},{9,8},{10,11... | collective-permute-start | bytes 491528 | tf_op jit(solution)/shard_map/ppermute | solution.py:490
  84.5 13.9 %collective-permute-start.25 = (bf16[5,128,128]{2,1,0:T(8,128)(2,1)}, bf16[5,128,128]{2,1,0:T(8,128)(2,1)S(1)}, u32[]{:S(2)}, u32[]{:S(2)}) collective-permute-start(bf16[5,128,128]{2,1,0:T(8,128)(2,1)} %get-tuple-element.195), channel_id=1, source_target_pairs={{0,2},{1,3},{2,0},{3,1},{4,6},{5,7},{6,4},{7,5},{8,10},{9,11},{10,... | collective-permute-start | bytes 491528 | tf_op jit(solution)/shard_map/ppermute | solution.py:490
  86.3 14.8 %collective-permute-start.26 = (bf16[5,128,128]{2,1,0:T(8,128)(2,1)}, bf16[5,128,128]{2,1,0:T(8,128)(2,1)S(1)}, u32[]{:S(2)}, u32[]{:S(2)}) collective-permute-start(bf16[5,128,128]{2,1,0:T(8,128)(2,1)} %get-tuple-element.196), channel_id=1, source_target_pairs={{0,3},{1,2},{2,1},{3,0},{4,7},{5,6},{6,5},{7,4},{8,11},{9,10},{10,... | collective-permute-start | bytes 491528 | tf_op jit(solution)/shard_map/ppermute | solution.py:490
  95.4 11.4 %collective-permute-start.29 = (bf16[5,128,128]{2,1,0:T(8,128)(2,1)}, bf16[5,128,128]{2,1,0:T(8,128)(2,1)}, u32[]{:S(2)}, u32[]{:S(2)}) collective-permute-start(bf16[5,128,128]{2,1,0:T(8,128)(2,1)} %get-tuple-element.199), channel_id=1, source_target_pairs={{0,6},{1,7},{2,4},{3,5},{4,2},{5,3},{6,0},{7,1},{8,14},{9,15},{10,... | collective-permute-start | bytes 491528 | tf_op jit(solution)/shard_map/ppermute | solution.py:490
  127.0 12.5 %collective-permute-start.50 = (bf16[5,128,128]{2,1,0:T(8,128)(2,1)}, bf16[5,128,128]{2,1,0:T(8,128)(2,1)S(1)}, u32[]{:S(2)}, u32[]{:S(2)}) collective-permute-start(bf16[5,128,128]{2,1,0:T(8,128)(2,1)} %get-tuple-element.239), channel_id=1, source_target_pairs={{0,6},{1,7},{2,4},{3,5},{4,2},{5,3},{6,0},{7,1},{8,14},{9,15},{10,... | collective-permute-start | bytes 491528 | tf_op jit(solution)/shard_map/ppermute | solution.py:490
  130.8 11.7 %collective-permute-start.51 = (bf16[5,128,128]{2,1,0:T(8,128)(2,1)}, bf16[5,128,128]{2,1,0:T(8,128)(2,1)S(1)}, u32[]{:S(2)}, u32[]{:S(2)}) collective-permute-start(bf16[5,128,128]{2,1,0:T(8,128)(2,1)} %get-tuple-element.240), channel_id=1, source_target_pairs={{0,7},{1,6},{2,5},{3,4},{4,3},{5,2},{6,1},{7,0},{8,15},{9,14},{10,... | collective-permute-start | bytes 491528 | tf_op jit(solution)/shard_map/ppermute | solution.py:490
  132.5 15.8 %collective-permute-start.31 = (bf16[5,128,128]{2,1,0:T(8,128)(2,1)}, bf16[5,128,128]{2,1,0:T(8,128)(2,1)S(1)}, u32[]{:S(2)}, u32[]{:S(2)}) collective-permute-start(bf16[5,128,128]{2,1,0:T(8,128)(2,1)} %get-tuple-element.210), channel_id=1, source_target_pairs={{0,1},{1,0},{2,3},{3,2},{4,5},{5,4},{6,7},{7,6},{8,9},{9,8},{10,11... | collective-permute-start | bytes 491528 | tf_op jit(solution)/shard_map/ppermute | solution.py:490
  133.6 16.2 %collective-permute-start.32 = (bf16[5,128,128]{2,1,0:T(8,128)(2,1)}, bf16[5,128,128]{2,1,0:T(8,128)(2,1)S(1)}, u32[]{:S(2)}, u32[]{:S(2)}) collective-permute-start(bf16[5,128,128]{2,1,0:T(8,128)(2,1)} %get-tuple-element.211), channel_id=1, source_target_pairs={{0,2},{1,3},{2,0},{3,1},{4,6},{5,7},{6,4},{7,5},{8,10},{9,11},{10,... | collective-permute-start | bytes 491528 | tf_op jit(solution)/shard_map/ppermute | solution.py:490
  146.7 35.4 %collective-permute-start.59 = (bf16[20,128,128]{2,1,0:T(8,128)(2,1)}, bf16[20,128,128]{2,1,0:T(8,128)(2,1)S(1)}, u32[]{:S(2)}, u32[]{:S(2)}) collective-permute-start(bf16[20,128,128]{2,1,0:T(8,128)(2,1)} %fold.7), channel_id=1, source_target_pairs={{0,8},{1,9},{2,10},{3,11},{4,12},{5,13},{6,14},{7,15},{16,0},{17,1... | collective-permute-start | bytes 1966088 | tf_op jit(solution)/shard_map/ppermute | solution.py:533
  149.7 12.4 %collective-permute-start.36 = (bf16[5,128,128]{2,1,0:T(8,128)(2,1)S(1)}, bf16[5,128,128]{2,1,0:T(8,128)(2,1)S(1)}, u32[]{:S(2)}, u32[]{:S(2)}) collective-permute-start(bf16[5,128,128]{2,1,0:T(8,128)(2,1)S(1)} %copy-done.110), channel_id=1, source_target_pairs={{0,6},{1,7},{2,4},{3,5},{4,2},{5,3},{6,0},{7,1},{8,14},{9,15},{10,... | collective-permute-start | bytes 491528 | tf_op jit(solution)/shard_map/ppermute | solution.py:490
  153.1 11.5 %collective-permute-start.37 = (bf16[5,128,128]{2,1,0:T(8,128)(2,1)S(1)}, bf16[5,128,128]{2,1,0:T(8,128)(2,1)S(1)}, u32[]{:S(2)}, u32[]{:S(2)}) collective-permute-start(bf16[5,128,128]{2,1,0:T(8,128)(2,1)S(1)} %copy-done.109), channel_id=1, source_target_pairs={{0,7},{1,6},{2,5},{3,4},{4,3},{5,2},{6,1},{7,0},{8,15},{9,14},{10,... | collective-permute-start | bytes 491528 | tf_op jit(solution)/shard_map/ppermute | solution.py:490
  157.4 11.2 %collective-permute-start.53 = (bf16[5,128,128]{2,1,0:T(8,128)(2,1)S(1)}, bf16[5,128,128]{2,1,0:T(8,128)(2,1)S(1)}, u32[]{:S(2)}, u32[]{:S(2)}) collective-permute-start(bf16[5,128,128]{2,1,0:T(8,128)(2,1)S(1)} %copy-done.107), channel_id=1, source_target_pairs={{0,2},{1,3},{2,0},{3,1},{4,6},{5,7},{6,4},{7,5},{8,10},{9,11},{10,... | collective-permute-start | bytes 491528 | tf_op jit(solution)/shard_map/ppermute | solution.py:490
  164.6 14.6 %collective-permute-start.55 = (bf16[5,128,128]{2,1,0:T(8,128)(2,1)}, bf16[5,128,128]{2,1,0:T(8,128)(2,1)S(1)}, u32[]{:S(2)}, u32[]{:S(2)}) collective-permute-start(bf16[5,128,128]{2,1,0:T(8,128)(2,1)} %get-tuple-element.245), channel_id=1, source_target_pairs={{0,4},{1,5},{2,6},{3,7},{4,0},{5,1},{6,2},{7,3},{8,12},{9,13},{10,... | collective-permute-start | bytes 491528 | tf_op jit(solution)/shard_map/ppermute | solution.py:490
  165.3 16.8 %collective-permute-start.56 = (bf16[5,128,128]{2,1,0:T(8,128)(2,1)}, bf16[5,128,128]{2,1,0:T(8,128)(2,1)S(1)}, u32[]{:S(2)}, u32[]{:S(2)}) collective-permute-start(bf16[5,128,128]{2,1,0:T(8,128)(2,1)} %get-tuple-element.246), channel_id=1, source_target_pairs={{0,5},{1,4},{2,7},{3,6},{4,1},{5,0},{6,3},{7,2},{8,13},{9,12},{10,... | collective-permute-start | bytes 491528 | tf_op jit(solution)/shard_map/ppermute | solution.py:490
  168.5 13.6 %collective-permute-start.57 = (bf16[5,128,128]{2,1,0:T(8,128)(2,1)}, bf16[5,128,128]{2,1,0:T(8,128)(2,1)}, u32[]{:S(2)}, u32[]{:S(2)}) collective-permute-start(bf16[5,128,128]{2,1,0:T(8,128)(2,1)} %get-tuple-element.247), channel_id=1, source_target_pairs={{0,6},{1,7},{2,4},{3,5},{4,2},{5,3},{6,0},{7,1},{8,14},{9,15},{10,... | collective-permute-start | bytes 491528 | tf_op jit(solution)/shard_map/ppermute | solution.py:490
  179.2 30.2 %collective-permute-start.61 = (bf16[20,128,128]{2,1,0:T(8,128)(2,1)}, bf16[20,128,128]{2,1,0:T(8,128)(2,1)S(1)}, u32[]{:S(2)}, u32[]{:S(2)}) collective-permute-start(bf16[20,128,128]{2,1,0:T(8,128)(2,1)} %fold.6), channel_id=1, source_target_pairs={{0,16},{1,17},{2,18},{3,19},{4,20},{5,21},{6,22},{7,23},{16,24},{1... | collective-permute-start | bytes 1966088 | tf_op jit(solution)/shard_map/ppermute | solution.py:533
  187.4 25.3 %collective-permute-start.60 = (bf16[20,128,128]{2,1,0:T(8,128)(2,1)}, bf16[20,128,128]{2,1,0:T(8,128)(2,1)S(1)}, u32[]{:S(2)}, u32[]{:S(2)}) collective-permute-start(bf16[20,128,128]{2,1,0:T(8,128)(2,1)} %fold.8), channel_id=1, source_target_pairs={{0,8},{1,9},{2,10},{3,11},{4,12},{5,13},{6,14},{7,15},{16,0},{17,1... | collective-permute-start | bytes 1966088 | tf_op jit(solution)/shard_map/ppermute | solution.py:533
  289.6 16.6 %collective-permute-start.69 = (bf16[20,128,128]{2,1,0:T(8,128)(2,1)S(1)}, bf16[20,128,128]{2,1,0:T(8,128)(2,1)S(1)}, u32[]{:S(2)}, u32[]{:S(2)}) collective-permute-start(bf16[20,128,128]{2,1,0:T(8,128)(2,1)S(1)} %get-tuple-element.336.chunk_ref), channel_id=1, source_target_pairs={{0,16},{1,17},{2,18},{3,19},{4,20},{5,21},{6,22},{7,23},{16,24},{1... | collective-permute-start | bytes 1966088 | tf_op jit(solution)/shard_map/ppermute | solution.py:513
  306.2 15.7 %collective-permute-start.77 = (bf16[20,128,128]{2,1,0:T(8,128)(2,1)S(1)}, bf16[20,128,128]{2,1,0:T(8,128)(2,1)S(1)}, u32[]{:S(2)}, u32[]{:S(2)}) collective-permute-start(bf16[20,128,128]{2,1,0:T(8,128)(2,1)S(1)} %collective-permute-done.69.chunk_ref), channel_id=1, source_target_pairs={{0,16},{1,17},{2,18},{3,19},{4,20},{5,21},{6,22},{7,23},{16,24},{1... | collective-permute-start | bytes 1966088 | tf_op jit(solution)/shard_map/ppermute | solution.py:513
  311.1 14.2 %collective-permute-start.62 = (bf16[5,128,128]{2,1,0:T(8,128)(2,1)}, bf16[5,128,128]{2,1,0:T(8,128)(2,1)S(1)}, u32[]{:S(2)}, u32[]{:S(2)}) collective-permute-start(bf16[5,128,128]{2,1,0:T(8,128)(2,1)} %get-tuple-element.254), channel_id=1, source_target_pairs={{0,1},{1,0},{2,3},{3,2},{4,5},{5,4},{6,7},{7,6},{8,9},{9,8},{10,11... | collective-permute-start | bytes 491528 | tf_op jit(solution)/shard_map/ppermute | solution.py:490
  321.9 36.4 %collective-permute-start.85 = (bf16[20,128,128]{2,1,0:T(8,128)(2,1)S(1)}, bf16[20,128,128]{2,1,0:T(8,128)(2,1)S(1)}, u32[]{:S(2)}, u32[]{:S(2)}) collective-permute-start(bf16[20,128,128]{2,1,0:T(8,128)(2,1)S(1)} %collective-permute-done.77.chunk_ref), channel_id=1, source_target_pairs={{0,16},{1,17},{2,18},{3,19},{4,20},{5,21},{6,22},{7,23},{16,24},{1... | collective-permute-start | bytes 1966088 | tf_op jit(solution)/shard_map/ppermute | solution.py:513
  342.7 11.4 %collective-permute-start.73 = (bf16[5,128,128]{2,1,0:T(8,128)(2,1)}, bf16[5,128,128]{2,1,0:T(8,128)(2,1)}, u32[]{:S(2)}, u32[]{:S(2)}) collective-permute-start(bf16[5,128,128]{2,1,0:T(8,128)(2,1)} %get-tuple-element.265), channel_id=1, source_target_pairs={{0,4},{1,5},{2,6},{3,7},{4,0},{5,1},{6,2},{7,3},{8,12},{9,13},{10,... | collective-permute-start | bytes 491528 | tf_op jit(solution)/shard_map/ppermute | solution.py:490
  343.5 11.3 %collective-permute-start.74 = (bf16[5,128,128]{2,1,0:T(8,128)(2,1)}, bf16[5,128,128]{2,1,0:T(8,128)(2,1)}, u32[]{:S(2)}, u32[]{:S(2)}) collective-permute-start(bf16[5,128,128]{2,1,0:T(8,128)(2,1)} %get-tuple-element.266), channel_id=1, source_target_pairs={{0,5},{1,4},{2,7},{3,6},{4,1},{5,0},{6,3},{7,2},{8,13},{9,12},{10,... | collective-permute-start | bytes 491528 | tf_op jit(solution)/shard_map/ppermute | solution.py:490
  365.9 11.2 %collective-permute-start.84 = (bf16[5,128,128]{2,1,0:T(8,128)(2,1)}, bf16[5,128,128]{2,1,0:T(8,128)(2,1)S(1)}, u32[]{:S(2)}, u32[]{:S(2)}) collective-permute-start(bf16[5,128,128]{2,1,0:T(8,128)(2,1)} %get-tuple-element.276), channel_id=1, source_target_pairs={{0,7},{1,6},{2,5},{3,4},{4,3},{5,2},{6,1},{7,0},{8,15},{9,14},{10,... | collective-permute-start | bytes 491528 | tf_op jit(solution)/shard_map/ppermute | solution.py:490
  368.0 13.2 %collective-permute-start.87 = (bf16[5,128,128]{2,1,0:T(8,128)(2,1)}, bf16[5,128,128]{2,1,0:T(8,128)(2,1)S(1)}, u32[]{:S(2)}, u32[]{:S(2)}) collective-permute-start(bf16[5,128,128]{2,1,0:T(8,128)(2,1)} %get-tuple-element.279), channel_id=1, source_target_pairs={{0,2},{1,3},{2,0},{3,1},{4,6},{5,7},{6,4},{7,5},{8,10},{9,11},{10,... | collective-permute-start | bytes 491528 | tf_op jit(solution)/shard_map/ppermute | solution.py:490
  369.3 15.8 %collective-permute-start.88 = (bf16[5,128,128]{2,1,0:T(8,128)(2,1)}, bf16[5,128,128]{2,1,0:T(8,128)(2,1)S(1)}, u32[]{:S(2)}, u32[]{:S(2)}) collective-permute-start(bf16[5,128,128]{2,1,0:T(8,128)(2,1)} %get-tuple-element.280), channel_id=1, source_target_pairs={{0,3},{1,2},{2,1},{3,0},{4,7},{5,6},{6,5},{7,4},{8,11},{9,10},{10,... | collective-permute-start | bytes 491528 | tf_op jit(solution)/shard_map/ppermute | solution.py:490
  377.7 11.2 %collective-permute-start.91 = (bf16[5,128,128]{2,1,0:T(8,128)(2,1)}, bf16[5,128,128]{2,1,0:T(8,128)(2,1)}, u32[]{:S(2)}, u32[]{:S(2)}) collective-permute-start(bf16[5,128,128]{2,1,0:T(8,128)(2,1)} %get-tuple-element.283), channel_id=1, source_target_pairs={{0,6},{1,7},{2,4},{3,5},{4,2},{5,3},{6,0},{7,1},{8,14},{9,15},{10,... | collective-permute-start | bytes 491528 | tf_op jit(solution)/shard_map/ppermute | solution.py:490
  409.6 12.4 %collective-permute-start.112 = (bf16[5,128,128]{2,1,0:T(8,128)(2,1)}, bf16[5,128,128]{2,1,0:T(8,128)(2,1)S(1)}, u32[]{:S(2)}, u32[]{:S(2)}) collective-permute-start(bf16[5,128,128]{2,1,0:T(8,128)(2,1)} %get-tuple-element.323), channel_id=1, source_target_pairs={{0,6},{1,7},{2,4},{3,5},{4,2},{5,3},{6,0},{7,1},{8,14},{9,15},{10,... | collective-permute-start | bytes 491528 | tf_op jit(solution)/shard_map/ppermute | solution.py:490
  413.3 11.6 %collective-permute-start.113 = (bf16[5,128,128]{2,1,0:T(8,128)(2,1)}, bf16[5,128,128]{2,1,0:T(8,128)(2,1)S(1)}, u32[]{:S(2)}, u32[]{:S(2)}) collective-permute-start(bf16[5,128,128]{2,1,0:T(8,128)(2,1)} %get-tuple-element.324), channel_id=1, source_target_pairs={{0,7},{1,6},{2,5},{3,4},{4,3},{5,2},{6,1},{7,0},{8,15},{9,14},{10,... | collective-permute-start | bytes 491528 | tf_op jit(solution)/shard_map/ppermute | solution.py:490
  415.1 16.6 %collective-permute-start.93 = (bf16[5,128,128]{2,1,0:T(8,128)(2,1)}, bf16[5,128,128]{2,1,0:T(8,128)(2,1)S(1)}, u32[]{:S(2)}, u32[]{:S(2)}) collective-permute-start(bf16[5,128,128]{2,1,0:T(8,128)(2,1)} %get-tuple-element.294), channel_id=1, source_target_pairs={{0,1},{1,0},{2,3},{3,2},{4,5},{5,4},{6,7},{7,6},{8,9},{9,8},{10,11... | collective-permute-start | bytes 491528 | tf_op jit(solution)/shard_map/ppermute | solution.py:490
  416.1 16.0 %collective-permute-start.94 = (bf16[5,128,128]{2,1,0:T(8,128)(2,1)}, bf16[5,128,128]{2,1,0:T(8,128)(2,1)S(1)}, u32[]{:S(2)}, u32[]{:S(2)}) collective-permute-start(bf16[5,128,128]{2,1,0:T(8,128)(2,1)} %get-tuple-element.295), channel_id=1, source_target_pairs={{0,2},{1,3},{2,0},{3,1},{4,6},{5,7},{6,4},{7,5},{8,10},{9,11},{10,... | collective-permute-start | bytes 491528 | tf_op jit(solution)/shard_map/ppermute | solution.py:490
  429.2 36.1 %collective-permute-start.121 = (bf16[20,128,128]{2,1,0:T(8,128)(2,1)}, bf16[20,128,128]{2,1,0:T(8,128)(2,1)S(1)}, u32[]{:S(2)}, u32[]{:S(2)}) collective-permute-start(bf16[20,128,128]{2,1,0:T(8,128)(2,1)} %fold.10), channel_id=1, source_target_pairs={{0,8},{1,9},{2,10},{3,11},{4,12},{5,13},{6,14},{7,15},{16,0},{17,1... | collective-permute-start | bytes 1966088 | tf_op jit(solution)/shard_map/ppermute | solution.py:533
  432.1 13.0 %collective-permute-start.98 = (bf16[5,128,128]{2,1,0:T(8,128)(2,1)S(1)}, bf16[5,128,128]{2,1,0:T(8,128)(2,1)S(1)}, u32[]{:S(2)}, u32[]{:S(2)}) collective-permute-start(bf16[5,128,128]{2,1,0:T(8,128)(2,1)S(1)} %copy-done.111), channel_id=1, source_target_pairs={{0,6},{1,7},{2,4},{3,5},{4,2},{5,3},{6,0},{7,1},{8,14},{9,15},{10,... | collective-permute-start | bytes 491528 | tf_op jit(solution)/shard_map/ppermute | solution.py:490
  436.4 11.5 %collective-permute-start.99 = (bf16[5,128,128]{2,1,0:T(8,128)(2,1)}, bf16[5,128,128]{2,1,0:T(8,128)(2,1)S(1)}, u32[]{:S(2)}, u32[]{:S(2)}) collective-permute-start(bf16[5,128,128]{2,1,0:T(8,128)(2,1)} %get-tuple-element.300), channel_id=1, source_target_pairs={{0,7},{1,6},{2,5},{3,4},{4,3},{5,2},{6,1},{7,0},{8,15},{9,14},{10,... | collective-permute-start | bytes 491528 | tf_op jit(solution)/shard_map/ppermute | solution.py:490
  440.0 11.7 %collective-permute-start.115 = (bf16[5,128,128]{2,1,0:T(8,128)(2,1)}, bf16[5,128,128]{2,1,0:T(8,128)(2,1)S(1)}, u32[]{:S(2)}, u32[]{:S(2)}) collective-permute-start(bf16[5,128,128]{2,1,0:T(8,128)(2,1)} %get-tuple-element.327), channel_id=1, source_target_pairs={{0,2},{1,3},{2,0},{3,1},{4,6},{5,7},{6,4},{7,5},{8,10},{9,11},{10,... | collective-permute-start | bytes 491528 | tf_op jit(solution)/shard_map/ppermute | solution.py:490
  448.0 14.7 %collective-permute-start.117 = (bf16[5,128,128]{2,1,0:T(8,128)(2,1)}, bf16[5,128,128]{2,1,0:T(8,128)(2,1)}, u32[]{:S(2)}, u32[]{:S(2)}) collective-permute-start(bf16[5,128,128]{2,1,0:T(8,128)(2,1)} %get-tuple-element.329), channel_id=1, source_target_pairs={{0,4},{1,5},{2,6},{3,7},{4,0},{5,1},{6,2},{7,3},{8,12},{9,13},{10,... | collective-permute-start | bytes 491528 | tf_op jit(solution)/shard_map/ppermute | solution.py:490
  449.1 16.1 %collective-permute-start.118 = (bf16[5,128,128]{2,1,0:T(8,128)(2,1)}, bf16[5,128,128]{2,1,0:T(8,128)(2,1)}, u32[]{:S(2)}, u32[]{:S(2)}) collective-permute-start(bf16[5,128,128]{2,1,0:T(8,128)(2,1)} %get-tuple-element.330), channel_id=1, source_target_pairs={{0,5},{1,4},{2,7},{3,6},{4,1},{5,0},{6,3},{7,2},{8,13},{9,12},{10,... | collective-permute-start | bytes 491528 | tf_op jit(solution)/shard_map/ppermute | solution.py:490
  451.7 13.6 %collective-permute-start.119 = (bf16[5,128,128]{2,1,0:T(8,128)(2,1)}, bf16[5,128,128]{2,1,0:T(8,128)(2,1)}, u32[]{:S(2)}, u32[]{:S(2)}) collective-permute-start(bf16[5,128,128]{2,1,0:T(8,128)(2,1)} %get-tuple-element.331), channel_id=1, source_target_pairs={{0,6},{1,7},{2,4},{3,5},{4,2},{5,3},{6,0},{7,1},{8,14},{9,15},{10,... | collective-permute-start | bytes 491528 | tf_op jit(solution)/shard_map/ppermute | solution.py:490
  462.7 30.6 %collective-permute-start.123 = (bf16[20,128,128]{2,1,0:T(8,128)(2,1)}, bf16[20,128,128]{2,1,0:T(8,128)(2,1)S(1)}, u32[]{:S(2)}, u32[]{:S(2)}) collective-permute-start(bf16[20,128,128]{2,1,0:T(8,128)(2,1)} %fold.9), channel_id=1, source_target_pairs={{0,16},{1,17},{2,18},{3,19},{4,20},{5,21},{6,22},{7,23},{16,24},{1... | collective-permute-start | bytes 1966088 | tf_op jit(solution)/shard_map/ppermute | solution.py:533
  469.9 26.9 %collective-permute-start.122 = (bf16[20,128,128]{2,1,0:T(8,128)(2,1)}, bf16[20,128,128]{2,1,0:T(8,128)(2,1)S(1)}, u32[]{:S(2)}, u32[]{:S(2)}) collective-permute-start(bf16[20,128,128]{2,1,0:T(8,128)(2,1)} %fold.11), channel_id=1, source_target_pairs={{0,8},{1,9},{2,10},{3,11},{4,12},{5,13},{6,14},{7,15},{16,0},{17,1... | collective-permute-start | bytes 1966088 | tf_op jit(solution)/shard_map/ppermute | solution.py:533
  (193 other events, 3037.0 us)

commit v2 on v1

--- a/solution.py
+++ b/solution.py
@@ -13,6 +13,14 @@
 AXES = ("arc", "vec")
 SMEM = pltpu.MemorySpace.SMEM
 VMEM = pltpu.MemorySpace.VMEM
+
+
+SMALL = pltpu.CompilerParams(vmem_limit_bytes=16 << 20)
+
+
+def in_vmem(*arrays):
+    placed = [pltpu.with_memory_space_constraint(array, pltpu.VMEM) for array in arrays]
+    return placed if len(placed) > 1 else placed[0]
 
 
 def inner_gram(left, right):
@@ -51,9 +59,8 @@
         entries = arcs_here * links
         self.cap = (entries + self.devices - 1) // self.devices + 1
         self.slots = self.plane * self.cap
-        self.pos_row = self.slots
-        self.own_row = self.slots + arcs_here
-        self.rows = self.slots + 2 * arcs_here
+        self.own_row = arcs_here
+        self.padded = -(-self.slots // 128) * 128
         self.order = [self.plane_at(i) for i in range(self.rings)]
         self.ring = [
             (self.order[i] * self.plane + p, self.order[(i + 1) % self.rings] * self.plane + p)
@@ -114,7 +121,9 @@
         return jnp.where(doubled < self.rings, doubled, 2 * self.rings - 1 - doubled)
 
 
-def tables_kernel(plan, me_ref, owner_cols, block_cols, tab_ref, owner_ref, block_ref):
+def tables_kernel(
+    plan, me_ref, owner_cols, block_cols, tab_ref, held_ref, owner_ref, block_ref, all_ref
+):
     me = me_ref[0]
     arcs, links, lanes = plan.arcs, plan.links, tab_ref.shape[1]
     z = lax.div(me, plan.plane)
@@ -139,13 +148,22 @@
         rank = jnp.dot(before, named, preferred_element_type=jnp.float32).astype(jnp.int32)
         return held, rank
 
+    all_ref[...] = jnp.zeros_like(all_ref)
     for q in range(plan.plane):
         held, rank = incidence(q * arcs)
         for r in range(plan.cap):
             at_rank = jnp.where(rank == r, held, 0)
-            tab_ref[r * plan.plane + q : r * plan.plane + q + 1, :] = jnp.sum(
+            all_ref[r * plan.plane + q : r * plan.plane + q + 1, :] = jnp.sum(
                 at_rank, axis=0, keepdims=True
             )
+    columns = jnp.zeros((held_ref.shape[1], 128), jnp.int32)
+    wide = lax.broadcasted_iota(jnp.int32, columns.shape, 1)
+    across = lax.broadcasted_iota(jnp.int32, all_ref.shape, 1)
+    for s in range(plan.rings):
+        column = plan.source_plane(me, s) * plan.plane + lax.rem(me, plan.plane)
+        picked = jnp.sum(jnp.where(across == column, all_ref[...], 0), axis=1, keepdims=True)
+        columns = jnp.where(wide == s, picked, columns)
+    held_ref[...] = columns.T[: held_ref.shape[0]]
     row = pl.multiple_of(lax.rem(me, plan.plane) * arcs, arcs)
     held, rank = incidence(row)
     place = plan.place_of(z)
@@ -154,7 +172,7 @@
     here, there = lax.rem(me, plan.plane), lax.rem(owners, plan.plane)
     offset = here ^ there if plan.paired else lax.rem(here - there + plan.plane, plan.plane)
     slot = step * plan.slots + offset * plan.cap + rank
-    tab_ref[plan.pos_row : plan.pos_row + arcs, :] = slot
+    tab_ref[:arcs, :] = slot
     mine = jnp.zeros((arcs, lanes), jnp.int32)
     owner = owner_ref[pl.ds(row, arcs), :]
     for k in range(links):
@@ -166,42 +184,46 @@
     lanes = -(-plan.devices // 128) * 128
     return pl.pallas_call(
         functools.partial(tables_kernel, plan),
-        out_shape=jax.ShapeDtypeStruct((plan.rows, lanes), jnp.int32),
+        out_shape=[
+            jax.ShapeDtypeStruct((2 * plan.arcs, lanes), jnp.int32),
+            jax.ShapeDtypeStruct((-(-plan.rings // 8) * 8, plan.padded), jnp.int32),
+        ],
         in_specs=[
             pl.BlockSpec(memory_space=SMEM),
             pl.BlockSpec(memory_space=VMEM),
             pl.BlockSpec(memory_space=VMEM),
         ],
-        out_specs=pl.BlockSpec(memory_space=VMEM),
-        scratch_shapes=[pltpu.VMEM((plan.plane * plan.arcs, plan.links), jnp.int32)] * 2,
+        out_specs=[pl.BlockSpec(memory_space=VMEM)] * 2,
+        scratch_shapes=[pltpu.VMEM((plan.plane * plan.arcs, plan.links), jnp.int32)] * 2
+        + [pltpu.VMEM((plan.padded, lanes), jnp.int32)],
+        compiler_params=SMALL,
         name="tables",
     )(me, coupling_owner.T, coupling_block.T)
 
 
-def pick_kernel(plan, step, me_ref, tab_ref, chunk_ref, *out_refs):
-    me = me_ref[0]
-    here = lax.rem(me, plan.plane)
-    column = plan.source_plane(me, step) * plan.plane + here
+def pick_kernel(plan, step, me_ref, held_ref, chunk_ref, *out_refs):
+    here = lax.rem(me_ref[0], plan.plane)
     for offset, out_ref in enumerate(out_refs):
         q = plan.target_traced(here, offset)
         for r in range(plan.cap):
-            block = jnp.maximum(tab_ref[r * plan.plane + q, column] - 1, 0)
+            block = jnp.maximum(held_ref[step, r * plan.plane + q] - 1, 0)
             out_ref[r] = chunk_ref[block]
 
 
-def pick(plan, step, me, tab, chunk):
+def pick(plan, step, me, held, chunk):
     shape = (plan.cap,) + chunk.shape[1:]
     return pl.pallas_call(
         functools.partial(pick_kernel, plan, step),
-        out_shape=[jax.ShapeDtypeStruct(shape, chunk.dtype)] * plan.plane,
+        out_shape=[pltpu.VMEM(shape, chunk.dtype)] * plan.plane,
         in_specs=[
             pl.BlockSpec(memory_space=SMEM),
             pl.BlockSpec(memory_space=SMEM),
             pl.BlockSpec(memory_space=VMEM),
         ],
         out_specs=[pl.BlockSpec(memory_space=VMEM)] * plan.plane,
+        compiler_params=SMALL,
         name="pick",
-    )(me, tab, chunk)
+    )(me, held, in_vmem(chunk))
 
 
 def narrow_dot(left, right, contract=1):
@@ -242,7 +264,7 @@
     for g in group:
         row = arc * len(group) + g
         for k in range(plan.links):
-            spot = tab_ref[plan.pos_row + row, tab_ref[plan.own_row + row, k]]
+            spot = tab_ref[row, tab_ref[plan.own_row + row, k]]
             spots[g].append(spot)
             fetched[g, k * rows : (k + 1) * rows, :] = arrived[spot]
     coupled = [narrow_dot(panel_ref[g], fetched[g]) for g in group]
@@ -277,7 +299,7 @@
                 pl.BlockSpec((group, arc_rows, width), lambda i, t: (i, 0, 0)),
                 pl.BlockSpec((group, arc_rows, arc_rows), lambda i, t: (i, 0, 0)),
             ],
-            out_specs=[anywhere] * (plan.rings * plan.plane),
+            out_specs=[pl.BlockSpec(memory_space=VMEM)] * (plan.rings * plan.plane),
             scratch_shapes=[
                 pltpu.VMEM((total,) + block, jnp.bfloat16),
                 pltpu.VMEM((total,) + block, jnp.bfloat16),
@@ -285,16 +307,14 @@
                 pltpu.SemaphoreType.DMA((plan.rings * plan.plane,)),
             ],
         ),
-        out_shape=[jax.ShapeDtypeStruct((plan.cap,) + block, jnp.bfloat16)]
-        * (plan.rings * plan.plane),
+        out_shape=[pltpu.VMEM((plan.cap,) + block, jnp.bfloat16)] * (plan.rings * plan.plane),
+        compiler_params=pltpu.CompilerParams(vmem_limit_bytes=32 << 20),
         name="arcs",
     )(tab, *arrived, coupling_panel, inv_factor)
 
 
-def add_up(plan, step, me_ref, tab_ref, got_refs, part_refs, acc):
-    me = me_ref[0]
-    here = lax.rem(me, plan.plane)
-    column = plan.source_plane(me, step) * plan.plane + here
+def add_up(plan, step, me_ref, held_ref, got_refs, part_refs, acc):
+    here = lax.rem(me_ref[0], plan.plane)
     start = jnp.zeros(acc.shape, jnp.float32)
     for part_ref in part_refs:
         start = start + part_ref[...].astype(jnp.float32)
@@ -302,24 +322,24 @@
     for offset, got_ref in enumerate(got_refs):
         q = plan.source_traced(here, offset)
         for r in range(plan.cap):
-            held = tab_ref[r * plan.plane + q, column]
+            held = held_ref[step, r * plan.plane + q]
 
             @pl.when(held > 0)
             def _():
                 acc[held - 1] += got_ref[r].astype(jnp.float32)
 
 
-def fold_kernel(plan, step, me_ref, tab_ref, *refs):
+def fold_kernel(plan, step, me_ref, held_ref, *refs):
     got_refs, part_refs = refs[: plan.plane], refs[plan.plane : -2]
     out_ref, acc = refs[-2], refs[-1]
-    add_up(plan, step, me_ref, tab_ref, got_refs, part_refs, acc)
+    add_up(plan, step, me_ref, held_ref, got_refs, part_refs, acc)
     out_ref[...] = acc[...].astype(out_ref.dtype)
 
 
-def image_kernel(plan, both, me_ref, tab_ref, field_ref, prior_ref, *refs):
+def image_kernel(plan, both, me_ref, held_ref, field_ref, prior_ref, *refs):
     got_refs, part_refs = refs[: plan.plane], refs[plan.plane : -3]
     image_ref, gram_ref, acc = refs[-3:]
-    add_up(plan, 0, me_ref, tab_ref, got_refs, part_refs, acc)
+    add_up(plan, 0, me_ref, held_ref, got_refs, part_refs, acc)
     rows = acc.shape[1]
     for b in range(plan.blocks):
         image_ref[b] = acc[b].T + prior_ref[:, b : b + 1] * field_ref[b]
@@ -351,22 +371,23 @@
     )
 
 
-def fold(plan, step, me, tab, got, parts):
+def fold(plan, step, me, held, got, parts):
     shape = (plan.blocks,) + got[0].shape[1:]
-    args = (me, tab, *got, *parts)
+    args = (me, held, *in_vmem(*got, *parts))
     return pl.pallas_call(
         functools.partial(fold_kernel, plan, step),
-        out_shape=jax.ShapeDtypeStruct(shape, jnp.bfloat16),
+        out_shape=pltpu.VMEM(shape, jnp.bfloat16),
         in_specs=fold_specs(args),
         out_specs=pl.BlockSpec(memory_space=VMEM),
         scratch_shapes=[pltpu.VMEM(shape, jnp.float32)],
+        compiler_params=SMALL,
         name="fold",
     )(*args)
 
 
-def fold_image(plan, me, tab, got, parts, field, prior_cols, both):
+def fold_image(plan, me, held, got, parts, field, prior_cols, both):
     shape, cols = field.shape, field.shape[2]
-    args = (me, tab, field, prior_cols, *got, *parts)
+    args = (me, held, field, prior_cols, *in_vmem(*got, *parts))
     return pl.pallas_call(
         functools.partial(image_kernel, plan, both),
         out_shape=[
@@ -376,6 +397,7 @@
         in_specs=fold_specs(args),
         out_specs=[pl.BlockSpec(memory_space=VMEM)] * 2,
         scratch_shapes=[pltpu.VMEM(shape, jnp.float32)],
+        compiler_params=SMALL,
         name="image",
     )(*args)
 
@@ -400,6 +422,7 @@
         out_shape=[jax.ShapeDtypeStruct(field.shape, jnp.float32)] * 2,
         in_specs=[spec] * 4 + [pl.BlockSpec((cols, cols), lambda i: (0, 0))],
         out_specs=[spec] * 2,
+        compiler_params=SMALL,
         name="update",
     )(field, image, solution_field, residual, step_mat)
 
@@ -479,6 +502,7 @@
         kernel,
         out_shape=[jax.ShapeDtypeStruct(shape, jnp.float32)] * outputs,
         scratch_shapes=[pltpu.VMEM(shape, jnp.float32)] * scratch,
+        compiler_params=SMALL,
         name="solve",
     )(*args)
 
@@ -501,17 +525,18 @@
         out_shape=jax.ShapeDtypeStruct(me.shape, me.dtype),
         in_specs=[pl.BlockSpec(memory_space=SMEM)],
         out_specs=pl.BlockSpec(memory_space=SMEM),
+        compiler_params=SMALL,
         name="gate",
     )(me)
 
 
-def apply_schur(plan, me, tab, field, prior_cols, coupling_panel, inv_factor, both):
+def apply_schur(plan, me, tab, held, field, prior_cols, coupling_panel, inv_factor, both):
     chunk, arrived = field.astype(jnp.bfloat16), []
     for s in range(plan.rings):
         following = None
         if s + 1 < plan.rings:
             following = lax.ppermute(chunk, AXES, plan.ring)
-        chosen = pick(plan, s, me, tab, chunk)
+        chosen = pick(plan, s, me, held, chunk)
         arrived += trade_plane(plan, chosen)
         if s + 1 < plan.rings:
             me = gate(me)
@@ -527,9 +552,9 @@
         if s:
             me = gate(me)
         if s == 0:
-            image, grams = fold_image(plan, me, tab, got, sources, field, prior_cols, both)
+            image, grams = fold_image(plan, me, held, got, sources, field, prior_cols, both)
             return image, grams, me
-        folded.append(fold(plan, s, me, tab, got, sources))
+        folded.append(fold(plan, s, me, held, got, sources))
         moved[s] = lax.ppermute(folded[j], AXES, plan.shift_back(s))
 
 
@@ -538,7 +563,7 @@
 ):
     plan = Plan(mesh, coupling_panel.shape[0], coupling_owner.shape[1], right_side.shape[0])
     me = lax.axis_index(AXES).astype(jnp.int32).reshape(1)
-    tab = make_tables(plan, me, coupling_owner, coupling_block)
+    tab, held = make_tables(plan, me, coupling_owner, coupling_block)
     prior_cols = prior_diag.T
     solution_field = None
     residual = right_side
@@ -547,7 +572,7 @@
     for sweep_index in range(ITERS):
         last = sweep_index + 1 == ITERS
         image_vec, grams, me = apply_schur(
-            plan, me, tab, direction, prior_cols, coupling_panel, inv_factor, not last
+            plan, me, tab, held, direction, prior_cols, coupling_panel, inv_factor, not last
         )
         if last:
             (step_mat,) = small_solve(last_kernel, (sum_all(grams), res_gram), 1, 1)

time: 552 us -> 553 us (level)
  Pallas kernels: 165 us -> 148 us
  waiting for transfers between devices: 196 us -> 209 us
  local copies, waits for them, and re-layouts: 8.26 us -> 15.2 us
    pallas_call x15, Pallas kernels: 48.2 us -> 23.8 us  [the longest x6 12.4 us: fold(): pl.pallas_call(functools.partial(fold_kernel, plan, step), out_shape=pltp...]
    pallas_call x2, Pallas kernels: 28.5 us -> 46 us  [run_arcs(): pl.pallas_call(functools.partial(arcs_kernel, plan), grid_spec=pltpu.Pref...]
    unnamed x233 -> x41, local copies, waits for them, and re-layouts: 6.89 us -> 14.5 us
    ppermute x112, waiting for transfers between devices: 135 us -> 142 us  [trade_plane(): lax.ppermute(buffers[offset], AXES, plan.shift_plane(offset))]
  transfers between devices with their start and end apart: 125 -> 125, of which waited for: 61 -> 67; matrix products, arithmetic and copies ran while one was open for 1% -> 1% of each run, Pallas kernels for 11% -> 7%
where the time goes in v2:
time: 553 us; the launch traced here: 552 us
  waiting for transfers between devices  209 us (38%)
  Pallas kernels  148 us (27%)
  starting transfers between devices  135 us (24%)
  blocking collectives  35.9 us (6%)
  local copies, waits for them, and re-layouts  15.2 us (3%)
  matrix products  6.81 us (1%)
    ppermute x112, waiting for transfers between devices, trade_plane(): lax.ppermute(buffers[offset], AXES, plan.shift_plane(offset))  142 us
    ppermute x112, starting transfers between devices, trade_plane(): lax.ppermute(buffers[offset], AXES, plan.shift_plane(offset))  106 us
    ppermute x6, waiting for transfers between devices, apply_schur(): following = lax.ppermute(chunk, AXES, plan.ring)  53.9 us
    pallas_call x2, Pallas kernels, small_solve(): pl.pallas_call(kernel, out_shape=[jax.ShapeDtypeStruct(shape, jnp.float32...  50.5 us
    pallas_call x2, Pallas kernels, run_arcs(): pl.pallas_call(functools.partial(arcs_kernel, plan), grid_spec=pltpu.Pref...  46 us
    all_to_all x3, blocking collectives, trade(): return lax.all_to_all(buffer, AXES, split_axis=0, concat_axis=0, tiled=True)  35.9 us
    ppermute x6, starting transfers between devices, apply_schur(): following = lax.ppermute(chunk, AXES, plan.ring)  16.5 us
    unnamed x41, local copies, waits for them, and re-layouts  14.5 us
  transfers between devices with their start and end apart: 125, of which 67 were waited for; matrix products, arithmetic and copies ran while one was open for 1% of the time, Pallas kernels for 7%

profile of v2, /device:TPU:0, one launch (start us, length us, event | category | flops | bytes accessed | tf_op | source)
XLA Modules:
  0.0 552.3 jit_solution(6623862606528783845)
XLA Ops:
  2.1 4.1 collective-permute-start.7
  6.2 14.0 %collective-permute-done.7.chunk_ref = bf16[20,128,128]{2,1,0:T(8,128)(2,1)S(1)} collective-permute-done((bf16[20,128,128]{2,1,0:T(8,128)(2,1)S(1)}, bf16[20,128,128]{2,1,0:T(8,128)(2,1)S(1)}, u32[]{:S(2)}, u32[]{:S(2)}) %collective-permute-start.7) | collective-permute-done | bytes 655392 | tf_op jit(solution)/shard_map/ppermute | solution.py:538
  20.2 3.4 collective-permute-start.15
  25.4 11.3 %collective-permute-done.15.chunk_ref = bf16[20,128,128]{2,1,0:T(8,128)(2,1)S(1)} collective-permute-done((bf16[20,128,128]{2,1,0:T(8,128)(2,1)S(1)}, bf16[20,128,128]{2,1,0:T(8,128)(2,1)S(1)}, u32[]{:S(2)}, u32[]{:S(2)}) %collective-permute-start.15) | collective-permute-done | bytes 655392 | tf_op jit(solution)/shard_map/ppermute | solution.py:538
  36.7 3.4 collective-permute-start.23
  46.2 3.3 collective-permute-start.5
  70.3 3.1 collective-permute-done.14.refs_15_
  86.2 3.6 collective-permute-done.21.refs_22_
  97.4 3.3 collective-permute-done.26.refs_27_
  100.8 3.7 collective-permute-done.29.refs_30_
  105.7 3.4 copy-done.1
  109.1 23.3 %arcs.2 = (bf16[5,128,128]{2,1,0:T(8,128)(2,1)S(1)}, bf16[5,128,128]{2,1,0:T(8,128)(2,1)S(1)}, bf16[5,128,128]{2,1,0:T(8,128)(2,1)}, bf16[5,128,128]{2,1,0:T(8,1...) custom-call(s32[32,128]{1,0:T(8,128)S(1)} %get-tuple-element.172.tab, ...), custom_call_target="tpu_custom_call" | custom-call | tf_op jit(solution)/shard_map/arcs/pallas_call | solution.py:292
  145.0 4.1 collective-permute-done.50.refs_6_
  149.1 2.9 collective-permute-done.51.refs_7_
  165.5 4.1 collective-permute-done.36.refs_6_
  185.1 3.0 collective-permute-start.61
  189.3 2.8 fold.8
  197.4 4.4 collective-permute-done.39.refs_2_
  208.8 2.9 collective-permute-done.43.refs_6_
  211.7 3.4 collective-permute-done.44.refs_7_
  215.1 3.3 collective-permute-done.60.refs_8_
  220.3 6.0 %image.2 = (f32[20,128,128]{2,1,0:T(8,128)S(1)}, f32[2,128,128]{2,1,0:T(8,128)S(1)}) custom-call(s32[1]{0:T(128)} %gate.17.me_ref.in_ref, s32[8,128]{1,0:T(8,128)S(1)} %get-tuple-element.171.held_ref, f32[20,128,128]{2,1,0:T(8,128)S(1)} %copy-done, f32[128,20]{1,0:T(8,128)S(1)} %bitcast.31, bf16[5,128,128]{2,1,0:T(8,128)(2,1)S(1)} %get-tuple-element.221.refs_0_, ...), custom_call_target="tpu_custom_call" | custom-call | tf_op jit(solution)/shard_map/image/pallas_call | solution.py:391
  226.5 13.8 %all_to_all.20 = f32[32,12,128]{2,1,0:T(8,128)S(1)} all-to-all(f32[32,12,128]{2,1,0:T(8,128)S(1)} %reshape.22), channel_id=1, replica_groups=mesh['arc'=8,'vec'=4] {'arc','vec'}, dimensions={0} | all-to-all | bytes 393216 | tf_op jit(solution)/shard_map/all_to_all | solution.py:39
  240.4 12.8 %all_to_all.21 = f32[32,12,128]{2,1,0:T(8,128)S(1)} all-to-all(f32[32,12,128]{2,1,0:T(8,128)S(1)} %broadcast_in_dim.7), channel_id=1, replica_groups=mesh['arc'=8,'vec'=4] {'arc','vec'}, dimensions={0} | all-to-all | bytes 393216 | tf_op jit(solution)/shard_map/all_to_all | solution.py:39
  253.2 33.5 %solve.2 = (f32[128,128]{1,0:T(8,128)S(1)}, f32[128,128]{1,0:T(8,128)S(1)}, f32[128,128]{1,0:T(8,128)S(1)}) custom-call(f32[3,128,128]{2,1,0:T(8,128)S(1)} %reshape.23.grams_ref), custom_call_target="tpu_custom_call" | custom-call | tf_op jit(solution)/shard_map/solve/pallas_call | solution.py:501
  289.4 16.3 %collective-permute-done.69.chunk_ref = bf16[20,128,128]{2,1,0:T(8,128)(2,1)S(1)} collective-permute-done((bf16[20,128,128]{2,1,0:T(8,128)(2,1)S(1)}, bf16[20,128,128]{2,1,0:T(8,128)(2,1)S(1)}, u32[]{:S(2)}, u32[]{:S(2)}) %collective-permute-start.69) | collective-permute-done | bytes 655392 | tf_op jit(solution)/shard_map/ppermute | solution.py:538
  309.0 12.4 %collective-permute-done.77.chunk_ref = bf16[20,128,128]{2,1,0:T(8,128)(2,1)S(1)} collective-permute-done((bf16[20,128,128]{2,1,0:T(8,128)(2,1)S(1)}, bf16[20,128,128]{2,1,0:T(8,128)(2,1)S(1)}, u32[]{:S(2)}, u32[]{:S(2)}) %collective-permute-start.77) | collective-permute-done | bytes 655392 | tf_op jit(solution)/shard_map/ppermute | solution.py:538
  321.4 3.4 collective-permute-start.85
  324.8 3.5 collective-permute-start.66
  336.5 3.9 collective-permute-done.67.refs_6_
  353.0 4.1 collective-permute-done.75.refs_14_
  368.2 3.6 collective-permute-done.83.refs_22_
  382.0 3.8 collective-permute-done.91.refs_30_
  385.8 3.0 collective-permute-done.92.refs_31_
  388.9 3.4 copy-done.2
  392.2 22.7 %arcs.3 = (bf16[5,128,128]{2,1,0:T(8,128)(2,1)S(1)}, bf16[5,128,128]{2,1,0:T(8,128)(2,1)S(1)}, bf16[5,128,128]{2,1,0:T(8,128)(2,1)S(1)}, bf16[5,128,128]{2,1,0:T...) custom-call(s32[32,128]{1,0:T(8,128)S(1)} %get-tuple-element.172.tab, ...), custom_call_target="tpu_custom_call" | custom-call | tf_op jit(solution)/shard_map/arcs/pallas_call | solution.py:292
  427.3 4.1 collective-permute-done.112.refs_6_
  447.7 4.0 collective-permute-done.98.refs_6_
  479.0 4.1 collective-permute-done.101.refs_2_
  489.4 4.2 collective-permute-done.105.refs_6_
  493.6 3.3 collective-permute-done.106.refs_7_
  496.8 5.0 collective-permute-done.122.refs_8_
  501.8 4.5 image.3
  507.4 9.3 %all_to_all.22 = f32[32,4,128]{2,1,0:T(4,128)S(1)} all-to-all(f32[32,4,128]{2,1,0:T(4,128)S(1)} %bitcast.34), channel_id=1, replica_groups=mesh['arc'=8,'vec'=4] {'arc','vec'}, dimensions={0} | all-to-all | bytes 131072 | tf_op jit(solution)/shard_map/all_to_all | solution.py:39
  517.4 2.8 all-to-all-start.3
  522.4 4.9 all-to-all-done.3
  527.3 17.0 %solve.3.step_ref = f32[128,128]{1,0:T(8,128)S(1)} custom-call(f32[1,128,128]{2,1,0:T(8,128)S(1)} %bitcast.33, f32[128,128]{1,0:T(8,128)S(1)} %get-tuple-element.339.res_ref), custom_call_target="tpu_custom_call" | custom-call | tf_op jit(solution)/shard_map/solve/pallas_call | solution.py:501
  548.3 4.1 update.1
  (292 shorter events, 227.0 us)
Async XLA Ops:
  2.1 18.1 %collective-permute-start.7 = (bf16[20,128,128]{2,1,0:T(8,128)(2,1)S(1)}, bf16[20,128,128]{2,1,0:T(8,128)(2,1)S(1)}, u32[]{:S(2)}, u32[]{:S(2)}) collective-permute-start(bf16[20,128,128]{2,1,0:T(8,128)(2,1)S(1)} %convert_element_type.6.chunk_ref), channel_id=1, source_target_pairs={{0,16},{1,17},{2,18},{3,19},{4,20},{5,21},{6,22},{7,23},{16,24},{1... | collective-permute-start | bytes 1966088 | tf_op jit(solution)/shard_map/ppermute | solution.py:538
  20.2 16.5 %collective-permute-start.15 = (bf16[20,128,128]{2,1,0:T(8,128)(2,1)S(1)}, bf16[20,128,128]{2,1,0:T(8,128)(2,1)S(1)}, u32[]{:S(2)}, u32[]{:S(2)}) collective-permute-start(bf16[20,128,128]{2,1,0:T(8,128)(2,1)S(1)} %collective-permute-done.7.chunk_ref), channel_id=1, source_target_pairs={{0,16},{1,17},{2,18},{3,19},{4,20},{5,21},{6,22},{7,23},{16,24},{1... | collective-permute-start | bytes 1966088 | tf_op jit(solution)/shard_map/ppermute | solution.py:538
  25.4 17.8 %collective-permute-start = (bf16[5,128,128]{2,1,0:T(8,128)(2,1)S(1)}, bf16[5,128,128]{2,1,0:T(8,128)(2,1)S(1)}, u32[]{:S(2)}, u32[]{:S(2)}) collective-permute-start(bf16[5,128,128]{2,1,0:T(8,128)(2,1)S(1)} %get-tuple-element.174), channel_id=1, source_target_pairs={{0,1},{1,0},{2,3},{3,2},{4,5},{5,4},{6,7},{7,6},{8,9},{9,8},{10,11... | collective-permute-start | bytes 491528 | tf_op jit(solution)/shard_map/ppermute | solution.py:514
  36.7 37.5 %collective-permute-start.23 = (bf16[20,128,128]{2,1,0:T(8,128)(2,1)S(1)}, bf16[20,128,128]{2,1,0:T(8,128)(2,1)S(1)}, u32[]{:S(2)}, u32[]{:S(2)}) collective-permute-start(bf16[20,128,128]{2,1,0:T(8,128)(2,1)S(1)} %collective-permute-done.15.chunk_ref), channel_id=1, source_target_pairs={{0,16},{1,17},{2,18},{3,19},{4,20},{5,21},{6,22},{7,23},{16,24},{1... | collective-permute-start | bytes 1966088 | tf_op jit(solution)/shard_map/ppermute | solution.py:538
  51.0 11.7 %collective-permute-start.10 = (bf16[5,128,128]{2,1,0:T(8,128)(2,1)S(1)}, bf16[5,128,128]{2,1,0:T(8,128)(2,1)S(1)}, u32[]{:S(2)}, u32[]{:S(2)}) collective-permute-start(bf16[5,128,128]{2,1,0:T(8,128)(2,1)S(1)} %get-tuple-element.184), channel_id=1, source_target_pairs={{0,3},{1,2},{2,1},{3,0},{4,7},{5,6},{6,5},{7,4},{8,11},{9,10},{10,... | collective-permute-start | bytes 491528 | tf_op jit(solution)/shard_map/ppermute | solution.py:514
  51.5 12.9 %collective-permute-start.11 = (bf16[5,128,128]{2,1,0:T(8,128)(2,1)S(1)}, bf16[5,128,128]{2,1,0:T(8,128)(2,1)S(1)}, u32[]{:S(2)}, u32[]{:S(2)}) collective-permute-start(bf16[5,128,128]{2,1,0:T(8,128)(2,1)S(1)} %get-tuple-element.185), channel_id=1, source_target_pairs={{0,4},{1,5},{2,6},{3,7},{4,0},{5,1},{6,2},{7,3},{8,12},{9,13},{10,... | collective-permute-start | bytes 491528 | tf_op jit(solution)/shard_map/ppermute | solution.py:514
  55.1 12.2 %collective-permute-start.12 = (bf16[5,128,128]{2,1,0:T(8,128)(2,1)S(1)}, bf16[5,128,128]{2,1,0:T(8,128)(2,1)S(1)}, u32[]{:S(2)}, u32[]{:S(2)}) collective-permute-start(bf16[5,128,128]{2,1,0:T(8,128)(2,1)S(1)} %get-tuple-element.186), channel_id=1, source_target_pairs={{0,5},{1,4},{2,7},{3,6},{4,1},{5,0},{6,3},{7,2},{8,13},{9,12},{10,... | collective-permute-start | bytes 491528 | tf_op jit(solution)/shard_map/ppermute | solution.py:514
  67.3 10.9 %collective-permute-start.9 = (bf16[5,128,128]{2,1,0:T(8,128)(2,1)S(1)}, bf16[5,128,128]{2,1,0:T(8,128)(2,1)S(1)}, u32[]{:S(2)}, u32[]{:S(2)}) collective-permute-start(bf16[5,128,128]{2,1,0:T(8,128)(2,1)S(1)} %get-tuple-element.183), channel_id=1, source_target_pairs={{0,2},{1,3},{2,0},{3,1},{4,6},{5,7},{6,4},{7,5},{8,10},{9,11},{10,... | collective-permute-start | bytes 491528 | tf_op jit(solution)/shard_map/ppermute | solution.py:514
  81.2 11.1 %collective-permute-start.22 = (bf16[5,128,128]{2,1,0:T(8,128)(2,1)S(1)}, bf16[5,128,128]{2,1,0:T(8,128)(2,1)S(1)}, u32[]{:S(2)}, u32[]{:S(2)}) collective-permute-start(bf16[5,128,128]{2,1,0:T(8,128)(2,1)S(1)} %get-tuple-element.196), channel_id=1, source_target_pairs={{0,7},{1,6},{2,5},{3,4},{4,3},{5,2},{6,1},{7,0},{8,15},{9,14},{10,... | collective-permute-start | bytes 491528 | tf_op jit(solution)/shard_map/ppermute | solution.py:514
  83.8 12.5 %collective-permute-start.25 = (bf16[5,128,128]{2,1,0:T(8,128)(2,1)S(1)}, bf16[5,128,128]{2,1,0:T(8,128)(2,1)S(1)}, u32[]{:S(2)}, u32[]{:S(2)}) collective-permute-start(bf16[5,128,128]{2,1,0:T(8,128)(2,1)S(1)} %get-tuple-element.199), channel_id=1, source_target_pairs={{0,2},{1,3},{2,0},{3,1},{4,6},{5,7},{6,4},{7,5},{8,10},{9,11},{10,... | collective-permute-start | bytes 491528 | tf_op jit(solution)/shard_map/ppermute | solution.py:514
  85.1 15.7 %collective-permute-start.26 = (bf16[5,128,128]{2,1,0:T(8,128)(2,1)S(1)}, bf16[5,128,128]{2,1,0:T(8,128)(2,1)S(1)}, u32[]{:S(2)}, u32[]{:S(2)}) collective-permute-start(bf16[5,128,128]{2,1,0:T(8,128)(2,1)S(1)} %get-tuple-element.200), channel_id=1, source_target_pairs={{0,3},{1,2},{2,1},{3,0},{4,7},{5,6},{6,5},{7,4},{8,11},{9,10},{10,... | collective-permute-start | bytes 491528 | tf_op jit(solution)/shard_map/ppermute | solution.py:514
  89.9 10.9 %collective-permute-start.27 = (bf16[5,128,128]{2,1,0:T(8,128)(2,1)S(1)}, bf16[5,128,128]{2,1,0:T(8,128)(2,1)S(1)}, u32[]{:S(2)}, u32[]{:S(2)}) collective-permute-start(bf16[5,128,128]{2,1,0:T(8,128)(2,1)S(1)} %get-tuple-element.201), channel_id=1, source_target_pairs={{0,4},{1,5},{2,6},{3,7},{4,0},{5,1},{6,2},{7,3},{8,12},{9,13},{10,... | collective-permute-start | bytes 491528 | tf_op jit(solution)/shard_map/ppermute | solution.py:514
  137.0 12.2 %collective-permute-start.50 = (bf16[5,128,128]{2,1,0:T(8,128)(2,1)S(1)}, bf16[5,128,128]{2,1,0:T(8,128)(2,1)S(1)}, u32[]{:S(2)}, u32[]{:S(2)}) collective-permute-start(bf16[5,128,128]{2,1,0:T(8,128)(2,1)S(1)} %get-tuple-element.243), channel_id=1, source_target_pairs={{0,6},{1,7},{2,4},{3,5},{4,2},{5,3},{6,0},{7,1},{8,14},{9,15},{10,... | collective-permute-start | bytes 491528 | tf_op jit(solution)/shard_map/ppermute | solution.py:514
  140.6 11.5 %collective-permute-start.51 = (bf16[5,128,128]{2,1,0:T(8,128)(2,1)S(1)}, bf16[5,128,128]{2,1,0:T(8,128)(2,1)S(1)}, u32[]{:S(2)}, u32[]{:S(2)}) collective-permute-start(bf16[5,128,128]{2,1,0:T(8,128)(2,1)S(1)} %get-tuple-element.244), channel_id=1, source_target_pairs={{0,7},{1,6},{2,5},{3,4},{4,3},{5,2},{6,1},{7,0},{8,15},{9,14},{10,... | collective-permute-start | bytes 491528 | tf_op jit(solution)/shard_map/ppermute | solution.py:514
  142.3 14.2 %collective-permute-start.31 = (bf16[5,128,128]{2,1,0:T(8,128)(2,1)S(1)}, bf16[5,128,128]{2,1,0:T(8,128)(2,1)S(1)}, u32[]{:S(2)}, u32[]{:S(2)}) collective-permute-start(bf16[5,128,128]{2,1,0:T(8,128)(2,1)S(1)} %get-tuple-element.214), channel_id=1, source_target_pairs={{0,1},{1,0},{2,3},{3,2},{4,5},{5,4},{6,7},{7,6},{8,9},{9,8},{10,11... | collective-permute-start | bytes 491528 | tf_op jit(solution)/shard_map/ppermute | solution.py:514
  143.3 13.8 %collective-permute-start.32 = (bf16[5,128,128]{2,1,0:T(8,128)(2,1)S(1)}, bf16[5,128,128]{2,1,0:T(8,128)(2,1)S(1)}, u32[]{:S(2)}, u32[]{:S(2)}) collective-permute-start(bf16[5,128,128]{2,1,0:T(8,128)(2,1)S(1)} %get-tuple-element.215), channel_id=1, source_target_pairs={{0,2},{1,3},{2,0},{3,1},{4,6},{5,7},{6,4},{7,5},{8,10},{9,11},{10,... | collective-permute-start | bytes 491528 | tf_op jit(solution)/shard_map/ppermute | solution.py:514
  154.0 35.2 %collective-permute-start.59 = (bf16[20,128,128]{2,1,0:T(8,128)(2,1)S(1)}, bf16[20,128,128]{2,1,0:T(8,128)(2,1)S(1)}, u32[]{:S(2)}, u32[]{:S(2)}) collective-permute-start(bf16[20,128,128]{2,1,0:T(8,128)(2,1)S(1)} %fold.7), channel_id=1, source_target_pairs={{0,8},{1,9},{2,10},{3,11},{4,12},{5,13},{6,14},{7,15},{16,0},{17,1... | collective-permute-start | bytes 1966088 | tf_op jit(solution)/shard_map/ppermute | solution.py:558
  157.1 12.4 %collective-permute-start.36 = (bf16[5,128,128]{2,1,0:T(8,128)(2,1)S(1)}, bf16[5,128,128]{2,1,0:T(8,128)(2,1)S(1)}, u32[]{:S(2)}, u32[]{:S(2)}) collective-permute-start(bf16[5,128,128]{2,1,0:T(8,128)(2,1)S(1)} %get-tuple-element.219), channel_id=1, source_target_pairs={{0,6},{1,7},{2,4},{3,5},{4,2},{5,3},{6,0},{7,1},{8,14},{9,15},{10,... | collective-permute-start | bytes 491528 | tf_op jit(solution)/shard_map/ppermute | solution.py:514
  160.4 11.5 %collective-permute-start.37 = (bf16[5,128,128]{2,1,0:T(8,128)(2,1)S(1)}, bf16[5,128,128]{2,1,0:T(8,128)(2,1)S(1)}, u32[]{:S(2)}, u32[]{:S(2)}) collective-permute-start(bf16[5,128,128]{2,1,0:T(8,128)(2,1)S(1)} %get-tuple-element.220), channel_id=1, source_target_pairs={{0,7},{1,6},{2,5},{3,4},{4,3},{5,2},{6,1},{7,0},{8,15},{9,14},{10,... | collective-permute-start | bytes 491528 | tf_op jit(solution)/shard_map/ppermute | solution.py:514
  164.8 11.0 %collective-permute-start.53 = (bf16[5,128,128]{2,1,0:T(8,128)(2,1)S(1)}, bf16[5,128,128]{2,1,0:T(8,128)(2,1)S(1)}, u32[]{:S(2)}, u32[]{:S(2)}) collective-permute-start(bf16[5,128,128]{2,1,0:T(8,128)(2,1)S(1)} %get-tuple-element.247), channel_id=1, source_target_pairs={{0,2},{1,3},{2,0},{3,1},{4,6},{5,7},{6,4},{7,5},{8,10},{9,11},{10,... | collective-permute-start | bytes 491528 | tf_op jit(solution)/shard_map/ppermute | solution.py:514
  171.9 13.1 %collective-permute-start.55 = (bf16[5,128,128]{2,1,0:T(8,128)(2,1)S(1)}, bf16[5,128,128]{2,1,0:T(8,128)(2,1)S(1)}, u32[]{:S(2)}, u32[]{:S(2)}) collective-permute-start(bf16[5,128,128]{2,1,0:T(8,128)(2,1)S(1)} %get-tuple-element.249), channel_id=1, source_target_pairs={{0,4},{1,5},{2,6},{3,7},{4,0},{5,1},{6,2},{7,3},{8,12},{9,13},{10,... | collective-permute-start | bytes 491528 | tf_op jit(solution)/shard_map/ppermute | solution.py:514
  172.9 15.1 %collective-permute-start.56 = (bf16[5,128,128]{2,1,0:T(8,128)(2,1)S(1)}, bf16[5,128,128]{2,1,0:T(8,128)(2,1)S(1)}, u32[]{:S(2)}, u32[]{:S(2)}) collective-permute-start(bf16[5,128,128]{2,1,0:T(8,128)(2,1)S(1)} %get-tuple-element.250), channel_id=1, source_target_pairs={{0,5},{1,4},{2,7},{3,6},{4,1},{5,0},{6,3},{7,2},{8,13},{9,12},{10,... | collective-permute-start | bytes 491528 | tf_op jit(solution)/shard_map/ppermute | solution.py:514
  175.9 12.2 %collective-permute-start.57 = (bf16[5,128,128]{2,1,0:T(8,128)(2,1)S(1)}, bf16[5,128,128]{2,1,0:T(8,128)(2,1)S(1)}, u32[]{:S(2)}, u32[]{:S(2)}) collective-permute-start(bf16[5,128,128]{2,1,0:T(8,128)(2,1)S(1)} %get-tuple-element.251), channel_id=1, source_target_pairs={{0,6},{1,7},{2,4},{3,5},{4,2},{5,3},{6,0},{7,1},{8,14},{9,15},{10,... | collective-permute-start | bytes 491528 | tf_op jit(solution)/shard_map/ppermute | solution.py:514
  185.1 30.0 %collective-permute-start.61 = (bf16[20,128,128]{2,1,0:T(8,128)(2,1)S(1)}, bf16[20,128,128]{2,1,0:T(8,128)(2,1)S(1)}, u32[]{:S(2)}, u32[]{:S(2)}) collective-permute-start(bf16[20,128,128]{2,1,0:T(8,128)(2,1)S(1)} %fold.6), channel_id=1, source_target_pairs={{0,16},{1,17},{2,18},{3,19},{4,20},{5,21},{6,22},{7,23},{16,24},{1... | collective-permute-start | bytes 1966088 | tf_op jit(solution)/shard_map/ppermute | solution.py:558
  192.1 26.4 %collective-permute-start.60 = (bf16[20,128,128]{2,1,0:T(8,128)(2,1)}, bf16[20,128,128]{2,1,0:T(8,128)(2,1)S(1)}, u32[]{:S(2)}, u32[]{:S(2)}) collective-permute-start(bf16[20,128,128]{2,1,0:T(8,128)(2,1)} %fold.8), channel_id=1, source_target_pairs={{0,8},{1,9},{2,10},{3,11},{4,12},{5,13},{6,14},{7,15},{16,0},{17,1... | collective-permute-start | bytes 1966088 | tf_op jit(solution)/shard_map/ppermute | solution.py:558
  289.1 16.6 %collective-permute-start.69 = (bf16[20,128,128]{2,1,0:T(8,128)(2,1)S(1)}, bf16[20,128,128]{2,1,0:T(8,128)(2,1)S(1)}, u32[]{:S(2)}, u32[]{:S(2)}) collective-permute-start(bf16[20,128,128]{2,1,0:T(8,128)(2,1)S(1)} %get-tuple-element.340.chunk_ref), channel_id=1, source_target_pairs={{0,16},{1,17},{2,18},{3,19},{4,20},{5,21},{6,22},{7,23},{16,24},{1... | collective-permute-start | bytes 1966088 | tf_op jit(solution)/shard_map/ppermute | solution.py:538
  305.7 15.7 %collective-permute-start.77 = (bf16[20,128,128]{2,1,0:T(8,128)(2,1)S(1)}, bf16[20,128,128]{2,1,0:T(8,128)(2,1)S(1)}, u32[]{:S(2)}, u32[]{:S(2)}) collective-permute-start(bf16[20,128,128]{2,1,0:T(8,128)(2,1)S(1)} %collective-permute-done.69.chunk_ref), channel_id=1, source_target_pairs={{0,16},{1,17},{2,18},{3,19},{4,20},{5,21},{6,22},{7,23},{16,24},{1... | collective-permute-start | bytes 1966088 | tf_op jit(solution)/shard_map/ppermute | solution.py:538
  308.9 15.9 %collective-permute-start.62 = (bf16[5,128,128]{2,1,0:T(8,128)(2,1)S(1)}, bf16[5,128,128]{2,1,0:T(8,128)(2,1)S(1)}, u32[]{:S(2)}, u32[]{:S(2)}) collective-permute-start(bf16[5,128,128]{2,1,0:T(8,128)(2,1)S(1)} %get-tuple-element.258), channel_id=1, source_target_pairs={{0,1},{1,0},{2,3},{3,2},{4,5},{5,4},{6,7},{7,6},{8,9},{9,8},{10,11... | collective-permute-start | bytes 491528 | tf_op jit(solution)/shard_map/ppermute | solution.py:514
  321.4 35.7 %collective-permute-start.85 = (bf16[20,128,128]{2,1,0:T(8,128)(2,1)S(1)}, bf16[20,128,128]{2,1,0:T(8,128)(2,1)S(1)}, u32[]{:S(2)}, u32[]{:S(2)}) collective-permute-start(bf16[20,128,128]{2,1,0:T(8,128)(2,1)S(1)} %collective-permute-done.77.chunk_ref), channel_id=1, source_target_pairs={{0,16},{1,17},{2,18},{3,19},{4,20},{5,21},{6,22},{7,23},{16,24},{1... | collective-permute-start | bytes 1966088 | tf_op jit(solution)/shard_map/ppermute | solution.py:538
  324.8 11.7 %collective-permute-start.66 = (bf16[5,128,128]{2,1,0:T(8,128)(2,1)S(1)}, bf16[5,128,128]{2,1,0:T(8,128)(2,1)S(1)}, u32[]{:S(2)}, u32[]{:S(2)}) collective-permute-start(bf16[5,128,128]{2,1,0:T(8,128)(2,1)S(1)} %get-tuple-element.262), channel_id=1, source_target_pairs={{0,5},{1,4},{2,7},{3,6},{4,1},{5,0},{6,3},{7,2},{8,13},{9,12},{10,... | collective-permute-start | bytes 491528 | tf_op jit(solution)/shard_map/ppermute | solution.py:514
  331.3 11.0 %collective-permute-start.68 = (bf16[5,128,128]{2,1,0:T(8,128)(2,1)S(1)}, bf16[5,128,128]{2,1,0:T(8,128)(2,1)S(1)}, u32[]{:S(2)}, u32[]{:S(2)}) collective-permute-start(bf16[5,128,128]{2,1,0:T(8,128)(2,1)S(1)} %get-tuple-element.264), channel_id=1, source_target_pairs={{0,7},{1,6},{2,5},{3,4},{4,3},{5,2},{6,1},{7,0},{8,15},{9,14},{10,... | collective-permute-start | bytes 491528 | tf_op jit(solution)/shard_map/ppermute | solution.py:514
  363.2 11.6 %collective-permute-start.84 = (bf16[5,128,128]{2,1,0:T(8,128)(2,1)S(1)}, bf16[5,128,128]{2,1,0:T(8,128)(2,1)S(1)}, u32[]{:S(2)}, u32[]{:S(2)}) collective-permute-start(bf16[5,128,128]{2,1,0:T(8,128)(2,1)S(1)} %get-tuple-element.280), channel_id=1, source_target_pairs={{0,7},{1,6},{2,5},{3,4},{4,3},{5,2},{6,1},{7,0},{8,15},{9,14},{10,... | collective-permute-start | bytes 491528 | tf_op jit(solution)/shard_map/ppermute | solution.py:514
  366.1 12.4 %collective-permute-start.87 = (bf16[5,128,128]{2,1,0:T(8,128)(2,1)S(1)}, bf16[5,128,128]{2,1,0:T(8,128)(2,1)S(1)}, u32[]{:S(2)}, u32[]{:S(2)}) collective-permute-start(bf16[5,128,128]{2,1,0:T(8,128)(2,1)S(1)} %get-tuple-element.283), channel_id=1, source_target_pairs={{0,2},{1,3},{2,0},{3,1},{4,6},{5,7},{6,4},{7,5},{8,10},{9,11},{10,... | collective-permute-start | bytes 491528 | tf_op jit(solution)/shard_map/ppermute | solution.py:514
  368.1 13.9 %collective-permute-start.88 = (bf16[5,128,128]{2,1,0:T(8,128)(2,1)S(1)}, bf16[5,128,128]{2,1,0:T(8,128)(2,1)S(1)}, u32[]{:S(2)}, u32[]{:S(2)}) collective-permute-start(bf16[5,128,128]{2,1,0:T(8,128)(2,1)S(1)} %get-tuple-element.284), channel_id=1, source_target_pairs={{0,3},{1,2},{2,1},{3,0},{4,7},{5,6},{6,5},{7,4},{8,11},{9,10},{10,... | collective-permute-start | bytes 491528 | tf_op jit(solution)/shard_map/ppermute | solution.py:514
  418.6 12.8 %collective-permute-start.112 = (bf16[5,128,128]{2,1,0:T(8,128)(2,1)S(1)}, bf16[5,128,128]{2,1,0:T(8,128)(2,1)S(1)}, u32[]{:S(2)}, u32[]{:S(2)}) collective-permute-start(bf16[5,128,128]{2,1,0:T(8,128)(2,1)S(1)} %get-tuple-element.327), channel_id=1, source_target_pairs={{0,6},{1,7},{2,4},{3,5},{4,2},{5,3},{6,0},{7,1},{8,14},{9,15},{10,... | collective-permute-start | bytes 491528 | tf_op jit(solution)/shard_map/ppermute | solution.py:514
  422.2 11.9 %collective-permute-start.113 = (bf16[5,128,128]{2,1,0:T(8,128)(2,1)S(1)}, bf16[5,128,128]{2,1,0:T(8,128)(2,1)S(1)}, u32[]{:S(2)}, u32[]{:S(2)}) collective-permute-start(bf16[5,128,128]{2,1,0:T(8,128)(2,1)S(1)} %get-tuple-element.328), channel_id=1, source_target_pairs={{0,7},{1,6},{2,5},{3,4},{4,3},{5,2},{6,1},{7,0},{8,15},{9,14},{10,... | collective-permute-start | bytes 491528 | tf_op jit(solution)/shard_map/ppermute | solution.py:514
  424.5 13.6 %collective-permute-start.93 = (bf16[5,128,128]{2,1,0:T(8,128)(2,1)S(1)}, bf16[5,128,128]{2,1,0:T(8,128)(2,1)S(1)}, u32[]{:S(2)}, u32[]{:S(2)}) collective-permute-start(bf16[5,128,128]{2,1,0:T(8,128)(2,1)S(1)} %get-tuple-element.298), channel_id=1, source_target_pairs={{0,1},{1,0},{2,3},{3,2},{4,5},{5,4},{6,7},{7,6},{8,9},{9,8},{10,11... | collective-permute-start | bytes 491528 | tf_op jit(solution)/shard_map/ppermute | solution.py:514
  425.2 13.5 %collective-permute-start.94 = (bf16[5,128,128]{2,1,0:T(8,128)(2,1)S(1)}, bf16[5,128,128]{2,1,0:T(8,128)(2,1)S(1)}, u32[]{:S(2)}, u32[]{:S(2)}) collective-permute-start(bf16[5,128,128]{2,1,0:T(8,128)(2,1)S(1)} %get-tuple-element.299), channel_id=1, source_target_pairs={{0,2},{1,3},{2,0},{3,1},{4,6},{5,7},{6,4},{7,5},{8,10},{9,11},{10,... | collective-permute-start | bytes 491528 | tf_op jit(solution)/shard_map/ppermute | solution.py:514
  436.0 34.9 %collective-permute-start.121 = (bf16[20,128,128]{2,1,0:T(8,128)(2,1)S(1)}, bf16[20,128,128]{2,1,0:T(8,128)(2,1)S(1)}, u32[]{:S(2)}, u32[]{:S(2)}) collective-permute-start(bf16[20,128,128]{2,1,0:T(8,128)(2,1)S(1)} %fold.10), channel_id=1, source_target_pairs={{0,8},{1,9},{2,10},{3,11},{4,12},{5,13},{6,14},{7,15},{16,0},{17,1... | collective-permute-start | bytes 1966088 | tf_op jit(solution)/shard_map/ppermute | solution.py:558
  438.8 12.9 %collective-permute-start.98 = (bf16[5,128,128]{2,1,0:T(8,128)(2,1)S(1)}, bf16[5,128,128]{2,1,0:T(8,128)(2,1)S(1)}, u32[]{:S(2)}, u32[]{:S(2)}) collective-permute-start(bf16[5,128,128]{2,1,0:T(8,128)(2,1)S(1)} %get-tuple-element.303), channel_id=1, source_target_pairs={{0,6},{1,7},{2,4},{3,5},{4,2},{5,3},{6,0},{7,1},{8,14},{9,15},{10,... | collective-permute-start | bytes 491528 | tf_op jit(solution)/shard_map/ppermute | solution.py:514
  442.7 11.5 %collective-permute-start.99 = (bf16[5,128,128]{2,1,0:T(8,128)(2,1)S(1)}, bf16[5,128,128]{2,1,0:T(8,128)(2,1)S(1)}, u32[]{:S(2)}, u32[]{:S(2)}) collective-permute-start(bf16[5,128,128]{2,1,0:T(8,128)(2,1)S(1)} %get-tuple-element.304), channel_id=1, source_target_pairs={{0,7},{1,6},{2,5},{3,4},{4,3},{5,2},{6,1},{7,0},{8,15},{9,14},{10,... | collective-permute-start | bytes 491528 | tf_op jit(solution)/shard_map/ppermute | solution.py:514
  444.4 10.9 %collective-permute-start.114 = (bf16[5,128,128]{2,1,0:T(8,128)(2,1)S(1)}, bf16[5,128,128]{2,1,0:T(8,128)(2,1)S(1)}, u32[]{:S(2)}, u32[]{:S(2)}) collective-permute-start(bf16[5,128,128]{2,1,0:T(8,128)(2,1)S(1)} %get-tuple-element.330), channel_id=1, source_target_pairs={{0,1},{1,0},{2,3},{3,2},{4,5},{5,4},{6,7},{7,6},{8,9},{9,8},{10,11... | collective-permute-start | bytes 491528 | tf_op jit(solution)/shard_map/ppermute | solution.py:514
  446.5 11.6 %collective-permute-start.115 = (bf16[5,128,128]{2,1,0:T(8,128)(2,1)S(1)}, bf16[5,128,128]{2,1,0:T(8,128)(2,1)S(1)}, u32[]{:S(2)}, u32[]{:S(2)}) collective-permute-start(bf16[5,128,128]{2,1,0:T(8,128)(2,1)S(1)} %get-tuple-element.331), channel_id=1, source_target_pairs={{0,2},{1,3},{2,0},{3,1},{4,6},{5,7},{6,4},{7,5},{8,10},{9,11},{10,... | collective-permute-start | bytes 491528 | tf_op jit(solution)/shard_map/ppermute | solution.py:514
  454.2 13.2 %collective-permute-start.117 = (bf16[5,128,128]{2,1,0:T(8,128)(2,1)S(1)}, bf16[5,128,128]{2,1,0:T(8,128)(2,1)S(1)}, u32[]{:S(2)}, u32[]{:S(2)}) collective-permute-start(bf16[5,128,128]{2,1,0:T(8,128)(2,1)S(1)} %get-tuple-element.333), channel_id=1, source_target_pairs={{0,4},{1,5},{2,6},{3,7},{4,0},{5,1},{6,2},{7,3},{8,12},{9,13},{10,... | collective-permute-start | bytes 491528 | tf_op jit(solution)/shard_map/ppermute | solution.py:514
  455.3 14.0 %collective-permute-start.118 = (bf16[5,128,128]{2,1,0:T(8,128)(2,1)S(1)}, bf16[5,128,128]{2,1,0:T(8,128)(2,1)S(1)}, u32[]{:S(2)}, u32[]{:S(2)}) collective-permute-start(bf16[5,128,128]{2,1,0:T(8,128)(2,1)S(1)} %get-tuple-element.334), channel_id=1, source_target_pairs={{0,5},{1,4},{2,7},{3,6},{4,1},{5,0},{6,3},{7,2},{8,13},{9,12},{10,... | collective-permute-start | bytes 491528 | tf_op jit(solution)/shard_map/ppermute | solution.py:514
  458.1 11.3 %collective-permute-start.119 = (bf16[5,128,128]{2,1,0:T(8,128)(2,1)S(1)}, bf16[5,128,128]{2,1,0:T(8,128)(2,1)S(1)}, u32[]{:S(2)}, u32[]{:S(2)}) collective-permute-start(bf16[5,128,128]{2,1,0:T(8,128)(2,1)S(1)} %get-tuple-element.335), channel_id=1, source_target_pairs={{0,6},{1,7},{2,4},{3,5},{4,2},{5,3},{6,0},{7,1},{8,14},{9,15},{10,... | collective-permute-start | bytes 491528 | tf_op jit(solution)/shard_map/ppermute | solution.py:514
  467.4 29.4 %collective-permute-start.123 = (bf16[20,128,128]{2,1,0:T(8,128)(2,1)S(1)}, bf16[20,128,128]{2,1,0:T(8,128)(2,1)S(1)}, u32[]{:S(2)}, u32[]{:S(2)}) collective-permute-start(bf16[20,128,128]{2,1,0:T(8,128)(2,1)S(1)} %fold.9), channel_id=1, source_target_pairs={{0,16},{1,17},{2,18},{3,19},{4,20},{5,21},{6,22},{7,23},{16,24},{1... | collective-permute-start | bytes 1966088 | tf_op jit(solution)/shard_map/ppermute | solution.py:558
  472.8 29.0 %collective-permute-start.122 = (bf16[20,128,128]{2,1,0:T(8,128)(2,1)S(1)}, bf16[20,128,128]{2,1,0:T(8,128)(2,1)S(1)}, u32[]{:S(2)}, u32[]{:S(2)}) collective-permute-start(bf16[20,128,128]{2,1,0:T(8,128)(2,1)S(1)} %fold.11), channel_id=1, source_target_pairs={{0,8},{1,9},{2,10},{3,11},{4,12},{5,13},{6,14},{7,15},{16,0},{17,1... | collective-permute-start | bytes 1966088 | tf_op jit(solution)/shard_map/ppermute | solution.py:558
  (97 other events, 1147.2 us)

commit v3 on v2

--- a/solution.py
+++ b/solution.py
@@ -43,8 +43,8 @@
     device_count = lax.axis_size(AXES)
     count, rows, cols = grams.shape
     pieces = grams.reshape(device_count, count * rows // device_count, cols)
-    mine = jnp.sum(trade(pieces), axis=0)
-    shared = jnp.broadcast_to(mine[None], pieces.shape)
+    pieces = trade(pieces)
+    shared = jnp.broadcast_to(jnp.sum(pieces, axis=0)[None], pieces.shape)
     return trade(shared).reshape(grams.shape)
 
 
@@ -299,7 +299,7 @@
                 pl.BlockSpec((group, arc_rows, width), lambda i, t: (i, 0, 0)),
                 pl.BlockSpec((group, arc_rows, arc_rows), lambda i, t: (i, 0, 0)),
             ],
-            out_specs=[pl.BlockSpec(memory_space=VMEM)] * (plan.rings * plan.plane),
+            out_specs=[anywhere] * (plan.rings * plan.plane),
             scratch_shapes=[
                 pltpu.VMEM((total,) + block, jnp.bfloat16),
                 pltpu.VMEM((total,) + block, jnp.bfloat16),
@@ -307,8 +307,8 @@
                 pltpu.SemaphoreType.DMA((plan.rings * plan.plane,)),
             ],
         ),
-        out_shape=[pltpu.VMEM((plan.cap,) + block, jnp.bfloat16)] * (plan.rings * plan.plane),
-        compiler_params=pltpu.CompilerParams(vmem_limit_bytes=32 << 20),
+        out_shape=[jax.ShapeDtypeStruct((plan.cap,) + block, jnp.bfloat16)]
+        * (plan.rings * plan.plane),
         name="arcs",
     )(tab, *arrived, coupling_panel, inv_factor)
 
@@ -422,7 +422,6 @@
         out_shape=[jax.ShapeDtypeStruct(field.shape, jnp.float32)] * 2,
         in_specs=[spec] * 4 + [pl.BlockSpec((cols, cols), lambda i: (0, 0))],
         out_specs=[spec] * 2,
-        compiler_params=SMALL,
         name="update",
     )(field, image, solution_field, residual, step_mat)
 
@@ -479,8 +478,8 @@
             out_ref[...] = y * down * along
 
 
-def step_kernel(grams_ref, step_ref, beta_ref, new_ref, first_inv, second_inv):
-    res, cross, image = grams_ref[0], grams_ref[1], grams_ref[2]
+def step_kernel(grams_ref, res_ref, step_ref, beta_ref, new_ref, first_inv, second_inv):
+    res, cross, image = res_ref[...], grams_ref[0], grams_ref[1]
     invert_into([first_inv, second_inv], [0.5 * (cross + cross.T), 0.5 * (res + res.T)])
     step = times_high(first_inv[...], res)
     step_ref[...] = step
@@ -568,7 +567,7 @@
     solution_field = None
     residual = right_side
     direction = right_side
-    start_gram = inner_gram(residual, residual)
+    res_gram = sum_all(inner_gram(residual, residual)[None])[0]
     for sweep_index in range(ITERS):
         last = sweep_index + 1 == ITERS
         image_vec, grams, me = apply_schur(
@@ -577,8 +576,8 @@
         if last:
             (step_mat,) = small_solve(last_kernel, (sum_all(grams), res_gram), 1, 1)
             return tuple(update(direction, image_vec, solution_field, residual, step_mat))
-        grams = jnp.concatenate([start_gram[None], grams], axis=0)
-        step_mat, beta_mat, res_gram = small_solve(step_kernel, (sum_all(grams),), 3, 2)
+        grams = sum_all(grams)
+        step_mat, beta_mat, res_gram = small_solve(step_kernel, (grams, res_gram), 3, 2)
         solution_field = combine_cols(direction, step_mat)
         residual = residual - combine_cols(image_vec, step_mat)
         direction = residual + combine_cols(direction, beta_mat)

time: 553 us -> 543 us (0.982)
  Pallas kernels: 148 us -> 132 us
  blocking collectives: 35.9 us -> 20.1 us
  waiting for transfers between devices: 209 us -> 219 us
  starting transfers between devices: 135 us -> 141 us
    pallas_call x2, Pallas kernels: 46 us -> 27.8 us  [run_arcs(): pl.pallas_call(functools.partial(arcs_kernel, plan), grid_spec=pltpu.Pref...]
    all_to_all x3 -> x2, blocking collectives: 35.9 us -> 20.1 us  [trade(): return lax.all_to_all(buffer, AXES, split_axis=0, concat_axis=0, tiled=True)]
    all_to_all x1 -> x4, waiting for transfers between devices: 4.91 us -> 19.5 us  [trade(): return lax.all_to_all(buffer, AXES, split_axis=0, concat_axis=0, tiled=True)]
    all_to_all x1 -> x4, starting transfers between devices: 2.81 us -> 12.5 us  [trade(): return lax.all_to_all(buffer, AXES, split_axis=0, concat_axis=0, tiled=True)]
    unnamed x41 -> x251, local copies, waits for them, and re-layouts: 14.5 us -> 16.4 us
  transfers between devices with their start and end apart: 125 -> 128, of which waited for: 67 -> 70; matrix products, arithmetic and copies ran while one was open for 1% -> 1% of each run, Pallas kernels for 7% -> 8%
where the time goes in v3:
time: 543 us; the launch traced here: 542 us
  waiting for transfers between devices  219 us (40%)
  starting transfers between devices  141 us (26%)
  Pallas kernels  132 us (24%)
  blocking collectives  20.1 us (4%)
  local copies, waits for them, and re-layouts  17.6 us (3%)
  matrix products  7.53 us (1%)
    ppermute x112, waiting for transfers between devices, trade_plane(): lax.ppermute(buffers[offset], AXES, plan.shift_plane(offset))  137 us
    ppermute x112, starting transfers between devices, trade_plane(): lax.ppermute(buffers[offset], AXES, plan.shift_plane(offset))  105 us
    ppermute x6, waiting for transfers between devices, apply_schur(): following = lax.ppermute(chunk, AXES, plan.ring)  53.6 us
    pallas_call x2, Pallas kernels, small_solve(): pl.pallas_call(kernel, out_shape=[jax.ShapeDtypeStruct(shape, jnp.float32...  50.5 us
    pallas_call x2, Pallas kernels, run_arcs(): pl.pallas_call(functools.partial(arcs_kernel, plan), grid_spec=pltpu.Pref...  27.8 us
    all_to_all x2, blocking collectives, trade(): return lax.all_to_all(buffer, AXES, split_axis=0, concat_axis=0, tiled=True)  20.1 us
    all_to_all x4, waiting for transfers between devices, trade(): return lax.all_to_all(buffer, AXES, split_axis=0, concat_axis=0, tiled=True)  19.5 us
    unnamed x251, local copies, waits for them, and re-layouts  16.4 us
  transfers between devices with their start and end apart: 128, of which 70 were waited for; matrix products, arithmetic and copies ran while one was open for 1% of the time, Pallas kernels for 8%

profile of v3, /device:TPU:0, one launch (start us, length us, event | category | flops | bytes accessed | tf_op | source)
XLA Modules:
  0.0 542.1 jit_solution(5954969141979744667)
XLA Ops:
  2.1 4.1 collective-permute-start.7
  6.2 14.0 %collective-permute-done.7.chunk_ref = bf16[20,128,128]{2,1,0:T(8,128)(2,1)S(1)} collective-permute-done((bf16[20,128,128]{2,1,0:T(8,128)(2,1)S(1)}, bf16[20,128,128]{2,1,0:T(8,128)(2,1)S(1)}, u32[]{:S(2)}, u32[]{:S(2)}) %collective-permute-start.7) | collective-permute-done | bytes 655392 | tf_op jit(solution)/shard_map/ppermute | solution.py:537
  20.2 3.4 collective-permute-start.15
  26.6 10.1 %collective-permute-done.15.chunk_ref = bf16[20,128,128]{2,1,0:T(8,128)(2,1)S(1)} collective-permute-done((bf16[20,128,128]{2,1,0:T(8,128)(2,1)S(1)}, bf16[20,128,128]{2,1,0:T(8,128)(2,1)S(1)}, u32[]{:S(2)}, u32[]{:S(2)}) %collective-permute-start.15) | collective-permute-done | bytes 655392 | tf_op jit(solution)/shard_map/ppermute | solution.py:537
  36.7 3.4 collective-permute-start.23
  46.2 3.3 collective-permute-start.5
  70.3 3.1 collective-permute-done.14.refs_15_
  86.8 3.6 collective-permute-done.21.refs_22_
  97.4 3.6 collective-permute-done.26.refs_27_
  101.1 4.0 collective-permute-done.29.refs_30_
  106.9 13.8 %arcs.2 = (bf16[5,128,128]{2,1,0:T(8,128)(2,1)}, bf16[5,128,128]{2,1,0:T(8,128)(2,1)}, bf16[5,128,128]{2,1,0:T(8,128)(2,1)}, bf16[5,128,128]{2,1,0:T(8,128)(2,1)...) custom-call(s32[32,128]{1,0:T(8,128)} %copy-done.31, ...), custom_call_target="tpu_custom_call" | custom-call | tf_op jit(solution)/shard_map/arcs/pallas_call | solution.py:292
  126.2 2.9 collective-permute-done.46.refs_2_
  133.6 4.1 collective-permute-done.50.refs_6_
  137.7 2.9 collective-permute-done.51.refs_7_
  147.6 2.7 collective-permute-done.33.refs_3_
  155.1 4.2 collective-permute-done.36.refs_6_
  175.2 2.9 collective-permute-start.61
  179.0 2.7 fold.8
  185.6 4.7 collective-permute-done.39.refs_2_
  197.1 2.8 fusion.5
  199.9 3.3 all-to-all-start.2
  204.6 3.8 collective-permute-done.60.refs_8_
  214.0 6.0 %image.2 = (f32[20,128,128]{2,1,0:T(8,128)S(1)}, f32[2,128,128]{2,1,0:T(8,128)S(1)}) custom-call(s32[1]{0:T(128)} %gate.17.me_ref.in_ref, s32[8,128]{1,0:T(8,128)S(1)} %get-tuple-element.171.held_ref, f32[20,128,128]{2,1,0:T(8,128)S(1)} %copy-done, f32[128,20]{1,0:T(8,128)S(1)} %bitcast.34, bf16[5,128,128]{2,1,0:T(8,128)(2,1)S(1)} %copy-done.14, ...), custom_call_target="tpu_custom_call" | custom-call | tf_op jit(solution)/shard_map/image/pallas_call | solution.py:391
  220.7 3.9 all-to-all-start
  225.4 7.3 %all-to-all-done = f32[32,8,128]{2,1,0:T(8,128)S(1)} async-done(((f32[32,8,128]{2,1,0:T(8,128)}), f32[32,8,128]{2,1,0:T(8,128)S(1)}, u32[]{:S(2)}, u32[]{:S(2)}) %all-to-all-start) | async-done | bytes 131104 | tf_op jit(solution)/shard_map/all_to_all | solution.py:39
  236.0 7.4 %all-to-all-done.3 = f32[32,4,128]{2,1,0:T(4,128)S(1)} async-done(((f32[32,4,128]{2,1,0:T(4,128)}), f32[32,4,128]{2,1,0:T(4,128)S(1)}, u32[]{:S(2)}, u32[]{:S(2)}) %all-to-all-start.3) | async-done | bytes 65568 | tf_op jit(solution)/shard_map/all_to_all | solution.py:39
  243.4 9.9 %all_to_all.30 = f32[32,8,128]{2,1,0:T(8,128)S(1)} all-to-all(f32[32,8,128]{2,1,0:T(8,128)S(1)} %broadcast_in_dim.6), channel_id=1, replica_groups=mesh['arc'=8,'vec'=4] {'arc','vec'}, dimensions={0} | all-to-all | bytes 262144 | tf_op jit(solution)/shard_map/all_to_all | solution.py:39
  253.3 33.5 %solve.2 = (f32[128,128]{1,0:T(8,128)S(1)}, f32[128,128]{1,0:T(8,128)S(1)}, f32[128,128]{1,0:T(8,128)S(1)}) custom-call(f32[2,128,128]{2,1,0:T(8,128)S(1)} %bitcast.36, f32[128,128]{1,0:T(8,128)S(1)} %bitcast.37), custom_call_target="tpu_custom_call" | custom-call | tf_op jit(solution)/shard_map/solve/pallas_call | solution.py:500
  290.0 16.1 %collective-permute-done.69.chunk_ref = bf16[20,128,128]{2,1,0:T(8,128)(2,1)S(1)} collective-permute-done((bf16[20,128,128]{2,1,0:T(8,128)(2,1)S(1)}, bf16[20,128,128]{2,1,0:T(8,128)(2,1)S(1)}, u32[]{:S(2)}, u32[]{:S(2)}) %collective-permute-start.69) | collective-permute-done | bytes 655392 | tf_op jit(solution)/shard_map/ppermute | solution.py:537
  308.7 13.4 %collective-permute-done.77.chunk_ref = bf16[20,128,128]{2,1,0:T(8,128)(2,1)S(1)} collective-permute-done((bf16[20,128,128]{2,1,0:T(8,128)(2,1)S(1)}, bf16[20,128,128]{2,1,0:T(8,128)(2,1)S(1)}, u32[]{:S(2)}, u32[]{:S(2)}) %collective-permute-start.77) | collective-permute-done | bytes 655392 | tf_op jit(solution)/shard_map/ppermute | solution.py:537
  340.1 2.8 collective-permute-done.68.refs_7_
  353.1 4.4 collective-permute-done.75.refs_14_
  369.0 3.6 collective-permute-done.83.refs_22_
  382.9 3.7 collective-permute-done.91.refs_30_
  386.6 2.9 collective-permute-done.92.refs_31_
  390.1 14.0 %arcs.3 = (bf16[5,128,128]{2,1,0:T(8,128)(2,1)}, bf16[5,128,128]{2,1,0:T(8,128)(2,1)}, bf16[5,128,128]{2,1,0:T(8,128)(2,1)}, bf16[5,128,128]{2,1,0:T(8,128)(2,1)...) custom-call(s32[32,128]{1,0:T(8,128)} %copy-done.31, ...), custom_call_target="tpu_custom_call" | custom-call | tf_op jit(solution)/shard_map/arcs/pallas_call | solution.py:292
  416.9 4.0 collective-permute-done.112.refs_6_
  437.8 4.4 collective-permute-done.98.refs_6_
  468.4 5.1 collective-permute-done.101.refs_2_
  479.1 4.1 collective-permute-done.105.refs_6_
  483.1 3.6 collective-permute-done.106.refs_7_
  486.7 4.8 collective-permute-done.122.refs_8_
  491.5 4.5 image.3
  497.0 10.2 %all_to_all.31 = f32[32,4,128]{2,1,0:T(4,128)S(1)} all-to-all(f32[32,4,128]{2,1,0:T(4,128)S(1)} %bitcast.40), channel_id=1, replica_groups=mesh['arc'=8,'vec'=4] {'arc','vec'}, dimensions={0} | all-to-all | bytes 131072 | tf_op jit(solution)/shard_map/all_to_all | solution.py:39
  507.9 2.8 all-to-all-start.5
  513.0 4.8 all-to-all-done.5
  517.9 17.0 %solve.3.step_ref = f32[128,128]{1,0:T(8,128)S(1)} custom-call(f32[1,128,128]{2,1,0:T(8,128)S(1)} %bitcast.38, f32[128,128]{1,0:T(8,128)S(1)} %get-tuple-element.339.res_ref), custom_call_target="tpu_custom_call" | custom-call | tf_op jit(solution)/shard_map/solve/pallas_call | solution.py:500
  535.5 6.6 %update.1 = (f32[20,128,128]{2,1,0:T(8,128)}, f32[20,128,128]{2,1,0:T(8,128)}) custom-call(f32[20,128,128]{2,1,0:T(8,128)} %copy-done.1, f32[20,128,128]{2,1,0:T(8,128)} %copy-done.2, f32[20,128,128]{2,1,0:T(8,128)} %convolution_bitcast_fusion.sol_ref, f32[20,128,128]{2,1,0:T(8,128)} %copy-done.34, f32[128,128]{1,0:T(8,128)} %copy-done.5), custom_call_target="tpu_custom_call" | custom-call | tf_op jit(solution)/shard_map/update/pallas_call | solution.py:419
  (506 shorter events, 236.0 us)
Async XLA Ops:
  2.1 18.1 %collective-permute-start.7 = (bf16[20,128,128]{2,1,0:T(8,128)(2,1)S(1)}, bf16[20,128,128]{2,1,0:T(8,128)(2,1)S(1)}, u32[]{:S(2)}, u32[]{:S(2)}) collective-permute-start(bf16[20,128,128]{2,1,0:T(8,128)(2,1)S(1)} %convert_element_type.6.chunk_ref), channel_id=1, source_target_pairs={{0,16},{1,17},{2,18},{3,19},{4,20},{5,21},{6,22},{7,23},{16,24},{1... | collective-permute-start | bytes 1966088 | tf_op jit(solution)/shard_map/ppermute | solution.py:537
  20.2 16.5 %collective-permute-start.15 = (bf16[20,128,128]{2,1,0:T(8,128)(2,1)S(1)}, bf16[20,128,128]{2,1,0:T(8,128)(2,1)S(1)}, u32[]{:S(2)}, u32[]{:S(2)}) collective-permute-start(bf16[20,128,128]{2,1,0:T(8,128)(2,1)S(1)} %collective-permute-done.7.chunk_ref), channel_id=1, source_target_pairs={{0,16},{1,17},{2,18},{3,19},{4,20},{5,21},{6,22},{7,23},{16,24},{1... | collective-permute-start | bytes 1966088 | tf_op jit(solution)/shard_map/ppermute | solution.py:537
  26.6 16.5 %collective-permute-start = (bf16[5,128,128]{2,1,0:T(8,128)(2,1)S(1)}, bf16[5,128,128]{2,1,0:T(8,128)(2,1)S(1)}, u32[]{:S(2)}, u32[]{:S(2)}) collective-permute-start(bf16[5,128,128]{2,1,0:T(8,128)(2,1)S(1)} %get-tuple-element.174), channel_id=1, source_target_pairs={{0,1},{1,0},{2,3},{3,2},{4,5},{5,4},{6,7},{7,6},{8,9},{9,8},{10,11... | collective-permute-start | bytes 491528 | tf_op jit(solution)/shard_map/ppermute | solution.py:513
  36.7 37.5 %collective-permute-start.23 = (bf16[20,128,128]{2,1,0:T(8,128)(2,1)S(1)}, bf16[20,128,128]{2,1,0:T(8,128)(2,1)S(1)}, u32[]{:S(2)}, u32[]{:S(2)}) collective-permute-start(bf16[20,128,128]{2,1,0:T(8,128)(2,1)S(1)} %collective-permute-done.15.chunk_ref), channel_id=1, source_target_pairs={{0,16},{1,17},{2,18},{3,19},{4,20},{5,21},{6,22},{7,23},{16,24},{1... | collective-permute-start | bytes 1966088 | tf_op jit(solution)/shard_map/ppermute | solution.py:537
  51.0 11.6 %collective-permute-start.10 = (bf16[5,128,128]{2,1,0:T(8,128)(2,1)S(1)}, bf16[5,128,128]{2,1,0:T(8,128)(2,1)S(1)}, u32[]{:S(2)}, u32[]{:S(2)}) collective-permute-start(bf16[5,128,128]{2,1,0:T(8,128)(2,1)S(1)} %get-tuple-element.184), channel_id=1, source_target_pairs={{0,3},{1,2},{2,1},{3,0},{4,7},{5,6},{6,5},{7,4},{8,11},{9,10},{10,... | collective-permute-start | bytes 491528 | tf_op jit(solution)/shard_map/ppermute | solution.py:513
  51.5 12.9 %collective-permute-start.11 = (bf16[5,128,128]{2,1,0:T(8,128)(2,1)S(1)}, bf16[5,128,128]{2,1,0:T(8,128)(2,1)S(1)}, u32[]{:S(2)}, u32[]{:S(2)}) collective-permute-start(bf16[5,128,128]{2,1,0:T(8,128)(2,1)S(1)} %get-tuple-element.185), channel_id=1, source_target_pairs={{0,4},{1,5},{2,6},{3,7},{4,0},{5,1},{6,2},{7,3},{8,12},{9,13},{10,... | collective-permute-start | bytes 491528 | tf_op jit(solution)/shard_map/ppermute | solution.py:513
  55.1 12.2 %collective-permute-start.12 = (bf16[5,128,128]{2,1,0:T(8,128)(2,1)S(1)}, bf16[5,128,128]{2,1,0:T(8,128)(2,1)S(1)}, u32[]{:S(2)}, u32[]{:S(2)}) collective-permute-start(bf16[5,128,128]{2,1,0:T(8,128)(2,1)S(1)} %get-tuple-element.186), channel_id=1, source_target_pairs={{0,5},{1,4},{2,7},{3,6},{4,1},{5,0},{6,3},{7,2},{8,13},{9,12},{10,... | collective-permute-start | bytes 491528 | tf_op jit(solution)/shard_map/ppermute | solution.py:513
  67.3 11.6 %collective-permute-start.9 = (bf16[5,128,128]{2,1,0:T(8,128)(2,1)S(1)}, bf16[5,128,128]{2,1,0:T(8,128)(2,1)S(1)}, u32[]{:S(2)}, u32[]{:S(2)}) collective-permute-start(bf16[5,128,128]{2,1,0:T(8,128)(2,1)S(1)} %get-tuple-element.183), channel_id=1, source_target_pairs={{0,2},{1,3},{2,0},{3,1},{4,6},{5,7},{6,4},{7,5},{8,10},{9,11},{10,... | collective-permute-start | bytes 491528 | tf_op jit(solution)/shard_map/ppermute | solution.py:513
  83.9 13.0 %collective-permute-start.25 = (bf16[5,128,128]{2,1,0:T(8,128)(2,1)S(1)}, bf16[5,128,128]{2,1,0:T(8,128)(2,1)S(1)}, u32[]{:S(2)}, u32[]{:S(2)}) collective-permute-start(bf16[5,128,128]{2,1,0:T(8,128)(2,1)S(1)} %get-tuple-element.199), channel_id=1, source_target_pairs={{0,2},{1,3},{2,0},{3,1},{4,6},{5,7},{6,4},{7,5},{8,10},{9,11},{10,... | collective-permute-start | bytes 491528 | tf_op jit(solution)/shard_map/ppermute | solution.py:513
  85.1 16.0 %collective-permute-start.26 = (bf16[5,128,128]{2,1,0:T(8,128)(2,1)S(1)}, bf16[5,128,128]{2,1,0:T(8,128)(2,1)S(1)}, u32[]{:S(2)}, u32[]{:S(2)}) collective-permute-start(bf16[5,128,128]{2,1,0:T(8,128)(2,1)S(1)} %get-tuple-element.200), channel_id=1, source_target_pairs={{0,3},{1,2},{2,1},{3,0},{4,7},{5,6},{6,5},{7,4},{8,11},{9,10},{10,... | collective-permute-start | bytes 491528 | tf_op jit(solution)/shard_map/ppermute | solution.py:513
  125.3 12.4 %collective-permute-start.50 = (bf16[5,128,128]{2,1,0:T(8,128)(2,1)}, bf16[5,128,128]{2,1,0:T(8,128)(2,1)S(1)}, u32[]{:S(2)}, u32[]{:S(2)}) collective-permute-start(bf16[5,128,128]{2,1,0:T(8,128)(2,1)} %get-tuple-element.243), channel_id=1, source_target_pairs={{0,6},{1,7},{2,4},{3,5},{4,2},{5,3},{6,0},{7,1},{8,14},{9,15},{10,... | collective-permute-start | bytes 491528 | tf_op jit(solution)/shard_map/ppermute | solution.py:513
  129.1 11.5 %collective-permute-start.51 = (bf16[5,128,128]{2,1,0:T(8,128)(2,1)}, bf16[5,128,128]{2,1,0:T(8,128)(2,1)S(1)}, u32[]{:S(2)}, u32[]{:S(2)}) collective-permute-start(bf16[5,128,128]{2,1,0:T(8,128)(2,1)} %get-tuple-element.244), channel_id=1, source_target_pairs={{0,7},{1,6},{2,5},{3,4},{4,3},{5,2},{6,1},{7,0},{8,15},{9,14},{10,... | collective-permute-start | bytes 491528 | tf_op jit(solution)/shard_map/ppermute | solution.py:513
  130.8 14.8 %collective-permute-start.31 = (bf16[5,128,128]{2,1,0:T(8,128)(2,1)}, bf16[5,128,128]{2,1,0:T(8,128)(2,1)S(1)}, u32[]{:S(2)}, u32[]{:S(2)}) collective-permute-start(bf16[5,128,128]{2,1,0:T(8,128)(2,1)} %get-tuple-element.214), channel_id=1, source_target_pairs={{0,1},{1,0},{2,3},{3,2},{4,5},{5,4},{6,7},{7,6},{8,9},{9,8},{10,11... | collective-permute-start | bytes 491528 | tf_op jit(solution)/shard_map/ppermute | solution.py:513
  131.9 15.0 %collective-permute-start.32 = (bf16[5,128,128]{2,1,0:T(8,128)(2,1)}, bf16[5,128,128]{2,1,0:T(8,128)(2,1)S(1)}, u32[]{:S(2)}, u32[]{:S(2)}) collective-permute-start(bf16[5,128,128]{2,1,0:T(8,128)(2,1)} %get-tuple-element.215), channel_id=1, source_target_pairs={{0,2},{1,3},{2,0},{3,1},{4,6},{5,7},{6,4},{7,5},{8,10},{9,11},{10,... | collective-permute-start | bytes 491528 | tf_op jit(solution)/shard_map/ppermute | solution.py:513
  143.7 35.2 %collective-permute-start.59 = (bf16[20,128,128]{2,1,0:T(8,128)(2,1)S(1)}, bf16[20,128,128]{2,1,0:T(8,128)(2,1)S(1)}, u32[]{:S(2)}, u32[]{:S(2)}) collective-permute-start(bf16[20,128,128]{2,1,0:T(8,128)(2,1)S(1)} %fold.7), channel_id=1, source_target_pairs={{0,8},{1,9},{2,10},{3,11},{4,12},{5,13},{6,14},{7,15},{16,0},{17,1... | collective-permute-start | bytes 1966088 | tf_op jit(solution)/shard_map/ppermute | solution.py:557
  146.8 12.4 %collective-permute-start.36 = (bf16[5,128,128]{2,1,0:T(8,128)(2,1)S(1)}, bf16[5,128,128]{2,1,0:T(8,128)(2,1)S(1)}, u32[]{:S(2)}, u32[]{:S(2)}) collective-permute-start(bf16[5,128,128]{2,1,0:T(8,128)(2,1)S(1)} %copy-done.120), channel_id=1, source_target_pairs={{0,6},{1,7},{2,4},{3,5},{4,2},{5,3},{6,0},{7,1},{8,14},{9,15},{10,... | collective-permute-start | bytes 491528 | tf_op jit(solution)/shard_map/ppermute | solution.py:513
  161.6 11.8 %collective-permute-start.55 = (bf16[5,128,128]{2,1,0:T(8,128)(2,1)S(1)}, bf16[5,128,128]{2,1,0:T(8,128)(2,1)S(1)}, u32[]{:S(2)}, u32[]{:S(2)}) collective-permute-start(bf16[5,128,128]{2,1,0:T(8,128)(2,1)S(1)} %copy-done.110), channel_id=1, source_target_pairs={{0,4},{1,5},{2,6},{3,7},{4,0},{5,1},{6,2},{7,3},{8,12},{9,13},{10,... | collective-permute-start | bytes 491528 | tf_op jit(solution)/shard_map/ppermute | solution.py:513
  162.4 12.8 %collective-permute-start.56 = (bf16[5,128,128]{2,1,0:T(8,128)(2,1)S(1)}, bf16[5,128,128]{2,1,0:T(8,128)(2,1)S(1)}, u32[]{:S(2)}, u32[]{:S(2)}) collective-permute-start(bf16[5,128,128]{2,1,0:T(8,128)(2,1)S(1)} %copy-done.108), channel_id=1, source_target_pairs={{0,5},{1,4},{2,7},{3,6},{4,1},{5,0},{6,3},{7,2},{8,13},{9,12},{10,... | collective-permute-start | bytes 491528 | tf_op jit(solution)/shard_map/ppermute | solution.py:513
  165.6 12.5 %collective-permute-start.57 = (bf16[5,128,128]{2,1,0:T(8,128)(2,1)S(1)}, bf16[5,128,128]{2,1,0:T(8,128)(2,1)S(1)}, u32[]{:S(2)}, u32[]{:S(2)}) collective-permute-start(bf16[5,128,128]{2,1,0:T(8,128)(2,1)S(1)} %copy-done.104), channel_id=1, source_target_pairs={{0,6},{1,7},{2,4},{3,5},{4,2},{5,3},{6,0},{7,1},{8,14},{9,15},{10,... | collective-permute-start | bytes 491528 | tf_op jit(solution)/shard_map/ppermute | solution.py:513
  173.4 11.7 %collective-permute-start.38 = (bf16[5,128,128]{2,1,0:T(8,128)(2,1)S(1)}, bf16[5,128,128]{2,1,0:T(8,128)(2,1)S(1)}, u32[]{:S(2)}, u32[]{:S(2)}) collective-permute-start(bf16[5,128,128]{2,1,0:T(8,128)(2,1)S(1)} %copy-done.102), channel_id=1, source_target_pairs={{0,1},{1,0},{2,3},{3,2},{4,5},{5,4},{6,7},{7,6},{8,9},{9,8},{10,11... | collective-permute-start | bytes 491528 | tf_op jit(solution)/shard_map/ppermute | solution.py:513
  175.2 29.5 %collective-permute-start.61 = (bf16[20,128,128]{2,1,0:T(8,128)(2,1)S(1)}, bf16[20,128,128]{2,1,0:T(8,128)(2,1)S(1)}, u32[]{:S(2)}, u32[]{:S(2)}) collective-permute-start(bf16[20,128,128]{2,1,0:T(8,128)(2,1)S(1)} %fold.6), channel_id=1, source_target_pairs={{0,16},{1,17},{2,18},{3,19},{4,20},{5,21},{6,22},{7,23},{16,24},{1... | collective-permute-start | bytes 1966088 | tf_op jit(solution)/shard_map/ppermute | solution.py:557
  181.7 26.7 %collective-permute-start.60 = (bf16[20,128,128]{2,1,0:T(8,128)(2,1)}, bf16[20,128,128]{2,1,0:T(8,128)(2,1)S(1)}, u32[]{:S(2)}, u32[]{:S(2)}) collective-permute-start(bf16[20,128,128]{2,1,0:T(8,128)(2,1)} %fold.8), channel_id=1, source_target_pairs={{0,8},{1,9},{2,10},{3,11},{4,12},{5,13},{6,14},{7,15},{16,0},{17,1... | collective-permute-start | bytes 1966088 | tf_op jit(solution)/shard_map/ppermute | solution.py:557
  191.0 12.3 %collective-permute-start.42 = (bf16[5,128,128]{2,1,0:T(8,128)(2,1)}, bf16[5,128,128]{2,1,0:T(8,128)(2,1)}, u32[]{:S(2)}, u32[]{:S(2)}) collective-permute-start(bf16[5,128,128]{2,1,0:T(8,128)(2,1)} %get-tuple-element.226), channel_id=1, source_target_pairs={{0,5},{1,4},{2,7},{3,6},{4,1},{5,0},{6,3},{7,2},{8,13},{9,12},{10,... | collective-permute-start | bytes 491528 | tf_op jit(solution)/shard_map/ppermute | solution.py:513
  199.9 20.8 %all-to-all-start.2 = ((f32[32,4,128]{2,1,0:T(4,128)}), f32[32,4,128]{2,1,0:T(4,128)}, u32[]{:S(2)}, u32[]{:S(2)}) async-start(f32[32,4,128]{2,1,0:T(4,128)} %bitcast.7), calls=%async_computation.2 | async-start | bytes 131072 | tf_op jit(solution)/shard_map/all_to_all | solution.py:39
  220.7 12.1 %all-to-all-start = ((f32[32,8,128]{2,1,0:T(8,128)}), f32[32,8,128]{2,1,0:T(8,128)S(1)}, u32[]{:S(2)}, u32[]{:S(2)}) async-start(f32[32,8,128]{2,1,0:T(8,128)} %bitcast.39), calls=%async_computation | async-start | bytes 262144 | tf_op jit(solution)/shard_map/all_to_all | solution.py:39
  289.2 16.9 %collective-permute-start.69 = (bf16[20,128,128]{2,1,0:T(8,128)(2,1)S(1)}, bf16[20,128,128]{2,1,0:T(8,128)(2,1)S(1)}, u32[]{:S(2)}, u32[]{:S(2)}) collective-permute-start(bf16[20,128,128]{2,1,0:T(8,128)(2,1)S(1)} %get-tuple-element.340.chunk_ref), channel_id=1, source_target_pairs={{0,16},{1,17},{2,18},{3,19},{4,20},{5,21},{6,22},{7,23},{16,24},{1... | collective-permute-start | bytes 1966088 | tf_op jit(solution)/shard_map/ppermute | solution.py:537
  306.1 16.0 %collective-permute-start.77 = (bf16[20,128,128]{2,1,0:T(8,128)(2,1)S(1)}, bf16[20,128,128]{2,1,0:T(8,128)(2,1)S(1)}, u32[]{:S(2)}, u32[]{:S(2)}) collective-permute-start(bf16[20,128,128]{2,1,0:T(8,128)(2,1)S(1)} %collective-permute-done.69.chunk_ref), channel_id=1, source_target_pairs={{0,16},{1,17},{2,18},{3,19},{4,20},{5,21},{6,22},{7,23},{16,24},{1... | collective-permute-start | bytes 1966088 | tf_op jit(solution)/shard_map/ppermute | solution.py:537
  308.6 16.4 %collective-permute-start.62 = (bf16[5,128,128]{2,1,0:T(8,128)(2,1)S(1)}, bf16[5,128,128]{2,1,0:T(8,128)(2,1)S(1)}, u32[]{:S(2)}, u32[]{:S(2)}) collective-permute-start(bf16[5,128,128]{2,1,0:T(8,128)(2,1)S(1)} %get-tuple-element.258), channel_id=1, source_target_pairs={{0,1},{1,0},{2,3},{3,2},{4,5},{5,4},{6,7},{7,6},{8,9},{9,8},{10,11... | collective-permute-start | bytes 491528 | tf_op jit(solution)/shard_map/ppermute | solution.py:513
  322.1 35.4 %collective-permute-start.85 = (bf16[20,128,128]{2,1,0:T(8,128)(2,1)S(1)}, bf16[20,128,128]{2,1,0:T(8,128)(2,1)S(1)}, u32[]{:S(2)}, u32[]{:S(2)}) collective-permute-start(bf16[20,128,128]{2,1,0:T(8,128)(2,1)S(1)} %collective-permute-done.77.chunk_ref), channel_id=1, source_target_pairs={{0,16},{1,17},{2,18},{3,19},{4,20},{5,21},{6,22},{7,23},{16,24},{1... | collective-permute-start | bytes 1966088 | tf_op jit(solution)/shard_map/ppermute | solution.py:537
  331.5 11.4 %collective-permute-start.68 = (bf16[5,128,128]{2,1,0:T(8,128)(2,1)S(1)}, bf16[5,128,128]{2,1,0:T(8,128)(2,1)S(1)}, u32[]{:S(2)}, u32[]{:S(2)}) collective-permute-start(bf16[5,128,128]{2,1,0:T(8,128)(2,1)S(1)} %get-tuple-element.264), channel_id=1, source_target_pairs={{0,7},{1,6},{2,5},{3,4},{4,3},{5,2},{6,1},{7,0},{8,15},{9,14},{10,... | collective-permute-start | bytes 491528 | tf_op jit(solution)/shard_map/ppermute | solution.py:513
  349.7 11.3 %collective-permute-start.76 = (bf16[5,128,128]{2,1,0:T(8,128)(2,1)S(1)}, bf16[5,128,128]{2,1,0:T(8,128)(2,1)S(1)}, u32[]{:S(2)}, u32[]{:S(2)}) collective-permute-start(bf16[5,128,128]{2,1,0:T(8,128)(2,1)S(1)} %get-tuple-element.272), channel_id=1, source_target_pairs={{0,7},{1,6},{2,5},{3,4},{4,3},{5,2},{6,1},{7,0},{8,15},{9,14},{10,... | collective-permute-start | bytes 491528 | tf_op jit(solution)/shard_map/ppermute | solution.py:513
  351.1 12.1 %collective-permute-start.78 = (bf16[5,128,128]{2,1,0:T(8,128)(2,1)S(1)}, bf16[5,128,128]{2,1,0:T(8,128)(2,1)S(1)}, u32[]{:S(2)}, u32[]{:S(2)}) collective-permute-start(bf16[5,128,128]{2,1,0:T(8,128)(2,1)S(1)} %get-tuple-element.274), channel_id=1, source_target_pairs={{0,1},{1,0},{2,3},{3,2},{4,5},{5,4},{6,7},{7,6},{8,9},{9,8},{10,11... | collective-permute-start | bytes 491528 | tf_op jit(solution)/shard_map/ppermute | solution.py:513
  351.9 12.1 %collective-permute-start.79 = (bf16[5,128,128]{2,1,0:T(8,128)(2,1)S(1)}, bf16[5,128,128]{2,1,0:T(8,128)(2,1)S(1)}, u32[]{:S(2)}, u32[]{:S(2)}) collective-permute-start(bf16[5,128,128]{2,1,0:T(8,128)(2,1)S(1)} %get-tuple-element.275), channel_id=1, source_target_pairs={{0,2},{1,3},{2,0},{3,1},{4,6},{5,7},{6,4},{7,5},{8,10},{9,11},{10,... | collective-permute-start | bytes 491528 | tf_op jit(solution)/shard_map/ppermute | solution.py:513
  364.0 11.4 %collective-permute-start.84 = (bf16[5,128,128]{2,1,0:T(8,128)(2,1)S(1)}, bf16[5,128,128]{2,1,0:T(8,128)(2,1)S(1)}, u32[]{:S(2)}, u32[]{:S(2)}) collective-permute-start(bf16[5,128,128]{2,1,0:T(8,128)(2,1)S(1)} %get-tuple-element.280), channel_id=1, source_target_pairs={{0,7},{1,6},{2,5},{3,4},{4,3},{5,2},{6,1},{7,0},{8,15},{9,14},{10,... | collective-permute-start | bytes 491528 | tf_op jit(solution)/shard_map/ppermute | solution.py:513
  367.2 12.0 %collective-permute-start.87 = (bf16[5,128,128]{2,1,0:T(8,128)(2,1)S(1)}, bf16[5,128,128]{2,1,0:T(8,128)(2,1)S(1)}, u32[]{:S(2)}, u32[]{:S(2)}) collective-permute-start(bf16[5,128,128]{2,1,0:T(8,128)(2,1)S(1)} %get-tuple-element.283), channel_id=1, source_target_pairs={{0,2},{1,3},{2,0},{3,1},{4,6},{5,7},{6,4},{7,5},{8,10},{9,11},{10,... | collective-permute-start | bytes 491528 | tf_op jit(solution)/shard_map/ppermute | solution.py:513
  367.8 15.0 %collective-permute-start.88 = (bf16[5,128,128]{2,1,0:T(8,128)(2,1)S(1)}, bf16[5,128,128]{2,1,0:T(8,128)(2,1)S(1)}, u32[]{:S(2)}, u32[]{:S(2)}) collective-permute-start(bf16[5,128,128]{2,1,0:T(8,128)(2,1)S(1)} %get-tuple-element.284), channel_id=1, source_target_pairs={{0,3},{1,2},{2,1},{3,0},{4,7},{5,6},{6,5},{7,4},{8,11},{9,10},{10,... | collective-permute-start | bytes 491528 | tf_op jit(solution)/shard_map/ppermute | solution.py:513
  407.8 13.1 %collective-permute-start.112 = (bf16[5,128,128]{2,1,0:T(8,128)(2,1)}, bf16[5,128,128]{2,1,0:T(8,128)(2,1)S(1)}, u32[]{:S(2)}, u32[]{:S(2)}) collective-permute-start(bf16[5,128,128]{2,1,0:T(8,128)(2,1)} %get-tuple-element.327), channel_id=1, source_target_pairs={{0,6},{1,7},{2,4},{3,5},{4,2},{5,3},{6,0},{7,1},{8,14},{9,15},{10,... | collective-permute-start | bytes 491528 | tf_op jit(solution)/shard_map/ppermute | solution.py:513
  411.6 11.7 %collective-permute-start.113 = (bf16[5,128,128]{2,1,0:T(8,128)(2,1)}, bf16[5,128,128]{2,1,0:T(8,128)(2,1)S(1)}, u32[]{:S(2)}, u32[]{:S(2)}) collective-permute-start(bf16[5,128,128]{2,1,0:T(8,128)(2,1)} %get-tuple-element.328), channel_id=1, source_target_pairs={{0,7},{1,6},{2,5},{3,4},{4,3},{5,2},{6,1},{7,0},{8,15},{9,14},{10,... | collective-permute-start | bytes 491528 | tf_op jit(solution)/shard_map/ppermute | solution.py:513
  413.9 14.8 %collective-permute-start.93 = (bf16[5,128,128]{2,1,0:T(8,128)(2,1)}, bf16[5,128,128]{2,1,0:T(8,128)(2,1)S(1)}, u32[]{:S(2)}, u32[]{:S(2)}) collective-permute-start(bf16[5,128,128]{2,1,0:T(8,128)(2,1)} %get-tuple-element.298), channel_id=1, source_target_pairs={{0,1},{1,0},{2,3},{3,2},{4,5},{5,4},{6,7},{7,6},{8,9},{9,8},{10,11... | collective-permute-start | bytes 491528 | tf_op jit(solution)/shard_map/ppermute | solution.py:513
  414.6 14.7 %collective-permute-start.94 = (bf16[5,128,128]{2,1,0:T(8,128)(2,1)}, bf16[5,128,128]{2,1,0:T(8,128)(2,1)S(1)}, u32[]{:S(2)}, u32[]{:S(2)}) collective-permute-start(bf16[5,128,128]{2,1,0:T(8,128)(2,1)} %get-tuple-element.299), channel_id=1, source_target_pairs={{0,2},{1,3},{2,0},{3,1},{4,6},{5,7},{6,4},{7,5},{8,10},{9,11},{10,... | collective-permute-start | bytes 491528 | tf_op jit(solution)/shard_map/ppermute | solution.py:513
  426.4 35.0 %collective-permute-start.121 = (bf16[20,128,128]{2,1,0:T(8,128)(2,1)S(1)}, bf16[20,128,128]{2,1,0:T(8,128)(2,1)S(1)}, u32[]{:S(2)}, u32[]{:S(2)}) collective-permute-start(bf16[20,128,128]{2,1,0:T(8,128)(2,1)S(1)} %fold.10), channel_id=1, source_target_pairs={{0,8},{1,9},{2,10},{3,11},{4,12},{5,13},{6,14},{7,15},{16,0},{17,1... | collective-permute-start | bytes 1966088 | tf_op jit(solution)/shard_map/ppermute | solution.py:557
  429.3 12.9 %collective-permute-start.98 = (bf16[5,128,128]{2,1,0:T(8,128)(2,1)S(1)}, bf16[5,128,128]{2,1,0:T(8,128)(2,1)S(1)}, u32[]{:S(2)}, u32[]{:S(2)}) collective-permute-start(bf16[5,128,128]{2,1,0:T(8,128)(2,1)S(1)} %copy-done.119), channel_id=1, source_target_pairs={{0,6},{1,7},{2,4},{3,5},{4,2},{5,3},{6,0},{7,1},{8,14},{9,15},{10,... | collective-permute-start | bytes 491528 | tf_op jit(solution)/shard_map/ppermute | solution.py:513
  437.0 11.4 %collective-permute-start.115 = (bf16[5,128,128]{2,1,0:T(8,128)(2,1)S(1)}, bf16[5,128,128]{2,1,0:T(8,128)(2,1)S(1)}, u32[]{:S(2)}, u32[]{:S(2)}) collective-permute-start(bf16[5,128,128]{2,1,0:T(8,128)(2,1)S(1)} %copy-done.113), channel_id=1, source_target_pairs={{0,2},{1,3},{2,0},{3,1},{4,6},{5,7},{6,4},{7,5},{8,10},{9,11},{10,... | collective-permute-start | bytes 491528 | tf_op jit(solution)/shard_map/ppermute | solution.py:513
  444.3 13.8 %collective-permute-start.117 = (bf16[5,128,128]{2,1,0:T(8,128)(2,1)S(1)}, bf16[5,128,128]{2,1,0:T(8,128)(2,1)S(1)}, u32[]{:S(2)}, u32[]{:S(2)}) collective-permute-start(bf16[5,128,128]{2,1,0:T(8,128)(2,1)S(1)} %copy-done.109), channel_id=1, source_target_pairs={{0,4},{1,5},{2,6},{3,7},{4,0},{5,1},{6,2},{7,3},{8,12},{9,13},{10,... | collective-permute-start | bytes 491528 | tf_op jit(solution)/shard_map/ppermute | solution.py:513
  446.2 14.5 %collective-permute-start.118 = (bf16[5,128,128]{2,1,0:T(8,128)(2,1)S(1)}, bf16[5,128,128]{2,1,0:T(8,128)(2,1)S(1)}, u32[]{:S(2)}, u32[]{:S(2)}) collective-permute-start(bf16[5,128,128]{2,1,0:T(8,128)(2,1)S(1)} %copy-done.107), channel_id=1, source_target_pairs={{0,5},{1,4},{2,7},{3,6},{4,1},{5,0},{6,3},{7,2},{8,13},{9,12},{10,... | collective-permute-start | bytes 491528 | tf_op jit(solution)/shard_map/ppermute | solution.py:513
  448.4 12.3 %collective-permute-start.119 = (bf16[5,128,128]{2,1,0:T(8,128)(2,1)S(1)}, bf16[5,128,128]{2,1,0:T(8,128)(2,1)S(1)}, u32[]{:S(2)}, u32[]{:S(2)}) collective-permute-start(bf16[5,128,128]{2,1,0:T(8,128)(2,1)S(1)} %copy-done.106), channel_id=1, source_target_pairs={{0,6},{1,7},{2,4},{3,5},{4,2},{5,3},{6,0},{7,1},{8,14},{9,15},{10,... | collective-permute-start | bytes 491528 | tf_op jit(solution)/shard_map/ppermute | solution.py:513
  458.1 28.6 %collective-permute-start.123 = (bf16[20,128,128]{2,1,0:T(8,128)(2,1)S(1)}, bf16[20,128,128]{2,1,0:T(8,128)(2,1)S(1)}, u32[]{:S(2)}, u32[]{:S(2)}) collective-permute-start(bf16[20,128,128]{2,1,0:T(8,128)(2,1)S(1)} %fold.9), channel_id=1, source_target_pairs={{0,16},{1,17},{2,18},{3,19},{4,20},{5,21},{6,22},{7,23},{16,24},{1... | collective-permute-start | bytes 1966088 | tf_op jit(solution)/shard_map/ppermute | solution.py:557
  463.4 28.1 %collective-permute-start.122 = (bf16[20,128,128]{2,1,0:T(8,128)(2,1)S(1)}, bf16[20,128,128]{2,1,0:T(8,128)(2,1)S(1)}, u32[]{:S(2)}, u32[]{:S(2)}) collective-permute-start(bf16[20,128,128]{2,1,0:T(8,128)(2,1)S(1)} %fold.11), channel_id=1, source_target_pairs={{0,8},{1,9},{2,10},{3,11},{4,12},{5,13},{6,14},{7,15},{16,0},{17,1... | collective-permute-start | bytes 1966088 | tf_op jit(solution)/shard_map/ppermute | solution.py:557
  (205 other events, 3288.7 us)

commit v4 on v3

--- a/solution.py
+++ b/solution.py
@@ -8,7 +8,7 @@
 from jax.sharding import PartitionSpec as P
 
 
-ITERS = 2
+BLEND = 0.5
 GROUP = 4
 AXES = ("arc", "vec")
 SMEM = pltpu.MemorySpace.SMEM
@@ -233,12 +233,26 @@
     return product.astype(jnp.bfloat16)
 
 
-def arcs_kernel(plan, tab_ref, *refs):
+def mix_in(earlier, fresh, mix):
+    def halves(wide):
+        high = wide.astype(jnp.bfloat16)
+        return high, (wide - high.astype(jnp.float32)).astype(jnp.bfloat16)
+
+    def product(left, right):
+        return jnp.dot(left, right, preferred_element_type=jnp.float32)
+
+    high, low = halves(jnp.concatenate([earlier, fresh], axis=1))
+    mix_high, mix_low = halves(mix)
+    return product(high, mix_high) + (product(high, mix_low) + product(low, mix_high))
+
+
+def arcs_kernel(plan, mixed, tab_ref, *refs):
     count, cap = plan.rings * plan.plane, plan.cap
     arrived_refs = refs[:count]
     panel_ref, factor_ref = refs[count], refs[count + 1]
-    out_refs = refs[count + 2 : 2 * count + 2]
-    arrived, leaving, fetched, sems = refs[2 * count + 2 :]
+    extra = refs[count + 2 : -4 - count] if mixed else ()
+    out_refs = refs[-4 - count : -4] if mixed else refs[count + 2 : -5]
+    arrived, leaving, fetched, sems = refs[-4:]
     arc = pl.program_id(0)
     rows = arrived.shape[1]
 
@@ -267,7 +281,14 @@
             spot = tab_ref[row, tab_ref[plan.own_row + row, k]]
             spots[g].append(spot)
             fetched[g, k * rows : (k + 1) * rows, :] = arrived[spot]
-    coupled = [narrow_dot(panel_ref[g], fetched[g]) for g in group]
+    coupled = []
+    for g in group:
+        wide = jnp.dot(panel_ref[g], fetched[g], preferred_element_type=jnp.float32)
+        if mixed:
+            wide = mix_in(extra[0][g], wide, extra[1][...])
+        else:
+            refs[-5][g] = wide
+        coupled.append(wide.astype(jnp.bfloat16))
     whitened = [narrow_dot(factor_ref[g], coupled[g]) for g in group]
     smoothed = [narrow_dot(whitened[g], factor_ref[g], 0) for g in group]
     for g in group:
@@ -283,14 +304,15 @@
             outward(s).wait()
 
 
-def run_arcs(plan, tab, arrived, coupling_panel, inv_factor):
+def run_arcs(plan, tab, arrived, coupling_panel, inv_factor, extra):
     arcs, arc_rows, width = coupling_panel.shape
     block = arrived[0].shape[1:]
     total = plan.rings * plan.slots
     group = GROUP if arcs % GROUP == 0 else 1
     anywhere = pl.BlockSpec(memory_space=pl.ANY)
-    return pl.pallas_call(
-        functools.partial(arcs_kernel, plan),
+    wide = pl.BlockSpec((group, arc_rows, block[1]), lambda i, t: (i, 0, 0))
+    return pl.pallas_call(
+        functools.partial(arcs_kernel, plan, bool(extra)),
         grid_spec=pltpu.PrefetchScalarGridSpec(
             num_scalar_prefetch=1,
             grid=(arcs // group,),
@@ -298,8 +320,9 @@
             + [
                 pl.BlockSpec((group, arc_rows, width), lambda i, t: (i, 0, 0)),
                 pl.BlockSpec((group, arc_rows, arc_rows), lambda i, t: (i, 0, 0)),
-            ],
-            out_specs=[anywhere] * (plan.rings * plan.plane),
+            ]
+            + ([wide, pl.BlockSpec(extra[1].shape, lambda i, t: (0, 0))] if extra else []),
+            out_specs=[anywhere] * (plan.rings * plan.plane) + ([] if extra else [wide]),
             scratch_shapes=[
                 pltpu.VMEM((total,) + block, jnp.bfloat16),
                 pltpu.VMEM((total,) + block, jnp.bfloat16),
@@ -308,9 +331,10 @@
             ],
         ),
         out_shape=[jax.ShapeDtypeStruct((plan.cap,) + block, jnp.bfloat16)]
-        * (plan.rings * plan.plane),
+        * (plan.rings * plan.plane)
+        + ([] if extra else [jax.ShapeDtypeStruct((arcs, arc_rows, block[1]), jnp.float32)]),
         name="arcs",
-    )(tab, *arrived, coupling_panel, inv_factor)
+    )(tab, *arrived, coupling_panel, inv_factor, *extra)
 
 
 def add_up(plan, step, me_ref, held_ref, got_refs, part_refs, acc):
@@ -337,12 +361,16 @@
 
 
 def image_kernel(plan, both, me_ref, held_ref, field_ref, prior_ref, *refs):
-    got_refs, part_refs = refs[: plan.plane], refs[plan.plane : -3]
-    image_ref, gram_ref, acc = refs[-3:]
+    outputs = 4 if both else 3
+    got_refs, part_refs = refs[: plan.plane], refs[plan.plane : -outputs]
+    image_ref, gram_ref, acc = refs[-outputs], refs[1 - outputs], refs[-1]
     add_up(plan, 0, me_ref, held_ref, got_refs, part_refs, acc)
     rows = acc.shape[1]
     for b in range(plan.blocks):
-        image_ref[b] = acc[b].T + prior_ref[:, b : b + 1] * field_ref[b]
+        image = acc[b].T + prior_ref[:, b : b + 1] * field_ref[b]
+        image_ref[b] = image
+        if both:
+            refs[-2][b] = (field_ref[b] - BLEND * image).astype(jnp.bfloat16)
     gram_ref[...] = jnp.zeros_like(gram_ref)
     batch = max(n for n in range(1, 6) if plan.blocks % n == 0)
 
@@ -393,9 +421,10 @@
         out_shape=[
             jax.ShapeDtypeStruct(shape, jnp.float32),
             jax.ShapeDtypeStruct((2 if both else 1, cols, cols), jnp.float32),
-        ],
+        ]
+        + ([pltpu.VMEM(shape, jnp.bfloat16)] if both else []),
         in_specs=fold_specs(args),
-        out_specs=[pl.BlockSpec(memory_space=VMEM)] * 2,
+        out_specs=[pl.BlockSpec(memory_space=VMEM)] * (3 if both else 2),
         scratch_shapes=[pltpu.VMEM(shape, jnp.float32)],
         compiler_params=SMALL,
         name="image",
@@ -478,7 +507,9 @@
             out_ref[...] = y * down * along
 
 
-def step_kernel(grams_ref, res_ref, step_ref, beta_ref, new_ref, first_inv, second_inv):
+def step_kernel(
+    grams_ref, res_ref, step_ref, beta_ref, new_ref, mix_ref, first_inv, second_inv
+):
     res, cross, image = res_ref[...], grams_ref[0], grams_ref[1]
     invert_into([first_inv, second_inv], [0.5 * (cross + cross.T), 0.5 * (res + res.T)])
     step = times_high(first_inv[...], res)
@@ -486,7 +517,11 @@
     moved = times_high(cross, step)
     new = res - moved.T - moved + times_high(step.T, times_high(image, step))
     new_ref[...] = new
-    beta_ref[...] = times_high(second_inv[...], new)
+    beta = times_high(second_inv[...], new)
+    beta_ref[...] = beta
+    size = beta.shape[0]
+    mix_ref[size:, :] = step * (1.0 / BLEND)
+    mix_ref[:size, :] = identity(size) + beta - step * (1.0 / BLEND)
 
 
 def last_kernel(grams_ref, res_ref, step_ref, first_inv):
@@ -495,11 +530,13 @@
     step_ref[...] = times_high(first_inv[...], res_ref[...])
 
 
-def small_solve(kernel, args, outputs, scratch):
+def small_solve(kernel, args, outputs, scratch, tall=0):
     shape = args[0].shape[1:]
+    double = (2 * shape[0], shape[1])
     return pl.pallas_call(
         kernel,
-        out_shape=[jax.ShapeDtypeStruct(shape, jnp.float32)] * outputs,
+        out_shape=[jax.ShapeDtypeStruct(shape, jnp.float32)] * outputs
+        + [jax.ShapeDtypeStruct(double, jnp.float32)] * tall,
         scratch_shapes=[pltpu.VMEM(shape, jnp.float32)] * scratch,
         compiler_params=SMALL,
         name="solve",
@@ -529,8 +566,10 @@
     )(me)
 
 
-def apply_schur(plan, me, tab, held, field, prior_cols, coupling_panel, inv_factor, both):
-    chunk, arrived = field.astype(jnp.bfloat16), []
+def apply_schur(
+    plan, me, tab, held, chunk, field, prior_cols, coupling_panel, inv_factor, extra=()
+):
+    arrived, both = [], not extra
     for s in range(plan.rings):
         following = None
         if s + 1 < plan.rings:
@@ -540,7 +579,7 @@
         if s + 1 < plan.rings:
             me = gate(me)
         chunk = following
-    leaving = run_arcs(plan, tab, arrived, coupling_panel, inv_factor)
+    leaving = run_arcs(plan, tab, arrived, coupling_panel, inv_factor, extra)
     moved, folded = {}, []
     for j, s in enumerate(plan.back):
         buffers = leaving[s * plan.plane : (s + 1) * plan.plane]
@@ -551,8 +590,8 @@
         if s:
             me = gate(me)
         if s == 0:
-            image, grams = fold_image(plan, me, held, got, sources, field, prior_cols, both)
-            return image, grams, me
+            made = fold_image(plan, me, held, got, sources, field, prior_cols, both)
+            return (*made, leaving[-1], me)
         folded.append(fold(plan, s, me, held, got, sources))
         moved[s] = lax.ppermute(folded[j], AXES, plan.shift_back(s))
 
@@ -564,23 +603,25 @@
     me = lax.axis_index(AXES).astype(jnp.int32).reshape(1)
     tab, held = make_tables(plan, me, coupling_owner, coupling_block)
     prior_cols = prior_diag.T
-    solution_field = None
-    residual = right_side
-    direction = right_side
-    res_gram = sum_all(inner_gram(residual, residual)[None])[0]
-    for sweep_index in range(ITERS):
-        last = sweep_index + 1 == ITERS
-        image_vec, grams, me = apply_schur(
-            plan, me, tab, held, direction, prior_cols, coupling_panel, inv_factor, not last
-        )
-        if last:
-            (step_mat,) = small_solve(last_kernel, (sum_all(grams), res_gram), 1, 1)
-            return tuple(update(direction, image_vec, solution_field, residual, step_mat))
-        grams = sum_all(grams)
-        step_mat, beta_mat, res_gram = small_solve(step_kernel, (grams, res_gram), 3, 2)
-        solution_field = combine_cols(direction, step_mat)
-        residual = residual - combine_cols(image_vec, step_mat)
-        direction = residual + combine_cols(direction, beta_mat)
+    common = (prior_cols, coupling_panel, inv_factor)
+    rounded = right_side.astype(jnp.bfloat16)
+    res_gram = sum_all(inner_gram(right_side, right_side)[None])[0]
+    image_vec, grams, blend, coupled, me = apply_schur(
+        plan, me, tab, held, rounded, right_side, *common
+    )
+    grams, res_gram = lax.optimization_barrier((grams, res_gram))
+    grams = sum_all(grams)
+    step_mat, beta_mat, res_gram, mix = small_solve(
+        step_kernel, (grams, res_gram), 3, 2, 1
+    )
+    solution_field = combine_cols(right_side, step_mat)
+    residual = right_side - combine_cols(image_vec, step_mat)
+    direction = residual + combine_cols(right_side, beta_mat)
+    image_vec, grams, _, _ = apply_schur(
+        plan, me, tab, held, blend, direction, *common, extra=(coupled, mix)
+    )
+    (step_mat,) = small_solve(last_kernel, (sum_all(grams), res_gram), 1, 1)
+    return tuple(update(direction, image_vec, solution_field, residual, step_mat))
 
 
 def solution(mesh):

time: 543 us -> 522 us (0.961)
  waiting for transfers between devices: 219 us -> 180 us
  Pallas kernels: 132 us -> 142 us
  local copies, waits for them, and re-layouts: 17.6 us -> 23.3 us
    ppermute x112, waiting for transfers between devices: 137 us -> 115 us  [trade_plane(): lax.ppermute(buffers[offset], AXES, plan.shift_plane(offset))]
    all_to_all x4, waiting for transfers between devices: 19.5 us -> 7.88 us  [trade(): return lax.all_to_all(buffer, AXES, split_axis=0, concat_axis=0, tiled=True)]
    unnamed x251 -> x231, local copies, waits for them, and re-layouts: 16.4 us -> 22 us
  transfers between devices with their start and end apart: 128 -> 128, of which waited for: 70 -> 54; matrix products, arithmetic and copies ran while one was open for 1% -> 2% of each run, Pallas kernels for 8% -> 14%
where the time goes in v4:
time: 522 us; the launch traced here: 520 us
  waiting for transfers between devices  180 us (34%)
  starting transfers between devices  145 us (28%)
  Pallas kernels  142 us (27%)
  local copies, waits for them, and re-layouts  23.3 us (4%)
  blocking collectives  18.2 us (3%)
  matrix products  7.7 us (1%)
    ppermute x112, waiting for transfers between devices, trade_plane(): lax.ppermute(buffers[offset], AXES, plan.shift_plane(offset))  115 us
    ppermute x112, starting transfers between devices, trade_plane(): lax.ppermute(buffers[offset], AXES, plan.shift_plane(offset))  104 us
    pallas_call x2, Pallas kernels, small_solve(): pl.pallas_call(kernel, out_shape=[jax.ShapeDtypeStruct(shape, jnp.float32...  50.7 us
    ppermute x6, waiting for transfers between devices, apply_schur(): following = lax.ppermute(chunk, AXES, plan.ring)  48.8 us
    pallas_call x2, Pallas kernels, run_arcs(): pl.pallas_call(functools.partial(arcs_kernel, plan, bool(extra)), grid_sp...  32.5 us
    unnamed x231, local copies, waits for them, and re-layouts  22 us
    all_to_all x2, blocking collectives, trade(): return lax.all_to_all(buffer, AXES, split_axis=0, concat_axis=0, tiled=True)  18.2 us
    all_to_all x4, starting transfers between devices, trade(): return lax.all_to_all(buffer, AXES, split_axis=0, concat_axis=0, tiled=True)  16 us
  transfers between devices with their start and end apart: 128, of which 54 were waited for; matrix products, arithmetic and copies ran while one was open for 2% of the time, Pallas kernels for 14%

profile of v4, /device:TPU:0, one launch (start us, length us, event | category | flops | bytes accessed | tf_op | source)
XLA Modules:
  0.0 520.3 jit_solution(14050939662229211100)
XLA Ops:
  2.1 4.1 collective-permute-start.7
  6.2 14.0 %collective-permute-done.7.chunk_ref = bf16[20,128,128]{2,1,0:T(8,128)(2,1)S(1)} collective-permute-done((bf16[20,128,128]{2,1,0:T(8,128)(2,1)S(1)}, bf16[20,128,128]{2,1,0:T(8,128)(2,1)S(1)}, u32[]{:S(2)}, u32[]{:S(2)}) %collective-permute-start.7) | collective-permute-done | bytes 655392 | tf_op jit(solution)/shard_map/ppermute | solution.py:576
  20.2 3.4 collective-permute-start.15
  26.6 10.1 %collective-permute-done.15.chunk_ref = bf16[20,128,128]{2,1,0:T(8,128)(2,1)S(1)} collective-permute-done((bf16[20,128,128]{2,1,0:T(8,128)(2,1)S(1)}, bf16[20,128,128]{2,1,0:T(8,128)(2,1)S(1)}, u32[]{:S(2)}, u32[]{:S(2)}) %collective-permute-start.15) | collective-permute-done | bytes 655392 | tf_op jit(solution)/shard_map/ppermute | solution.py:576
  36.7 3.4 collective-permute-start.23
  46.2 3.3 collective-permute-start.5
  70.3 3.1 collective-permute-done.14.refs_15_
  86.8 3.6 collective-permute-done.21.refs_22_
  97.4 3.7 collective-permute-done.26.refs_27_
  101.1 3.9 collective-permute-done.29.refs_30_
  107.1 15.1 %arcs.2 = (bf16[5,128,128]{2,1,0:T(8,128)(2,1)}, bf16[5,128,128]{2,1,0:T(8,128)(2,1)}, bf16[5,128,128]{2,1,0:T(8,128)(2,1)}, bf16[5,128,128]{2,1,0:T(8,128)(2,1)...) custom-call(s32[32,128]{1,0:T(8,128)} %copy-done.31, ...), custom_call_target="tpu_custom_call" | custom-call | tf_op jit(solution)/shard_map/arcs/pallas_call | solution.py:314
  127.7 2.8 collective-permute-done.46.refs_2_
  134.9 4.1 collective-permute-done.50.refs_6_
  139.1 2.9 collective-permute-done.51.refs_7_
  149.0 2.7 collective-permute-done.33.refs_3_
  156.4 4.2 collective-permute-done.36.refs_6_
  176.0 3.0 collective-permute-start.61
  180.3 2.7 fold.8
  187.8 4.7 collective-permute-done.39.refs_2_
  198.9 4.2 collective-permute-done.43.refs_6_
  203.1 3.6 collective-permute-done.44.refs_7_
  206.6 2.7 collective-permute-done.60.refs_8_
  215.0 6.9 %image.2 = (f32[20,128,128]{2,1,0:T(8,128)S(1)}, f32[2,128,128]{2,1,0:T(8,128)}, bf16[20,128,128]{2,1,0:T(8,128)(2,1)S(1)}) custom-call(s32[1]{0:T(128)} %gate.17.me_ref.in_ref, s32[8,128]{1,0:T(8,128)S(1)} %get-tuple-element.176.held_ref, f32[20,128,128]{2,1,0:T(8,128)S(1)} %copy-done, f32[128,20]{1,0:T(8,128)S(1)} %bitcast.32, ...), custom_call_target="tpu_custom_call" | custom-call | tf_op jit(solution)/shard_map/image/pallas_call | solution.py:419
  222.4 16.2 %collective-permute-done.69.chunk_ref = bf16[20,128,128]{2,1,0:T(8,128)(2,1)S(1)} collective-permute-done((bf16[20,128,128]{2,1,0:T(8,128)(2,1)S(1)}, bf16[20,128,128]{2,1,0:T(8,128)(2,1)S(1)}, u32[]{:S(2)}, u32[]{:S(2)}) %collective-permute-start.69) | collective-permute-done | bytes 655392 | tf_op jit(solution)/shard_map/ppermute | solution.py:576
  245.9 8.6 %collective-permute-done.77.chunk_ref = bf16[20,128,128]{2,1,0:T(8,128)(2,1)S(1)} collective-permute-done((bf16[20,128,128]{2,1,0:T(8,128)(2,1)S(1)}, bf16[20,128,128]{2,1,0:T(8,128)(2,1)S(1)}, u32[]{:S(2)}, u32[]{:S(2)}) %collective-permute-start.77) | collective-permute-done | bytes 655392 | tf_op jit(solution)/shard_map/ppermute | solution.py:576
  263.5 2.9 fusion.4
  266.5 4.6 all-to-all-start
  275.8 2.8 all-to-all-done
  279.5 9.1 %all_to_all.30 = f32[32,4,128]{2,1,0:T(4,128)S(1)} all-to-all(f32[32,4,128]{2,1,0:T(4,128)S(1)} %broadcast_in_dim.6), channel_id=1, replica_groups=mesh['arc'=8,'vec'=4] {'arc','vec'}, dimensions={0} | all-to-all | bytes 131072 | tf_op jit(solution)/shard_map/all_to_all | solution.py:39
  288.6 4.0 all-to-all-start.2
  315.5 4.6 all-to-all-start.3
  328.6 33.7 %solve.2 = (f32[128,128]{1,0:T(8,128)S(1)}, f32[128,128]{1,0:T(8,128)S(1)}, f32[128,128]{1,0:T(8,128)S(1)}, f32[256,128]{1,0:T(8,128)S(1)}) custom-call(f32[2,128,128]{2,1,0:T(8,128)S(1)} %bitcast.34, f32[128,128]{1,0:T(8,128)S(1)} %bitcast.35), custom_call_target="tpu_custom_call" | custom-call | tf_op jit(solution)/shard_map/solve/pallas_call | solution.py:536
  363.0 17.4 %arcs.3 = (bf16[5,128,128]{2,1,0:T(8,128)(2,1)}, bf16[5,128,128]{2,1,0:T(8,128)(2,1)}, bf16[5,128,128]{2,1,0:T(8,128)(2,1)}, bf16[5,128,128]{2,1,0:T(8,128)(2,1)...) custom-call(s32[32,128]{1,0:T(8,128)} %copy-done.31, ...), custom_call_target="tpu_custom_call" | custom-call | tf_op jit(solution)/shard_map/arcs/pallas_call | solution.py:314
  386.2 2.9 collective-permute-done.108.refs_2_
  394.0 4.1 collective-permute-done.112.refs_6_
  398.1 3.0 collective-permute-done.113.refs_7_
  409.2 3.1 collective-permute-done.95.refs_3_
  417.1 3.7 collective-permute-done.98.refs_6_
  448.4 3.4 collective-permute-done.101.refs_2_
  458.4 3.8 collective-permute-done.105.refs_6_
  462.2 2.8 collective-permute-done.106.refs_7_
  465.0 5.4 %collective-permute-done.122.refs_8_ = bf16[20,128,128]{2,1,0:T(8,128)(2,1)S(1)} collective-permute-done((bf16[20,128,128]{2,1,0:T(8,128)(2,1)S(1)}, bf16[20,128,128]{2,1,0:T(8,128)(2,1)S(1)}, u32[]{:S(2)}, u32[]{:S(2)}) %collective-permute-start.122) | collective-permute-done | bytes 655392 | tf_op jit(solution)/shard_map/ppermute | solution.py:596
  470.5 4.5 image.3
  476.0 9.1 %all_to_all.31 = f32[32,4,128]{2,1,0:T(4,128)S(1)} all-to-all(f32[32,4,128]{2,1,0:T(4,128)S(1)} %bitcast.37), channel_id=1, replica_groups=mesh['arc'=8,'vec'=4] {'arc','vec'}, dimensions={0} | all-to-all | bytes 131072 | tf_op jit(solution)/shard_map/all_to_all | solution.py:39
  485.8 2.8 all-to-all-start.5
  491.0 5.1 all-to-all-done.5
  496.1 17.0 %solve.3.step_ref = f32[128,128]{1,0:T(8,128)S(1)} custom-call(f32[1,128,128]{2,1,0:T(8,128)S(1)} %bitcast.36, f32[128,128]{1,0:T(8,128)S(1)} %get-tuple-element.349.res_ref), custom_call_target="tpu_custom_call" | custom-call | tf_op jit(solution)/shard_map/solve/pallas_call | solution.py:536
  513.7 6.6 %update.1 = (f32[20,128,128]{2,1,0:T(8,128)}, f32[20,128,128]{2,1,0:T(8,128)}) custom-call(f32[20,128,128]{2,1,0:T(8,128)} %copy-done.1, f32[20,128,128]{2,1,0:T(8,128)} %copy-done.2, f32[20,128,128]{2,1,0:T(8,128)} %convolution_bitcast_fusion.sol_ref, f32[20,128,128]{2,1,0:T(8,128)} %copy-done.40, f32[128,128]{1,0:T(8,128)} %copy-done.5), custom_call_target="tpu_custom_call" | custom-call | tf_op jit(solution)/shard_map/update/pallas_call | solution.py:448
  (486 shorter events, 225.1 us)
Async XLA Ops:
  2.1 18.1 %collective-permute-start.7 = (bf16[20,128,128]{2,1,0:T(8,128)(2,1)S(1)}, bf16[20,128,128]{2,1,0:T(8,128)(2,1)S(1)}, u32[]{:S(2)}, u32[]{:S(2)}) collective-permute-start(bf16[20,128,128]{2,1,0:T(8,128)(2,1)S(1)} %convert_element_type.3.chunk_ref), channel_id=1, source_target_pairs={{0,16},{1,17},{2,18},{3,19},{4,20},{5,21},{6,22},{7,23},{16,24},{1... | collective-permute-start | bytes 1966088 | tf_op jit(solution)/shard_map/ppermute | solution.py:576
  20.2 16.5 %collective-permute-start.15 = (bf16[20,128,128]{2,1,0:T(8,128)(2,1)S(1)}, bf16[20,128,128]{2,1,0:T(8,128)(2,1)S(1)}, u32[]{:S(2)}, u32[]{:S(2)}) collective-permute-start(bf16[20,128,128]{2,1,0:T(8,128)(2,1)S(1)} %collective-permute-done.7.chunk_ref), channel_id=1, source_target_pairs={{0,16},{1,17},{2,18},{3,19},{4,20},{5,21},{6,22},{7,23},{16,24},{1... | collective-permute-start | bytes 1966088 | tf_op jit(solution)/shard_map/ppermute | solution.py:576
  26.6 16.5 %collective-permute-start = (bf16[5,128,128]{2,1,0:T(8,128)(2,1)S(1)}, bf16[5,128,128]{2,1,0:T(8,128)(2,1)S(1)}, u32[]{:S(2)}, u32[]{:S(2)}) collective-permute-start(bf16[5,128,128]{2,1,0:T(8,128)(2,1)S(1)} %get-tuple-element.179), channel_id=1, source_target_pairs={{0,1},{1,0},{2,3},{3,2},{4,5},{5,4},{6,7},{7,6},{8,9},{9,8},{10,11... | collective-permute-start | bytes 491528 | tf_op jit(solution)/shard_map/ppermute | solution.py:550
  36.7 37.5 %collective-permute-start.23 = (bf16[20,128,128]{2,1,0:T(8,128)(2,1)S(1)}, bf16[20,128,128]{2,1,0:T(8,128)(2,1)S(1)}, u32[]{:S(2)}, u32[]{:S(2)}) collective-permute-start(bf16[20,128,128]{2,1,0:T(8,128)(2,1)S(1)} %collective-permute-done.15.chunk_ref), channel_id=1, source_target_pairs={{0,16},{1,17},{2,18},{3,19},{4,20},{5,21},{6,22},{7,23},{16,24},{1... | collective-permute-start | bytes 1966088 | tf_op jit(solution)/shard_map/ppermute | solution.py:576
  51.5 12.9 %collective-permute-start.11 = (bf16[5,128,128]{2,1,0:T(8,128)(2,1)S(1)}, bf16[5,128,128]{2,1,0:T(8,128)(2,1)S(1)}, u32[]{:S(2)}, u32[]{:S(2)}) collective-permute-start(bf16[5,128,128]{2,1,0:T(8,128)(2,1)S(1)} %get-tuple-element.190), channel_id=1, source_target_pairs={{0,4},{1,5},{2,6},{3,7},{4,0},{5,1},{6,2},{7,3},{8,12},{9,13},{10,... | collective-permute-start | bytes 491528 | tf_op jit(solution)/shard_map/ppermute | solution.py:550
  83.9 13.0 %collective-permute-start.25 = (bf16[5,128,128]{2,1,0:T(8,128)(2,1)S(1)}, bf16[5,128,128]{2,1,0:T(8,128)(2,1)S(1)}, u32[]{:S(2)}, u32[]{:S(2)}) collective-permute-start(bf16[5,128,128]{2,1,0:T(8,128)(2,1)S(1)} %get-tuple-element.204), channel_id=1, source_target_pairs={{0,2},{1,3},{2,0},{3,1},{4,6},{5,7},{6,4},{7,5},{8,10},{9,11},{10,... | collective-permute-start | bytes 491528 | tf_op jit(solution)/shard_map/ppermute | solution.py:550
  85.1 16.0 %collective-permute-start.26 = (bf16[5,128,128]{2,1,0:T(8,128)(2,1)S(1)}, bf16[5,128,128]{2,1,0:T(8,128)(2,1)S(1)}, u32[]{:S(2)}, u32[]{:S(2)}) collective-permute-start(bf16[5,128,128]{2,1,0:T(8,128)(2,1)S(1)} %get-tuple-element.205), channel_id=1, source_target_pairs={{0,3},{1,2},{2,1},{3,0},{4,7},{5,6},{6,5},{7,4},{8,11},{9,10},{10,... | collective-permute-start | bytes 491528 | tf_op jit(solution)/shard_map/ppermute | solution.py:550
  126.7 12.4 %collective-permute-start.50 = (bf16[5,128,128]{2,1,0:T(8,128)(2,1)}, bf16[5,128,128]{2,1,0:T(8,128)(2,1)S(1)}, u32[]{:S(2)}, u32[]{:S(2)}) collective-permute-start(bf16[5,128,128]{2,1,0:T(8,128)(2,1)} %get-tuple-element.248), channel_id=1, source_target_pairs={{0,6},{1,7},{2,4},{3,5},{4,2},{5,3},{6,0},{7,1},{8,14},{9,15},{10,... | collective-permute-start | bytes 491528 | tf_op jit(solution)/shard_map/ppermute | solution.py:550
  132.2 14.8 %collective-permute-start.31 = (bf16[5,128,128]{2,1,0:T(8,128)(2,1)}, bf16[5,128,128]{2,1,0:T(8,128)(2,1)S(1)}, u32[]{:S(2)}, u32[]{:S(2)}) collective-permute-start(bf16[5,128,128]{2,1,0:T(8,128)(2,1)} %get-tuple-element.219), channel_id=1, source_target_pairs={{0,1},{1,0},{2,3},{3,2},{4,5},{5,4},{6,7},{7,6},{8,9},{9,8},{10,11... | collective-permute-start | bytes 491528 | tf_op jit(solution)/shard_map/ppermute | solution.py:550
  133.2 15.0 %collective-permute-start.32 = (bf16[5,128,128]{2,1,0:T(8,128)(2,1)}, bf16[5,128,128]{2,1,0:T(8,128)(2,1)S(1)}, u32[]{:S(2)}, u32[]{:S(2)}) collective-permute-start(bf16[5,128,128]{2,1,0:T(8,128)(2,1)} %get-tuple-element.220), channel_id=1, source_target_pairs={{0,2},{1,3},{2,0},{3,1},{4,6},{5,7},{6,4},{7,5},{8,10},{9,11},{10,... | collective-permute-start | bytes 491528 | tf_op jit(solution)/shard_map/ppermute | solution.py:550
  145.1 35.2 %collective-permute-start.59 = (bf16[20,128,128]{2,1,0:T(8,128)(2,1)S(1)}, bf16[20,128,128]{2,1,0:T(8,128)(2,1)S(1)}, u32[]{:S(2)}, u32[]{:S(2)}) collective-permute-start(bf16[20,128,128]{2,1,0:T(8,128)(2,1)S(1)} %fold.7), channel_id=1, source_target_pairs={{0,8},{1,9},{2,10},{3,11},{4,12},{5,13},{6,14},{7,15},{16,0},{17,1... | collective-permute-start | bytes 1966088 | tf_op jit(solution)/shard_map/ppermute | solution.py:596
  148.2 12.4 %collective-permute-start.36 = (bf16[5,128,128]{2,1,0:T(8,128)(2,1)S(1)}, bf16[5,128,128]{2,1,0:T(8,128)(2,1)S(1)}, u32[]{:S(2)}, u32[]{:S(2)}) collective-permute-start(bf16[5,128,128]{2,1,0:T(8,128)(2,1)S(1)} %copy-done.110), channel_id=1, source_target_pairs={{0,6},{1,7},{2,4},{3,5},{4,2},{5,3},{6,0},{7,1},{8,14},{9,15},{10,... | collective-permute-start | bytes 491528 | tf_op jit(solution)/shard_map/ppermute | solution.py:550
  163.0 13.0 %collective-permute-start.55 = (bf16[5,128,128]{2,1,0:T(8,128)(2,1)S(1)}, bf16[5,128,128]{2,1,0:T(8,128)(2,1)S(1)}, u32[]{:S(2)}, u32[]{:S(2)}) collective-permute-start(bf16[5,128,128]{2,1,0:T(8,128)(2,1)S(1)} %copy-done.99), channel_id=1, source_target_pairs={{0,4},{1,5},{2,6},{3,7},{4,0},{5,1},{6,2},{7,3},{8,12},{9,13},{10,... | collective-permute-start | bytes 491528 | tf_op jit(solution)/shard_map/ppermute | solution.py:550
  163.6 15.4 %collective-permute-start.56 = (bf16[5,128,128]{2,1,0:T(8,128)(2,1)S(1)}, bf16[5,128,128]{2,1,0:T(8,128)(2,1)S(1)}, u32[]{:S(2)}, u32[]{:S(2)}) collective-permute-start(bf16[5,128,128]{2,1,0:T(8,128)(2,1)S(1)} %copy-done.98), channel_id=1, source_target_pairs={{0,5},{1,4},{2,7},{3,6},{4,1},{5,0},{6,3},{7,2},{8,13},{9,12},{10,... | collective-permute-start | bytes 491528 | tf_op jit(solution)/shard_map/ppermute | solution.py:550
  176.0 30.6 %collective-permute-start.61 = (bf16[20,128,128]{2,1,0:T(8,128)(2,1)S(1)}, bf16[20,128,128]{2,1,0:T(8,128)(2,1)S(1)}, u32[]{:S(2)}, u32[]{:S(2)}) collective-permute-start(bf16[20,128,128]{2,1,0:T(8,128)(2,1)S(1)} %fold.6), channel_id=1, source_target_pairs={{0,16},{1,17},{2,18},{3,19},{4,20},{5,21},{6,22},{7,23},{16,24},{1... | collective-permute-start | bytes 1966088 | tf_op jit(solution)/shard_map/ppermute | solution.py:596
  183.1 26.3 %collective-permute-start.60 = (bf16[20,128,128]{2,1,0:T(8,128)(2,1)}, bf16[20,128,128]{2,1,0:T(8,128)(2,1)S(1)}, u32[]{:S(2)}, u32[]{:S(2)}) collective-permute-start(bf16[20,128,128]{2,1,0:T(8,128)(2,1)} %fold.8), channel_id=1, source_target_pairs={{0,8},{1,9},{2,10},{3,11},{4,12},{5,13},{6,14},{7,15},{16,0},{17,1... | collective-permute-start | bytes 1966088 | tf_op jit(solution)/shard_map/ppermute | solution.py:596
  221.8 16.8 %collective-permute-start.69 = (bf16[20,128,128]{2,1,0:T(8,128)(2,1)S(1)}, bf16[20,128,128]{2,1,0:T(8,128)(2,1)S(1)}, u32[]{:S(2)}, u32[]{:S(2)}) collective-permute-start(bf16[20,128,128]{2,1,0:T(8,128)(2,1)S(1)} %get-tuple-element.264.chunk_ref), channel_id=1, source_target_pairs={{0,16},{1,17},{2,18},{3,19},{4,20},{5,21},{6,22},{7,23},{16,24},{1... | collective-permute-start | bytes 1966088 | tf_op jit(solution)/shard_map/ppermute | solution.py:576
  238.6 15.9 %collective-permute-start.77 = (bf16[20,128,128]{2,1,0:T(8,128)(2,1)S(1)}, bf16[20,128,128]{2,1,0:T(8,128)(2,1)S(1)}, u32[]{:S(2)}, u32[]{:S(2)}) collective-permute-start(bf16[20,128,128]{2,1,0:T(8,128)(2,1)S(1)} %collective-permute-done.69.chunk_ref), channel_id=1, source_target_pairs={{0,16},{1,17},{2,18},{3,19},{4,20},{5,21},{6,22},{7,23},{16,24},{1... | collective-permute-start | bytes 1966088 | tf_op jit(solution)/shard_map/ppermute | solution.py:576
  242.4 17.3 %collective-permute-start.63 = (bf16[5,128,128]{2,1,0:T(8,128)(2,1)S(1)}, bf16[5,128,128]{2,1,0:T(8,128)(2,1)S(1)}, u32[]{:S(2)}, u32[]{:S(2)}) collective-permute-start(bf16[5,128,128]{2,1,0:T(8,128)(2,1)S(1)} %get-tuple-element.267), channel_id=1, source_target_pairs={{0,2},{1,3},{2,0},{3,1},{4,6},{5,7},{6,4},{7,5},{8,10},{9,11},{10,... | collective-permute-start | bytes 491528 | tf_op jit(solution)/shard_map/ppermute | solution.py:550
  243.1 18.1 %collective-permute-start.64 = (bf16[5,128,128]{2,1,0:T(8,128)(2,1)S(1)}, bf16[5,128,128]{2,1,0:T(8,128)(2,1)S(1)}, u32[]{:S(2)}, u32[]{:S(2)}) collective-permute-start(bf16[5,128,128]{2,1,0:T(8,128)(2,1)S(1)} %get-tuple-element.268), channel_id=1, source_target_pairs={{0,3},{1,2},{2,1},{3,0},{4,7},{5,6},{6,5},{7,4},{8,11},{9,10},{10,... | collective-permute-start | bytes 491528 | tf_op jit(solution)/shard_map/ppermute | solution.py:550
  244.3 16.9 %collective-permute-start.65 = (bf16[5,128,128]{2,1,0:T(8,128)(2,1)S(1)}, bf16[5,128,128]{2,1,0:T(8,128)(2,1)S(1)}, u32[]{:S(2)}, u32[]{:S(2)}) collective-permute-start(bf16[5,128,128]{2,1,0:T(8,128)(2,1)S(1)} %get-tuple-element.269), channel_id=1, source_target_pairs={{0,4},{1,5},{2,6},{3,7},{4,0},{5,1},{6,2},{7,3},{8,12},{9,13},{10,... | collective-permute-start | bytes 491528 | tf_op jit(solution)/shard_map/ppermute | solution.py:550
  245.7 17.2 %collective-permute-start.66 = (bf16[5,128,128]{2,1,0:T(8,128)(2,1)S(1)}, bf16[5,128,128]{2,1,0:T(8,128)(2,1)S(1)}, u32[]{:S(2)}, u32[]{:S(2)}) collective-permute-start(bf16[5,128,128]{2,1,0:T(8,128)(2,1)S(1)} %get-tuple-element.270), channel_id=1, source_target_pairs={{0,5},{1,4},{2,7},{3,6},{4,1},{5,0},{6,3},{7,2},{8,13},{9,12},{10,... | collective-permute-start | bytes 491528 | tf_op jit(solution)/shard_map/ppermute | solution.py:550
  254.5 46.3 %collective-permute-start.85 = (bf16[20,128,128]{2,1,0:T(8,128)(2,1)S(1)}, bf16[20,128,128]{2,1,0:T(8,128)(2,1)}, u32[]{:S(2)}, u32[]{:S(2)}) collective-permute-start(bf16[20,128,128]{2,1,0:T(8,128)(2,1)S(1)} %collective-permute-done.77.chunk_ref), channel_id=1, source_target_pairs={{0,16},{1,17},{2,18},{3,19},{4,20},{5,21},{6,22},{7,23},{16,24},{1... | collective-permute-start | bytes 1966088 | tf_op jit(solution)/shard_map/ppermute | solution.py:576
  261.2 12.8 %collective-permute-start.70 = (bf16[5,128,128]{2,1,0:T(8,128)(2,1)}, bf16[5,128,128]{2,1,0:T(8,128)(2,1)}, u32[]{:S(2)}, u32[]{:S(2)}) collective-permute-start(bf16[5,128,128]{2,1,0:T(8,128)(2,1)} %get-tuple-element.274), channel_id=1, source_target_pairs={{0,1},{1,0},{2,3},{3,2},{4,5},{5,4},{6,7},{7,6},{8,9},{9,8},{10,11... | collective-permute-start | bytes 491528 | tf_op jit(solution)/shard_map/ppermute | solution.py:550
  271.1 25.4 %collective-permute-start.72 = (bf16[5,128,128]{2,1,0:T(8,128)(2,1)}, bf16[5,128,128]{2,1,0:T(8,128)(2,1)}, u32[]{:S(2)}, u32[]{:S(2)}) collective-permute-start(bf16[5,128,128]{2,1,0:T(8,128)(2,1)} %get-tuple-element.276), channel_id=1, source_target_pairs={{0,3},{1,2},{2,1},{3,0},{4,7},{5,6},{6,5},{7,4},{8,11},{9,10},{10,... | collective-permute-start | bytes 491528 | tf_op jit(solution)/shard_map/ppermute | solution.py:550
  272.6 26.3 %collective-permute-start.73 = (bf16[5,128,128]{2,1,0:T(8,128)(2,1)}, bf16[5,128,128]{2,1,0:T(8,128)(2,1)}, u32[]{:S(2)}, u32[]{:S(2)}) collective-permute-start(bf16[5,128,128]{2,1,0:T(8,128)(2,1)} %get-tuple-element.277), channel_id=1, source_target_pairs={{0,4},{1,5},{2,6},{3,7},{4,0},{5,1},{6,2},{7,3},{8,12},{9,13},{10,... | collective-permute-start | bytes 491528 | tf_op jit(solution)/shard_map/ppermute | solution.py:550
  274.0 25.2 %collective-permute-start.74 = (bf16[5,128,128]{2,1,0:T(8,128)(2,1)}, bf16[5,128,128]{2,1,0:T(8,128)(2,1)}, u32[]{:S(2)}, u32[]{:S(2)}) collective-permute-start(bf16[5,128,128]{2,1,0:T(8,128)(2,1)} %get-tuple-element.278), channel_id=1, source_target_pairs={{0,5},{1,4},{2,7},{3,6},{4,1},{5,0},{6,3},{7,2},{8,13},{9,12},{10,... | collective-permute-start | bytes 491528 | tf_op jit(solution)/shard_map/ppermute | solution.py:550
  274.3 25.5 %collective-permute-start.75 = (bf16[5,128,128]{2,1,0:T(8,128)(2,1)}, bf16[5,128,128]{2,1,0:T(8,128)(2,1)}, u32[]{:S(2)}, u32[]{:S(2)}) collective-permute-start(bf16[5,128,128]{2,1,0:T(8,128)(2,1)} %get-tuple-element.279), channel_id=1, source_target_pairs={{0,6},{1,7},{2,4},{3,5},{4,2},{5,3},{6,0},{7,1},{8,14},{9,15},{10,... | collective-permute-start | bytes 491528 | tf_op jit(solution)/shard_map/ppermute | solution.py:550
  288.6 26.2 %all-to-all-start.2 = ((f32[32,8,128]{2,1,0:T(8,128)}), f32[32,8,128]{2,1,0:T(8,128)S(1)}, u32[]{:S(2)}, u32[]{:S(2)}) async-start(f32[32,8,128]{2,1,0:T(8,128)} %bitcast.7), calls=%async_computation.2 | async-start | bytes 262144 | tf_op jit(solution)/shard_map/all_to_all | solution.py:39
  296.5 12.6 %collective-permute-start.76 = (bf16[5,128,128]{2,1,0:T(8,128)(2,1)}, bf16[5,128,128]{2,1,0:T(8,128)(2,1)S(1)}, u32[]{:S(2)}, u32[]{:S(2)}) collective-permute-start(bf16[5,128,128]{2,1,0:T(8,128)(2,1)} %copy-done.34), channel_id=1, source_target_pairs={{0,7},{1,6},{2,5},{3,4},{4,3},{5,2},{6,1},{7,0},{8,15},{9,14},{10,... | collective-permute-start | bytes 491528 | tf_op jit(solution)/shard_map/ppermute | solution.py:550
  299.8 13.1 %collective-permute-start.80 = (bf16[5,128,128]{2,1,0:T(8,128)(2,1)S(1)}, bf16[5,128,128]{2,1,0:T(8,128)(2,1)S(1)}, u32[]{:S(2)}, u32[]{:S(2)}) collective-permute-start(bf16[5,128,128]{2,1,0:T(8,128)(2,1)S(1)} %get-tuple-element.284), channel_id=1, source_target_pairs={{0,3},{1,2},{2,1},{3,0},{4,7},{5,6},{6,5},{7,4},{8,11},{9,10},{10,... | collective-permute-start | bytes 491528 | tf_op jit(solution)/shard_map/ppermute | solution.py:550
  300.7 12.8 %collective-permute-start.81 = (bf16[5,128,128]{2,1,0:T(8,128)(2,1)S(1)}, bf16[5,128,128]{2,1,0:T(8,128)(2,1)S(1)}, u32[]{:S(2)}, u32[]{:S(2)}) collective-permute-start(bf16[5,128,128]{2,1,0:T(8,128)(2,1)S(1)} %get-tuple-element.285), channel_id=1, source_target_pairs={{0,4},{1,5},{2,6},{3,7},{4,0},{5,1},{6,2},{7,3},{8,12},{9,13},{10,... | collective-permute-start | bytes 491528 | tf_op jit(solution)/shard_map/ppermute | solution.py:550
  310.8 12.4 %collective-permute-start.84 = (bf16[5,128,128]{2,1,0:T(8,128)(2,1)}, bf16[5,128,128]{2,1,0:T(8,128)(2,1)}, u32[]{:S(2)}, u32[]{:S(2)}) collective-permute-start(bf16[5,128,128]{2,1,0:T(8,128)(2,1)} %get-tuple-element.288), channel_id=1, source_target_pairs={{0,7},{1,6},{2,5},{3,4},{4,3},{5,2},{6,1},{7,0},{8,15},{9,14},{10,... | collective-permute-start | bytes 491528 | tf_op jit(solution)/shard_map/ppermute | solution.py:550
  314.2 13.5 %collective-permute-start.87 = (bf16[5,128,128]{2,1,0:T(8,128)(2,1)}, bf16[5,128,128]{2,1,0:T(8,128)(2,1)}, u32[]{:S(2)}, u32[]{:S(2)}) collective-permute-start(bf16[5,128,128]{2,1,0:T(8,128)(2,1)} %get-tuple-element.291), channel_id=1, source_target_pairs={{0,2},{1,3},{2,0},{3,1},{4,6},{5,7},{6,4},{7,5},{8,10},{9,11},{10,... | collective-permute-start | bytes 491528 | tf_op jit(solution)/shard_map/ppermute | solution.py:550
  315.5 13.1 %all-to-all-start.3 = ((f32[32,8,128]{2,1,0:T(8,128)}), f32[32,8,128]{2,1,0:T(8,128)S(1)}, u32[]{:S(2)}, u32[]{:S(2)}) async-start(f32[32,8,128]{2,1,0:T(8,128)} %broadcast_in_dim.7), calls=%async_computation.3 | async-start | bytes 262144 | tf_op jit(solution)/shard_map/all_to_all | solution.py:39
  320.2 42.8 %collective-permute-start.88 = (bf16[5,128,128]{2,1,0:T(8,128)(2,1)}, bf16[5,128,128]{2,1,0:T(8,128)(2,1)}, u32[]{:S(2)}, u32[]{:S(2)}) collective-permute-start(bf16[5,128,128]{2,1,0:T(8,128)(2,1)} %copy-done.39), channel_id=1, source_target_pairs={{0,3},{1,2},{2,1},{3,0},{4,7},{5,6},{6,5},{7,4},{8,11},{9,10},{10,... | collective-permute-start | bytes 491528 | tf_op jit(solution)/shard_map/ppermute | solution.py:550
  321.7 41.3 %collective-permute-start.89 = (bf16[5,128,128]{2,1,0:T(8,128)(2,1)}, bf16[5,128,128]{2,1,0:T(8,128)(2,1)}, u32[]{:S(2)}, u32[]{:S(2)}) collective-permute-start(bf16[5,128,128]{2,1,0:T(8,128)(2,1)} %copy-done.38), channel_id=1, source_target_pairs={{0,4},{1,5},{2,6},{3,7},{4,0},{5,1},{6,2},{7,3},{8,12},{9,13},{10,... | collective-permute-start | bytes 491528 | tf_op jit(solution)/shard_map/ppermute | solution.py:550
  323.2 39.8 %collective-permute-start.90 = (bf16[5,128,128]{2,1,0:T(8,128)(2,1)}, bf16[5,128,128]{2,1,0:T(8,128)(2,1)}, u32[]{:S(2)}, u32[]{:S(2)}) collective-permute-start(bf16[5,128,128]{2,1,0:T(8,128)(2,1)} %copy-done.37), channel_id=1, source_target_pairs={{0,5},{1,4},{2,7},{3,6},{4,1},{5,0},{6,3},{7,2},{8,13},{9,12},{10,... | collective-permute-start | bytes 491528 | tf_op jit(solution)/shard_map/ppermute | solution.py:550
  323.9 39.1 %collective-permute-start.91 = (bf16[5,128,128]{2,1,0:T(8,128)(2,1)}, bf16[5,128,128]{2,1,0:T(8,128)(2,1)}, u32[]{:S(2)}, u32[]{:S(2)}) collective-permute-start(bf16[5,128,128]{2,1,0:T(8,128)(2,1)} %copy-done.36), channel_id=1, source_target_pairs={{0,6},{1,7},{2,4},{3,5},{4,2},{5,3},{6,0},{7,1},{8,14},{9,15},{10,... | collective-permute-start | bytes 491528 | tf_op jit(solution)/shard_map/ppermute | solution.py:550
  327.7 35.3 %collective-permute-start.92 = (bf16[5,128,128]{2,1,0:T(8,128)(2,1)}, bf16[5,128,128]{2,1,0:T(8,128)(2,1)}, u32[]{:S(2)}, u32[]{:S(2)}) collective-permute-start(bf16[5,128,128]{2,1,0:T(8,128)(2,1)} %copy-done.35), channel_id=1, source_target_pairs={{0,7},{1,6},{2,5},{3,4},{4,3},{5,2},{6,1},{7,0},{8,15},{9,14},{10,... | collective-permute-start | bytes 491528 | tf_op jit(solution)/shard_map/ppermute | solution.py:550
  385.3 12.7 %collective-permute-start.112 = (bf16[5,128,128]{2,1,0:T(8,128)(2,1)}, bf16[5,128,128]{2,1,0:T(8,128)(2,1)S(1)}, u32[]{:S(2)}, u32[]{:S(2)}) collective-permute-start(bf16[5,128,128]{2,1,0:T(8,128)(2,1)} %get-tuple-element.337), channel_id=1, source_target_pairs={{0,6},{1,7},{2,4},{3,5},{4,2},{5,3},{6,0},{7,1},{8,14},{9,15},{10,... | collective-permute-start | bytes 491528 | tf_op jit(solution)/shard_map/ppermute | solution.py:550
  390.9 16.1 %collective-permute-start.93 = (bf16[5,128,128]{2,1,0:T(8,128)(2,1)}, bf16[5,128,128]{2,1,0:T(8,128)(2,1)S(1)}, u32[]{:S(2)}, u32[]{:S(2)}) collective-permute-start(bf16[5,128,128]{2,1,0:T(8,128)(2,1)} %get-tuple-element.308), channel_id=1, source_target_pairs={{0,1},{1,0},{2,3},{3,2},{4,5},{5,4},{6,7},{7,6},{8,9},{9,8},{10,11... | collective-permute-start | bytes 491528 | tf_op jit(solution)/shard_map/ppermute | solution.py:550
  391.9 16.5 %collective-permute-start.94 = (bf16[5,128,128]{2,1,0:T(8,128)(2,1)}, bf16[5,128,128]{2,1,0:T(8,128)(2,1)S(1)}, u32[]{:S(2)}, u32[]{:S(2)}) collective-permute-start(bf16[5,128,128]{2,1,0:T(8,128)(2,1)} %get-tuple-element.309), channel_id=1, source_target_pairs={{0,2},{1,3},{2,0},{3,1},{4,6},{5,7},{6,4},{7,5},{8,10},{9,11},{10,... | collective-permute-start | bytes 491528 | tf_op jit(solution)/shard_map/ppermute | solution.py:550
  404.1 36.0 %collective-permute-start.121 = (bf16[20,128,128]{2,1,0:T(8,128)(2,1)S(1)}, bf16[20,128,128]{2,1,0:T(8,128)(2,1)S(1)}, u32[]{:S(2)}, u32[]{:S(2)}) collective-permute-start(bf16[20,128,128]{2,1,0:T(8,128)(2,1)S(1)} %fold.10), channel_id=1, source_target_pairs={{0,8},{1,9},{2,10},{3,11},{4,12},{5,13},{6,14},{7,15},{16,0},{17,1... | collective-permute-start | bytes 1966088 | tf_op jit(solution)/shard_map/ppermute | solution.py:596
  408.3 12.4 %collective-permute-start.98 = (bf16[5,128,128]{2,1,0:T(8,128)(2,1)S(1)}, bf16[5,128,128]{2,1,0:T(8,128)(2,1)S(1)}, u32[]{:S(2)}, u32[]{:S(2)}) collective-permute-start(bf16[5,128,128]{2,1,0:T(8,128)(2,1)S(1)} %copy-done.109), channel_id=1, source_target_pairs={{0,6},{1,7},{2,4},{3,5},{4,2},{5,3},{6,0},{7,1},{8,14},{9,15},{10,... | collective-permute-start | bytes 491528 | tf_op jit(solution)/shard_map/ppermute | solution.py:550
  424.3 12.4 %collective-permute-start.118 = (bf16[5,128,128]{2,1,0:T(8,128)(2,1)S(1)}, bf16[5,128,128]{2,1,0:T(8,128)(2,1)S(1)}, u32[]{:S(2)}, u32[]{:S(2)}) collective-permute-start(bf16[5,128,128]{2,1,0:T(8,128)(2,1)S(1)} %copy-done.97), channel_id=1, source_target_pairs={{0,5},{1,4},{2,7},{3,6},{4,1},{5,0},{6,3},{7,2},{8,13},{9,12},{10,... | collective-permute-start | bytes 491528 | tf_op jit(solution)/shard_map/ppermute | solution.py:550
  436.8 28.3 %collective-permute-start.123 = (bf16[20,128,128]{2,1,0:T(8,128)(2,1)S(1)}, bf16[20,128,128]{2,1,0:T(8,128)(2,1)S(1)}, u32[]{:S(2)}, u32[]{:S(2)}) collective-permute-start(bf16[20,128,128]{2,1,0:T(8,128)(2,1)S(1)} %fold.9), channel_id=1, source_target_pairs={{0,16},{1,17},{2,18},{3,19},{4,20},{5,21},{6,22},{7,23},{16,24},{1... | collective-permute-start | bytes 1966088 | tf_op jit(solution)/shard_map/ppermute | solution.py:596
  442.1 28.3 %collective-permute-start.122 = (bf16[20,128,128]{2,1,0:T(8,128)(2,1)S(1)}, bf16[20,128,128]{2,1,0:T(8,128)(2,1)S(1)}, u32[]{:S(2)}, u32[]{:S(2)}) collective-permute-start(bf16[20,128,128]{2,1,0:T(8,128)(2,1)S(1)} %fold.11), channel_id=1, source_target_pairs={{0,8},{1,9},{2,10},{3,11},{4,12},{5,13},{6,14},{7,15},{16,0},{17,1... | collective-permute-start | bytes 1966088 | tf_op jit(solution)/shard_map/ppermute | solution.py:596
  (195 other events, 2542.7 us)

commit v5 on v4

--- a/solution.py
+++ b/solution.py
@@ -20,7 +20,7 @@
 
 def in_vmem(*arrays):
     placed = [pltpu.with_memory_space_constraint(array, pltpu.VMEM) for array in arrays]
-    return placed if len(placed) > 1 else placed[0]
+    return placed
 
 
 def inner_gram(left, right):
@@ -214,7 +214,8 @@
     shape = (plan.cap,) + chunk.shape[1:]
     return pl.pallas_call(
         functools.partial(pick_kernel, plan, step),
-        out_shape=[pltpu.VMEM(shape, chunk.dtype)] * plan.plane,
+        out_shape=[jax.ShapeDtypeStruct(shape, chunk.dtype)]
+        + [pltpu.VMEM(shape, chunk.dtype)] * (plan.plane - 1),
         in_specs=[
             pl.BlockSpec(memory_space=SMEM),
             pl.BlockSpec(memory_space=SMEM),
@@ -223,7 +224,7 @@
         out_specs=[pl.BlockSpec(memory_space=VMEM)] * plan.plane,
         compiler_params=SMALL,
         name="pick",
-    )(me, held, in_vmem(chunk))
+    )(me, held, *in_vmem(chunk))
 
 
 def narrow_dot(left, right, contract=1):
@@ -401,7 +402,7 @@
 
 def fold(plan, step, me, held, got, parts):
     shape = (plan.blocks,) + got[0].shape[1:]
-    args = (me, held, *in_vmem(*got, *parts))
+    args = (me, held, got[0], *in_vmem(*got[1:], *parts))
     return pl.pallas_call(
         functools.partial(fold_kernel, plan, step),
         out_shape=pltpu.VMEM(shape, jnp.bfloat16),
@@ -415,7 +416,7 @@
 
 def fold_image(plan, me, held, got, parts, field, prior_cols, both):
     shape, cols = field.shape, field.shape[2]
-    args = (me, held, field, prior_cols, *in_vmem(*got, *parts))
+    args = (me, held, field, prior_cols, got[0], *in_vmem(*got[1:], *parts))
     return pl.pallas_call(
         functools.partial(image_kernel, plan, both),
         out_shape=[

time: 522 us -> 522 us (level)
  no operation moved by 1% of the time
where the time goes in v5:
time: 522 us; the launch traced here: 520 us
  waiting for transfers between devices  180 us (34%)
  starting transfers between devices  145 us (28%)
  Pallas kernels  142 us (27%)
  local copies, waits for them, and re-layouts  23.3 us (4%)
  blocking collectives  18.2 us (3%)
  matrix products  7.7 us (1%)
    ppermute x112, waiting for transfers between devices, trade_plane(): lax.ppermute(buffers[offset], AXES, plan.shift_plane(offset))  115 us
    ppermute x112, starting transfers between devices, trade_plane(): lax.ppermute(buffers[offset], AXES, plan.shift_plane(offset))  104 us
    pallas_call x2, Pallas kernels, small_solve(): pl.pallas_call(kernel, out_shape=[jax.ShapeDtypeStruct(shape, jnp.float32...  50.7 us
    ppermute x6, waiting for transfers between devices, apply_schur(): following = lax.ppermute(chunk, AXES, plan.ring)  48.8 us
    pallas_call x2, Pallas kernels, run_arcs(): pl.pallas_call(functools.partial(arcs_kernel, plan, bool(extra)), grid_sp...  32.5 us
    unnamed x231, local copies, waits for them, and re-layouts  22 us
    all_to_all x2, blocking collectives, trade(): return lax.all_to_all(buffer, AXES, split_axis=0, concat_axis=0, tiled=True)  18.2 us
    all_to_all x4, starting transfers between devices, trade(): return lax.all_to_all(buffer, AXES, split_axis=0, concat_axis=0, tiled=True)  16 us
  transfers between devices with their start and end apart: 128, of which 54 were waited for; matrix products, arithmetic and copies ran while one was open for 2% of the time, Pallas kernels for 14%

profile of v5, /device:TPU:0, one launch (start us, length us, event | category | flops | bytes accessed | tf_op | source)
XLA Modules:
  0.0 520.3 jit_solution(14050939662229211100)
XLA Ops:
  2.1 4.1 collective-permute-start.7
  6.2 14.0 %collective-permute-done.7.chunk_ref = bf16[20,128,128]{2,1,0:T(8,128)(2,1)S(1)} collective-permute-done((bf16[20,128,128]{2,1,0:T(8,128)(2,1)S(1)}, bf16[20,128,128]{2,1,0:T(8,128)(2,1)S(1)}, u32[]{:S(2)}, u32[]{:S(2)}) %collective-permute-start.7) | collective-permute-done | bytes 655392 | tf_op jit(solution)/shard_map/ppermute | solution.py:577
  20.2 3.4 collective-permute-start.15
  26.6 10.1 %collective-permute-done.15.chunk_ref = bf16[20,128,128]{2,1,0:T(8,128)(2,1)S(1)} collective-permute-done((bf16[20,128,128]{2,1,0:T(8,128)(2,1)S(1)}, bf16[20,128,128]{2,1,0:T(8,128)(2,1)S(1)}, u32[]{:S(2)}, u32[]{:S(2)}) %collective-permute-start.15) | collective-permute-done | bytes 655392 | tf_op jit(solution)/shard_map/ppermute | solution.py:577
  36.7 3.4 collective-permute-start.23
  46.2 3.3 collective-permute-start.5
  70.3 3.1 collective-permute-done.14.refs_15_
  86.8 3.6 collective-permute-done.21.refs_22_
  97.4 3.7 collective-permute-done.26.refs_27_
  101.1 3.9 collective-permute-done.29.refs_30_
  107.1 15.1 %arcs.2 = (bf16[5,128,128]{2,1,0:T(8,128)(2,1)}, bf16[5,128,128]{2,1,0:T(8,128)(2,1)}, bf16[5,128,128]{2,1,0:T(8,128)(2,1)}, bf16[5,128,128]{2,1,0:T(8,128)(2,1)...) custom-call(s32[32,128]{1,0:T(8,128)} %copy-done.31, ...), custom_call_target="tpu_custom_call" | custom-call | tf_op jit(solution)/shard_map/arcs/pallas_call | solution.py:315
  127.7 2.8 collective-permute-done.46.refs_2_
  134.9 4.1 collective-permute-done.50.refs_6_
  139.1 2.9 collective-permute-done.51.refs_7_
  149.0 2.7 collective-permute-done.33.refs_3_
  156.4 4.2 collective-permute-done.36.refs_6_
  176.0 3.0 collective-permute-start.61
  180.3 2.7 fold.8
  187.8 4.7 collective-permute-done.39.refs_2_
  198.9 4.2 collective-permute-done.43.refs_6_
  203.1 3.6 collective-permute-done.44.refs_7_
  206.6 2.7 collective-permute-done.60.refs_8_
  215.0 6.9 %image.2 = (f32[20,128,128]{2,1,0:T(8,128)S(1)}, f32[2,128,128]{2,1,0:T(8,128)}, bf16[20,128,128]{2,1,0:T(8,128)(2,1)S(1)}) custom-call(s32[1]{0:T(128)} %gate.17.me_ref.in_ref, s32[8,128]{1,0:T(8,128)S(1)} %get-tuple-element.176.held_ref, f32[20,128,128]{2,1,0:T(8,128)S(1)} %copy-done, f32[128,20]{1,0:T(8,128)S(1)} %bitcast.32, ...), custom_call_target="tpu_custom_call" | custom-call | tf_op jit(solution)/shard_map/image/pallas_call | solution.py:420
  222.4 16.2 %collective-permute-done.69.chunk_ref = bf16[20,128,128]{2,1,0:T(8,128)(2,1)S(1)} collective-permute-done((bf16[20,128,128]{2,1,0:T(8,128)(2,1)S(1)}, bf16[20,128,128]{2,1,0:T(8,128)(2,1)S(1)}, u32[]{:S(2)}, u32[]{:S(2)}) %collective-permute-start.69) | collective-permute-done | bytes 655392 | tf_op jit(solution)/shard_map/ppermute | solution.py:577
  245.9 8.6 %collective-permute-done.77.chunk_ref = bf16[20,128,128]{2,1,0:T(8,128)(2,1)S(1)} collective-permute-done((bf16[20,128,128]{2,1,0:T(8,128)(2,1)S(1)}, bf16[20,128,128]{2,1,0:T(8,128)(2,1)S(1)}, u32[]{:S(2)}, u32[]{:S(2)}) %collective-permute-start.77) | collective-permute-done | bytes 655392 | tf_op jit(solution)/shard_map/ppermute | solution.py:577
  263.5 2.9 fusion.4
  266.5 4.6 all-to-all-start
  275.8 2.8 all-to-all-done
  279.5 9.1 %all_to_all.30 = f32[32,4,128]{2,1,0:T(4,128)S(1)} all-to-all(f32[32,4,128]{2,1,0:T(4,128)S(1)} %broadcast_in_dim.6), channel_id=1, replica_groups=mesh['arc'=8,'vec'=4] {'arc','vec'}, dimensions={0} | all-to-all | bytes 131072 | tf_op jit(solution)/shard_map/all_to_all | solution.py:39
  288.6 4.0 all-to-all-start.2
  315.5 4.6 all-to-all-start.3
  328.6 33.7 %solve.2 = (f32[128,128]{1,0:T(8,128)S(1)}, f32[128,128]{1,0:T(8,128)S(1)}, f32[128,128]{1,0:T(8,128)S(1)}, f32[256,128]{1,0:T(8,128)S(1)}) custom-call(f32[2,128,128]{2,1,0:T(8,128)S(1)} %bitcast.34, f32[128,128]{1,0:T(8,128)S(1)} %bitcast.35), custom_call_target="tpu_custom_call" | custom-call | tf_op jit(solution)/shard_map/solve/pallas_call | solution.py:537
  363.0 17.4 %arcs.3 = (bf16[5,128,128]{2,1,0:T(8,128)(2,1)}, bf16[5,128,128]{2,1,0:T(8,128)(2,1)}, bf16[5,128,128]{2,1,0:T(8,128)(2,1)}, bf16[5,128,128]{2,1,0:T(8,128)(2,1)...) custom-call(s32[32,128]{1,0:T(8,128)} %copy-done.31, ...), custom_call_target="tpu_custom_call" | custom-call | tf_op jit(solution)/shard_map/arcs/pallas_call | solution.py:315
  386.2 2.9 collective-permute-done.108.refs_2_
  394.0 4.1 collective-permute-done.112.refs_6_
  398.1 3.0 collective-permute-done.113.refs_7_
  409.2 3.1 collective-permute-done.95.refs_3_
  417.1 3.7 collective-permute-done.98.refs_6_
  448.4 3.4 collective-permute-done.101.refs_2_
  458.4 3.8 collective-permute-done.105.refs_6_
  462.2 2.8 collective-permute-done.106.refs_7_
  465.0 5.4 %collective-permute-done.122.refs_8_ = bf16[20,128,128]{2,1,0:T(8,128)(2,1)S(1)} collective-permute-done((bf16[20,128,128]{2,1,0:T(8,128)(2,1)S(1)}, bf16[20,128,128]{2,1,0:T(8,128)(2,1)S(1)}, u32[]{:S(2)}, u32[]{:S(2)}) %collective-permute-start.122) | collective-permute-done | bytes 655392 | tf_op jit(solution)/shard_map/ppermute | solution.py:597
  470.5 4.5 image.3
  476.0 9.1 %all_to_all.31 = f32[32,4,128]{2,1,0:T(4,128)S(1)} all-to-all(f32[32,4,128]{2,1,0:T(4,128)S(1)} %bitcast.37), channel_id=1, replica_groups=mesh['arc'=8,'vec'=4] {'arc','vec'}, dimensions={0} | all-to-all | bytes 131072 | tf_op jit(solution)/shard_map/all_to_all | solution.py:39
  485.8 2.8 all-to-all-start.5
  491.0 5.1 all-to-all-done.5
  496.1 17.0 %solve.3.step_ref = f32[128,128]{1,0:T(8,128)S(1)} custom-call(f32[1,128,128]{2,1,0:T(8,128)S(1)} %bitcast.36, f32[128,128]{1,0:T(8,128)S(1)} %get-tuple-element.349.res_ref), custom_call_target="tpu_custom_call" | custom-call | tf_op jit(solution)/shard_map/solve/pallas_call | solution.py:537
  513.7 6.6 %update.1 = (f32[20,128,128]{2,1,0:T(8,128)}, f32[20,128,128]{2,1,0:T(8,128)}) custom-call(f32[20,128,128]{2,1,0:T(8,128)} %copy-done.1, f32[20,128,128]{2,1,0:T(8,128)} %copy-done.2, f32[20,128,128]{2,1,0:T(8,128)} %convolution_bitcast_fusion.sol_ref, f32[20,128,128]{2,1,0:T(8,128)} %copy-done.40, f32[128,128]{1,0:T(8,128)} %copy-done.5), custom_call_target="tpu_custom_call" | custom-call | tf_op jit(solution)/shard_map/update/pallas_call | solution.py:449
  (486 shorter events, 225.1 us)
Async XLA Ops:
  2.1 18.1 %collective-permute-start.7 = (bf16[20,128,128]{2,1,0:T(8,128)(2,1)S(1)}, bf16[20,128,128]{2,1,0:T(8,128)(2,1)S(1)}, u32[]{:S(2)}, u32[]{:S(2)}) collective-permute-start(bf16[20,128,128]{2,1,0:T(8,128)(2,1)S(1)} %convert_element_type.3.chunk_ref), channel_id=1, source_target_pairs={{0,16},{1,17},{2,18},{3,19},{4,20},{5,21},{6,22},{7,23},{16,24},{1... | collective-permute-start | bytes 1966088 | tf_op jit(solution)/shard_map/ppermute | solution.py:577
  20.2 16.5 %collective-permute-start.15 = (bf16[20,128,128]{2,1,0:T(8,128)(2,1)S(1)}, bf16[20,128,128]{2,1,0:T(8,128)(2,1)S(1)}, u32[]{:S(2)}, u32[]{:S(2)}) collective-permute-start(bf16[20,128,128]{2,1,0:T(8,128)(2,1)S(1)} %collective-permute-done.7.chunk_ref), channel_id=1, source_target_pairs={{0,16},{1,17},{2,18},{3,19},{4,20},{5,21},{6,22},{7,23},{16,24},{1... | collective-permute-start | bytes 1966088 | tf_op jit(solution)/shard_map/ppermute | solution.py:577
  26.6 16.5 %collective-permute-start = (bf16[5,128,128]{2,1,0:T(8,128)(2,1)S(1)}, bf16[5,128,128]{2,1,0:T(8,128)(2,1)S(1)}, u32[]{:S(2)}, u32[]{:S(2)}) collective-permute-start(bf16[5,128,128]{2,1,0:T(8,128)(2,1)S(1)} %get-tuple-element.179), channel_id=1, source_target_pairs={{0,1},{1,0},{2,3},{3,2},{4,5},{5,4},{6,7},{7,6},{8,9},{9,8},{10,11... | collective-permute-start | bytes 491528 | tf_op jit(solution)/shard_map/ppermute | solution.py:551
  36.7 37.5 %collective-permute-start.23 = (bf16[20,128,128]{2,1,0:T(8,128)(2,1)S(1)}, bf16[20,128,128]{2,1,0:T(8,128)(2,1)S(1)}, u32[]{:S(2)}, u32[]{:S(2)}) collective-permute-start(bf16[20,128,128]{2,1,0:T(8,128)(2,1)S(1)} %collective-permute-done.15.chunk_ref), channel_id=1, source_target_pairs={{0,16},{1,17},{2,18},{3,19},{4,20},{5,21},{6,22},{7,23},{16,24},{1... | collective-permute-start | bytes 1966088 | tf_op jit(solution)/shard_map/ppermute | solution.py:577
  51.5 12.9 %collective-permute-start.11 = (bf16[5,128,128]{2,1,0:T(8,128)(2,1)S(1)}, bf16[5,128,128]{2,1,0:T(8,128)(2,1)S(1)}, u32[]{:S(2)}, u32[]{:S(2)}) collective-permute-start(bf16[5,128,128]{2,1,0:T(8,128)(2,1)S(1)} %get-tuple-element.190), channel_id=1, source_target_pairs={{0,4},{1,5},{2,6},{3,7},{4,0},{5,1},{6,2},{7,3},{8,12},{9,13},{10,... | collective-permute-start | bytes 491528 | tf_op jit(solution)/shard_map/ppermute | solution.py:551
  83.9 13.0 %collective-permute-start.25 = (bf16[5,128,128]{2,1,0:T(8,128)(2,1)S(1)}, bf16[5,128,128]{2,1,0:T(8,128)(2,1)S(1)}, u32[]{:S(2)}, u32[]{:S(2)}) collective-permute-start(bf16[5,128,128]{2,1,0:T(8,128)(2,1)S(1)} %get-tuple-element.204), channel_id=1, source_target_pairs={{0,2},{1,3},{2,0},{3,1},{4,6},{5,7},{6,4},{7,5},{8,10},{9,11},{10,... | collective-permute-start | bytes 491528 | tf_op jit(solution)/shard_map/ppermute | solution.py:551
  85.1 16.0 %collective-permute-start.26 = (bf16[5,128,128]{2,1,0:T(8,128)(2,1)S(1)}, bf16[5,128,128]{2,1,0:T(8,128)(2,1)S(1)}, u32[]{:S(2)}, u32[]{:S(2)}) collective-permute-start(bf16[5,128,128]{2,1,0:T(8,128)(2,1)S(1)} %get-tuple-element.205), channel_id=1, source_target_pairs={{0,3},{1,2},{2,1},{3,0},{4,7},{5,6},{6,5},{7,4},{8,11},{9,10},{10,... | collective-permute-start | bytes 491528 | tf_op jit(solution)/shard_map/ppermute | solution.py:551
  126.7 12.4 %collective-permute-start.50 = (bf16[5,128,128]{2,1,0:T(8,128)(2,1)}, bf16[5,128,128]{2,1,0:T(8,128)(2,1)S(1)}, u32[]{:S(2)}, u32[]{:S(2)}) collective-permute-start(bf16[5,128,128]{2,1,0:T(8,128)(2,1)} %get-tuple-element.248), channel_id=1, source_target_pairs={{0,6},{1,7},{2,4},{3,5},{4,2},{5,3},{6,0},{7,1},{8,14},{9,15},{10,... | collective-permute-start | bytes 491528 | tf_op jit(solution)/shard_map/ppermute | solution.py:551
  132.2 14.8 %collective-permute-start.31 = (bf16[5,128,128]{2,1,0:T(8,128)(2,1)}, bf16[5,128,128]{2,1,0:T(8,128)(2,1)S(1)}, u32[]{:S(2)}, u32[]{:S(2)}) collective-permute-start(bf16[5,128,128]{2,1,0:T(8,128)(2,1)} %get-tuple-element.219), channel_id=1, source_target_pairs={{0,1},{1,0},{2,3},{3,2},{4,5},{5,4},{6,7},{7,6},{8,9},{9,8},{10,11... | collective-permute-start | bytes 491528 | tf_op jit(solution)/shard_map/ppermute | solution.py:551
  133.2 15.0 %collective-permute-start.32 = (bf16[5,128,128]{2,1,0:T(8,128)(2,1)}, bf16[5,128,128]{2,1,0:T(8,128)(2,1)S(1)}, u32[]{:S(2)}, u32[]{:S(2)}) collective-permute-start(bf16[5,128,128]{2,1,0:T(8,128)(2,1)} %get-tuple-element.220), channel_id=1, source_target_pairs={{0,2},{1,3},{2,0},{3,1},{4,6},{5,7},{6,4},{7,5},{8,10},{9,11},{10,... | collective-permute-start | bytes 491528 | tf_op jit(solution)/shard_map/ppermute | solution.py:551
  145.1 35.2 %collective-permute-start.59 = (bf16[20,128,128]{2,1,0:T(8,128)(2,1)S(1)}, bf16[20,128,128]{2,1,0:T(8,128)(2,1)S(1)}, u32[]{:S(2)}, u32[]{:S(2)}) collective-permute-start(bf16[20,128,128]{2,1,0:T(8,128)(2,1)S(1)} %fold.7), channel_id=1, source_target_pairs={{0,8},{1,9},{2,10},{3,11},{4,12},{5,13},{6,14},{7,15},{16,0},{17,1... | collective-permute-start | bytes 1966088 | tf_op jit(solution)/shard_map/ppermute | solution.py:597
  148.2 12.4 %collective-permute-start.36 = (bf16[5,128,128]{2,1,0:T(8,128)(2,1)S(1)}, bf16[5,128,128]{2,1,0:T(8,128)(2,1)S(1)}, u32[]{:S(2)}, u32[]{:S(2)}) collective-permute-start(bf16[5,128,128]{2,1,0:T(8,128)(2,1)S(1)} %copy-done.110), channel_id=1, source_target_pairs={{0,6},{1,7},{2,4},{3,5},{4,2},{5,3},{6,0},{7,1},{8,14},{9,15},{10,... | collective-permute-start | bytes 491528 | tf_op jit(solution)/shard_map/ppermute | solution.py:551
  163.0 13.0 %collective-permute-start.55 = (bf16[5,128,128]{2,1,0:T(8,128)(2,1)S(1)}, bf16[5,128,128]{2,1,0:T(8,128)(2,1)S(1)}, u32[]{:S(2)}, u32[]{:S(2)}) collective-permute-start(bf16[5,128,128]{2,1,0:T(8,128)(2,1)S(1)} %copy-done.99), channel_id=1, source_target_pairs={{0,4},{1,5},{2,6},{3,7},{4,0},{5,1},{6,2},{7,3},{8,12},{9,13},{10,... | collective-permute-start | bytes 491528 | tf_op jit(solution)/shard_map/ppermute | solution.py:551
  163.6 15.4 %collective-permute-start.56 = (bf16[5,128,128]{2,1,0:T(8,128)(2,1)S(1)}, bf16[5,128,128]{2,1,0:T(8,128)(2,1)S(1)}, u32[]{:S(2)}, u32[]{:S(2)}) collective-permute-start(bf16[5,128,128]{2,1,0:T(8,128)(2,1)S(1)} %copy-done.98), channel_id=1, source_target_pairs={{0,5},{1,4},{2,7},{3,6},{4,1},{5,0},{6,3},{7,2},{8,13},{9,12},{10,... | collective-permute-start | bytes 491528 | tf_op jit(solution)/shard_map/ppermute | solution.py:551
  176.0 30.6 %collective-permute-start.61 = (bf16[20,128,128]{2,1,0:T(8,128)(2,1)S(1)}, bf16[20,128,128]{2,1,0:T(8,128)(2,1)S(1)}, u32[]{:S(2)}, u32[]{:S(2)}) collective-permute-start(bf16[20,128,128]{2,1,0:T(8,128)(2,1)S(1)} %fold.6), channel_id=1, source_target_pairs={{0,16},{1,17},{2,18},{3,19},{4,20},{5,21},{6,22},{7,23},{16,24},{1... | collective-permute-start | bytes 1966088 | tf_op jit(solution)/shard_map/ppermute | solution.py:597
  183.1 26.3 %collective-permute-start.60 = (bf16[20,128,128]{2,1,0:T(8,128)(2,1)}, bf16[20,128,128]{2,1,0:T(8,128)(2,1)S(1)}, u32[]{:S(2)}, u32[]{:S(2)}) collective-permute-start(bf16[20,128,128]{2,1,0:T(8,128)(2,1)} %fold.8), channel_id=1, source_target_pairs={{0,8},{1,9},{2,10},{3,11},{4,12},{5,13},{6,14},{7,15},{16,0},{17,1... | collective-permute-start | bytes 1966088 | tf_op jit(solution)/shard_map/ppermute | solution.py:597
  221.8 16.8 %collective-permute-start.69 = (bf16[20,128,128]{2,1,0:T(8,128)(2,1)S(1)}, bf16[20,128,128]{2,1,0:T(8,128)(2,1)S(1)}, u32[]{:S(2)}, u32[]{:S(2)}) collective-permute-start(bf16[20,128,128]{2,1,0:T(8,128)(2,1)S(1)} %get-tuple-element.264.chunk_ref), channel_id=1, source_target_pairs={{0,16},{1,17},{2,18},{3,19},{4,20},{5,21},{6,22},{7,23},{16,24},{1... | collective-permute-start | bytes 1966088 | tf_op jit(solution)/shard_map/ppermute | solution.py:577
  238.6 15.9 %collective-permute-start.77 = (bf16[20,128,128]{2,1,0:T(8,128)(2,1)S(1)}, bf16[20,128,128]{2,1,0:T(8,128)(2,1)S(1)}, u32[]{:S(2)}, u32[]{:S(2)}) collective-permute-start(bf16[20,128,128]{2,1,0:T(8,128)(2,1)S(1)} %collective-permute-done.69.chunk_ref), channel_id=1, source_target_pairs={{0,16},{1,17},{2,18},{3,19},{4,20},{5,21},{6,22},{7,23},{16,24},{1... | collective-permute-start | bytes 1966088 | tf_op jit(solution)/shard_map/ppermute | solution.py:577
  242.4 17.3 %collective-permute-start.63 = (bf16[5,128,128]{2,1,0:T(8,128)(2,1)S(1)}, bf16[5,128,128]{2,1,0:T(8,128)(2,1)S(1)}, u32[]{:S(2)}, u32[]{:S(2)}) collective-permute-start(bf16[5,128,128]{2,1,0:T(8,128)(2,1)S(1)} %get-tuple-element.267), channel_id=1, source_target_pairs={{0,2},{1,3},{2,0},{3,1},{4,6},{5,7},{6,4},{7,5},{8,10},{9,11},{10,... | collective-permute-start | bytes 491528 | tf_op jit(solution)/shard_map/ppermute | solution.py:551
  243.1 18.1 %collective-permute-start.64 = (bf16[5,128,128]{2,1,0:T(8,128)(2,1)S(1)}, bf16[5,128,128]{2,1,0:T(8,128)(2,1)S(1)}, u32[]{:S(2)}, u32[]{:S(2)}) collective-permute-start(bf16[5,128,128]{2,1,0:T(8,128)(2,1)S(1)} %get-tuple-element.268), channel_id=1, source_target_pairs={{0,3},{1,2},{2,1},{3,0},{4,7},{5,6},{6,5},{7,4},{8,11},{9,10},{10,... | collective-permute-start | bytes 491528 | tf_op jit(solution)/shard_map/ppermute | solution.py:551
  244.3 16.9 %collective-permute-start.65 = (bf16[5,128,128]{2,1,0:T(8,128)(2,1)S(1)}, bf16[5,128,128]{2,1,0:T(8,128)(2,1)S(1)}, u32[]{:S(2)}, u32[]{:S(2)}) collective-permute-start(bf16[5,128,128]{2,1,0:T(8,128)(2,1)S(1)} %get-tuple-element.269), channel_id=1, source_target_pairs={{0,4},{1,5},{2,6},{3,7},{4,0},{5,1},{6,2},{7,3},{8,12},{9,13},{10,... | collective-permute-start | bytes 491528 | tf_op jit(solution)/shard_map/ppermute | solution.py:551
  245.7 17.2 %collective-permute-start.66 = (bf16[5,128,128]{2,1,0:T(8,128)(2,1)S(1)}, bf16[5,128,128]{2,1,0:T(8,128)(2,1)S(1)}, u32[]{:S(2)}, u32[]{:S(2)}) collective-permute-start(bf16[5,128,128]{2,1,0:T(8,128)(2,1)S(1)} %get-tuple-element.270), channel_id=1, source_target_pairs={{0,5},{1,4},{2,7},{3,6},{4,1},{5,0},{6,3},{7,2},{8,13},{9,12},{10,... | collective-permute-start | bytes 491528 | tf_op jit(solution)/shard_map/ppermute | solution.py:551
  254.5 46.3 %collective-permute-start.85 = (bf16[20,128,128]{2,1,0:T(8,128)(2,1)S(1)}, bf16[20,128,128]{2,1,0:T(8,128)(2,1)}, u32[]{:S(2)}, u32[]{:S(2)}) collective-permute-start(bf16[20,128,128]{2,1,0:T(8,128)(2,1)S(1)} %collective-permute-done.77.chunk_ref), channel_id=1, source_target_pairs={{0,16},{1,17},{2,18},{3,19},{4,20},{5,21},{6,22},{7,23},{16,24},{1... | collective-permute-start | bytes 1966088 | tf_op jit(solution)/shard_map/ppermute | solution.py:577
  261.2 12.8 %collective-permute-start.70 = (bf16[5,128,128]{2,1,0:T(8,128)(2,1)}, bf16[5,128,128]{2,1,0:T(8,128)(2,1)}, u32[]{:S(2)}, u32[]{:S(2)}) collective-permute-start(bf16[5,128,128]{2,1,0:T(8,128)(2,1)} %get-tuple-element.274), channel_id=1, source_target_pairs={{0,1},{1,0},{2,3},{3,2},{4,5},{5,4},{6,7},{7,6},{8,9},{9,8},{10,11... | collective-permute-start | bytes 491528 | tf_op jit(solution)/shard_map/ppermute | solution.py:551
  271.1 25.4 %collective-permute-start.72 = (bf16[5,128,128]{2,1,0:T(8,128)(2,1)}, bf16[5,128,128]{2,1,0:T(8,128)(2,1)}, u32[]{:S(2)}, u32[]{:S(2)}) collective-permute-start(bf16[5,128,128]{2,1,0:T(8,128)(2,1)} %get-tuple-element.276), channel_id=1, source_target_pairs={{0,3},{1,2},{2,1},{3,0},{4,7},{5,6},{6,5},{7,4},{8,11},{9,10},{10,... | collective-permute-start | bytes 491528 | tf_op jit(solution)/shard_map/ppermute | solution.py:551
  272.6 26.3 %collective-permute-start.73 = (bf16[5,128,128]{2,1,0:T(8,128)(2,1)}, bf16[5,128,128]{2,1,0:T(8,128)(2,1)}, u32[]{:S(2)}, u32[]{:S(2)}) collective-permute-start(bf16[5,128,128]{2,1,0:T(8,128)(2,1)} %get-tuple-element.277), channel_id=1, source_target_pairs={{0,4},{1,5},{2,6},{3,7},{4,0},{5,1},{6,2},{7,3},{8,12},{9,13},{10,... | collective-permute-start | bytes 491528 | tf_op jit(solution)/shard_map/ppermute | solution.py:551
  274.0 25.2 %collective-permute-start.74 = (bf16[5,128,128]{2,1,0:T(8,128)(2,1)}, bf16[5,128,128]{2,1,0:T(8,128)(2,1)}, u32[]{:S(2)}, u32[]{:S(2)}) collective-permute-start(bf16[5,128,128]{2,1,0:T(8,128)(2,1)} %get-tuple-element.278), channel_id=1, source_target_pairs={{0,5},{1,4},{2,7},{3,6},{4,1},{5,0},{6,3},{7,2},{8,13},{9,12},{10,... | collective-permute-start | bytes 491528 | tf_op jit(solution)/shard_map/ppermute | solution.py:551
  274.3 25.5 %collective-permute-start.75 = (bf16[5,128,128]{2,1,0:T(8,128)(2,1)}, bf16[5,128,128]{2,1,0:T(8,128)(2,1)}, u32[]{:S(2)}, u32[]{:S(2)}) collective-permute-start(bf16[5,128,128]{2,1,0:T(8,128)(2,1)} %get-tuple-element.279), channel_id=1, source_target_pairs={{0,6},{1,7},{2,4},{3,5},{4,2},{5,3},{6,0},{7,1},{8,14},{9,15},{10,... | collective-permute-start | bytes 491528 | tf_op jit(solution)/shard_map/ppermute | solution.py:551
  288.6 26.2 %all-to-all-start.2 = ((f32[32,8,128]{2,1,0:T(8,128)}), f32[32,8,128]{2,1,0:T(8,128)S(1)}, u32[]{:S(2)}, u32[]{:S(2)}) async-start(f32[32,8,128]{2,1,0:T(8,128)} %bitcast.7), calls=%async_computation.2 | async-start | bytes 262144 | tf_op jit(solution)/shard_map/all_to_all | solution.py:39
  296.5 12.6 %collective-permute-start.76 = (bf16[5,128,128]{2,1,0:T(8,128)(2,1)}, bf16[5,128,128]{2,1,0:T(8,128)(2,1)S(1)}, u32[]{:S(2)}, u32[]{:S(2)}) collective-permute-start(bf16[5,128,128]{2,1,0:T(8,128)(2,1)} %copy-done.34), channel_id=1, source_target_pairs={{0,7},{1,6},{2,5},{3,4},{4,3},{5,2},{6,1},{7,0},{8,15},{9,14},{10,... | collective-permute-start | bytes 491528 | tf_op jit(solution)/shard_map/ppermute | solution.py:551
  299.8 13.1 %collective-permute-start.80 = (bf16[5,128,128]{2,1,0:T(8,128)(2,1)S(1)}, bf16[5,128,128]{2,1,0:T(8,128)(2,1)S(1)}, u32[]{:S(2)}, u32[]{:S(2)}) collective-permute-start(bf16[5,128,128]{2,1,0:T(8,128)(2,1)S(1)} %get-tuple-element.284), channel_id=1, source_target_pairs={{0,3},{1,2},{2,1},{3,0},{4,7},{5,6},{6,5},{7,4},{8,11},{9,10},{10,... | collective-permute-start | bytes 491528 | tf_op jit(solution)/shard_map/ppermute | solution.py:551
  300.7 12.8 %collective-permute-start.81 = (bf16[5,128,128]{2,1,0:T(8,128)(2,1)S(1)}, bf16[5,128,128]{2,1,0:T(8,128)(2,1)S(1)}, u32[]{:S(2)}, u32[]{:S(2)}) collective-permute-start(bf16[5,128,128]{2,1,0:T(8,128)(2,1)S(1)} %get-tuple-element.285), channel_id=1, source_target_pairs={{0,4},{1,5},{2,6},{3,7},{4,0},{5,1},{6,2},{7,3},{8,12},{9,13},{10,... | collective-permute-start | bytes 491528 | tf_op jit(solution)/shard_map/ppermute | solution.py:551
  310.8 12.4 %collective-permute-start.84 = (bf16[5,128,128]{2,1,0:T(8,128)(2,1)}, bf16[5,128,128]{2,1,0:T(8,128)(2,1)}, u32[]{:S(2)}, u32[]{:S(2)}) collective-permute-start(bf16[5,128,128]{2,1,0:T(8,128)(2,1)} %get-tuple-element.288), channel_id=1, source_target_pairs={{0,7},{1,6},{2,5},{3,4},{4,3},{5,2},{6,1},{7,0},{8,15},{9,14},{10,... | collective-permute-start | bytes 491528 | tf_op jit(solution)/shard_map/ppermute | solution.py:551
  314.2 13.5 %collective-permute-start.87 = (bf16[5,128,128]{2,1,0:T(8,128)(2,1)}, bf16[5,128,128]{2,1,0:T(8,128)(2,1)}, u32[]{:S(2)}, u32[]{:S(2)}) collective-permute-start(bf16[5,128,128]{2,1,0:T(8,128)(2,1)} %get-tuple-element.291), channel_id=1, source_target_pairs={{0,2},{1,3},{2,0},{3,1},{4,6},{5,7},{6,4},{7,5},{8,10},{9,11},{10,... | collective-permute-start | bytes 491528 | tf_op jit(solution)/shard_map/ppermute | solution.py:551
  315.5 13.1 %all-to-all-start.3 = ((f32[32,8,128]{2,1,0:T(8,128)}), f32[32,8,128]{2,1,0:T(8,128)S(1)}, u32[]{:S(2)}, u32[]{:S(2)}) async-start(f32[32,8,128]{2,1,0:T(8,128)} %broadcast_in_dim.7), calls=%async_computation.3 | async-start | bytes 262144 | tf_op jit(solution)/shard_map/all_to_all | solution.py:39
  320.2 42.8 %collective-permute-start.88 = (bf16[5,128,128]{2,1,0:T(8,128)(2,1)}, bf16[5,128,128]{2,1,0:T(8,128)(2,1)}, u32[]{:S(2)}, u32[]{:S(2)}) collective-permute-start(bf16[5,128,128]{2,1,0:T(8,128)(2,1)} %copy-done.39), channel_id=1, source_target_pairs={{0,3},{1,2},{2,1},{3,0},{4,7},{5,6},{6,5},{7,4},{8,11},{9,10},{10,... | collective-permute-start | bytes 491528 | tf_op jit(solution)/shard_map/ppermute | solution.py:551
  321.7 41.3 %collective-permute-start.89 = (bf16[5,128,128]{2,1,0:T(8,128)(2,1)}, bf16[5,128,128]{2,1,0:T(8,128)(2,1)}, u32[]{:S(2)}, u32[]{:S(2)}) collective-permute-start(bf16[5,128,128]{2,1,0:T(8,128)(2,1)} %copy-done.38), channel_id=1, source_target_pairs={{0,4},{1,5},{2,6},{3,7},{4,0},{5,1},{6,2},{7,3},{8,12},{9,13},{10,... | collective-permute-start | bytes 491528 | tf_op jit(solution)/shard_map/ppermute | solution.py:551
  323.2 39.8 %collective-permute-start.90 = (bf16[5,128,128]{2,1,0:T(8,128)(2,1)}, bf16[5,128,128]{2,1,0:T(8,128)(2,1)}, u32[]{:S(2)}, u32[]{:S(2)}) collective-permute-start(bf16[5,128,128]{2,1,0:T(8,128)(2,1)} %copy-done.37), channel_id=1, source_target_pairs={{0,5},{1,4},{2,7},{3,6},{4,1},{5,0},{6,3},{7,2},{8,13},{9,12},{10,... | collective-permute-start | bytes 491528 | tf_op jit(solution)/shard_map/ppermute | solution.py:551
  323.9 39.1 %collective-permute-start.91 = (bf16[5,128,128]{2,1,0:T(8,128)(2,1)}, bf16[5,128,128]{2,1,0:T(8,128)(2,1)}, u32[]{:S(2)}, u32[]{:S(2)}) collective-permute-start(bf16[5,128,128]{2,1,0:T(8,128)(2,1)} %copy-done.36), channel_id=1, source_target_pairs={{0,6},{1,7},{2,4},{3,5},{4,2},{5,3},{6,0},{7,1},{8,14},{9,15},{10,... | collective-permute-start | bytes 491528 | tf_op jit(solution)/shard_map/ppermute | solution.py:551
  327.7 35.3 %collective-permute-start.92 = (bf16[5,128,128]{2,1,0:T(8,128)(2,1)}, bf16[5,128,128]{2,1,0:T(8,128)(2,1)}, u32[]{:S(2)}, u32[]{:S(2)}) collective-permute-start(bf16[5,128,128]{2,1,0:T(8,128)(2,1)} %copy-done.35), channel_id=1, source_target_pairs={{0,7},{1,6},{2,5},{3,4},{4,3},{5,2},{6,1},{7,0},{8,15},{9,14},{10,... | collective-permute-start | bytes 491528 | tf_op jit(solution)/shard_map/ppermute | solution.py:551
  385.3 12.7 %collective-permute-start.112 = (bf16[5,128,128]{2,1,0:T(8,128)(2,1)}, bf16[5,128,128]{2,1,0:T(8,128)(2,1)S(1)}, u32[]{:S(2)}, u32[]{:S(2)}) collective-permute-start(bf16[5,128,128]{2,1,0:T(8,128)(2,1)} %get-tuple-element.337), channel_id=1, source_target_pairs={{0,6},{1,7},{2,4},{3,5},{4,2},{5,3},{6,0},{7,1},{8,14},{9,15},{10,... | collective-permute-start | bytes 491528 | tf_op jit(solution)/shard_map/ppermute | solution.py:551
  390.9 16.1 %collective-permute-start.93 = (bf16[5,128,128]{2,1,0:T(8,128)(2,1)}, bf16[5,128,128]{2,1,0:T(8,128)(2,1)S(1)}, u32[]{:S(2)}, u32[]{:S(2)}) collective-permute-start(bf16[5,128,128]{2,1,0:T(8,128)(2,1)} %get-tuple-element.308), channel_id=1, source_target_pairs={{0,1},{1,0},{2,3},{3,2},{4,5},{5,4},{6,7},{7,6},{8,9},{9,8},{10,11... | collective-permute-start | bytes 491528 | tf_op jit(solution)/shard_map/ppermute | solution.py:551
  391.9 16.5 %collective-permute-start.94 = (bf16[5,128,128]{2,1,0:T(8,128)(2,1)}, bf16[5,128,128]{2,1,0:T(8,128)(2,1)S(1)}, u32[]{:S(2)}, u32[]{:S(2)}) collective-permute-start(bf16[5,128,128]{2,1,0:T(8,128)(2,1)} %get-tuple-element.309), channel_id=1, source_target_pairs={{0,2},{1,3},{2,0},{3,1},{4,6},{5,7},{6,4},{7,5},{8,10},{9,11},{10,... | collective-permute-start | bytes 491528 | tf_op jit(solution)/shard_map/ppermute | solution.py:551
  404.1 36.0 %collective-permute-start.121 = (bf16[20,128,128]{2,1,0:T(8,128)(2,1)S(1)}, bf16[20,128,128]{2,1,0:T(8,128)(2,1)S(1)}, u32[]{:S(2)}, u32[]{:S(2)}) collective-permute-start(bf16[20,128,128]{2,1,0:T(8,128)(2,1)S(1)} %fold.10), channel_id=1, source_target_pairs={{0,8},{1,9},{2,10},{3,11},{4,12},{5,13},{6,14},{7,15},{16,0},{17,1... | collective-permute-start | bytes 1966088 | tf_op jit(solution)/shard_map/ppermute | solution.py:597
  408.3 12.4 %collective-permute-start.98 = (bf16[5,128,128]{2,1,0:T(8,128)(2,1)S(1)}, bf16[5,128,128]{2,1,0:T(8,128)(2,1)S(1)}, u32[]{:S(2)}, u32[]{:S(2)}) collective-permute-start(bf16[5,128,128]{2,1,0:T(8,128)(2,1)S(1)} %copy-done.109), channel_id=1, source_target_pairs={{0,6},{1,7},{2,4},{3,5},{4,2},{5,3},{6,0},{7,1},{8,14},{9,15},{10,... | collective-permute-start | bytes 491528 | tf_op jit(solution)/shard_map/ppermute | solution.py:551
  424.3 12.4 %collective-permute-start.118 = (bf16[5,128,128]{2,1,0:T(8,128)(2,1)S(1)}, bf16[5,128,128]{2,1,0:T(8,128)(2,1)S(1)}, u32[]{:S(2)}, u32[]{:S(2)}) collective-permute-start(bf16[5,128,128]{2,1,0:T(8,128)(2,1)S(1)} %copy-done.97), channel_id=1, source_target_pairs={{0,5},{1,4},{2,7},{3,6},{4,1},{5,0},{6,3},{7,2},{8,13},{9,12},{10,... | collective-permute-start | bytes 491528 | tf_op jit(solution)/shard_map/ppermute | solution.py:551
  436.8 28.3 %collective-permute-start.123 = (bf16[20,128,128]{2,1,0:T(8,128)(2,1)S(1)}, bf16[20,128,128]{2,1,0:T(8,128)(2,1)S(1)}, u32[]{:S(2)}, u32[]{:S(2)}) collective-permute-start(bf16[20,128,128]{2,1,0:T(8,128)(2,1)S(1)} %fold.9), channel_id=1, source_target_pairs={{0,16},{1,17},{2,18},{3,19},{4,20},{5,21},{6,22},{7,23},{16,24},{1... | collective-permute-start | bytes 1966088 | tf_op jit(solution)/shard_map/ppermute | solution.py:597
  442.1 28.3 %collective-permute-start.122 = (bf16[20,128,128]{2,1,0:T(8,128)(2,1)S(1)}, bf16[20,128,128]{2,1,0:T(8,128)(2,1)S(1)}, u32[]{:S(2)}, u32[]{:S(2)}) collective-permute-start(bf16[20,128,128]{2,1,0:T(8,128)(2,1)S(1)} %fold.11), channel_id=1, source_target_pairs={{0,8},{1,9},{2,10},{3,11},{4,12},{5,13},{6,14},{7,15},{16,0},{17,1... | collective-permute-start | bytes 1966088 | tf_op jit(solution)/shard_map/ppermute | solution.py:597
  (195 other events, 2542.7 us)

commit v6 on v5

--- a/solution.py
+++ b/solution.py
@@ -205,7 +205,9 @@
     here = lax.rem(me_ref[0], plan.plane)
     for offset, out_ref in enumerate(out_refs):
         q = plan.target_traced(here, offset)
-        for r in range(plan.cap):
+
+        @pl.loop(0, plan.cap)
+        def _(r):
             block = jnp.maximum(held_ref[step, r * plan.plane + q] - 1, 0)
             out_ref[r] = chunk_ref[block]
 
@@ -346,7 +348,9 @@
     acc[...] = start
     for offset, got_ref in enumerate(got_refs):
         q = plan.source_traced(here, offset)
-        for r in range(plan.cap):
+
+        @pl.loop(0, plan.cap)
+        def _(r):
             held = held_ref[step, r * plan.plane + q]
 
             @pl.when(held > 0)

time: 522 us -> 524 us (level)
  transfers between devices with their start and end apart: 128 -> 128, of which waited for: 54 -> 53; matrix products, arithmetic and copies ran while one was open for 2% -> 2% of each run, Pallas kernels for 14% -> 15%
where the time goes in v6:
time: 524 us; the launch traced here: 523 us
  waiting for transfers between devices  178 us (34%)
  Pallas kernels  147 us (28%)
  starting transfers between devices  145 us (28%)
  local copies, waits for them, and re-layouts  23.3 us (4%)
  blocking collectives  18.2 us (3%)
  matrix products  7.7 us (1%)
    ppermute x112, waiting for transfers between devices, trade_plane(): lax.ppermute(buffers[offset], AXES, plan.shift_plane(offset))  114 us
    ppermute x112, starting transfers between devices, trade_plane(): lax.ppermute(buffers[offset], AXES, plan.shift_plane(offset))  104 us
    pallas_call x2, Pallas kernels, small_solve(): pl.pallas_call(kernel, out_shape=[jax.ShapeDtypeStruct(shape, jnp.float32...  50.5 us
    ppermute x6, waiting for transfers between devices, apply_schur(): following = lax.ppermute(chunk, AXES, plan.ring)  48.2 us
    pallas_call x2, Pallas kernels, run_arcs(): pl.pallas_call(functools.partial(arcs_kernel, plan, bool(extra)), grid_sp...  32.5 us
    unnamed x231, local copies, waits for them, and re-layouts  22 us
    all_to_all x2, blocking collectives, trade(): return lax.all_to_all(buffer, AXES, split_axis=0, concat_axis=0, tiled=True)  18.2 us
    pallas_call x8, Pallas kernels, pick(): pl.pallas_call(functools.partial(pick_kernel, plan, step), out_shape=[jax...  16.7 us
  transfers between devices with their start and end apart: 128, of which 53 were waited for; matrix products, arithmetic and copies ran while one was open for 2% of the time, Pallas kernels for 15%

profile of v6, /device:TPU:0, one launch (start us, length us, event | category | flops | bytes accessed | tf_op | source)
XLA Modules:
  0.0 523.2 jit_solution(10115964077553594618)
XLA Ops:
  2.1 4.1 collective-permute-start.7
  6.2 14.0 %collective-permute-done.7.chunk_ref = bf16[20,128,128]{2,1,0:T(8,128)(2,1)S(1)} collective-permute-done((bf16[20,128,128]{2,1,0:T(8,128)(2,1)S(1)}, bf16[20,128,128]{2,1,0:T(8,128)(2,1)S(1)}, u32[]{:S(2)}, u32[]{:S(2)}) %collective-permute-start.7) | collective-permute-done | bytes 655392 | tf_op jit(solution)/shard_map/ppermute | solution.py:581
  20.2 3.4 collective-permute-start.15
  26.9 9.8 %collective-permute-done.15.chunk_ref = bf16[20,128,128]{2,1,0:T(8,128)(2,1)S(1)} collective-permute-done((bf16[20,128,128]{2,1,0:T(8,128)(2,1)S(1)}, bf16[20,128,128]{2,1,0:T(8,128)(2,1)S(1)}, u32[]{:S(2)}, u32[]{:S(2)}) %collective-permute-start.15) | collective-permute-done | bytes 655392 | tf_op jit(solution)/shard_map/ppermute | solution.py:581
  36.7 3.4 collective-permute-start.23
  46.6 3.0 collective-permute-start.5
  70.2 3.1 collective-permute-done.14.refs_15_
  87.1 3.6 collective-permute-done.21.refs_22_
  97.7 3.1 collective-permute-done.26.refs_27_
  100.9 4.6 collective-permute-done.29.refs_30_
  107.4 15.1 %arcs.2 = (bf16[5,128,128]{2,1,0:T(8,128)(2,1)}, bf16[5,128,128]{2,1,0:T(8,128)(2,1)}, bf16[5,128,128]{2,1,0:T(8,128)(2,1)}, bf16[5,128,128]{2,1,0:T(8,128)(2,1)...) custom-call(s32[32,128]{1,0:T(8,128)} %copy-done.31, ...), custom_call_target="tpu_custom_call" | custom-call | tf_op jit(solution)/shard_map/arcs/pallas_call | solution.py:317
  127.9 2.9 collective-permute-done.46.refs_2_
  135.3 4.1 collective-permute-done.50.refs_6_
  139.4 2.9 collective-permute-done.51.refs_7_
  149.6 2.7 collective-permute-done.33.refs_3_
  157.1 4.2 collective-permute-done.36.refs_6_
  176.9 3.0 collective-permute-start.61
  181.0 3.0 fold.8
  188.6 4.8 collective-permute-done.39.refs_2_
  199.8 4.2 collective-permute-done.43.refs_6_
  204.0 3.6 collective-permute-done.44.refs_7_
  215.8 7.0 %image.2 = (f32[20,128,128]{2,1,0:T(8,128)S(1)}, f32[2,128,128]{2,1,0:T(8,128)}, bf16[20,128,128]{2,1,0:T(8,128)(2,1)S(1)}) custom-call(s32[1]{0:T(128)} %gate.17.me_ref.in_ref, s32[8,128]{1,0:T(8,128)S(1)} %get-tuple-element.176.held_ref, f32[20,128,128]{2,1,0:T(8,128)S(1)} %copy-done, f32[128,20]{1,0:T(8,128)S(1)} %bitcast.32, ...), custom_call_target="tpu_custom_call" | custom-call | tf_op jit(solution)/shard_map/image/pallas_call | solution.py:424
  223.4 16.2 %collective-permute-done.69.chunk_ref = bf16[20,128,128]{2,1,0:T(8,128)(2,1)S(1)} collective-permute-done((bf16[20,128,128]{2,1,0:T(8,128)(2,1)S(1)}, bf16[20,128,128]{2,1,0:T(8,128)(2,1)S(1)}, u32[]{:S(2)}, u32[]{:S(2)}) %collective-permute-start.69) | collective-permute-done | bytes 655392 | tf_op jit(solution)/shard_map/ppermute | solution.py:581
  247.2 8.3 %collective-permute-done.77.chunk_ref = bf16[20,128,128]{2,1,0:T(8,128)(2,1)S(1)} collective-permute-done((bf16[20,128,128]{2,1,0:T(8,128)(2,1)S(1)}, bf16[20,128,128]{2,1,0:T(8,128)(2,1)S(1)}, u32[]{:S(2)}, u32[]{:S(2)}) %collective-permute-start.77) | collective-permute-done | bytes 655392 | tf_op jit(solution)/shard_map/ppermute | solution.py:581
  258.4 2.7 pick.13
  264.9 2.9 fusion.4
  267.8 4.7 all-to-all-start
  277.2 2.8 all-to-all-done
  280.9 9.1 %all_to_all.30 = f32[32,4,128]{2,1,0:T(4,128)S(1)} all-to-all(f32[32,4,128]{2,1,0:T(4,128)S(1)} %broadcast_in_dim.6), channel_id=1, replica_groups=mesh['arc'=8,'vec'=4] {'arc','vec'}, dimensions={0} | all-to-all | bytes 131072 | tf_op jit(solution)/shard_map/all_to_all | solution.py:39
  290.0 4.0 all-to-all-start.2
  304.3 3.0 pick.15
  317.7 4.6 all-to-all-start.3
  330.9 33.5 %solve.2 = (f32[128,128]{1,0:T(8,128)S(1)}, f32[128,128]{1,0:T(8,128)S(1)}, f32[128,128]{1,0:T(8,128)S(1)}, f32[256,128]{1,0:T(8,128)S(1)}) custom-call(f32[2,128,128]{2,1,0:T(8,128)S(1)} %bitcast.34, f32[128,128]{1,0:T(8,128)S(1)} %bitcast.35), custom_call_target="tpu_custom_call" | custom-call | tf_op jit(solution)/shard_map/solve/pallas_call | solution.py:541
  365.1 17.4 %arcs.3 = (bf16[5,128,128]{2,1,0:T(8,128)(2,1)}, bf16[5,128,128]{2,1,0:T(8,128)(2,1)}, bf16[5,128,128]{2,1,0:T(8,128)(2,1)}, bf16[5,128,128]{2,1,0:T(8,128)(2,1)...) custom-call(s32[32,128]{1,0:T(8,128)} %copy-done.31, ...), custom_call_target="tpu_custom_call" | custom-call | tf_op jit(solution)/shard_map/arcs/pallas_call | solution.py:317
  388.2 2.9 collective-permute-done.108.refs_2_
  396.0 4.1 collective-permute-done.112.refs_6_
  400.1 3.0 collective-permute-done.113.refs_7_
  411.7 3.1 collective-permute-done.95.refs_3_
  419.6 3.7 collective-permute-done.98.refs_6_
  451.2 3.4 collective-permute-done.101.refs_2_
  461.2 3.8 collective-permute-done.105.refs_6_
  465.0 2.8 collective-permute-done.106.refs_7_
  467.9 5.4 %collective-permute-done.122.refs_8_ = bf16[20,128,128]{2,1,0:T(8,128)(2,1)S(1)} collective-permute-done((bf16[20,128,128]{2,1,0:T(8,128)(2,1)S(1)}, bf16[20,128,128]{2,1,0:T(8,128)(2,1)S(1)}, u32[]{:S(2)}, u32[]{:S(2)}) %collective-permute-start.122) | collective-permute-done | bytes 655392 | tf_op jit(solution)/shard_map/ppermute | solution.py:601
  473.3 4.8 image.3
  479.2 9.1 %all_to_all.31 = f32[32,4,128]{2,1,0:T(4,128)S(1)} all-to-all(f32[32,4,128]{2,1,0:T(4,128)S(1)} %bitcast.37), channel_id=1, replica_groups=mesh['arc'=8,'vec'=4] {'arc','vec'}, dimensions={0} | all-to-all | bytes 131072 | tf_op jit(solution)/shard_map/all_to_all | solution.py:39
  493.8 5.1 all-to-all-done.5
  498.9 17.0 %solve.3.step_ref = f32[128,128]{1,0:T(8,128)S(1)} custom-call(f32[1,128,128]{2,1,0:T(8,128)S(1)} %bitcast.36, f32[128,128]{1,0:T(8,128)S(1)} %get-tuple-element.349.res_ref), custom_call_target="tpu_custom_call" | custom-call | tf_op jit(solution)/shard_map/solve/pallas_call | solution.py:541
  516.5 6.6 %update.1 = (f32[20,128,128]{2,1,0:T(8,128)}, f32[20,128,128]{2,1,0:T(8,128)}) custom-call(f32[20,128,128]{2,1,0:T(8,128)} %copy-done.1, f32[20,128,128]{2,1,0:T(8,128)} %copy-done.2, f32[20,128,128]{2,1,0:T(8,128)} %convolution_bitcast_fusion.sol_ref, f32[20,128,128]{2,1,0:T(8,128)} %copy-done.40, f32[128,128]{1,0:T(8,128)} %copy-done.5), custom_call_target="tpu_custom_call" | custom-call | tf_op jit(solution)/shard_map/update/pallas_call | solution.py:453
  (486 shorter events, 227.8 us)
Async XLA Ops:
  2.1 18.1 %collective-permute-start.7 = (bf16[20,128,128]{2,1,0:T(8,128)(2,1)S(1)}, bf16[20,128,128]{2,1,0:T(8,128)(2,1)S(1)}, u32[]{:S(2)}, u32[]{:S(2)}) collective-permute-start(bf16[20,128,128]{2,1,0:T(8,128)(2,1)S(1)} %convert_element_type.3.chunk_ref), channel_id=1, source_target_pairs={{0,16},{1,17},{2,18},{3,19},{4,20},{5,21},{6,22},{7,23},{16,24},{1... | collective-permute-start | bytes 1966088 | tf_op jit(solution)/shard_map/ppermute | solution.py:581
  20.2 16.5 %collective-permute-start.15 = (bf16[20,128,128]{2,1,0:T(8,128)(2,1)S(1)}, bf16[20,128,128]{2,1,0:T(8,128)(2,1)S(1)}, u32[]{:S(2)}, u32[]{:S(2)}) collective-permute-start(bf16[20,128,128]{2,1,0:T(8,128)(2,1)S(1)} %collective-permute-done.7.chunk_ref), channel_id=1, source_target_pairs={{0,16},{1,17},{2,18},{3,19},{4,20},{5,21},{6,22},{7,23},{16,24},{1... | collective-permute-start | bytes 1966088 | tf_op jit(solution)/shard_map/ppermute | solution.py:581
  26.9 16.2 %collective-permute-start = (bf16[5,128,128]{2,1,0:T(8,128)(2,1)S(1)}, bf16[5,128,128]{2,1,0:T(8,128)(2,1)S(1)}, u32[]{:S(2)}, u32[]{:S(2)}) collective-permute-start(bf16[5,128,128]{2,1,0:T(8,128)(2,1)S(1)} %get-tuple-element.179), channel_id=1, source_target_pairs={{0,1},{1,0},{2,3},{3,2},{4,5},{5,4},{6,7},{7,6},{8,9},{9,8},{10,11... | collective-permute-start | bytes 491528 | tf_op jit(solution)/shard_map/ppermute | solution.py:555
  36.7 37.5 %collective-permute-start.23 = (bf16[20,128,128]{2,1,0:T(8,128)(2,1)S(1)}, bf16[20,128,128]{2,1,0:T(8,128)(2,1)S(1)}, u32[]{:S(2)}, u32[]{:S(2)}) collective-permute-start(bf16[20,128,128]{2,1,0:T(8,128)(2,1)S(1)} %collective-permute-done.15.chunk_ref), channel_id=1, source_target_pairs={{0,16},{1,17},{2,18},{3,19},{4,20},{5,21},{6,22},{7,23},{16,24},{1... | collective-permute-start | bytes 1966088 | tf_op jit(solution)/shard_map/ppermute | solution.py:581
  51.5 12.9 %collective-permute-start.11 = (bf16[5,128,128]{2,1,0:T(8,128)(2,1)S(1)}, bf16[5,128,128]{2,1,0:T(8,128)(2,1)S(1)}, u32[]{:S(2)}, u32[]{:S(2)}) collective-permute-start(bf16[5,128,128]{2,1,0:T(8,128)(2,1)S(1)} %get-tuple-element.190), channel_id=1, source_target_pairs={{0,4},{1,5},{2,6},{3,7},{4,0},{5,1},{6,2},{7,3},{8,12},{9,13},{10,... | collective-permute-start | bytes 491528 | tf_op jit(solution)/shard_map/ppermute | solution.py:555
  55.1 12.6 %collective-permute-start.12 = (bf16[5,128,128]{2,1,0:T(8,128)(2,1)S(1)}, bf16[5,128,128]{2,1,0:T(8,128)(2,1)S(1)}, u32[]{:S(2)}, u32[]{:S(2)}) collective-permute-start(bf16[5,128,128]{2,1,0:T(8,128)(2,1)S(1)} %get-tuple-element.191), channel_id=1, source_target_pairs={{0,5},{1,4},{2,7},{3,6},{4,1},{5,0},{6,3},{7,2},{8,13},{9,12},{10,... | collective-permute-start | bytes 491528 | tf_op jit(solution)/shard_map/ppermute | solution.py:555
  83.9 13.3 %collective-permute-start.25 = (bf16[5,128,128]{2,1,0:T(8,128)(2,1)S(1)}, bf16[5,128,128]{2,1,0:T(8,128)(2,1)S(1)}, u32[]{:S(2)}, u32[]{:S(2)}) collective-permute-start(bf16[5,128,128]{2,1,0:T(8,128)(2,1)S(1)} %get-tuple-element.204), channel_id=1, source_target_pairs={{0,2},{1,3},{2,0},{3,1},{4,6},{5,7},{6,4},{7,5},{8,10},{9,11},{10,... | collective-permute-start | bytes 491528 | tf_op jit(solution)/shard_map/ppermute | solution.py:555
  85.1 15.7 %collective-permute-start.26 = (bf16[5,128,128]{2,1,0:T(8,128)(2,1)S(1)}, bf16[5,128,128]{2,1,0:T(8,128)(2,1)S(1)}, u32[]{:S(2)}, u32[]{:S(2)}) collective-permute-start(bf16[5,128,128]{2,1,0:T(8,128)(2,1)S(1)} %get-tuple-element.205), channel_id=1, source_target_pairs={{0,3},{1,2},{2,1},{3,0},{4,7},{5,6},{6,5},{7,4},{8,11},{9,10},{10,... | collective-permute-start | bytes 491528 | tf_op jit(solution)/shard_map/ppermute | solution.py:555
  132.6 15.0 %collective-permute-start.31 = (bf16[5,128,128]{2,1,0:T(8,128)(2,1)}, bf16[5,128,128]{2,1,0:T(8,128)(2,1)S(1)}, u32[]{:S(2)}, u32[]{:S(2)}) collective-permute-start(bf16[5,128,128]{2,1,0:T(8,128)(2,1)} %get-tuple-element.219), channel_id=1, source_target_pairs={{0,1},{1,0},{2,3},{3,2},{4,5},{5,4},{6,7},{7,6},{8,9},{9,8},{10,11... | collective-permute-start | bytes 491528 | tf_op jit(solution)/shard_map/ppermute | solution.py:555
  133.6 15.3 %collective-permute-start.32 = (bf16[5,128,128]{2,1,0:T(8,128)(2,1)}, bf16[5,128,128]{2,1,0:T(8,128)(2,1)S(1)}, u32[]{:S(2)}, u32[]{:S(2)}) collective-permute-start(bf16[5,128,128]{2,1,0:T(8,128)(2,1)} %get-tuple-element.220), channel_id=1, source_target_pairs={{0,2},{1,3},{2,0},{3,1},{4,6},{5,7},{6,4},{7,5},{8,10},{9,11},{10,... | collective-permute-start | bytes 491528 | tf_op jit(solution)/shard_map/ppermute | solution.py:555
  145.8 35.2 %collective-permute-start.59 = (bf16[20,128,128]{2,1,0:T(8,128)(2,1)S(1)}, bf16[20,128,128]{2,1,0:T(8,128)(2,1)S(1)}, u32[]{:S(2)}, u32[]{:S(2)}) collective-permute-start(bf16[20,128,128]{2,1,0:T(8,128)(2,1)S(1)} %fold.7), channel_id=1, source_target_pairs={{0,8},{1,9},{2,10},{3,11},{4,12},{5,13},{6,14},{7,15},{16,0},{17,1... | collective-permute-start | bytes 1966088 | tf_op jit(solution)/shard_map/ppermute | solution.py:601
  148.9 12.4 %collective-permute-start.36 = (bf16[5,128,128]{2,1,0:T(8,128)(2,1)S(1)}, bf16[5,128,128]{2,1,0:T(8,128)(2,1)S(1)}, u32[]{:S(2)}, u32[]{:S(2)}) collective-permute-start(bf16[5,128,128]{2,1,0:T(8,128)(2,1)S(1)} %copy-done.110), channel_id=1, source_target_pairs={{0,6},{1,7},{2,4},{3,5},{4,2},{5,3},{6,0},{7,1},{8,14},{9,15},{10,... | collective-permute-start | bytes 491528 | tf_op jit(solution)/shard_map/ppermute | solution.py:555
  163.6 13.3 %collective-permute-start.55 = (bf16[5,128,128]{2,1,0:T(8,128)(2,1)S(1)}, bf16[5,128,128]{2,1,0:T(8,128)(2,1)S(1)}, u32[]{:S(2)}, u32[]{:S(2)}) collective-permute-start(bf16[5,128,128]{2,1,0:T(8,128)(2,1)S(1)} %copy-done.99), channel_id=1, source_target_pairs={{0,4},{1,5},{2,6},{3,7},{4,0},{5,1},{6,2},{7,3},{8,12},{9,13},{10,... | collective-permute-start | bytes 491528 | tf_op jit(solution)/shard_map/ppermute | solution.py:555
  164.4 15.5 %collective-permute-start.56 = (bf16[5,128,128]{2,1,0:T(8,128)(2,1)S(1)}, bf16[5,128,128]{2,1,0:T(8,128)(2,1)S(1)}, u32[]{:S(2)}, u32[]{:S(2)}) collective-permute-start(bf16[5,128,128]{2,1,0:T(8,128)(2,1)S(1)} %copy-done.98), channel_id=1, source_target_pairs={{0,5},{1,4},{2,7},{3,6},{4,1},{5,0},{6,3},{7,2},{8,13},{9,12},{10,... | collective-permute-start | bytes 491528 | tf_op jit(solution)/shard_map/ppermute | solution.py:555
  176.9 30.7 %collective-permute-start.61 = (bf16[20,128,128]{2,1,0:T(8,128)(2,1)S(1)}, bf16[20,128,128]{2,1,0:T(8,128)(2,1)S(1)}, u32[]{:S(2)}, u32[]{:S(2)}) collective-permute-start(bf16[20,128,128]{2,1,0:T(8,128)(2,1)S(1)} %fold.6), channel_id=1, source_target_pairs={{0,16},{1,17},{2,18},{3,19},{4,20},{5,21},{6,22},{7,23},{16,24},{1... | collective-permute-start | bytes 1966088 | tf_op jit(solution)/shard_map/ppermute | solution.py:601
  184.0 26.2 %collective-permute-start.60 = (bf16[20,128,128]{2,1,0:T(8,128)(2,1)}, bf16[20,128,128]{2,1,0:T(8,128)(2,1)S(1)}, u32[]{:S(2)}, u32[]{:S(2)}) collective-permute-start(bf16[20,128,128]{2,1,0:T(8,128)(2,1)} %fold.8), channel_id=1, source_target_pairs={{0,8},{1,9},{2,10},{3,11},{4,12},{5,13},{6,14},{7,15},{16,0},{17,1... | collective-permute-start | bytes 1966088 | tf_op jit(solution)/shard_map/ppermute | solution.py:601
  222.8 16.8 %collective-permute-start.69 = (bf16[20,128,128]{2,1,0:T(8,128)(2,1)S(1)}, bf16[20,128,128]{2,1,0:T(8,128)(2,1)S(1)}, u32[]{:S(2)}, u32[]{:S(2)}) collective-permute-start(bf16[20,128,128]{2,1,0:T(8,128)(2,1)S(1)} %get-tuple-element.264.chunk_ref), channel_id=1, source_target_pairs={{0,16},{1,17},{2,18},{3,19},{4,20},{5,21},{6,22},{7,23},{16,24},{1... | collective-permute-start | bytes 1966088 | tf_op jit(solution)/shard_map/ppermute | solution.py:581
  239.6 15.9 %collective-permute-start.77 = (bf16[20,128,128]{2,1,0:T(8,128)(2,1)S(1)}, bf16[20,128,128]{2,1,0:T(8,128)(2,1)S(1)}, u32[]{:S(2)}, u32[]{:S(2)}) collective-permute-start(bf16[20,128,128]{2,1,0:T(8,128)(2,1)S(1)} %collective-permute-done.69.chunk_ref), channel_id=1, source_target_pairs={{0,16},{1,17},{2,18},{3,19},{4,20},{5,21},{6,22},{7,23},{16,24},{1... | collective-permute-start | bytes 1966088 | tf_op jit(solution)/shard_map/ppermute | solution.py:581
  243.7 17.4 %collective-permute-start.63 = (bf16[5,128,128]{2,1,0:T(8,128)(2,1)S(1)}, bf16[5,128,128]{2,1,0:T(8,128)(2,1)S(1)}, u32[]{:S(2)}, u32[]{:S(2)}) collective-permute-start(bf16[5,128,128]{2,1,0:T(8,128)(2,1)S(1)} %get-tuple-element.267), channel_id=1, source_target_pairs={{0,2},{1,3},{2,0},{3,1},{4,6},{5,7},{6,4},{7,5},{8,10},{9,11},{10,... | collective-permute-start | bytes 491528 | tf_op jit(solution)/shard_map/ppermute | solution.py:555
  244.4 18.4 %collective-permute-start.64 = (bf16[5,128,128]{2,1,0:T(8,128)(2,1)S(1)}, bf16[5,128,128]{2,1,0:T(8,128)(2,1)S(1)}, u32[]{:S(2)}, u32[]{:S(2)}) collective-permute-start(bf16[5,128,128]{2,1,0:T(8,128)(2,1)S(1)} %get-tuple-element.268), channel_id=1, source_target_pairs={{0,3},{1,2},{2,1},{3,0},{4,7},{5,6},{6,5},{7,4},{8,11},{9,10},{10,... | collective-permute-start | bytes 491528 | tf_op jit(solution)/shard_map/ppermute | solution.py:555
  245.6 17.2 %collective-permute-start.65 = (bf16[5,128,128]{2,1,0:T(8,128)(2,1)S(1)}, bf16[5,128,128]{2,1,0:T(8,128)(2,1)S(1)}, u32[]{:S(2)}, u32[]{:S(2)}) collective-permute-start(bf16[5,128,128]{2,1,0:T(8,128)(2,1)S(1)} %get-tuple-element.269), channel_id=1, source_target_pairs={{0,4},{1,5},{2,6},{3,7},{4,0},{5,1},{6,2},{7,3},{8,12},{9,13},{10,... | collective-permute-start | bytes 491528 | tf_op jit(solution)/shard_map/ppermute | solution.py:555
  247.1 17.2 %collective-permute-start.66 = (bf16[5,128,128]{2,1,0:T(8,128)(2,1)S(1)}, bf16[5,128,128]{2,1,0:T(8,128)(2,1)S(1)}, u32[]{:S(2)}, u32[]{:S(2)}) collective-permute-start(bf16[5,128,128]{2,1,0:T(8,128)(2,1)S(1)} %get-tuple-element.270), channel_id=1, source_target_pairs={{0,5},{1,4},{2,7},{3,6},{4,1},{5,0},{6,3},{7,2},{8,13},{9,12},{10,... | collective-permute-start | bytes 491528 | tf_op jit(solution)/shard_map/ppermute | solution.py:555
  255.5 47.1 %collective-permute-start.85 = (bf16[20,128,128]{2,1,0:T(8,128)(2,1)S(1)}, bf16[20,128,128]{2,1,0:T(8,128)(2,1)}, u32[]{:S(2)}, u32[]{:S(2)}) collective-permute-start(bf16[20,128,128]{2,1,0:T(8,128)(2,1)S(1)} %collective-permute-done.77.chunk_ref), channel_id=1, source_target_pairs={{0,16},{1,17},{2,18},{3,19},{4,20},{5,21},{6,22},{7,23},{16,24},{1... | collective-permute-start | bytes 1966088 | tf_op jit(solution)/shard_map/ppermute | solution.py:581
  262.8 12.7 %collective-permute-start.70 = (bf16[5,128,128]{2,1,0:T(8,128)(2,1)}, bf16[5,128,128]{2,1,0:T(8,128)(2,1)}, u32[]{:S(2)}, u32[]{:S(2)}) collective-permute-start(bf16[5,128,128]{2,1,0:T(8,128)(2,1)} %get-tuple-element.274), channel_id=1, source_target_pairs={{0,1},{1,0},{2,3},{3,2},{4,5},{5,4},{6,7},{7,6},{8,9},{9,8},{10,11... | collective-permute-start | bytes 491528 | tf_op jit(solution)/shard_map/ppermute | solution.py:555
  272.5 25.8 %collective-permute-start.72 = (bf16[5,128,128]{2,1,0:T(8,128)(2,1)}, bf16[5,128,128]{2,1,0:T(8,128)(2,1)}, u32[]{:S(2)}, u32[]{:S(2)}) collective-permute-start(bf16[5,128,128]{2,1,0:T(8,128)(2,1)} %get-tuple-element.276), channel_id=1, source_target_pairs={{0,3},{1,2},{2,1},{3,0},{4,7},{5,6},{6,5},{7,4},{8,11},{9,10},{10,... | collective-permute-start | bytes 491528 | tf_op jit(solution)/shard_map/ppermute | solution.py:555
  274.0 26.7 %collective-permute-start.73 = (bf16[5,128,128]{2,1,0:T(8,128)(2,1)}, bf16[5,128,128]{2,1,0:T(8,128)(2,1)}, u32[]{:S(2)}, u32[]{:S(2)}) collective-permute-start(bf16[5,128,128]{2,1,0:T(8,128)(2,1)} %get-tuple-element.277), channel_id=1, source_target_pairs={{0,4},{1,5},{2,6},{3,7},{4,0},{5,1},{6,2},{7,3},{8,12},{9,13},{10,... | collective-permute-start | bytes 491528 | tf_op jit(solution)/shard_map/ppermute | solution.py:555
  275.5 25.7 %collective-permute-start.74 = (bf16[5,128,128]{2,1,0:T(8,128)(2,1)}, bf16[5,128,128]{2,1,0:T(8,128)(2,1)}, u32[]{:S(2)}, u32[]{:S(2)}) collective-permute-start(bf16[5,128,128]{2,1,0:T(8,128)(2,1)} %get-tuple-element.278), channel_id=1, source_target_pairs={{0,5},{1,4},{2,7},{3,6},{4,1},{5,0},{6,3},{7,2},{8,13},{9,12},{10,... | collective-permute-start | bytes 491528 | tf_op jit(solution)/shard_map/ppermute | solution.py:555
  275.8 25.9 %collective-permute-start.75 = (bf16[5,128,128]{2,1,0:T(8,128)(2,1)}, bf16[5,128,128]{2,1,0:T(8,128)(2,1)}, u32[]{:S(2)}, u32[]{:S(2)}) collective-permute-start(bf16[5,128,128]{2,1,0:T(8,128)(2,1)} %get-tuple-element.279), channel_id=1, source_target_pairs={{0,6},{1,7},{2,4},{3,5},{4,2},{5,3},{6,0},{7,1},{8,14},{9,15},{10,... | collective-permute-start | bytes 491528 | tf_op jit(solution)/shard_map/ppermute | solution.py:555
  290.0 27.0 %all-to-all-start.2 = ((f32[32,8,128]{2,1,0:T(8,128)}), f32[32,8,128]{2,1,0:T(8,128)S(1)}, u32[]{:S(2)}, u32[]{:S(2)}) async-start(f32[32,8,128]{2,1,0:T(8,128)} %bitcast.7), calls=%async_computation.2 | async-start | bytes 262144 | tf_op jit(solution)/shard_map/all_to_all | solution.py:39
  298.3 12.9 %collective-permute-start.76 = (bf16[5,128,128]{2,1,0:T(8,128)(2,1)}, bf16[5,128,128]{2,1,0:T(8,128)(2,1)S(1)}, u32[]{:S(2)}, u32[]{:S(2)}) collective-permute-start(bf16[5,128,128]{2,1,0:T(8,128)(2,1)} %copy-done.34), channel_id=1, source_target_pairs={{0,7},{1,6},{2,5},{3,4},{4,3},{5,2},{6,1},{7,0},{8,15},{9,14},{10,... | collective-permute-start | bytes 491528 | tf_op jit(solution)/shard_map/ppermute | solution.py:555
  301.7 13.4 %collective-permute-start.80 = (bf16[5,128,128]{2,1,0:T(8,128)(2,1)S(1)}, bf16[5,128,128]{2,1,0:T(8,128)(2,1)S(1)}, u32[]{:S(2)}, u32[]{:S(2)}) collective-permute-start(bf16[5,128,128]{2,1,0:T(8,128)(2,1)S(1)} %get-tuple-element.284), channel_id=1, source_target_pairs={{0,3},{1,2},{2,1},{3,0},{4,7},{5,6},{6,5},{7,4},{8,11},{9,10},{10,... | collective-permute-start | bytes 491528 | tf_op jit(solution)/shard_map/ppermute | solution.py:555
  302.6 13.2 %collective-permute-start.81 = (bf16[5,128,128]{2,1,0:T(8,128)(2,1)S(1)}, bf16[5,128,128]{2,1,0:T(8,128)(2,1)S(1)}, u32[]{:S(2)}, u32[]{:S(2)}) collective-permute-start(bf16[5,128,128]{2,1,0:T(8,128)(2,1)S(1)} %get-tuple-element.285), channel_id=1, source_target_pairs={{0,4},{1,5},{2,6},{3,7},{4,0},{5,1},{6,2},{7,3},{8,12},{9,13},{10,... | collective-permute-start | bytes 491528 | tf_op jit(solution)/shard_map/ppermute | solution.py:555
  313.0 12.4 %collective-permute-start.84 = (bf16[5,128,128]{2,1,0:T(8,128)(2,1)}, bf16[5,128,128]{2,1,0:T(8,128)(2,1)}, u32[]{:S(2)}, u32[]{:S(2)}) collective-permute-start(bf16[5,128,128]{2,1,0:T(8,128)(2,1)} %get-tuple-element.288), channel_id=1, source_target_pairs={{0,7},{1,6},{2,5},{3,4},{4,3},{5,2},{6,1},{7,0},{8,15},{9,14},{10,... | collective-permute-start | bytes 491528 | tf_op jit(solution)/shard_map/ppermute | solution.py:555
  316.5 13.5 %collective-permute-start.87 = (bf16[5,128,128]{2,1,0:T(8,128)(2,1)}, bf16[5,128,128]{2,1,0:T(8,128)(2,1)}, u32[]{:S(2)}, u32[]{:S(2)}) collective-permute-start(bf16[5,128,128]{2,1,0:T(8,128)(2,1)} %get-tuple-element.291), channel_id=1, source_target_pairs={{0,2},{1,3},{2,0},{3,1},{4,6},{5,7},{6,4},{7,5},{8,10},{9,11},{10,... | collective-permute-start | bytes 491528 | tf_op jit(solution)/shard_map/ppermute | solution.py:555
  317.7 13.1 %all-to-all-start.3 = ((f32[32,8,128]{2,1,0:T(8,128)}), f32[32,8,128]{2,1,0:T(8,128)S(1)}, u32[]{:S(2)}, u32[]{:S(2)}) async-start(f32[32,8,128]{2,1,0:T(8,128)} %broadcast_in_dim.7), calls=%async_computation.3 | async-start | bytes 262144 | tf_op jit(solution)/shard_map/all_to_all | solution.py:39
  322.4 42.6 %collective-permute-start.88 = (bf16[5,128,128]{2,1,0:T(8,128)(2,1)}, bf16[5,128,128]{2,1,0:T(8,128)(2,1)}, u32[]{:S(2)}, u32[]{:S(2)}) collective-permute-start(bf16[5,128,128]{2,1,0:T(8,128)(2,1)} %copy-done.39), channel_id=1, source_target_pairs={{0,3},{1,2},{2,1},{3,0},{4,7},{5,6},{6,5},{7,4},{8,11},{9,10},{10,... | collective-permute-start | bytes 491528 | tf_op jit(solution)/shard_map/ppermute | solution.py:555
  323.9 41.1 %collective-permute-start.89 = (bf16[5,128,128]{2,1,0:T(8,128)(2,1)}, bf16[5,128,128]{2,1,0:T(8,128)(2,1)}, u32[]{:S(2)}, u32[]{:S(2)}) collective-permute-start(bf16[5,128,128]{2,1,0:T(8,128)(2,1)} %copy-done.38), channel_id=1, source_target_pairs={{0,4},{1,5},{2,6},{3,7},{4,0},{5,1},{6,2},{7,3},{8,12},{9,13},{10,... | collective-permute-start | bytes 491528 | tf_op jit(solution)/shard_map/ppermute | solution.py:555
  325.4 39.6 %collective-permute-start.90 = (bf16[5,128,128]{2,1,0:T(8,128)(2,1)}, bf16[5,128,128]{2,1,0:T(8,128)(2,1)}, u32[]{:S(2)}, u32[]{:S(2)}) collective-permute-start(bf16[5,128,128]{2,1,0:T(8,128)(2,1)} %copy-done.37), channel_id=1, source_target_pairs={{0,5},{1,4},{2,7},{3,6},{4,1},{5,0},{6,3},{7,2},{8,13},{9,12},{10,... | collective-permute-start | bytes 491528 | tf_op jit(solution)/shard_map/ppermute | solution.py:555
  326.2 38.9 %collective-permute-start.91 = (bf16[5,128,128]{2,1,0:T(8,128)(2,1)}, bf16[5,128,128]{2,1,0:T(8,128)(2,1)}, u32[]{:S(2)}, u32[]{:S(2)}) collective-permute-start(bf16[5,128,128]{2,1,0:T(8,128)(2,1)} %copy-done.36), channel_id=1, source_target_pairs={{0,6},{1,7},{2,4},{3,5},{4,2},{5,3},{6,0},{7,1},{8,14},{9,15},{10,... | collective-permute-start | bytes 491528 | tf_op jit(solution)/shard_map/ppermute | solution.py:555
  329.9 35.1 %collective-permute-start.92 = (bf16[5,128,128]{2,1,0:T(8,128)(2,1)}, bf16[5,128,128]{2,1,0:T(8,128)(2,1)}, u32[]{:S(2)}, u32[]{:S(2)}) collective-permute-start(bf16[5,128,128]{2,1,0:T(8,128)(2,1)} %copy-done.35), channel_id=1, source_target_pairs={{0,7},{1,6},{2,5},{3,4},{4,3},{5,2},{6,1},{7,0},{8,15},{9,14},{10,... | collective-permute-start | bytes 491528 | tf_op jit(solution)/shard_map/ppermute | solution.py:555
  387.4 12.7 %collective-permute-start.112 = (bf16[5,128,128]{2,1,0:T(8,128)(2,1)}, bf16[5,128,128]{2,1,0:T(8,128)(2,1)S(1)}, u32[]{:S(2)}, u32[]{:S(2)}) collective-permute-start(bf16[5,128,128]{2,1,0:T(8,128)(2,1)} %get-tuple-element.337), channel_id=1, source_target_pairs={{0,6},{1,7},{2,4},{3,5},{4,2},{5,3},{6,0},{7,1},{8,14},{9,15},{10,... | collective-permute-start | bytes 491528 | tf_op jit(solution)/shard_map/ppermute | solution.py:555
  392.9 16.6 %collective-permute-start.93 = (bf16[5,128,128]{2,1,0:T(8,128)(2,1)}, bf16[5,128,128]{2,1,0:T(8,128)(2,1)S(1)}, u32[]{:S(2)}, u32[]{:S(2)}) collective-permute-start(bf16[5,128,128]{2,1,0:T(8,128)(2,1)} %get-tuple-element.308), channel_id=1, source_target_pairs={{0,1},{1,0},{2,3},{3,2},{4,5},{5,4},{6,7},{7,6},{8,9},{9,8},{10,11... | collective-permute-start | bytes 491528 | tf_op jit(solution)/shard_map/ppermute | solution.py:555
  393.9 17.0 %collective-permute-start.94 = (bf16[5,128,128]{2,1,0:T(8,128)(2,1)}, bf16[5,128,128]{2,1,0:T(8,128)(2,1)S(1)}, u32[]{:S(2)}, u32[]{:S(2)}) collective-permute-start(bf16[5,128,128]{2,1,0:T(8,128)(2,1)} %get-tuple-element.309), channel_id=1, source_target_pairs={{0,2},{1,3},{2,0},{3,1},{4,6},{5,7},{6,4},{7,5},{8,10},{9,11},{10,... | collective-permute-start | bytes 491528 | tf_op jit(solution)/shard_map/ppermute | solution.py:555
  406.5 36.2 %collective-permute-start.121 = (bf16[20,128,128]{2,1,0:T(8,128)(2,1)S(1)}, bf16[20,128,128]{2,1,0:T(8,128)(2,1)S(1)}, u32[]{:S(2)}, u32[]{:S(2)}) collective-permute-start(bf16[20,128,128]{2,1,0:T(8,128)(2,1)S(1)} %fold.10), channel_id=1, source_target_pairs={{0,8},{1,9},{2,10},{3,11},{4,12},{5,13},{6,14},{7,15},{16,0},{17,1... | collective-permute-start | bytes 1966088 | tf_op jit(solution)/shard_map/ppermute | solution.py:601
  410.9 12.4 %collective-permute-start.98 = (bf16[5,128,128]{2,1,0:T(8,128)(2,1)S(1)}, bf16[5,128,128]{2,1,0:T(8,128)(2,1)S(1)}, u32[]{:S(2)}, u32[]{:S(2)}) collective-permute-start(bf16[5,128,128]{2,1,0:T(8,128)(2,1)S(1)} %copy-done.109), channel_id=1, source_target_pairs={{0,6},{1,7},{2,4},{3,5},{4,2},{5,3},{6,0},{7,1},{8,14},{9,15},{10,... | collective-permute-start | bytes 491528 | tf_op jit(solution)/shard_map/ppermute | solution.py:555
  426.9 12.7 %collective-permute-start.118 = (bf16[5,128,128]{2,1,0:T(8,128)(2,1)S(1)}, bf16[5,128,128]{2,1,0:T(8,128)(2,1)S(1)}, u32[]{:S(2)}, u32[]{:S(2)}) collective-permute-start(bf16[5,128,128]{2,1,0:T(8,128)(2,1)S(1)} %copy-done.97), channel_id=1, source_target_pairs={{0,5},{1,4},{2,7},{3,6},{4,1},{5,0},{6,3},{7,2},{8,13},{9,12},{10,... | collective-permute-start | bytes 491528 | tf_op jit(solution)/shard_map/ppermute | solution.py:555
  439.6 28.3 %collective-permute-start.123 = (bf16[20,128,128]{2,1,0:T(8,128)(2,1)S(1)}, bf16[20,128,128]{2,1,0:T(8,128)(2,1)S(1)}, u32[]{:S(2)}, u32[]{:S(2)}) collective-permute-start(bf16[20,128,128]{2,1,0:T(8,128)(2,1)S(1)} %fold.9), channel_id=1, source_target_pairs={{0,16},{1,17},{2,18},{3,19},{4,20},{5,21},{6,22},{7,23},{16,24},{1... | collective-permute-start | bytes 1966088 | tf_op jit(solution)/shard_map/ppermute | solution.py:601
  444.9 28.4 %collective-permute-start.122 = (bf16[20,128,128]{2,1,0:T(8,128)(2,1)S(1)}, bf16[20,128,128]{2,1,0:T(8,128)(2,1)S(1)}, u32[]{:S(2)}, u32[]{:S(2)}) collective-permute-start(bf16[20,128,128]{2,1,0:T(8,128)(2,1)S(1)} %fold.11), channel_id=1, source_target_pairs={{0,8},{1,9},{2,10},{3,11},{4,12},{5,13},{6,14},{7,15},{16,0},{17,1... | collective-permute-start | bytes 1966088 | tf_op jit(solution)/shard_map/ppermute | solution.py:601
  (195 other events, 2558.8 us)

commit v7 on v5

--- a/solution.py
+++ b/solution.py
@@ -234,7 +234,7 @@
     return product.astype(jnp.bfloat16)
 
 
-def mix_in(earlier, fresh, mix):
+def split_dot(left, right):
     def halves(wide):
         high = wide.astype(jnp.bfloat16)
         return high, (wide - high.astype(jnp.float32)).astype(jnp.bfloat16)
@@ -242,9 +242,9 @@
     def product(left, right):
         return jnp.dot(left, right, preferred_element_type=jnp.float32)
 
-    high, low = halves(jnp.concatenate([earlier, fresh], axis=1))
-    mix_high, mix_low = halves(mix)
-    return product(high, mix_high) + (product(high, mix_low) + product(low, mix_high))
+    high, low = halves(left)
+    right_high, right_low = halves(right)
+    return product(high, right_high) + (product(high, right_low) + product(low, right_high))
 
 
 def arcs_kernel(plan, mixed, tab_ref, *refs):
@@ -286,7 +286,7 @@
     for g in group:
         wide = jnp.dot(panel_ref[g], fetched[g], preferred_element_type=jnp.float32)
         if mixed:
-            wide = mix_in(extra[0][g], wide, extra[1][...])
+            wide = split_dot(jnp.concatenate([extra[0][g], wide], axis=1), extra[1][...])
         else:
             refs[-5][g] = wide
         coupled.append(wide.astype(jnp.bfloat16))
@@ -436,9 +436,9 @@
     blocks, rows, cols = field_ref.shape
     step = step_ref[...]
     size = (blocks * rows, cols)
-    moved = times_high(field_ref[...].reshape(size), step).reshape(field_ref.shape)
+    moved = split_dot(field_ref[...].reshape(size), step).reshape(field_ref.shape)
     sol_out[...] = sol_ref[...] + moved
-    moved = times_high(image_ref[...].reshape(size), step).reshape(field_ref.shape)
+    moved = split_dot(image_ref[...].reshape(size), step).reshape(field_ref.shape)
     res_out[...] = res_ref[...] - moved
 
 

time: 522 us -> 521 us (level)
  no operation moved by 1% of the time
where the time goes in v7:
time: 521 us; the launch traced here: 520 us
  waiting for transfers between devices  180 us (35%)
  starting transfers between devices  145 us (28%)
  Pallas kernels  141 us (27%)
  local copies, waits for them, and re-layouts  23.3 us (4%)
  blocking collectives  18.2 us (3%)
  matrix products  7.7 us (1%)
    ppermute x112, waiting for transfers between devices, trade_plane(): lax.ppermute(buffers[offset], AXES, plan.shift_plane(offset))  115 us
    ppermute x112, starting transfers between devices, trade_plane(): lax.ppermute(buffers[offset], AXES, plan.shift_plane(offset))  104 us
    pallas_call x2, Pallas kernels, small_solve(): pl.pallas_call(kernel, out_shape=[jax.ShapeDtypeStruct(shape, jnp.float32...  50.7 us
    ppermute x6, waiting for transfers between devices, apply_schur(): following = lax.ppermute(chunk, AXES, plan.ring)  48.8 us
    pallas_call x2, Pallas kernels, run_arcs(): pl.pallas_call(functools.partial(arcs_kernel, plan, bool(extra)), grid_sp...  32.5 us
    unnamed x231, local copies, waits for them, and re-layouts  22 us
    all_to_all x2, blocking collectives, trade(): return lax.all_to_all(buffer, AXES, split_axis=0, concat_axis=0, tiled=True)  18.2 us
    all_to_all x4, starting transfers between devices, trade(): return lax.all_to_all(buffer, AXES, split_axis=0, concat_axis=0, tiled=True)  16 us
  transfers between devices with their start and end apart: 128, of which 54 were waited for; matrix products, arithmetic and copies ran while one was open for 2% of the time, Pallas kernels for 14%

profile of v7, /device:TPU:0, one launch (start us, length us, event | category | flops | bytes accessed | tf_op | source)
XLA Modules:
  0.0 519.9 jit_solution(4703459335157732215)
XLA Ops:
  2.1 4.1 collective-permute-start.7
  6.2 14.0 %collective-permute-done.7.chunk_ref = bf16[20,128,128]{2,1,0:T(8,128)(2,1)S(1)} collective-permute-done((bf16[20,128,128]{2,1,0:T(8,128)(2,1)S(1)}, bf16[20,128,128]{2,1,0:T(8,128)(2,1)S(1)}, u32[]{:S(2)}, u32[]{:S(2)}) %collective-permute-start.7) | collective-permute-done | bytes 655392 | tf_op jit(solution)/shard_map/ppermute | solution.py:577
  20.2 3.4 collective-permute-start.15
  26.6 10.1 %collective-permute-done.15.chunk_ref = bf16[20,128,128]{2,1,0:T(8,128)(2,1)S(1)} collective-permute-done((bf16[20,128,128]{2,1,0:T(8,128)(2,1)S(1)}, bf16[20,128,128]{2,1,0:T(8,128)(2,1)S(1)}, u32[]{:S(2)}, u32[]{:S(2)}) %collective-permute-start.15) | collective-permute-done | bytes 655392 | tf_op jit(solution)/shard_map/ppermute | solution.py:577
  36.7 3.4 collective-permute-start.23
  46.2 3.3 collective-permute-start.5
  70.3 3.1 collective-permute-done.14.refs_15_
  86.8 3.6 collective-permute-done.21.refs_22_
  97.4 3.7 collective-permute-done.26.refs_27_
  101.1 3.9 collective-permute-done.29.refs_30_
  107.1 15.1 %arcs.2 = (bf16[5,128,128]{2,1,0:T(8,128)(2,1)}, bf16[5,128,128]{2,1,0:T(8,128)(2,1)}, bf16[5,128,128]{2,1,0:T(8,128)(2,1)}, bf16[5,128,128]{2,1,0:T(8,128)(2,1)...) custom-call(s32[32,128]{1,0:T(8,128)} %copy-done.31, ...), custom_call_target="tpu_custom_call" | custom-call | tf_op jit(solution)/shard_map/arcs/pallas_call | solution.py:315
  127.7 2.8 collective-permute-done.46.refs_2_
  134.9 4.1 collective-permute-done.50.refs_6_
  139.1 2.9 collective-permute-done.51.refs_7_
  149.0 2.7 collective-permute-done.33.refs_3_
  156.4 4.2 collective-permute-done.36.refs_6_
  176.0 3.0 collective-permute-start.61
  180.3 2.7 fold.8
  187.8 4.7 collective-permute-done.39.refs_2_
  198.9 4.2 collective-permute-done.43.refs_6_
  203.1 3.6 collective-permute-done.44.refs_7_
  206.6 2.7 collective-permute-done.60.refs_8_
  215.0 6.9 %image.2 = (f32[20,128,128]{2,1,0:T(8,128)S(1)}, f32[2,128,128]{2,1,0:T(8,128)}, bf16[20,128,128]{2,1,0:T(8,128)(2,1)S(1)}) custom-call(s32[1]{0:T(128)} %gate.17.me_ref.in_ref, s32[8,128]{1,0:T(8,128)S(1)} %get-tuple-element.176.held_ref, f32[20,128,128]{2,1,0:T(8,128)S(1)} %copy-done, f32[128,20]{1,0:T(8,128)S(1)} %bitcast.32, ...), custom_call_target="tpu_custom_call" | custom-call | tf_op jit(solution)/shard_map/image/pallas_call | solution.py:420
  222.4 16.2 %collective-permute-done.69.chunk_ref = bf16[20,128,128]{2,1,0:T(8,128)(2,1)S(1)} collective-permute-done((bf16[20,128,128]{2,1,0:T(8,128)(2,1)S(1)}, bf16[20,128,128]{2,1,0:T(8,128)(2,1)S(1)}, u32[]{:S(2)}, u32[]{:S(2)}) %collective-permute-start.69) | collective-permute-done | bytes 655392 | tf_op jit(solution)/shard_map/ppermute | solution.py:577
  245.9 8.6 %collective-permute-done.77.chunk_ref = bf16[20,128,128]{2,1,0:T(8,128)(2,1)S(1)} collective-permute-done((bf16[20,128,128]{2,1,0:T(8,128)(2,1)S(1)}, bf16[20,128,128]{2,1,0:T(8,128)(2,1)S(1)}, u32[]{:S(2)}, u32[]{:S(2)}) %collective-permute-start.77) | collective-permute-done | bytes 655392 | tf_op jit(solution)/shard_map/ppermute | solution.py:577
  263.5 2.9 fusion.4
  266.5 4.6 all-to-all-start
  275.8 2.8 all-to-all-done
  279.5 9.1 %all_to_all.30 = f32[32,4,128]{2,1,0:T(4,128)S(1)} all-to-all(f32[32,4,128]{2,1,0:T(4,128)S(1)} %broadcast_in_dim.6), channel_id=1, replica_groups=mesh['arc'=8,'vec'=4] {'arc','vec'}, dimensions={0} | all-to-all | bytes 131072 | tf_op jit(solution)/shard_map/all_to_all | solution.py:39
  288.6 4.0 all-to-all-start.2
  315.5 4.6 all-to-all-start.3
  328.6 33.7 %solve.2 = (f32[128,128]{1,0:T(8,128)S(1)}, f32[128,128]{1,0:T(8,128)S(1)}, f32[128,128]{1,0:T(8,128)S(1)}, f32[256,128]{1,0:T(8,128)S(1)}) custom-call(f32[2,128,128]{2,1,0:T(8,128)S(1)} %bitcast.34, f32[128,128]{1,0:T(8,128)S(1)} %bitcast.35), custom_call_target="tpu_custom_call" | custom-call | tf_op jit(solution)/shard_map/solve/pallas_call | solution.py:537
  363.0 17.4 %arcs.3 = (bf16[5,128,128]{2,1,0:T(8,128)(2,1)}, bf16[5,128,128]{2,1,0:T(8,128)(2,1)}, bf16[5,128,128]{2,1,0:T(8,128)(2,1)}, bf16[5,128,128]{2,1,0:T(8,128)(2,1)...) custom-call(s32[32,128]{1,0:T(8,128)} %copy-done.31, ...), custom_call_target="tpu_custom_call" | custom-call | tf_op jit(solution)/shard_map/arcs/pallas_call | solution.py:315
  386.2 2.9 collective-permute-done.108.refs_2_
  394.0 4.1 collective-permute-done.112.refs_6_
  398.1 3.0 collective-permute-done.113.refs_7_
  409.2 3.1 collective-permute-done.95.refs_3_
  417.1 3.7 collective-permute-done.98.refs_6_
  448.4 3.4 collective-permute-done.101.refs_2_
  458.4 3.8 collective-permute-done.105.refs_6_
  462.2 2.8 collective-permute-done.106.refs_7_
  465.0 5.4 %collective-permute-done.122.refs_8_ = bf16[20,128,128]{2,1,0:T(8,128)(2,1)S(1)} collective-permute-done((bf16[20,128,128]{2,1,0:T(8,128)(2,1)S(1)}, bf16[20,128,128]{2,1,0:T(8,128)(2,1)S(1)}, u32[]{:S(2)}, u32[]{:S(2)}) %collective-permute-start.122) | collective-permute-done | bytes 655392 | tf_op jit(solution)/shard_map/ppermute | solution.py:597
  470.5 4.5 image.3
  476.0 9.1 %all_to_all.31 = f32[32,4,128]{2,1,0:T(4,128)S(1)} all-to-all(f32[32,4,128]{2,1,0:T(4,128)S(1)} %bitcast.37), channel_id=1, replica_groups=mesh['arc'=8,'vec'=4] {'arc','vec'}, dimensions={0} | all-to-all | bytes 131072 | tf_op jit(solution)/shard_map/all_to_all | solution.py:39
  485.8 2.8 all-to-all-start.5
  491.0 5.1 all-to-all-done.5
  496.1 17.0 %solve.3.step_ref = f32[128,128]{1,0:T(8,128)S(1)} custom-call(f32[1,128,128]{2,1,0:T(8,128)S(1)} %bitcast.36, f32[128,128]{1,0:T(8,128)S(1)} %get-tuple-element.349.res_ref), custom_call_target="tpu_custom_call" | custom-call | tf_op jit(solution)/shard_map/solve/pallas_call | solution.py:537
  513.7 6.2 %update.1 = (f32[20,128,128]{2,1,0:T(8,128)}, f32[20,128,128]{2,1,0:T(8,128)}) custom-call(f32[20,128,128]{2,1,0:T(8,128)} %copy-done.1, f32[20,128,128]{2,1,0:T(8,128)} %copy-done.2, f32[20,128,128]{2,1,0:T(8,128)} %convolution_bitcast_fusion.sol_ref, f32[20,128,128]{2,1,0:T(8,128)} %copy-done.40, f32[128,128]{1,0:T(8,128)} %copy-done.5), custom_call_target="tpu_custom_call" | custom-call | tf_op jit(solution)/shard_map/update/pallas_call | solution.py:449
  (486 shorter events, 225.1 us)
Async XLA Ops:
  2.1 18.1 %collective-permute-start.7 = (bf16[20,128,128]{2,1,0:T(8,128)(2,1)S(1)}, bf16[20,128,128]{2,1,0:T(8,128)(2,1)S(1)}, u32[]{:S(2)}, u32[]{:S(2)}) collective-permute-start(bf16[20,128,128]{2,1,0:T(8,128)(2,1)S(1)} %convert_element_type.3.chunk_ref), channel_id=1, source_target_pairs={{0,16},{1,17},{2,18},{3,19},{4,20},{5,21},{6,22},{7,23},{16,24},{1... | collective-permute-start | bytes 1966088 | tf_op jit(solution)/shard_map/ppermute | solution.py:577
  20.2 16.5 %collective-permute-start.15 = (bf16[20,128,128]{2,1,0:T(8,128)(2,1)S(1)}, bf16[20,128,128]{2,1,0:T(8,128)(2,1)S(1)}, u32[]{:S(2)}, u32[]{:S(2)}) collective-permute-start(bf16[20,128,128]{2,1,0:T(8,128)(2,1)S(1)} %collective-permute-done.7.chunk_ref), channel_id=1, source_target_pairs={{0,16},{1,17},{2,18},{3,19},{4,20},{5,21},{6,22},{7,23},{16,24},{1... | collective-permute-start | bytes 1966088 | tf_op jit(solution)/shard_map/ppermute | solution.py:577
  26.6 16.5 %collective-permute-start = (bf16[5,128,128]{2,1,0:T(8,128)(2,1)S(1)}, bf16[5,128,128]{2,1,0:T(8,128)(2,1)S(1)}, u32[]{:S(2)}, u32[]{:S(2)}) collective-permute-start(bf16[5,128,128]{2,1,0:T(8,128)(2,1)S(1)} %get-tuple-element.179), channel_id=1, source_target_pairs={{0,1},{1,0},{2,3},{3,2},{4,5},{5,4},{6,7},{7,6},{8,9},{9,8},{10,11... | collective-permute-start | bytes 491528 | tf_op jit(solution)/shard_map/ppermute | solution.py:551
  36.7 37.5 %collective-permute-start.23 = (bf16[20,128,128]{2,1,0:T(8,128)(2,1)S(1)}, bf16[20,128,128]{2,1,0:T(8,128)(2,1)S(1)}, u32[]{:S(2)}, u32[]{:S(2)}) collective-permute-start(bf16[20,128,128]{2,1,0:T(8,128)(2,1)S(1)} %collective-permute-done.15.chunk_ref), channel_id=1, source_target_pairs={{0,16},{1,17},{2,18},{3,19},{4,20},{5,21},{6,22},{7,23},{16,24},{1... | collective-permute-start | bytes 1966088 | tf_op jit(solution)/shard_map/ppermute | solution.py:577
  51.5 12.9 %collective-permute-start.11 = (bf16[5,128,128]{2,1,0:T(8,128)(2,1)S(1)}, bf16[5,128,128]{2,1,0:T(8,128)(2,1)S(1)}, u32[]{:S(2)}, u32[]{:S(2)}) collective-permute-start(bf16[5,128,128]{2,1,0:T(8,128)(2,1)S(1)} %get-tuple-element.190), channel_id=1, source_target_pairs={{0,4},{1,5},{2,6},{3,7},{4,0},{5,1},{6,2},{7,3},{8,12},{9,13},{10,... | collective-permute-start | bytes 491528 | tf_op jit(solution)/shard_map/ppermute | solution.py:551
  83.9 13.0 %collective-permute-start.25 = (bf16[5,128,128]{2,1,0:T(8,128)(2,1)S(1)}, bf16[5,128,128]{2,1,0:T(8,128)(2,1)S(1)}, u32[]{:S(2)}, u32[]{:S(2)}) collective-permute-start(bf16[5,128,128]{2,1,0:T(8,128)(2,1)S(1)} %get-tuple-element.204), channel_id=1, source_target_pairs={{0,2},{1,3},{2,0},{3,1},{4,6},{5,7},{6,4},{7,5},{8,10},{9,11},{10,... | collective-permute-start | bytes 491528 | tf_op jit(solution)/shard_map/ppermute | solution.py:551
  85.1 16.0 %collective-permute-start.26 = (bf16[5,128,128]{2,1,0:T(8,128)(2,1)S(1)}, bf16[5,128,128]{2,1,0:T(8,128)(2,1)S(1)}, u32[]{:S(2)}, u32[]{:S(2)}) collective-permute-start(bf16[5,128,128]{2,1,0:T(8,128)(2,1)S(1)} %get-tuple-element.205), channel_id=1, source_target_pairs={{0,3},{1,2},{2,1},{3,0},{4,7},{5,6},{6,5},{7,4},{8,11},{9,10},{10,... | collective-permute-start | bytes 491528 | tf_op jit(solution)/shard_map/ppermute | solution.py:551
  126.7 12.4 %collective-permute-start.50 = (bf16[5,128,128]{2,1,0:T(8,128)(2,1)}, bf16[5,128,128]{2,1,0:T(8,128)(2,1)S(1)}, u32[]{:S(2)}, u32[]{:S(2)}) collective-permute-start(bf16[5,128,128]{2,1,0:T(8,128)(2,1)} %get-tuple-element.248), channel_id=1, source_target_pairs={{0,6},{1,7},{2,4},{3,5},{4,2},{5,3},{6,0},{7,1},{8,14},{9,15},{10,... | collective-permute-start | bytes 491528 | tf_op jit(solution)/shard_map/ppermute | solution.py:551
  132.2 14.8 %collective-permute-start.31 = (bf16[5,128,128]{2,1,0:T(8,128)(2,1)}, bf16[5,128,128]{2,1,0:T(8,128)(2,1)S(1)}, u32[]{:S(2)}, u32[]{:S(2)}) collective-permute-start(bf16[5,128,128]{2,1,0:T(8,128)(2,1)} %get-tuple-element.219), channel_id=1, source_target_pairs={{0,1},{1,0},{2,3},{3,2},{4,5},{5,4},{6,7},{7,6},{8,9},{9,8},{10,11... | collective-permute-start | bytes 491528 | tf_op jit(solution)/shard_map/ppermute | solution.py:551
  133.2 15.0 %collective-permute-start.32 = (bf16[5,128,128]{2,1,0:T(8,128)(2,1)}, bf16[5,128,128]{2,1,0:T(8,128)(2,1)S(1)}, u32[]{:S(2)}, u32[]{:S(2)}) collective-permute-start(bf16[5,128,128]{2,1,0:T(8,128)(2,1)} %get-tuple-element.220), channel_id=1, source_target_pairs={{0,2},{1,3},{2,0},{3,1},{4,6},{5,7},{6,4},{7,5},{8,10},{9,11},{10,... | collective-permute-start | bytes 491528 | tf_op jit(solution)/shard_map/ppermute | solution.py:551
  145.1 35.2 %collective-permute-start.59 = (bf16[20,128,128]{2,1,0:T(8,128)(2,1)S(1)}, bf16[20,128,128]{2,1,0:T(8,128)(2,1)S(1)}, u32[]{:S(2)}, u32[]{:S(2)}) collective-permute-start(bf16[20,128,128]{2,1,0:T(8,128)(2,1)S(1)} %fold.7), channel_id=1, source_target_pairs={{0,8},{1,9},{2,10},{3,11},{4,12},{5,13},{6,14},{7,15},{16,0},{17,1... | collective-permute-start | bytes 1966088 | tf_op jit(solution)/shard_map/ppermute | solution.py:597
  148.2 12.4 %collective-permute-start.36 = (bf16[5,128,128]{2,1,0:T(8,128)(2,1)S(1)}, bf16[5,128,128]{2,1,0:T(8,128)(2,1)S(1)}, u32[]{:S(2)}, u32[]{:S(2)}) collective-permute-start(bf16[5,128,128]{2,1,0:T(8,128)(2,1)S(1)} %copy-done.110), channel_id=1, source_target_pairs={{0,6},{1,7},{2,4},{3,5},{4,2},{5,3},{6,0},{7,1},{8,14},{9,15},{10,... | collective-permute-start | bytes 491528 | tf_op jit(solution)/shard_map/ppermute | solution.py:551
  163.0 13.0 %collective-permute-start.55 = (bf16[5,128,128]{2,1,0:T(8,128)(2,1)S(1)}, bf16[5,128,128]{2,1,0:T(8,128)(2,1)S(1)}, u32[]{:S(2)}, u32[]{:S(2)}) collective-permute-start(bf16[5,128,128]{2,1,0:T(8,128)(2,1)S(1)} %copy-done.99), channel_id=1, source_target_pairs={{0,4},{1,5},{2,6},{3,7},{4,0},{5,1},{6,2},{7,3},{8,12},{9,13},{10,... | collective-permute-start | bytes 491528 | tf_op jit(solution)/shard_map/ppermute | solution.py:551
  163.6 15.4 %collective-permute-start.56 = (bf16[5,128,128]{2,1,0:T(8,128)(2,1)S(1)}, bf16[5,128,128]{2,1,0:T(8,128)(2,1)S(1)}, u32[]{:S(2)}, u32[]{:S(2)}) collective-permute-start(bf16[5,128,128]{2,1,0:T(8,128)(2,1)S(1)} %copy-done.98), channel_id=1, source_target_pairs={{0,5},{1,4},{2,7},{3,6},{4,1},{5,0},{6,3},{7,2},{8,13},{9,12},{10,... | collective-permute-start | bytes 491528 | tf_op jit(solution)/shard_map/ppermute | solution.py:551
  176.0 30.6 %collective-permute-start.61 = (bf16[20,128,128]{2,1,0:T(8,128)(2,1)S(1)}, bf16[20,128,128]{2,1,0:T(8,128)(2,1)S(1)}, u32[]{:S(2)}, u32[]{:S(2)}) collective-permute-start(bf16[20,128,128]{2,1,0:T(8,128)(2,1)S(1)} %fold.6), channel_id=1, source_target_pairs={{0,16},{1,17},{2,18},{3,19},{4,20},{5,21},{6,22},{7,23},{16,24},{1... | collective-permute-start | bytes 1966088 | tf_op jit(solution)/shard_map/ppermute | solution.py:597
  183.1 26.3 %collective-permute-start.60 = (bf16[20,128,128]{2,1,0:T(8,128)(2,1)}, bf16[20,128,128]{2,1,0:T(8,128)(2,1)S(1)}, u32[]{:S(2)}, u32[]{:S(2)}) collective-permute-start(bf16[20,128,128]{2,1,0:T(8,128)(2,1)} %fold.8), channel_id=1, source_target_pairs={{0,8},{1,9},{2,10},{3,11},{4,12},{5,13},{6,14},{7,15},{16,0},{17,1... | collective-permute-start | bytes 1966088 | tf_op jit(solution)/shard_map/ppermute | solution.py:597
  221.8 16.8 %collective-permute-start.69 = (bf16[20,128,128]{2,1,0:T(8,128)(2,1)S(1)}, bf16[20,128,128]{2,1,0:T(8,128)(2,1)S(1)}, u32[]{:S(2)}, u32[]{:S(2)}) collective-permute-start(bf16[20,128,128]{2,1,0:T(8,128)(2,1)S(1)} %get-tuple-element.264.chunk_ref), channel_id=1, source_target_pairs={{0,16},{1,17},{2,18},{3,19},{4,20},{5,21},{6,22},{7,23},{16,24},{1... | collective-permute-start | bytes 1966088 | tf_op jit(solution)/shard_map/ppermute | solution.py:577
  238.6 15.9 %collective-permute-start.77 = (bf16[20,128,128]{2,1,0:T(8,128)(2,1)S(1)}, bf16[20,128,128]{2,1,0:T(8,128)(2,1)S(1)}, u32[]{:S(2)}, u32[]{:S(2)}) collective-permute-start(bf16[20,128,128]{2,1,0:T(8,128)(2,1)S(1)} %collective-permute-done.69.chunk_ref), channel_id=1, source_target_pairs={{0,16},{1,17},{2,18},{3,19},{4,20},{5,21},{6,22},{7,23},{16,24},{1... | collective-permute-start | bytes 1966088 | tf_op jit(solution)/shard_map/ppermute | solution.py:577
  242.4 17.3 %collective-permute-start.63 = (bf16[5,128,128]{2,1,0:T(8,128)(2,1)S(1)}, bf16[5,128,128]{2,1,0:T(8,128)(2,1)S(1)}, u32[]{:S(2)}, u32[]{:S(2)}) collective-permute-start(bf16[5,128,128]{2,1,0:T(8,128)(2,1)S(1)} %get-tuple-element.267), channel_id=1, source_target_pairs={{0,2},{1,3},{2,0},{3,1},{4,6},{5,7},{6,4},{7,5},{8,10},{9,11},{10,... | collective-permute-start | bytes 491528 | tf_op jit(solution)/shard_map/ppermute | solution.py:551
  243.1 18.1 %collective-permute-start.64 = (bf16[5,128,128]{2,1,0:T(8,128)(2,1)S(1)}, bf16[5,128,128]{2,1,0:T(8,128)(2,1)S(1)}, u32[]{:S(2)}, u32[]{:S(2)}) collective-permute-start(bf16[5,128,128]{2,1,0:T(8,128)(2,1)S(1)} %get-tuple-element.268), channel_id=1, source_target_pairs={{0,3},{1,2},{2,1},{3,0},{4,7},{5,6},{6,5},{7,4},{8,11},{9,10},{10,... | collective-permute-start | bytes 491528 | tf_op jit(solution)/shard_map/ppermute | solution.py:551
  244.3 16.9 %collective-permute-start.65 = (bf16[5,128,128]{2,1,0:T(8,128)(2,1)S(1)}, bf16[5,128,128]{2,1,0:T(8,128)(2,1)S(1)}, u32[]{:S(2)}, u32[]{:S(2)}) collective-permute-start(bf16[5,128,128]{2,1,0:T(8,128)(2,1)S(1)} %get-tuple-element.269), channel_id=1, source_target_pairs={{0,4},{1,5},{2,6},{3,7},{4,0},{5,1},{6,2},{7,3},{8,12},{9,13},{10,... | collective-permute-start | bytes 491528 | tf_op jit(solution)/shard_map/ppermute | solution.py:551
  245.7 17.2 %collective-permute-start.66 = (bf16[5,128,128]{2,1,0:T(8,128)(2,1)S(1)}, bf16[5,128,128]{2,1,0:T(8,128)(2,1)S(1)}, u32[]{:S(2)}, u32[]{:S(2)}) collective-permute-start(bf16[5,128,128]{2,1,0:T(8,128)(2,1)S(1)} %get-tuple-element.270), channel_id=1, source_target_pairs={{0,5},{1,4},{2,7},{3,6},{4,1},{5,0},{6,3},{7,2},{8,13},{9,12},{10,... | collective-permute-start | bytes 491528 | tf_op jit(solution)/shard_map/ppermute | solution.py:551
  254.5 46.3 %collective-permute-start.85 = (bf16[20,128,128]{2,1,0:T(8,128)(2,1)S(1)}, bf16[20,128,128]{2,1,0:T(8,128)(2,1)}, u32[]{:S(2)}, u32[]{:S(2)}) collective-permute-start(bf16[20,128,128]{2,1,0:T(8,128)(2,1)S(1)} %collective-permute-done.77.chunk_ref), channel_id=1, source_target_pairs={{0,16},{1,17},{2,18},{3,19},{4,20},{5,21},{6,22},{7,23},{16,24},{1... | collective-permute-start | bytes 1966088 | tf_op jit(solution)/shard_map/ppermute | solution.py:577
  261.2 12.8 %collective-permute-start.70 = (bf16[5,128,128]{2,1,0:T(8,128)(2,1)}, bf16[5,128,128]{2,1,0:T(8,128)(2,1)}, u32[]{:S(2)}, u32[]{:S(2)}) collective-permute-start(bf16[5,128,128]{2,1,0:T(8,128)(2,1)} %get-tuple-element.274), channel_id=1, source_target_pairs={{0,1},{1,0},{2,3},{3,2},{4,5},{5,4},{6,7},{7,6},{8,9},{9,8},{10,11... | collective-permute-start | bytes 491528 | tf_op jit(solution)/shard_map/ppermute | solution.py:551
  271.1 25.4 %collective-permute-start.72 = (bf16[5,128,128]{2,1,0:T(8,128)(2,1)}, bf16[5,128,128]{2,1,0:T(8,128)(2,1)}, u32[]{:S(2)}, u32[]{:S(2)}) collective-permute-start(bf16[5,128,128]{2,1,0:T(8,128)(2,1)} %get-tuple-element.276), channel_id=1, source_target_pairs={{0,3},{1,2},{2,1},{3,0},{4,7},{5,6},{6,5},{7,4},{8,11},{9,10},{10,... | collective-permute-start | bytes 491528 | tf_op jit(solution)/shard_map/ppermute | solution.py:551
  272.6 26.3 %collective-permute-start.73 = (bf16[5,128,128]{2,1,0:T(8,128)(2,1)}, bf16[5,128,128]{2,1,0:T(8,128)(2,1)}, u32[]{:S(2)}, u32[]{:S(2)}) collective-permute-start(bf16[5,128,128]{2,1,0:T(8,128)(2,1)} %get-tuple-element.277), channel_id=1, source_target_pairs={{0,4},{1,5},{2,6},{3,7},{4,0},{5,1},{6,2},{7,3},{8,12},{9,13},{10,... | collective-permute-start | bytes 491528 | tf_op jit(solution)/shard_map/ppermute | solution.py:551
  274.0 25.2 %collective-permute-start.74 = (bf16[5,128,128]{2,1,0:T(8,128)(2,1)}, bf16[5,128,128]{2,1,0:T(8,128)(2,1)}, u32[]{:S(2)}, u32[]{:S(2)}) collective-permute-start(bf16[5,128,128]{2,1,0:T(8,128)(2,1)} %get-tuple-element.278), channel_id=1, source_target_pairs={{0,5},{1,4},{2,7},{3,6},{4,1},{5,0},{6,3},{7,2},{8,13},{9,12},{10,... | collective-permute-start | bytes 491528 | tf_op jit(solution)/shard_map/ppermute | solution.py:551
  274.3 25.5 %collective-permute-start.75 = (bf16[5,128,128]{2,1,0:T(8,128)(2,1)}, bf16[5,128,128]{2,1,0:T(8,128)(2,1)}, u32[]{:S(2)}, u32[]{:S(2)}) collective-permute-start(bf16[5,128,128]{2,1,0:T(8,128)(2,1)} %get-tuple-element.279), channel_id=1, source_target_pairs={{0,6},{1,7},{2,4},{3,5},{4,2},{5,3},{6,0},{7,1},{8,14},{9,15},{10,... | collective-permute-start | bytes 491528 | tf_op jit(solution)/shard_map/ppermute | solution.py:551
  288.6 26.2 %all-to-all-start.2 = ((f32[32,8,128]{2,1,0:T(8,128)}), f32[32,8,128]{2,1,0:T(8,128)S(1)}, u32[]{:S(2)}, u32[]{:S(2)}) async-start(f32[32,8,128]{2,1,0:T(8,128)} %bitcast.7), calls=%async_computation.2 | async-start | bytes 262144 | tf_op jit(solution)/shard_map/all_to_all | solution.py:39
  296.5 12.6 %collective-permute-start.76 = (bf16[5,128,128]{2,1,0:T(8,128)(2,1)}, bf16[5,128,128]{2,1,0:T(8,128)(2,1)S(1)}, u32[]{:S(2)}, u32[]{:S(2)}) collective-permute-start(bf16[5,128,128]{2,1,0:T(8,128)(2,1)} %copy-done.34), channel_id=1, source_target_pairs={{0,7},{1,6},{2,5},{3,4},{4,3},{5,2},{6,1},{7,0},{8,15},{9,14},{10,... | collective-permute-start | bytes 491528 | tf_op jit(solution)/shard_map/ppermute | solution.py:551
  299.8 13.1 %collective-permute-start.80 = (bf16[5,128,128]{2,1,0:T(8,128)(2,1)S(1)}, bf16[5,128,128]{2,1,0:T(8,128)(2,1)S(1)}, u32[]{:S(2)}, u32[]{:S(2)}) collective-permute-start(bf16[5,128,128]{2,1,0:T(8,128)(2,1)S(1)} %get-tuple-element.284), channel_id=1, source_target_pairs={{0,3},{1,2},{2,1},{3,0},{4,7},{5,6},{6,5},{7,4},{8,11},{9,10},{10,... | collective-permute-start | bytes 491528 | tf_op jit(solution)/shard_map/ppermute | solution.py:551
  300.7 12.8 %collective-permute-start.81 = (bf16[5,128,128]{2,1,0:T(8,128)(2,1)S(1)}, bf16[5,128,128]{2,1,0:T(8,128)(2,1)S(1)}, u32[]{:S(2)}, u32[]{:S(2)}) collective-permute-start(bf16[5,128,128]{2,1,0:T(8,128)(2,1)S(1)} %get-tuple-element.285), channel_id=1, source_target_pairs={{0,4},{1,5},{2,6},{3,7},{4,0},{5,1},{6,2},{7,3},{8,12},{9,13},{10,... | collective-permute-start | bytes 491528 | tf_op jit(solution)/shard_map/ppermute | solution.py:551
  310.8 12.4 %collective-permute-start.84 = (bf16[5,128,128]{2,1,0:T(8,128)(2,1)}, bf16[5,128,128]{2,1,0:T(8,128)(2,1)}, u32[]{:S(2)}, u32[]{:S(2)}) collective-permute-start(bf16[5,128,128]{2,1,0:T(8,128)(2,1)} %get-tuple-element.288), channel_id=1, source_target_pairs={{0,7},{1,6},{2,5},{3,4},{4,3},{5,2},{6,1},{7,0},{8,15},{9,14},{10,... | collective-permute-start | bytes 491528 | tf_op jit(solution)/shard_map/ppermute | solution.py:551
  314.2 13.5 %collective-permute-start.87 = (bf16[5,128,128]{2,1,0:T(8,128)(2,1)}, bf16[5,128,128]{2,1,0:T(8,128)(2,1)}, u32[]{:S(2)}, u32[]{:S(2)}) collective-permute-start(bf16[5,128,128]{2,1,0:T(8,128)(2,1)} %get-tuple-element.291), channel_id=1, source_target_pairs={{0,2},{1,3},{2,0},{3,1},{4,6},{5,7},{6,4},{7,5},{8,10},{9,11},{10,... | collective-permute-start | bytes 491528 | tf_op jit(solution)/shard_map/ppermute | solution.py:551
  315.5 13.1 %all-to-all-start.3 = ((f32[32,8,128]{2,1,0:T(8,128)}), f32[32,8,128]{2,1,0:T(8,128)S(1)}, u32[]{:S(2)}, u32[]{:S(2)}) async-start(f32[32,8,128]{2,1,0:T(8,128)} %broadcast_in_dim.7), calls=%async_computation.3 | async-start | bytes 262144 | tf_op jit(solution)/shard_map/all_to_all | solution.py:39
  320.2 42.8 %collective-permute-start.88 = (bf16[5,128,128]{2,1,0:T(8,128)(2,1)}, bf16[5,128,128]{2,1,0:T(8,128)(2,1)}, u32[]{:S(2)}, u32[]{:S(2)}) collective-permute-start(bf16[5,128,128]{2,1,0:T(8,128)(2,1)} %copy-done.39), channel_id=1, source_target_pairs={{0,3},{1,2},{2,1},{3,0},{4,7},{5,6},{6,5},{7,4},{8,11},{9,10},{10,... | collective-permute-start | bytes 491528 | tf_op jit(solution)/shard_map/ppermute | solution.py:551
  321.7 41.3 %collective-permute-start.89 = (bf16[5,128,128]{2,1,0:T(8,128)(2,1)}, bf16[5,128,128]{2,1,0:T(8,128)(2,1)}, u32[]{:S(2)}, u32[]{:S(2)}) collective-permute-start(bf16[5,128,128]{2,1,0:T(8,128)(2,1)} %copy-done.38), channel_id=1, source_target_pairs={{0,4},{1,5},{2,6},{3,7},{4,0},{5,1},{6,2},{7,3},{8,12},{9,13},{10,... | collective-permute-start | bytes 491528 | tf_op jit(solution)/shard_map/ppermute | solution.py:551
  323.2 39.8 %collective-permute-start.90 = (bf16[5,128,128]{2,1,0:T(8,128)(2,1)}, bf16[5,128,128]{2,1,0:T(8,128)(2,1)}, u32[]{:S(2)}, u32[]{:S(2)}) collective-permute-start(bf16[5,128,128]{2,1,0:T(8,128)(2,1)} %copy-done.37), channel_id=1, source_target_pairs={{0,5},{1,4},{2,7},{3,6},{4,1},{5,0},{6,3},{7,2},{8,13},{9,12},{10,... | collective-permute-start | bytes 491528 | tf_op jit(solution)/shard_map/ppermute | solution.py:551
  323.9 39.1 %collective-permute-start.91 = (bf16[5,128,128]{2,1,0:T(8,128)(2,1)}, bf16[5,128,128]{2,1,0:T(8,128)(2,1)}, u32[]{:S(2)}, u32[]{:S(2)}) collective-permute-start(bf16[5,128,128]{2,1,0:T(8,128)(2,1)} %copy-done.36), channel_id=1, source_target_pairs={{0,6},{1,7},{2,4},{3,5},{4,2},{5,3},{6,0},{7,1},{8,14},{9,15},{10,... | collective-permute-start | bytes 491528 | tf_op jit(solution)/shard_map/ppermute | solution.py:551
  327.7 35.3 %collective-permute-start.92 = (bf16[5,128,128]{2,1,0:T(8,128)(2,1)}, bf16[5,128,128]{2,1,0:T(8,128)(2,1)}, u32[]{:S(2)}, u32[]{:S(2)}) collective-permute-start(bf16[5,128,128]{2,1,0:T(8,128)(2,1)} %copy-done.35), channel_id=1, source_target_pairs={{0,7},{1,6},{2,5},{3,4},{4,3},{5,2},{6,1},{7,0},{8,15},{9,14},{10,... | collective-permute-start | bytes 491528 | tf_op jit(solution)/shard_map/ppermute | solution.py:551
  385.3 12.7 %collective-permute-start.112 = (bf16[5,128,128]{2,1,0:T(8,128)(2,1)}, bf16[5,128,128]{2,1,0:T(8,128)(2,1)S(1)}, u32[]{:S(2)}, u32[]{:S(2)}) collective-permute-start(bf16[5,128,128]{2,1,0:T(8,128)(2,1)} %get-tuple-element.337), channel_id=1, source_target_pairs={{0,6},{1,7},{2,4},{3,5},{4,2},{5,3},{6,0},{7,1},{8,14},{9,15},{10,... | collective-permute-start | bytes 491528 | tf_op jit(solution)/shard_map/ppermute | solution.py:551
  390.9 16.1 %collective-permute-start.93 = (bf16[5,128,128]{2,1,0:T(8,128)(2,1)}, bf16[5,128,128]{2,1,0:T(8,128)(2,1)S(1)}, u32[]{:S(2)}, u32[]{:S(2)}) collective-permute-start(bf16[5,128,128]{2,1,0:T(8,128)(2,1)} %get-tuple-element.308), channel_id=1, source_target_pairs={{0,1},{1,0},{2,3},{3,2},{4,5},{5,4},{6,7},{7,6},{8,9},{9,8},{10,11... | collective-permute-start | bytes 491528 | tf_op jit(solution)/shard_map/ppermute | solution.py:551
  391.9 16.5 %collective-permute-start.94 = (bf16[5,128,128]{2,1,0:T(8,128)(2,1)}, bf16[5,128,128]{2,1,0:T(8,128)(2,1)S(1)}, u32[]{:S(2)}, u32[]{:S(2)}) collective-permute-start(bf16[5,128,128]{2,1,0:T(8,128)(2,1)} %get-tuple-element.309), channel_id=1, source_target_pairs={{0,2},{1,3},{2,0},{3,1},{4,6},{5,7},{6,4},{7,5},{8,10},{9,11},{10,... | collective-permute-start | bytes 491528 | tf_op jit(solution)/shard_map/ppermute | solution.py:551
  404.1 36.0 %collective-permute-start.121 = (bf16[20,128,128]{2,1,0:T(8,128)(2,1)S(1)}, bf16[20,128,128]{2,1,0:T(8,128)(2,1)S(1)}, u32[]{:S(2)}, u32[]{:S(2)}) collective-permute-start(bf16[20,128,128]{2,1,0:T(8,128)(2,1)S(1)} %fold.10), channel_id=1, source_target_pairs={{0,8},{1,9},{2,10},{3,11},{4,12},{5,13},{6,14},{7,15},{16,0},{17,1... | collective-permute-start | bytes 1966088 | tf_op jit(solution)/shard_map/ppermute | solution.py:597
  408.3 12.4 %collective-permute-start.98 = (bf16[5,128,128]{2,1,0:T(8,128)(2,1)S(1)}, bf16[5,128,128]{2,1,0:T(8,128)(2,1)S(1)}, u32[]{:S(2)}, u32[]{:S(2)}) collective-permute-start(bf16[5,128,128]{2,1,0:T(8,128)(2,1)S(1)} %copy-done.109), channel_id=1, source_target_pairs={{0,6},{1,7},{2,4},{3,5},{4,2},{5,3},{6,0},{7,1},{8,14},{9,15},{10,... | collective-permute-start | bytes 491528 | tf_op jit(solution)/shard_map/ppermute | solution.py:551
  424.3 12.4 %collective-permute-start.118 = (bf16[5,128,128]{2,1,0:T(8,128)(2,1)S(1)}, bf16[5,128,128]{2,1,0:T(8,128)(2,1)S(1)}, u32[]{:S(2)}, u32[]{:S(2)}) collective-permute-start(bf16[5,128,128]{2,1,0:T(8,128)(2,1)S(1)} %copy-done.97), channel_id=1, source_target_pairs={{0,5},{1,4},{2,7},{3,6},{4,1},{5,0},{6,3},{7,2},{8,13},{9,12},{10,... | collective-permute-start | bytes 491528 | tf_op jit(solution)/shard_map/ppermute | solution.py:551
  436.8 28.3 %collective-permute-start.123 = (bf16[20,128,128]{2,1,0:T(8,128)(2,1)S(1)}, bf16[20,128,128]{2,1,0:T(8,128)(2,1)S(1)}, u32[]{:S(2)}, u32[]{:S(2)}) collective-permute-start(bf16[20,128,128]{2,1,0:T(8,128)(2,1)S(1)} %fold.9), channel_id=1, source_target_pairs={{0,16},{1,17},{2,18},{3,19},{4,20},{5,21},{6,22},{7,23},{16,24},{1... | collective-permute-start | bytes 1966088 | tf_op jit(solution)/shard_map/ppermute | solution.py:597
  442.1 28.3 %collective-permute-start.122 = (bf16[20,128,128]{2,1,0:T(8,128)(2,1)S(1)}, bf16[20,128,128]{2,1,0:T(8,128)(2,1)S(1)}, u32[]{:S(2)}, u32[]{:S(2)}) collective-permute-start(bf16[20,128,128]{2,1,0:T(8,128)(2,1)S(1)} %fold.11), channel_id=1, source_target_pairs={{0,8},{1,9},{2,10},{3,11},{4,12},{5,13},{6,14},{7,15},{16,0},{17,1... | collective-permute-start | bytes 1966088 | tf_op jit(solution)/shard_map/ppermute | solution.py:597
  (195 other events, 2542.7 us)
